TPU v7x, 128 devices: a whole 4x4x4 slice. The times are simulated.
128 devices in a mesh: mat: 8 (over x, core), frac: 16 (over z, y).
Axes of the slice: x: 4, y: 4, z: 4, core: 2. Of those that a mesh axis runs over, the one named last changes fastest.
Arguments:
- pressure_start: float32 [128, 1024, 256], P('mat', 'frac'), may hold values from -6 to 6
- face_trans: float32 [3, 128, 1024, 256], P(None, 'mat', 'frac'), may hold values from 0.2 to 2
- cell_coef: float32 [128, 1024, 256], P('mat', 'frac'), may hold values from 0.05 to 0.5
- matrix_source: float32 [128, 1024, 256], P('mat', 'frac'), may hold values from -6 to 6
- mortar_owner: int32 [65536, 1], P(('mat', 'frac')), may hold values from 0 to 127; in each aligned block of 512 rows (0 to 511, 512 to 1023, ...) at most 8 rows name the same one
- mortar_cell: int32 [65536], P(('mat', 'frac')), may hold values from 0 to 262143
- mortar_frac: int32 [65536], P(('mat', 'frac')), may hold values from 0 to 16383
- mortar_kappa: float32 [65536], P(('mat', 'frac')), may hold values from 0.5 to 2
- tiles: float32 [128, 4, 128, 128], P('frac'), may hold values from -0.25 to 0.25
- tile_cols: int32 [128, 4], P('frac'), may hold values from 0 to 127
- frac_diag: float32 [16384], P('frac'), may hold values from 4 to 8
- frac_source: float32 [16384], P('frac'), may hold values from -6 to 6
- fracture_start: float32 [16384], P('frac'), may hold values from -6 to 6
Outputs:
- pressure: float32 [128, 1024, 256], P('mat', 'frac')
- fracture: float32 [16384], P('frac')
- flux: float32 [65536], P(('mat', 'frac'))
Inputs may be any that keep to these rules, and one draw needn't show every extreme that they name: `mortar_owner`: among the 512 mortar cells of one device, at most 8 name the same owner, and in some devices some owner is named exactly 8 times.
All inputs are finite; a program needn't handle non-finite values.
Results may differ from a plain program's by a relative error of at most 0.00015.
Values sent between devices are 32-bit elements; how exact they have to be, the bound alone decides.
No kernel may reach another device: no remote copies, remote signals or barrier semaphores. Data moves between devices by JAX's collectives and lax.ppermute only.
A program may use at most 128 MiB of HBM per device.

v0:
```python
import jax
import jax.numpy as jnp
from jax import lax
from jax.sharding import PartitionSpec as P

SWEEPS = 2
CG_ITERS = 3
OUTER = 2


relax_weight = 0.8


def with_halo(block, sides, width):
    for axis, dim in sides:
        count = lax.axis_size(axis)
        forward = [(i, i + 1) for i in range(count - 1)]
        backward = [(target, source) for source, target in forward]
        low = lax.ppermute(
            lax.slice_in_dim(block, block.shape[dim] - width, None, axis=dim), axis, forward
        )
        high = lax.ppermute(lax.slice_in_dim(block, 0, width, axis=dim), axis, backward)
        block = jnp.concatenate([low, block, high], axis=dim)
    return block


def copy_for_each(x, axis):
    length = lax.axis_size(axis)
    return lax.all_to_all(jnp.broadcast_to(x[None], (length, *x.shape)), axis, 0, 0, tiled=True)


def in_order(blocks, dim):
    lengths = list(blocks.shape[1:])
    lengths[dim] *= blocks.shape[0]
    return jnp.moveaxis(blocks, 0, dim).reshape(lengths)


def gather_directly(x, axis, dim):
    blocks = copy_for_each(x, axis)
    return in_order(blocks, dim)


def split_up(x, dim, length):
    lengths = x.shape
    blocks = x.reshape(*lengths[:dim], length, lengths[dim] // length, *lengths[dim + 1 :])
    return jnp.moveaxis(blocks, dim, 0)


def summed_on_arrival(x, axis, dim):
    length = lax.axis_size(axis)
    blocks = lax.all_to_all(split_up(x, dim, length), axis, 0, 0, tiled=True)
    return jnp.sum(blocks, axis=0)


def of_everyone(x, axis):
    return copy_for_each(x, axis).sum(axis=0)


def in_one(arrays, axis):
    ends = [0]
    for a in arrays:
        ends.append(ends[-1] + a.size)
    running = of_everyone(jnp.concatenate([a.ravel() for a in arrays]), axis)
    return tuple((running[b:e].reshape(a.shape) for a, b, e in zip(arrays, ends, ends[1:])))


def shift_next(values, along):
    padding = [(0, 0)] * values.ndim
    padding[along] = (0, 1)
    return lax.slice_in_dim(jnp.pad(values, padding), 1, values.shape[along] + 1, axis=along)


def shift_prev(values, along):
    padding = [(0, 0)] * values.ndim
    padding[along] = (1, 0)
    return lax.slice_in_dim(jnp.pad(values, padding), 0, values.shape[along], axis=along)


def relax(padded, coef_part, source_part, inside):
    centre = padded[1:-1, 1:-1]
    tx_here = coef_part[0, 1:-1, 1:-1]
    tx_low = coef_part[0, :-2, 1:-1]
    ty_here = coef_part[1, 1:-1, 1:-1]
    ty_low = coef_part[1, 1:-1, :-2]
    tz_here = coef_part[2, 1:-1, 1:-1]
    tz_low = shift_prev(tz_here, 2)
    cell_part = coef_part[3, 1:-1, 1:-1]
    base_part = coef_part[4, 1:-1, 1:-1]
    diagonal = cell_part + tx_here + tx_low + ty_here + ty_low + tz_here + tz_low
    diagonal = jnp.where(inside, diagonal, 1.0)
    applied = (
        diagonal * centre
        - tx_here * padded[2:, 1:-1]
        - tx_low * padded[:-2, 1:-1]
        - ty_here * padded[1:-1, 2:]
        - ty_low * padded[1:-1, :-2]
        - tz_here * shift_next(centre, 2)
        - tz_low * shift_prev(centre, 2)
    )
    updated = centre + relax_weight * (base_part + source_part - applied) / diagonal
    return jnp.where(inside, updated, 0.0)


def body(
    pressure_start,
    face_trans,
    cell_coef,
    matrix_source,
    mortar_owner,
    mortar_cell,
    mortar_frac,
    mortar_kappa,
    tiles,
    tile_cols,
    frac_diag,
    frac_source,
    fracture_start,
):
    width_x, width_y, depth_z = pressure_start.shape
    cells = width_x * width_y * depth_z
    mat_count = lax.axis_size("mat")
    frac_count = lax.axis_size("frac")
    devices = mat_count * frac_count
    row_mat = lax.axis_index("mat")
    row_frac = lax.axis_index("frac")
    size_b = tiles.shape[2]
    coefs = jnp.concatenate([face_trans, cell_coef[None], matrix_source[None]], 0)
    coef_ext = with_halo(coefs, (("mat", 1), ("frac", 2)), SWEEPS)
    owner = mortar_owner[:, 0]
    mortar_count = owner.shape[0]
    capacity = max(2, 2 * mortar_count // devices)
    hits = (owner[:, None] == jnp.arange(devices, dtype=jnp.int32)[None, :]).astype(jnp.int32)
    ranks = jnp.cumsum(hits, axis=0)
    slot = jnp.sum(ranks * hits, axis=1) - 1
    place = owner * capacity + slot
    index_slots = (
        jnp.full((devices * capacity,), cells, jnp.int32)
        .at[place]
        .set(mortar_cell)
        .reshape(devices, capacity)
    )
    asked = lax.all_to_all(index_slots, ("mat", "frac"), split_axis=0, concat_axis=0, tiled=True)
    asked_safe = jnp.minimum(asked, cells - 1)

    def fracture_apply(vector):
        whole = gather_directly(vector, "frac", 0)
        blocks = whole.reshape(-1, size_b)
        forward = jnp.einsum(
            "rtij,rtj->ri", tiles, blocks[tile_cols], precision=lax.Precision.HIGHEST
        )
        backward = jnp.einsum(
            "rtij,ri->rtj", tiles, vector.reshape(-1, size_b), precision=lax.Precision.HIGHEST
        )
        spread = jnp.zeros_like(blocks).at[tile_cols.reshape(-1)].add(backward.reshape(-1, size_b))
        returned = summed_on_arrival(spread, "frac", 0)
        return frac_diag * vector + 0.5 * (forward + returned).reshape(-1)

    def two_products(residual, image):
        return in_one((jnp.sum(residual * residual), jnp.sum(residual * image)), "frac")

    def solve_fracture(fracture, target):
        residual = target - fracture_apply(fracture)
        image = fracture_apply(residual)
        norm_now, product = two_products(residual, image)
        alpha = norm_now / product
        direction, along_image = (residual, image)
        for step in range(CG_ITERS):
            fracture = fracture + alpha * direction
            residual = residual - alpha * along_image
            if step + 1 < CG_ITERS:
                image = fracture_apply(residual)
                norm_next, product = two_products(residual, image)
                ratio = norm_next / norm_now
                alpha = norm_next / (product - ratio * norm_next / alpha)
                direction = residual + ratio * direction
                along_image = image + ratio * along_image
                norm_now = norm_next
        return fracture

    pressure = pressure_start
    fracture = fracture_start
    flux = jnp.zeros(mortar_kappa.shape, jnp.float32)
    for outer_no in range(OUTER):
        local_values = pressure.reshape(-1)[asked_safe]
        returned = lax.all_to_all(
            local_values, ("mat", "frac"), split_axis=0, concat_axis=0, tiled=True
        )
        trace = returned.reshape(-1)[place]
        fracture_whole = lax.all_gather(fracture, "frac", axis=0, tiled=True)
        flux = mortar_kappa * (trace - fracture_whole[mortar_frac])
        landed = jax.ops.segment_sum(flux, mortar_frac, num_segments=fracture_whole.shape[0])
        rows_part = summed_on_arrival(landed, "frac", 0)
        load = lax.psum(rows_part, "mat")
        fracture = solve_fracture(fracture, frac_source + load)
        flux_slots = (
            jnp.zeros((devices * capacity,), jnp.float32)
            .at[place]
            .set(flux)
            .reshape(devices, capacity)
        )
        arrived = lax.all_to_all(
            flux_slots, ("mat", "frac"), split_axis=0, concat_axis=0, tiled=True
        )
        source = jax.ops.segment_sum(
            arrived.reshape(-1), asked_safe.reshape(-1), num_segments=cells
        ).reshape(pressure.shape)
        stacked = with_halo(jnp.stack([pressure, source]), (("mat", 1), ("frac", 2)), SWEEPS)
        current = stacked[0]
        source_ext = stacked[1]
        for sweep_no in range(SWEEPS):
            span_x = current.shape[0]
            span_y = current.shape[1]
            coef_part = coef_ext[:, sweep_no : sweep_no + span_x, sweep_no : sweep_no + span_y]
            source_part = source_ext[
                sweep_no + 1 : sweep_no + span_x - 1, sweep_no + 1 : sweep_no + span_y - 1
            ]
            offset = SWEEPS - sweep_no - 1
            global_x = row_mat * width_x - offset + jnp.arange(span_x - 2)
            global_y = row_frac * width_y - offset + jnp.arange(span_y - 2)
            keep_x = (global_x >= 0) & (global_x < width_x * mat_count)
            keep_y = (global_y >= 0) & (global_y < width_y * frac_count)
            current = relax(
                current, coef_part, source_part, (keep_x[:, None] & keep_y[None, :])[:, :, None]
            )
        pressure = current
    return (pressure, fracture, flux)


def solution(mesh):
    in_specs = (
        P("mat", "frac", None),
        P(None, "mat", "frac", None),
        P("mat", "frac", None),
        P("mat", "frac", None),
        P(("mat", "frac"), None),
        P(("mat", "frac")),
        P(("mat", "frac")),
        P(("mat", "frac")),
        P("frac", None, None, None),
        P("frac", None),
        P("frac"),
        P("frac"),
        P("frac"),
    )
    out_specs = (P("mat", "frac", None), P("frac"), P(("mat", "frac")))
    return jax.shard_map(body, mesh=mesh, in_specs=in_specs, out_specs=out_specs, check_vma=False)
```

profile of v0, /device:TPU:32, one launch (start us, length us, event | category | flops | bytes accessed | tf_op | source)
XLA Modules:
  0.0 576.4 jit_solution(5136005277119866546)
XLA Ops:
  5.5 10.2 %all-to-all-start = ((s32[128,1,8]{2,1,0:T(1,128)}), s32[128,1,8]{2,1,0:T(1,128)S(1)}, u32[]{:S(2)}, u32[]{:S(2)}) async-start(s32[128,1,8]{2,1,0:T(1,128)} %bitcast.8), calls=%async_computation | async-start | bytes 131072 | tf_op jit(solution)/shard_map/all_to_all | solution.py:142
  30.0 6.2 %gather_fusion = f32[1024]{0:T(1024)S(1)} fusion(f32[262144]{0:T(1024)S(1)} %bitcast.386, s32[1024]{0:T(1024)S(1)} %broadcast_clamp_fusion), kind=kCustom, calls=%fused_computation | custom fusion | bytes 12288 | tf_op jit(solution)/shard_map/gather | solution.py:184
  36.9 9.9 %all-to-all-start.1 = ((f32[128,1,8]{2,1,0:T(1,128)}), f32[128,1,8]{2,1,0:T(1,128)S(1)}, u32[]{:S(2)}, u32[]{:S(2)}) async-start(f32[128,1,8]{2,1,0:T(1,128)} %bitcast.10), calls=%async_computation.1 | async-start | bytes 131072 | tf_op jit(solution)/shard_map/all_to_all | solution.py:185
  46.8 24.0 %all_gather.6 = f32[16384]{0:T(1024)S(1)} all-gather(f32[1024]{0:T(1024)S(1)} %copy-done.26), channel_id=1, replica_groups=mesh['mat'=8,'frac'=16] {'frac'}, dimensions={0}, use_global_device_ids=true | all-gather | bytes 69632 | tf_op jit(solution)/shard_map/all_gather | solution.py:189
  81.0 7.6 %all-to-all-start.2 = ((f32[128,1,8]{2,1,0:T(1,128)}), f32[128,1,8]{2,1,0:T(1,128)S(1)}, u32[]{:S(2)}, u32[]{:S(2)}) async-start(f32[128,1,8]{2,1,0:T(1,128)} %bitcast.11), calls=%async_computation.2 | async-start | bytes 131072 | tf_op jit(solution)/shard_map/all_to_all | solution.py:201
  89.4 8.3 %all-to-all-done.2 = f32[128,1,8]{2,1,0:T(1,128)S(1)} async-done(((f32[128,1,8]{2,1,0:T(1,128)}), f32[128,1,8]{2,1,0:T(1,128)S(1)}, u32[]{:S(2)}, u32[]{:S(2)}) %all-to-all-start.2) | async-done | bytes 4128 | tf_op jit(solution)/shard_map/all_to_all | solution.py:201
  98.4 4.5 all-to-all-start.5
  104.4 4.9 all-to-all-done.5
  109.2 4.8 all-to-all-start.6
  114.1 4.3 scatter_custom_fusion.3
  119.3 6.2 %scatter_custom_fusion.2 = f32[262144]{0:T(1024)S(1)} fusion(s32[1024]{0:T(1024)S(1)} %reshape.678, f32[1024]{0:T(1024)S(1)} %reshape.680, f32[]{:T(128)} %constant.26.clone.1), kind=kCustom, calls=%fused_computation.155 | custom fusion | flops 1024 | bytes 1048580 | tf_op jit(solution)/shard_map/scatter-add | solution.py:204
  127.4 7.3 %all-to-all-start.4 = ((f32[16,1,1024]{2,1,0:T(1,128)}), f32[16,1,1024]{2,1,0:T(1,128)S(1)}, u32[]{:S(2)}, u32[]{:S(2)}) async-start(f32[16,1,1024]{2,1,0:T(1,128)} %bitcast.30), calls=%async_computation.4 | async-start | bytes 131072 | tf_op jit(solution)/shard_map/all_to_all | solution.py:51
  136.5 4.4 all-to-all-done.4
  141.0 12.4 %psum.14 = f32[1024]{0:T(1024)S(1)} all-reduce(f32[1024]{0:T(1024)S(1)} %reduce_sum.262), channel_id=1, replica_groups=mesh['mat'=8,'frac'=16] {'mat'}, use_global_device_ids=true, to_apply=%region_8.9 | all-reduce | flops 1024 | bytes 8192 | tf_op jit(solution)/shard_map/psum | solution.py:193
  154.1 4.8 all-to-all-start.7
  165.2 4.8 all-to-all-start.8
  179.1 4.8 all-to-all-start.9
  192.5 4.9 all-to-all-start.10
  203.8 4.8 all-to-all-start.11
  217.4 4.8 all-to-all-start.12
  223.4 4.8 all-to-all-done.12
  234.0 5.2 all-to-all-start.13
  245.4 4.8 all-to-all-start.14
  259.2 4.8 all-to-all-start.15
  275.3 4.9 all-to-all-start.18
  281.3 4.7 collective-permute-start.3
  289.1 5.4 collective-permute-done.2
  312.0 5.9 %fusion.32 = (f32[18,66,256]{2,1,0:T(8,128)S(1)}, f32[18,66,256]{2,1,0:T(8,128)}) fusion(f32[18,66,256]{2,1,0:T(8,128)S(1)} %slice.378, f32[18,66,256]{2,1,0:T(8,128)S(1)} %slice_bitcast_fusion.4, f32[20,68,256]{2,1,0:T(8,128)S(1)} %get-tuple-element.29, f32[5,20,68,256]{3,2,1,0:T(8,128)S(1)} %pad_maximum_fusion, f32[20,68,256]{2,1,0:T(8,128)S(1)} %get-tuple-element.28, ...), kind=kLoop, calls=%fused_computation.95 | loop fusion | flops 9427968 | bytes 23790756 | tf_op jit(solution)/shard_map/jit(_where)/select_n | solution.py:101
  319.1 4.6 fusion.65
  325.3 6.2 %gather_fusion.3 = f32[1024]{0:T(1024)S(1)} fusion(f32[262144]{0:T(1024)S(1)} %bitcast.387, s32[1024]{0:T(1024)S(1)} %broadcast_clamp_fusion), kind=kCustom, calls=%fused_computation.3 | custom fusion | bytes 12288 | tf_op jit(solution)/shard_map/gather | solution.py:184
  332.2 4.6 all-to-all-start.3
  336.7 24.2 %all_gather.7 = f32[16384]{0:T(1024)S(1)} all-gather(f32[1024]{0:T(1024)S(1)} %multiply_add_fusion.1), channel_id=1, replica_groups=mesh['mat'=8,'frac'=16] {'frac'}, dimensions={0}, use_global_device_ids=true | all-gather | bytes 69632 | tf_op jit(solution)/shard_map/all_gather | solution.py:189
  366.1 5.4 all-to-all-start.19
  378.1 9.4 %all-to-all-start.16 = ((f32[128,1,8]{2,1,0:T(1,128)}), f32[128,1,8]{2,1,0:T(1,128)S(1)}, u32[]{:S(2)}, u32[]{:S(2)}) async-start(f32[128,1,8]{2,1,0:T(1,128)} %bitcast.100), calls=%async_computation.16 | async-start | bytes 131072 | tf_op jit(solution)/shard_map/all_to_all | solution.py:201
  396.7 4.5 all-to-all-start.17
  402.1 7.2 %scatter_custom_fusion.9 = f32[262144]{0:T(1024)} fusion(s32[1024]{0:T(1024)} %copy-done.49, f32[1024]{0:T(1024)S(1)} %reshape.736, f32[]{:T(128)} %constant.26.clone.1), kind=kCustom, calls=%fused_computation.153 | custom fusion | flops 1024 | bytes 1049088 | tf_op jit(solution)/shard_map/scatter-add | solution.py:204
  413.8 14.0 %psum.15 = f32[1024]{0:T(1024)S(1)} all-reduce(f32[1024]{0:T(1024)S(1)} %reduce_sum.276), channel_id=1, replica_groups=mesh['mat'=8,'frac'=16] {'mat'}, use_global_device_ids=true, to_apply=%region_30.31 | all-reduce | flops 1024 | bytes 8192 | tf_op jit(solution)/shard_map/psum | solution.py:193
  428.5 7.2 %all-to-all-start.20 = ((f32[16,1,1024]{2,1,0:T(1,128)}), f32[16,1,1024]{2,1,0:T(1,128)S(1)}, u32[]{:S(2)}, u32[]{:S(2)}) async-start(f32[16,1,1024]{2,1,0:T(1,128)} %broadcast_in_dim.112), calls=%async_computation.20 | async-start | bytes 131072 | tf_op jit(solution)/shard_map/all_to_all | solution.py:29
  442.0 4.8 all-to-all-start.21
  455.7 4.8 all-to-all-start.22
  461.8 4.8 all-to-all-done.22
  469.1 5.2 all-to-all-start.23
  480.6 4.8 all-to-all-start.24
  494.3 4.8 all-to-all-start.25
  510.8 4.9 all-to-all-start.26
  522.0 4.8 all-to-all-start.27
  535.1 10.7 %all_to_all.187 = f32[16,1,2]{2,1,0:T(1,128)S(1)} all-to-all(f32[16,1,2]{2,1,0:T(1,128)S(1)} %broadcast_in_dim.216), channel_id=1, replica_groups=mesh['mat'=8,'frac'=16] {'frac'}, dimensions={0} | all-to-all | bytes 256 | tf_op jit(solution)/shard_map/all_to_all | solution.py:29
  558.1 5.9 %collective-permute-done.10 = f32[2,20,2,256]{3,2,1,0:T(2,128)S(1)} collective-permute-done((f32[2,20,2,256]{3,2,1,0:T(2,128)S(1)}, f32[2,20,2,256]{3,2,1,0:T(2,128)S(1)}, u32[]{:S(2)}, u32[]{:S(2)}) %collective-permute-start.10) | collective-permute-done | bytes 81952 | tf_op jit(solution)/shard_map/ppermute | solution.py:19
  (322 shorter events, 228.2 us)
Async XLA Ops:
  2.2 75.6 %copy-start.45 = (s32[512,1]{0,1:T(1,128)}, s32[512,1]{0,1:T(1,128)S(1)}, u32[]{:S(2)}) copy-start(s32[512,1]{0,1:T(1,128)S(1)} %compare_select_fusion.1) | copy-start | bytes 6148
  5.5 24.1 %all-to-all-start = ((s32[128,1,8]{2,1,0:T(1,128)}), s32[128,1,8]{2,1,0:T(1,128)S(1)}, u32[]{:S(2)}, u32[]{:S(2)}) async-start(s32[128,1,8]{2,1,0:T(1,128)} %bitcast.8), calls=%async_computation | async-start | bytes 131072 | tf_op jit(solution)/shard_map/all_to_all | solution.py:142
  18.2 277.6 %collective-permute-start.5 = (f32[5,2,64,256]{3,2,1,0:T(8,128)}, f32[5,2,64,256]{3,2,1,0:T(8,128)}, u32[]{:S(2)}, u32[]{:S(2)}) collective-permute-start(f32[5,2,64,256]{3,2,1,0:T(8,128)} %get-tuple-element.25), channel_id=1, source_target_pairs={{16,0},{32,16},{48,32},{64,48},{80,64},{96,80},{112,96},{17,1},{33... | collective-permute-start | bytes 1966088 | tf_op jit(solution)/shard_map/ppermute | solution.py:22
  19.7 276.1 %collective-permute-start.4 = (f32[5,2,64,256]{3,2,1,0:T(8,128)}, f32[5,2,64,256]{3,2,1,0:T(8,128)}, u32[]{:S(2)}, u32[]{:S(2)}) collective-permute-start(f32[5,2,64,256]{3,2,1,0:T(8,128)} %get-tuple-element.24), channel_id=1, source_target_pairs={{0,16},{16,32},{32,48},{48,64},{64,80},{80,96},{96,112},{1,17},{17... | collective-permute-start | bytes 1966088 | tf_op jit(solution)/shard_map/ppermute | solution.py:19
  23.6 51.9 %copy-start.41 = (s32[1024]{0:T(1024)}, s32[1024]{0:T(1024)S(1)}, u32[]{:S(2)}) copy-start(s32[1024]{0:T(1024)S(1)} %pad_clamp_fusion.2) | copy-start | bytes 12292
  25.9 44.9 %copy-start.43 = (s32[1024]{0:T(1024)}, s32[1024]{0:T(1024)S(1)}, u32[]{:S(2)}) copy-start(s32[1024]{0:T(1024)S(1)} %pad_clamp_fusion.1) | copy-start | bytes 12292
  36.9 37.0 %all-to-all-start.1 = ((f32[128,1,8]{2,1,0:T(1,128)}), f32[128,1,8]{2,1,0:T(1,128)S(1)}, u32[]{:S(2)}, u32[]{:S(2)}) async-start(f32[128,1,8]{2,1,0:T(1,128)} %bitcast.10), calls=%async_computation.1 | async-start | bytes 131072 | tf_op jit(solution)/shard_map/all_to_all | solution.py:185
  81.0 16.7 %all-to-all-start.2 = ((f32[128,1,8]{2,1,0:T(1,128)}), f32[128,1,8]{2,1,0:T(1,128)S(1)}, u32[]{:S(2)}, u32[]{:S(2)}) async-start(f32[128,1,8]{2,1,0:T(1,128)} %bitcast.11), calls=%async_computation.2 | async-start | bytes 131072 | tf_op jit(solution)/shard_map/all_to_all | solution.py:201
  98.4 10.8 %all-to-all-start.5 = ((f32[16,1,1024]{2,1,0:T(1,128)}), f32[16,1,1024]{2,1,0:T(1,128)S(1)}, u32[]{:S(2)}, u32[]{:S(2)}) async-start(f32[16,1,1024]{2,1,0:T(1,128)} %broadcast_in_dim.103), calls=%async_computation.5 | async-start | bytes 131072 | tf_op jit(solution)/shard_map/all_to_all | solution.py:29
  102.9 137.4 %copy-start.52 = (s32[32]{0:T(128)}, s32[32]{0:T(128)S(1)}, u32[]{:S(2)}) copy-start(s32[32]{0:T(128)S(1)} %fusion.106) | copy-start | bytes 388
  109.2 18.2 %all-to-all-start.6 = ((f32[16,8,128]{2,1,0:T(8,128)}), f32[16,8,128]{2,1,0:T(8,128)S(1)}, u32[]{:S(2)}, u32[]{:S(2)}) async-start(f32[16,8,128]{2,1,0:T(8,128)} %bitcast.44), calls=%async_computation.6 | async-start | bytes 131072 | tf_op jit(solution)/shard_map/all_to_all | solution.py:51
  127.4 13.5 %all-to-all-start.4 = ((f32[16,1,1024]{2,1,0:T(1,128)}), f32[16,1,1024]{2,1,0:T(1,128)S(1)}, u32[]{:S(2)}, u32[]{:S(2)}) async-start(f32[16,1,1024]{2,1,0:T(1,128)} %bitcast.30), calls=%async_computation.4 | async-start | bytes 131072 | tf_op jit(solution)/shard_map/all_to_all | solution.py:51
  153.4 38.4 %copy-start.24 = (f32[1024]{0:T(1024)}, f32[1024]{0:T(1024)S(1)}, u32[]{:S(2)}) copy-start(f32[1024]{0:T(1024)S(1)} %fusion.99) | copy-start | bytes 12292
  154.1 11.1 %all-to-all-start.7 = ((f32[16,1,1024]{2,1,0:T(1,128)}), f32[16,1,1024]{2,1,0:T(1,128)S(1)}, u32[]{:S(2)}, u32[]{:S(2)}) async-start(f32[16,1,1024]{2,1,0:T(1,128)} %broadcast_in_dim.105), calls=%async_computation.7 | async-start | bytes 131072 | tf_op jit(solution)/shard_map/all_to_all | solution.py:29
  165.2 11.1 %all-to-all-start.8 = ((f32[16,8,128]{2,1,0:T(8,128)}), f32[16,8,128]{2,1,0:T(8,128)S(1)}, u32[]{:S(2)}, u32[]{:S(2)}) async-start(f32[16,8,128]{2,1,0:T(8,128)} %bitcast.59), calls=%async_computation.8 | async-start | bytes 131072 | tf_op jit(solution)/shard_map/all_to_all | solution.py:51
  179.1 10.8 %all-to-all-start.9 = ((f32[16,1,2]{2,1,0:T(1,128)}), f32[16,1,2]{2,1,0:T(1,128)S(1)}, u32[]{:S(2)}, u32[]{:S(2)}) async-start(f32[16,1,2]{2,1,0:T(1,128)} %broadcast_in_dim.106), calls=%async_computation.9 | async-start | bytes 16384 | tf_op jit(solution)/shard_map/all_to_all | solution.py:29
  192.5 11.2 %all-to-all-start.10 = ((f32[16,1,1024]{2,1,0:T(1,128)}), f32[16,1,1024]{2,1,0:T(1,128)S(1)}, u32[]{:S(2)}, u32[]{:S(2)}) async-start(f32[16,1,1024]{2,1,0:T(1,128)} %broadcast_in_dim.107), calls=%async_computation.10 | async-start | bytes 131072 | tf_op jit(solution)/shard_map/all_to_all | solution.py:29
  203.8 11.1 %all-to-all-start.11 = ((f32[16,8,128]{2,1,0:T(8,128)}), f32[16,8,128]{2,1,0:T(8,128)S(1)}, u32[]{:S(2)}, u32[]{:S(2)}) async-start(f32[16,8,128]{2,1,0:T(8,128)} %bitcast.77), calls=%async_computation.11 | async-start | bytes 131072 | tf_op jit(solution)/shard_map/all_to_all | solution.py:51
  217.4 10.8 %all-to-all-start.12 = ((f32[16,1,2]{2,1,0:T(1,128)}), f32[16,1,2]{2,1,0:T(1,128)S(1)}, u32[]{:S(2)}, u32[]{:S(2)}) async-start(f32[16,1,2]{2,1,0:T(1,128)} %broadcast_in_dim.108), calls=%async_computation.12 | async-start | bytes 16384 | tf_op jit(solution)/shard_map/all_to_all | solution.py:29
  222.1 58.1 %collective-permute-start.1 = (f32[2,2,64,256]{3,2,1,0:T(8,128)}, f32[2,2,64,256]{3,2,1,0:T(8,128)S(1)}, u32[]{:S(2)}, u32[]{:S(2)}) collective-permute-start(f32[2,2,64,256]{3,2,1,0:T(8,128)} %get-tuple-element.37), channel_id=1, source_target_pairs={{16,0},{32,16},{48,32},{64,48},{80,64},{96,80},{112,96},{17,1},{33... | collective-permute-start | bytes 786440 | tf_op jit(solution)/shard_map/ppermute | solution.py:22
  234.0 11.4 %all-to-all-start.13 = ((f32[16,1,1024]{2,1,0:T(1,128)}), f32[16,1,1024]{2,1,0:T(1,128)S(1)}, u32[]{:S(2)}, u32[]{:S(2)}) async-start(f32[16,1,1024]{2,1,0:T(1,128)} %broadcast_in_dim.109), calls=%async_computation.13 | async-start | bytes 131072 | tf_op jit(solution)/shard_map/all_to_all | solution.py:29
  245.4 11.1 %all-to-all-start.14 = ((f32[16,8,128]{2,1,0:T(8,128)}), f32[16,8,128]{2,1,0:T(8,128)S(1)}, u32[]{:S(2)}, u32[]{:S(2)}) async-start(f32[16,8,128]{2,1,0:T(8,128)} %bitcast.95), calls=%async_computation.14 | async-start | bytes 131072 | tf_op jit(solution)/shard_map/all_to_all | solution.py:51
  259.2 10.8 %all-to-all-start.15 = ((f32[16,1,2]{2,1,0:T(1,128)}), f32[16,1,2]{2,1,0:T(1,128)S(1)}, u32[]{:S(2)}, u32[]{:S(2)}) async-start(f32[16,1,2]{2,1,0:T(1,128)} %broadcast_in_dim.110), calls=%async_computation.15 | async-start | bytes 16384 | tf_op jit(solution)/shard_map/all_to_all | solution.py:29
  263.9 16.3 %collective-permute-start = (f32[2,2,64,256]{3,2,1,0:T(8,128)}, f32[2,2,64,256]{3,2,1,0:T(8,128)}, u32[]{:S(2)}, u32[]{:S(2)}) collective-permute-start(f32[2,2,64,256]{3,2,1,0:T(8,128)} %get-tuple-element.36), channel_id=1, source_target_pairs={{0,16},{16,32},{32,48},{48,64},{64,80},{80,96},{96,112},{1,17},{17... | collective-permute-start | bytes 786440 | tf_op jit(solution)/shard_map/ppermute | solution.py:19
  274.6 153.2 %copy-start.22 = (f32[1024]{0:T(1024)}, f32[1024]{0:T(1024)S(1)}, u32[]{:S(2)}) copy-start(f32[1024]{0:T(1024)S(1)} %multiply_add_fusion.1) | copy-start | bytes 12292
  275.3 56.9 %all-to-all-start.18 = ((f32[16,1,1024]{2,1,0:T(1,128)}), f32[16,1,1024]{2,1,0:T(1,128)S(1)}, u32[]{:S(2)}, u32[]{:S(2)}) async-start(f32[16,1,1024]{2,1,0:T(1,128)} %broadcast_in_dim.111), calls=%async_computation.18 | async-start | bytes 131072 | tf_op jit(solution)/shard_map/all_to_all | solution.py:29
  281.3 7.8 %collective-permute-start.3 = (f32[2,20,2,256]{3,2,1,0:T(2,128)S(1)}, f32[2,20,2,256]{3,2,1,0:T(2,128)S(1)}, u32[]{:S(2)}, u32[]{:S(2)}) collective-permute-start(f32[2,20,2,256]{3,2,1,0:T(2,128)S(1)} %get-tuple-element.33), channel_id=1, source_target_pairs={{1,0},{2,1},{3,2},{4,3},{5,4},{6,5},{7,6},{8,7},{9,8},{10,9},{11,1... | collective-permute-start | bytes 245768 | tf_op jit(solution)/shard_map/ppermute | solution.py:22
  286.0 8.4 %collective-permute-start.2 = (f32[2,20,2,256]{3,2,1,0:T(2,128)S(1)}, f32[2,20,2,256]{3,2,1,0:T(2,128)S(1)}, u32[]{:S(2)}, u32[]{:S(2)}) collective-permute-start(f32[2,20,2,256]{3,2,1,0:T(2,128)S(1)} %get-tuple-element.32), channel_id=1, source_target_pairs={{0,1},{1,2},{2,3},{3,4},{4,5},{5,6},{6,7},{7,8},{8,9},{9,10},{10,1... | collective-permute-start | bytes 245768 | tf_op jit(solution)/shard_map/ppermute | solution.py:19
  297.0 7.7 %collective-permute-start.7 = (f32[5,20,2,256]{3,2,1,0:T(2,128)S(1)}, f32[5,20,2,256]{3,2,1,0:T(2,128)S(1)}, u32[]{:S(2)}, u32[]{:S(2)}) collective-permute-start(f32[5,20,2,256]{3,2,1,0:T(2,128)S(1)} %get-tuple-element.23), channel_id=1, source_target_pairs={{1,0},{2,1},{3,2},{4,3},{5,4},{6,5},{7,6},{8,7},{9,8},{10,9},{11,1... | collective-permute-start | bytes 614408 | tf_op jit(solution)/shard_map/ppermute | solution.py:22
  299.0 9.8 %collective-permute-start.6 = (f32[5,20,2,256]{3,2,1,0:T(2,128)S(1)}, f32[5,20,2,256]{3,2,1,0:T(2,128)S(1)}, u32[]{:S(2)}, u32[]{:S(2)}) collective-permute-start(f32[5,20,2,256]{3,2,1,0:T(2,128)S(1)} %get-tuple-element.22), channel_id=1, source_target_pairs={{0,1},{1,2},{2,3},{3,4},{4,5},{5,6},{6,7},{7,8},{8,9},{9,10},{10,1... | collective-permute-start | bytes 614408 | tf_op jit(solution)/shard_map/ppermute | solution.py:19
  325.3 35.7 %copy-start.44 = (s32[1024]{0:T(1024)S(1)}, s32[1024]{0:T(1024)}, u32[]{:S(2)}) copy-start(s32[1024]{0:T(1024)} %copy-done.43) | copy-start | bytes 12292
  331.4 41.0 %copy-start.42 = (s32[1024]{0:T(1024)S(1)}, s32[1024]{0:T(1024)}, u32[]{:S(2)}) copy-start(s32[1024]{0:T(1024)} %copy-done.41) | copy-start | bytes 12292
  332.2 33.9 %all-to-all-start.3 = ((f32[128,1,8]{2,1,0:T(1,128)}), f32[128,1,8]{2,1,0:T(1,128)S(1)}, u32[]{:S(2)}, u32[]{:S(2)}) async-start(f32[128,1,8]{2,1,0:T(1,128)} %bitcast.29), calls=%async_computation.3 | async-start | bytes 131072 | tf_op jit(solution)/shard_map/all_to_all | solution.py:185
  366.1 12.0 %all-to-all-start.19 = ((f32[16,8,128]{2,1,0:T(8,128)}), f32[16,8,128]{2,1,0:T(8,128)S(1)}, u32[]{:S(2)}, u32[]{:S(2)}) async-start(f32[16,8,128]{2,1,0:T(8,128)} %bitcast.116), calls=%async_computation.19 | async-start | bytes 131072 | tf_op jit(solution)/shard_map/all_to_all | solution.py:51
  378.1 18.6 %all-to-all-start.16 = ((f32[128,1,8]{2,1,0:T(1,128)}), f32[128,1,8]{2,1,0:T(1,128)S(1)}, u32[]{:S(2)}, u32[]{:S(2)}) async-start(f32[128,1,8]{2,1,0:T(1,128)} %bitcast.100), calls=%async_computation.16 | async-start | bytes 131072 | tf_op jit(solution)/shard_map/all_to_all | solution.py:201
  396.7 17.1 %all-to-all-start.17 = ((f32[16,1,1024]{2,1,0:T(1,128)}), f32[16,1,1024]{2,1,0:T(1,128)S(1)}, u32[]{:S(2)}, u32[]{:S(2)}) async-start(f32[16,1,1024]{2,1,0:T(1,128)} %bitcast.103), calls=%async_computation.17 | async-start | bytes 131072 | tf_op jit(solution)/shard_map/all_to_all | solution.py:51
  428.5 13.5 %all-to-all-start.20 = ((f32[16,1,1024]{2,1,0:T(1,128)}), f32[16,1,1024]{2,1,0:T(1,128)S(1)}, u32[]{:S(2)}, u32[]{:S(2)}) async-start(f32[16,1,1024]{2,1,0:T(1,128)} %broadcast_in_dim.112), calls=%async_computation.20 | async-start | bytes 131072 | tf_op jit(solution)/shard_map/all_to_all | solution.py:29
  442.0 11.1 %all-to-all-start.21 = ((f32[16,8,128]{2,1,0:T(8,128)}), f32[16,8,128]{2,1,0:T(8,128)S(1)}, u32[]{:S(2)}, u32[]{:S(2)}) async-start(f32[16,8,128]{2,1,0:T(8,128)} %bitcast.131), calls=%async_computation.21 | async-start | bytes 131072 | tf_op jit(solution)/shard_map/all_to_all | solution.py:51
  455.7 10.8 %all-to-all-start.22 = ((f32[16,1,2]{2,1,0:T(1,128)}), f32[16,1,2]{2,1,0:T(1,128)S(1)}, u32[]{:S(2)}, u32[]{:S(2)}) async-start(f32[16,1,2]{2,1,0:T(1,128)} %broadcast_in_dim.113), calls=%async_computation.22 | async-start | bytes 16384 | tf_op jit(solution)/shard_map/all_to_all | solution.py:29
  460.5 89.9 %collective-permute-start.9 = (f32[2,2,64,256]{3,2,1,0:T(8,128)}, f32[2,2,64,256]{3,2,1,0:T(8,128)S(1)}, u32[]{:S(2)}, u32[]{:S(2)}) collective-permute-start(f32[2,2,64,256]{3,2,1,0:T(8,128)} %get-tuple-element.35), channel_id=1, source_target_pairs={{16,0},{32,16},{48,32},{64,48},{80,64},{96,80},{112,96},{17,1},{33... | collective-permute-start | bytes 786440 | tf_op jit(solution)/shard_map/ppermute | solution.py:22
  469.1 11.5 %all-to-all-start.23 = ((f32[16,1,1024]{2,1,0:T(1,128)}), f32[16,1,1024]{2,1,0:T(1,128)S(1)}, u32[]{:S(2)}, u32[]{:S(2)}) async-start(f32[16,1,1024]{2,1,0:T(1,128)} %broadcast_in_dim.114), calls=%async_computation.23 | async-start | bytes 131072 | tf_op jit(solution)/shard_map/all_to_all | solution.py:29
  480.6 11.1 %all-to-all-start.24 = ((f32[16,8,128]{2,1,0:T(8,128)}), f32[16,8,128]{2,1,0:T(8,128)S(1)}, u32[]{:S(2)}, u32[]{:S(2)}) async-start(f32[16,8,128]{2,1,0:T(8,128)} %bitcast.149), calls=%async_computation.24 | async-start | bytes 131072 | tf_op jit(solution)/shard_map/all_to_all | solution.py:51
  494.3 10.8 %all-to-all-start.25 = ((f32[16,1,2]{2,1,0:T(1,128)}), f32[16,1,2]{2,1,0:T(1,128)S(1)}, u32[]{:S(2)}, u32[]{:S(2)}) async-start(f32[16,1,2]{2,1,0:T(1,128)} %broadcast_in_dim.214), calls=%async_computation.25 | async-start | bytes 16384 | tf_op jit(solution)/shard_map/all_to_all | solution.py:29
  499.0 51.4 %collective-permute-start.8 = (f32[2,2,64,256]{3,2,1,0:T(8,128)}, f32[2,2,64,256]{3,2,1,0:T(8,128)}, u32[]{:S(2)}, u32[]{:S(2)}) collective-permute-start(f32[2,2,64,256]{3,2,1,0:T(8,128)} %get-tuple-element.34), channel_id=1, source_target_pairs={{0,16},{16,32},{32,48},{48,64},{64,80},{80,96},{96,112},{1,17},{17... | collective-permute-start | bytes 786440 | tf_op jit(solution)/shard_map/ppermute | solution.py:19
  510.8 11.2 %all-to-all-start.26 = ((f32[16,1,1024]{2,1,0:T(1,128)}), f32[16,1,1024]{2,1,0:T(1,128)S(1)}, u32[]{:S(2)}, u32[]{:S(2)}) async-start(f32[16,1,1024]{2,1,0:T(1,128)} %broadcast_in_dim.215), calls=%async_computation.26 | async-start | bytes 131072 | tf_op jit(solution)/shard_map/all_to_all | solution.py:29
  522.0 11.1 %all-to-all-start.27 = ((f32[16,8,128]{2,1,0:T(8,128)}), f32[16,8,128]{2,1,0:T(8,128)S(1)}, u32[]{:S(2)}, u32[]{:S(2)}) async-start(f32[16,8,128]{2,1,0:T(8,128)} %bitcast.167), calls=%async_computation.27 | async-start | bytes 131072 | tf_op jit(solution)/shard_map/all_to_all | solution.py:51
  551.6 6.5 %collective-permute-start.11 = (f32[2,20,2,256]{3,2,1,0:T(2,128)S(1)}, f32[2,20,2,256]{3,2,1,0:T(2,128)S(1)}, u32[]{:S(2)}, u32[]{:S(2)}) collective-permute-start(f32[2,20,2,256]{3,2,1,0:T(2,128)S(1)} %get-tuple-element.31), channel_id=1, source_target_pairs={{1,0},{2,1},{3,2},{4,3},{5,4},{6,5},{7,6},{8,7},{9,8},{10,9},{11,1... | collective-permute-start | bytes 245768 | tf_op jit(solution)/shard_map/ppermute | solution.py:22
  555.6 8.4 %collective-permute-start.10 = (f32[2,20,2,256]{3,2,1,0:T(2,128)S(1)}, f32[2,20,2,256]{3,2,1,0:T(2,128)S(1)}, u32[]{:S(2)}, u32[]{:S(2)}) collective-permute-start(f32[2,20,2,256]{3,2,1,0:T(2,128)S(1)} %get-tuple-element.30), channel_id=1, source_target_pairs={{0,1},{1,2},{2,3},{3,4},{4,5},{5,6},{6,7},{7,8},{8,9},{9,10},{10,1... | collective-permute-start | bytes 245768 | tf_op jit(solution)/shard_map/ppermute | solution.py:19
  (47 other events, 458.4 us)
where the time goes:
time: 587 us; the launch traced here: 576 us
  starting transfers between devices  188 us (32%)
  waiting for transfers between devices  103 us (18%)
  blocking collectives  85.4 us (15%)
  other arithmetic  82.5 us (14%)
  local copies, waits for them, and re-layouts  70.8 us (12%)
  matrix products  25.7 us (4%)
  between operations  21.6 us (4%)
    all_to_all x13, starting transfers between devices, copy_for_each(): lax.all_to_all(jnp.broadcast_to(x[None], (length, *x.shape)), axis, 0, 0,...  65.4 us
    all_to_all x10, starting transfers between devices, summed_on_arrival(): blocks = lax.all_to_all(split_up(x, dim, length), axis, 0, 0, tiled=True)  50.7 us
    all_to_all x13, waiting for transfers between devices, copy_for_each(): lax.all_to_all(jnp.broadcast_to(x[None], (length, *x.shape)), axis, 0, 0,...  49.9 us
    all_gather x2, blocking collectives, body(): fracture_whole = lax.all_gather(fracture, 'frac', axis=0, tiled=True)  48.2 us
    psum x2, blocking collectives, body(): load = lax.psum(rows_part, 'mat')  26.5 us
    all_to_all x10, waiting for transfers between devices, summed_on_arrival(): blocks = lax.all_to_all(split_up(x, dim, length), axis, 0, 0, tiled=True)  24 us
    all_to_all x2, starting transfers between devices, body(): lax.all_to_all(flux_slots, ('mat', 'frac'), split_axis=0, concat_axis=0,...  16.9 us
    dot_general x8, matrix products, fracture_apply(): jnp.einsum('rtij,rtj->ri', tiles, blocks[tile_cols], precision=lax.Precis...  16.8 us
  transfers between devices with their start and end apart: 40, of which 25 were waited for; matrix products, arithmetic and copies ran while one was open for 26% of the time, Pallas kernels for 0%

commit v1 on v0

--- a/solution.py
+++ b/solution.py
@@ -129,9 +129,9 @@
     owner = mortar_owner[:, 0]
     mortar_count = owner.shape[0]
     capacity = max(2, 2 * mortar_count // devices)
-    hits = (owner[:, None] == jnp.arange(devices, dtype=jnp.int32)[None, :]).astype(jnp.int32)
-    ranks = jnp.cumsum(hits, axis=0)
-    slot = jnp.sum(ranks * hits, axis=1) - 1
+    rows = jnp.arange(mortar_count, dtype=jnp.int32)
+    earlier = (owner[:, None] == owner[None, :]) & (rows[None, :] < rows[:, None])
+    slot = jnp.sum(earlier.astype(jnp.int32), axis=1)
     place = owner * capacity + slot
     index_slots = (
         jnp.full((devices * capacity,), cells, jnp.int32)

time: 587 us -> 587 us (level)
  no operation moved by 1% of the time
where the time goes in v1:
time: 587 us; the launch traced here: 577 us
  starting transfers between devices  188 us (32%)
  waiting for transfers between devices  103 us (18%)
  blocking collectives  85.4 us (15%)
  other arithmetic  83.8 us (14%)
  local copies, waits for them, and re-layouts  69.9 us (12%)
  matrix products  25.7 us (4%)
  between operations  21.5 us (4%)
    all_to_all x13, starting transfers between devices, copy_for_each(): lax.all_to_all(jnp.broadcast_to(x[None], (length, *x.shape)), axis, 0, 0,...  65.3 us
    all_to_all x10, starting transfers between devices, summed_on_arrival(): blocks = lax.all_to_all(split_up(x, dim, length), axis, 0, 0, tiled=True)  50.7 us
    all_to_all x13, waiting for transfers between devices, copy_for_each(): lax.all_to_all(jnp.broadcast_to(x[None], (length, *x.shape)), axis, 0, 0,...  49.9 us
    all_gather x2, blocking collectives, body(): fracture_whole = lax.all_gather(fracture, 'frac', axis=0, tiled=True)  48.2 us
    psum x2, blocking collectives, body(): load = lax.psum(rows_part, 'mat')  26.5 us
    all_to_all x10, waiting for transfers between devices, summed_on_arrival(): blocks = lax.all_to_all(split_up(x, dim, length), axis, 0, 0, tiled=True)  24 us
    all_to_all x2, starting transfers between devices, body(): lax.all_to_all(flux_slots, ('mat', 'frac'), split_axis=0, concat_axis=0,...  16.9 us
    dot_general x8, matrix products, fracture_apply(): jnp.einsum('rtij,rtj->ri', tiles, blocks[tile_cols], precision=lax.Precis...  16.8 us
  transfers between devices with their start and end apart: 40, of which 25 were waited for; matrix products, arithmetic and copies ran while one was open for 26% of the time, Pallas kernels for 0%

profile of v1, /device:TPU:32, one launch (start us, length us, event | category | flops | bytes accessed | tf_op | source)
XLA Modules:
  0.0 576.7 jit_solution(12743596823609701940)
XLA Ops:
  5.8 10.2 %all-to-all-start = ((s32[128,1,8]{2,1,0:T(1,128)}), s32[128,1,8]{2,1,0:T(1,128)S(1)}, u32[]{:S(2)}, u32[]{:S(2)}) async-start(s32[128,1,8]{2,1,0:T(1,128)} %bitcast.4), calls=%async_computation | async-start | bytes 131072 | tf_op jit(solution)/shard_map/all_to_all | solution.py:142
  30.4 6.2 %gather_fusion = f32[1024]{0:T(1024)S(1)} fusion(f32[262144]{0:T(1024)S(1)} %bitcast.374, s32[1024]{0:T(1024)S(1)} %broadcast_clamp_fusion), kind=kCustom, calls=%fused_computation | custom fusion | bytes 12288 | tf_op jit(solution)/shard_map/gather | solution.py:184
  37.2 9.9 %all-to-all-start.1 = ((f32[128,1,8]{2,1,0:T(1,128)}), f32[128,1,8]{2,1,0:T(1,128)S(1)}, u32[]{:S(2)}, u32[]{:S(2)}) async-start(f32[128,1,8]{2,1,0:T(1,128)} %bitcast.6), calls=%async_computation.1 | async-start | bytes 131072 | tf_op jit(solution)/shard_map/all_to_all | solution.py:185
  47.1 24.0 %all_gather.6 = f32[16384]{0:T(1024)S(1)} all-gather(f32[1024]{0:T(1024)S(1)} %copy-done.25), channel_id=1, replica_groups=mesh['mat'=8,'frac'=16] {'frac'}, dimensions={0}, use_global_device_ids=true | all-gather | bytes 69632 | tf_op jit(solution)/shard_map/all_gather | solution.py:189
  81.3 7.6 %all-to-all-start.2 = ((f32[128,1,8]{2,1,0:T(1,128)}), f32[128,1,8]{2,1,0:T(1,128)S(1)}, u32[]{:S(2)}, u32[]{:S(2)}) async-start(f32[128,1,8]{2,1,0:T(1,128)} %bitcast.7), calls=%async_computation.2 | async-start | bytes 131072 | tf_op jit(solution)/shard_map/all_to_all | solution.py:201
  89.7 8.3 %all-to-all-done.2 = f32[128,1,8]{2,1,0:T(1,128)S(1)} async-done(((f32[128,1,8]{2,1,0:T(1,128)}), f32[128,1,8]{2,1,0:T(1,128)S(1)}, u32[]{:S(2)}, u32[]{:S(2)}) %all-to-all-start.2) | async-done | bytes 4128 | tf_op jit(solution)/shard_map/all_to_all | solution.py:201
  98.7 4.5 all-to-all-start.5
  104.7 4.9 all-to-all-done.5
  109.6 4.8 all-to-all-start.6
  114.5 4.3 scatter_custom_fusion.3
  119.7 6.2 %scatter_custom_fusion.2 = f32[262144]{0:T(1024)S(1)} fusion(s32[1024]{0:T(1024)S(1)} %reshape.654, f32[1024]{0:T(1024)S(1)} %reshape.656, f32[]{:T(128)} %constant.26.clone.1), kind=kCustom, calls=%fused_computation.158 | custom fusion | flops 1024 | bytes 1048580 | tf_op jit(solution)/shard_map/scatter-add | solution.py:204
  127.7 7.3 %all-to-all-start.4 = ((f32[16,1,1024]{2,1,0:T(1,128)}), f32[16,1,1024]{2,1,0:T(1,128)S(1)}, u32[]{:S(2)}, u32[]{:S(2)}) async-start(f32[16,1,1024]{2,1,0:T(1,128)} %bitcast.26), calls=%async_computation.4 | async-start | bytes 131072 | tf_op jit(solution)/shard_map/all_to_all | solution.py:51
  136.9 4.4 all-to-all-done.4
  141.3 12.4 %psum.14 = f32[1024]{0:T(1024)S(1)} all-reduce(f32[1024]{0:T(1024)S(1)} %reduce_sum.265), channel_id=1, replica_groups=mesh['mat'=8,'frac'=16] {'mat'}, use_global_device_ids=true, to_apply=%region_6.0 | all-reduce | flops 1024 | bytes 8192 | tf_op jit(solution)/shard_map/psum | solution.py:193
  154.4 4.8 all-to-all-start.7
  165.6 4.8 all-to-all-start.8
  179.4 4.8 all-to-all-start.9
  192.9 4.9 all-to-all-start.10
  204.1 4.8 all-to-all-start.11
  217.7 4.8 all-to-all-start.12
  223.8 4.8 all-to-all-done.12
  234.3 5.2 all-to-all-start.13
  245.7 4.8 all-to-all-start.14
  259.5 4.8 all-to-all-start.15
  275.6 4.9 all-to-all-start.18
  281.7 4.7 collective-permute-start.3
  289.4 5.4 collective-permute-done.2
  312.4 5.9 %fusion.32 = (f32[18,66,256]{2,1,0:T(8,128)S(1)}, f32[18,66,256]{2,1,0:T(8,128)}) fusion(f32[18,66,256]{2,1,0:T(8,128)S(1)} %slice.369, f32[18,66,256]{2,1,0:T(8,128)S(1)} %slice_bitcast_fusion.4, f32[20,68,256]{2,1,0:T(8,128)S(1)} %get-tuple-element.29, f32[5,20,68,256]{3,2,1,0:T(8,128)S(1)} %pad_maximum_fusion, f32[20,68,256]{2,1,0:T(8,128)S(1)} %get-tuple-element.28, ...), kind=kLoop, calls=%fused_computation.95 | loop fusion | flops 9427968 | bytes 23790756 | tf_op jit(solution)/shard_map/jit(_where)/select_n | solution.py:101
  319.5 4.5 fusion.66
  325.5 6.2 %gather_fusion.3 = f32[1024]{0:T(1024)S(1)} fusion(f32[262144]{0:T(1024)S(1)} %bitcast.375, s32[1024]{0:T(1024)S(1)} %broadcast_clamp_fusion), kind=kCustom, calls=%fused_computation.3 | custom fusion | bytes 12288 | tf_op jit(solution)/shard_map/gather | solution.py:184
  332.4 4.6 all-to-all-start.3
  337.0 24.2 %all_gather.7 = f32[16384]{0:T(1024)S(1)} all-gather(f32[1024]{0:T(1024)S(1)} %multiply_add_fusion.1), channel_id=1, replica_groups=mesh['mat'=8,'frac'=16] {'frac'}, dimensions={0}, use_global_device_ids=true | all-gather | bytes 69632 | tf_op jit(solution)/shard_map/all_gather | solution.py:189
  366.3 5.4 all-to-all-start.19
  378.3 9.4 %all-to-all-start.16 = ((f32[128,1,8]{2,1,0:T(1,128)}), f32[128,1,8]{2,1,0:T(1,128)S(1)}, u32[]{:S(2)}, u32[]{:S(2)}) async-start(f32[128,1,8]{2,1,0:T(1,128)} %bitcast.96), calls=%async_computation.16 | async-start | bytes 131072 | tf_op jit(solution)/shard_map/all_to_all | solution.py:201
  396.9 4.5 all-to-all-start.17
  402.4 7.2 %scatter_custom_fusion.9 = f32[262144]{0:T(1024)} fusion(s32[1024]{0:T(1024)} %copy-done.47, f32[1024]{0:T(1024)S(1)} %reshape.712, f32[]{:T(128)} %constant.26.clone.1), kind=kCustom, calls=%fused_computation.156 | custom fusion | flops 1024 | bytes 1049088 | tf_op jit(solution)/shard_map/scatter-add | solution.py:204
  414.0 14.1 %psum.15 = f32[1024]{0:T(1024)S(1)} all-reduce(f32[1024]{0:T(1024)S(1)} %reduce_sum.279), channel_id=1, replica_groups=mesh['mat'=8,'frac'=16] {'mat'}, use_global_device_ids=true, to_apply=%region_28.29 | all-reduce | flops 1024 | bytes 8192 | tf_op jit(solution)/shard_map/psum | solution.py:193
  428.8 7.2 %all-to-all-start.20 = ((f32[16,1,1024]{2,1,0:T(1,128)}), f32[16,1,1024]{2,1,0:T(1,128)S(1)}, u32[]{:S(2)}, u32[]{:S(2)}) async-start(f32[16,1,1024]{2,1,0:T(1,128)} %broadcast_in_dim.112), calls=%async_computation.20 | async-start | bytes 131072 | tf_op jit(solution)/shard_map/all_to_all | solution.py:29
  442.3 4.8 all-to-all-start.21
  456.0 4.8 all-to-all-start.22
  462.0 4.8 all-to-all-done.22
  469.4 5.2 all-to-all-start.23
  480.8 4.8 all-to-all-start.24
  494.5 4.8 all-to-all-start.25
  511.1 4.9 all-to-all-start.26
  522.3 4.8 all-to-all-start.27
  535.4 10.7 %all_to_all.187 = f32[16,1,2]{2,1,0:T(1,128)S(1)} all-to-all(f32[16,1,2]{2,1,0:T(1,128)S(1)} %broadcast_in_dim.217), channel_id=1, replica_groups=mesh['mat'=8,'frac'=16] {'frac'}, dimensions={0} | all-to-all | bytes 256 | tf_op jit(solution)/shard_map/all_to_all | solution.py:29
  558.4 5.9 %collective-permute-done.10 = f32[2,20,2,256]{3,2,1,0:T(2,128)S(1)} collective-permute-done((f32[2,20,2,256]{3,2,1,0:T(2,128)S(1)}, f32[2,20,2,256]{3,2,1,0:T(2,128)S(1)}, u32[]{:S(2)}, u32[]{:S(2)}) %collective-permute-start.10) | collective-permute-done | bytes 81952 | tf_op jit(solution)/shard_map/ppermute | solution.py:19
  (309 shorter events, 228.7 us)
Async XLA Ops:
  2.4 75.7 %copy-start.43 = (s32[512,1]{0,1:T(1,128)}, s32[512,1]{0,1:T(1,128)S(1)}, u32[]{:S(2)}) copy-start(s32[512,1]{0,1:T(1,128)S(1)} %compare_select_fusion.1) | copy-start | bytes 6148
  5.8 24.3 %all-to-all-start = ((s32[128,1,8]{2,1,0:T(1,128)}), s32[128,1,8]{2,1,0:T(1,128)S(1)}, u32[]{:S(2)}, u32[]{:S(2)}) async-start(s32[128,1,8]{2,1,0:T(1,128)} %bitcast.4), calls=%async_computation | async-start | bytes 131072 | tf_op jit(solution)/shard_map/all_to_all | solution.py:142
  18.6 277.5 %collective-permute-start.5 = (f32[5,2,64,256]{3,2,1,0:T(8,128)}, f32[5,2,64,256]{3,2,1,0:T(8,128)}, u32[]{:S(2)}, u32[]{:S(2)}) collective-permute-start(f32[5,2,64,256]{3,2,1,0:T(8,128)} %get-tuple-element.25), channel_id=1, source_target_pairs={{16,0},{32,16},{48,32},{64,48},{80,64},{96,80},{112,96},{17,1},{33... | collective-permute-start | bytes 1966088 | tf_op jit(solution)/shard_map/ppermute | solution.py:22
  20.0 276.1 %collective-permute-start.4 = (f32[5,2,64,256]{3,2,1,0:T(8,128)}, f32[5,2,64,256]{3,2,1,0:T(8,128)}, u32[]{:S(2)}, u32[]{:S(2)}) collective-permute-start(f32[5,2,64,256]{3,2,1,0:T(8,128)} %get-tuple-element.24), channel_id=1, source_target_pairs={{0,16},{16,32},{32,48},{48,64},{64,80},{80,96},{96,112},{1,17},{17... | collective-permute-start | bytes 1966088 | tf_op jit(solution)/shard_map/ppermute | solution.py:19
  23.9 51.9 %copy-start.39 = (s32[1024]{0:T(1024)}, s32[1024]{0:T(1024)S(1)}, u32[]{:S(2)}) copy-start(s32[1024]{0:T(1024)S(1)} %pad_clamp_fusion.2) | copy-start | bytes 12292
  26.3 44.9 %copy-start.41 = (s32[1024]{0:T(1024)}, s32[1024]{0:T(1024)S(1)}, u32[]{:S(2)}) copy-start(s32[1024]{0:T(1024)S(1)} %pad_clamp_fusion.1) | copy-start | bytes 12292
  37.2 37.0 %all-to-all-start.1 = ((f32[128,1,8]{2,1,0:T(1,128)}), f32[128,1,8]{2,1,0:T(1,128)S(1)}, u32[]{:S(2)}, u32[]{:S(2)}) async-start(f32[128,1,8]{2,1,0:T(1,128)} %bitcast.6), calls=%async_computation.1 | async-start | bytes 131072 | tf_op jit(solution)/shard_map/all_to_all | solution.py:185
  81.3 16.7 %all-to-all-start.2 = ((f32[128,1,8]{2,1,0:T(1,128)}), f32[128,1,8]{2,1,0:T(1,128)S(1)}, u32[]{:S(2)}, u32[]{:S(2)}) async-start(f32[128,1,8]{2,1,0:T(1,128)} %bitcast.7), calls=%async_computation.2 | async-start | bytes 131072 | tf_op jit(solution)/shard_map/all_to_all | solution.py:201
  98.7 10.8 %all-to-all-start.5 = ((f32[16,1,1024]{2,1,0:T(1,128)}), f32[16,1,1024]{2,1,0:T(1,128)S(1)}, u32[]{:S(2)}, u32[]{:S(2)}) async-start(f32[16,1,1024]{2,1,0:T(1,128)} %broadcast_in_dim.103), calls=%async_computation.5 | async-start | bytes 131072 | tf_op jit(solution)/shard_map/all_to_all | solution.py:29
  103.2 137.3 %copy-start.50 = (s32[32]{0:T(128)}, s32[32]{0:T(128)S(1)}, u32[]{:S(2)}) copy-start(s32[32]{0:T(128)S(1)} %fusion.103) | copy-start | bytes 388
  109.6 18.2 %all-to-all-start.6 = ((f32[16,8,128]{2,1,0:T(8,128)}), f32[16,8,128]{2,1,0:T(8,128)S(1)}, u32[]{:S(2)}, u32[]{:S(2)}) async-start(f32[16,8,128]{2,1,0:T(8,128)} %bitcast.40), calls=%async_computation.6 | async-start | bytes 131072 | tf_op jit(solution)/shard_map/all_to_all | solution.py:51
  127.7 13.5 %all-to-all-start.4 = ((f32[16,1,1024]{2,1,0:T(1,128)}), f32[16,1,1024]{2,1,0:T(1,128)S(1)}, u32[]{:S(2)}, u32[]{:S(2)}) async-start(f32[16,1,1024]{2,1,0:T(1,128)} %bitcast.26), calls=%async_computation.4 | async-start | bytes 131072 | tf_op jit(solution)/shard_map/all_to_all | solution.py:51
  153.8 38.4 %copy-start.23 = (f32[1024]{0:T(1024)}, f32[1024]{0:T(1024)S(1)}, u32[]{:S(2)}) copy-start(f32[1024]{0:T(1024)S(1)} %fusion.96) | copy-start | bytes 12292
  154.4 11.1 %all-to-all-start.7 = ((f32[16,1,1024]{2,1,0:T(1,128)}), f32[16,1,1024]{2,1,0:T(1,128)S(1)}, u32[]{:S(2)}, u32[]{:S(2)}) async-start(f32[16,1,1024]{2,1,0:T(1,128)} %broadcast_in_dim.105), calls=%async_computation.7 | async-start | bytes 131072 | tf_op jit(solution)/shard_map/all_to_all | solution.py:29
  165.6 11.1 %all-to-all-start.8 = ((f32[16,8,128]{2,1,0:T(8,128)}), f32[16,8,128]{2,1,0:T(8,128)S(1)}, u32[]{:S(2)}, u32[]{:S(2)}) async-start(f32[16,8,128]{2,1,0:T(8,128)} %bitcast.55), calls=%async_computation.8 | async-start | bytes 131072 | tf_op jit(solution)/shard_map/all_to_all | solution.py:51
  179.4 10.8 %all-to-all-start.9 = ((f32[16,1,2]{2,1,0:T(1,128)}), f32[16,1,2]{2,1,0:T(1,128)S(1)}, u32[]{:S(2)}, u32[]{:S(2)}) async-start(f32[16,1,2]{2,1,0:T(1,128)} %broadcast_in_dim.106), calls=%async_computation.9 | async-start | bytes 16384 | tf_op jit(solution)/shard_map/all_to_all | solution.py:29
  192.9 11.2 %all-to-all-start.10 = ((f32[16,1,1024]{2,1,0:T(1,128)}), f32[16,1,1024]{2,1,0:T(1,128)S(1)}, u32[]{:S(2)}, u32[]{:S(2)}) async-start(f32[16,1,1024]{2,1,0:T(1,128)} %broadcast_in_dim.107), calls=%async_computation.10 | async-start | bytes 131072 | tf_op jit(solution)/shard_map/all_to_all | solution.py:29
  204.1 11.1 %all-to-all-start.11 = ((f32[16,8,128]{2,1,0:T(8,128)}), f32[16,8,128]{2,1,0:T(8,128)S(1)}, u32[]{:S(2)}, u32[]{:S(2)}) async-start(f32[16,8,128]{2,1,0:T(8,128)} %bitcast.73), calls=%async_computation.11 | async-start | bytes 131072 | tf_op jit(solution)/shard_map/all_to_all | solution.py:51
  217.7 10.8 %all-to-all-start.12 = ((f32[16,1,2]{2,1,0:T(1,128)}), f32[16,1,2]{2,1,0:T(1,128)S(1)}, u32[]{:S(2)}, u32[]{:S(2)}) async-start(f32[16,1,2]{2,1,0:T(1,128)} %broadcast_in_dim.108), calls=%async_computation.12 | async-start | bytes 16384 | tf_op jit(solution)/shard_map/all_to_all | solution.py:29
  222.5 58.1 %collective-permute-start.1 = (f32[2,2,64,256]{3,2,1,0:T(8,128)}, f32[2,2,64,256]{3,2,1,0:T(8,128)S(1)}, u32[]{:S(2)}, u32[]{:S(2)}) collective-permute-start(f32[2,2,64,256]{3,2,1,0:T(8,128)} %get-tuple-element.37), channel_id=1, source_target_pairs={{16,0},{32,16},{48,32},{64,48},{80,64},{96,80},{112,96},{17,1},{33... | collective-permute-start | bytes 786440 | tf_op jit(solution)/shard_map/ppermute | solution.py:22
  234.3 11.4 %all-to-all-start.13 = ((f32[16,1,1024]{2,1,0:T(1,128)}), f32[16,1,1024]{2,1,0:T(1,128)S(1)}, u32[]{:S(2)}, u32[]{:S(2)}) async-start(f32[16,1,1024]{2,1,0:T(1,128)} %broadcast_in_dim.109), calls=%async_computation.13 | async-start | bytes 131072 | tf_op jit(solution)/shard_map/all_to_all | solution.py:29
  245.7 11.1 %all-to-all-start.14 = ((f32[16,8,128]{2,1,0:T(8,128)}), f32[16,8,128]{2,1,0:T(8,128)S(1)}, u32[]{:S(2)}, u32[]{:S(2)}) async-start(f32[16,8,128]{2,1,0:T(8,128)} %bitcast.91), calls=%async_computation.14 | async-start | bytes 131072 | tf_op jit(solution)/shard_map/all_to_all | solution.py:51
  259.5 10.8 %all-to-all-start.15 = ((f32[16,1,2]{2,1,0:T(1,128)}), f32[16,1,2]{2,1,0:T(1,128)S(1)}, u32[]{:S(2)}, u32[]{:S(2)}) async-start(f32[16,1,2]{2,1,0:T(1,128)} %broadcast_in_dim.110), calls=%async_computation.15 | async-start | bytes 16384 | tf_op jit(solution)/shard_map/all_to_all | solution.py:29
  264.3 16.3 %collective-permute-start = (f32[2,2,64,256]{3,2,1,0:T(8,128)}, f32[2,2,64,256]{3,2,1,0:T(8,128)}, u32[]{:S(2)}, u32[]{:S(2)}) collective-permute-start(f32[2,2,64,256]{3,2,1,0:T(8,128)} %get-tuple-element.36), channel_id=1, source_target_pairs={{0,16},{16,32},{32,48},{48,64},{64,80},{80,96},{96,112},{1,17},{17... | collective-permute-start | bytes 786440 | tf_op jit(solution)/shard_map/ppermute | solution.py:19
  275.0 153.1 %copy-start.21 = (f32[1024]{0:T(1024)}, f32[1024]{0:T(1024)S(1)}, u32[]{:S(2)}) copy-start(f32[1024]{0:T(1024)S(1)} %multiply_add_fusion.1) | copy-start | bytes 12292
  275.6 56.8 %all-to-all-start.18 = ((f32[16,1,1024]{2,1,0:T(1,128)}), f32[16,1,1024]{2,1,0:T(1,128)S(1)}, u32[]{:S(2)}, u32[]{:S(2)}) async-start(f32[16,1,1024]{2,1,0:T(1,128)} %broadcast_in_dim.111), calls=%async_computation.18 | async-start | bytes 131072 | tf_op jit(solution)/shard_map/all_to_all | solution.py:29
  281.7 7.8 %collective-permute-start.3 = (f32[2,20,2,256]{3,2,1,0:T(2,128)S(1)}, f32[2,20,2,256]{3,2,1,0:T(2,128)S(1)}, u32[]{:S(2)}, u32[]{:S(2)}) collective-permute-start(f32[2,20,2,256]{3,2,1,0:T(2,128)S(1)} %get-tuple-element.33), channel_id=1, source_target_pairs={{1,0},{2,1},{3,2},{4,3},{5,4},{6,5},{7,6},{8,7},{9,8},{10,9},{11,1... | collective-permute-start | bytes 245768 | tf_op jit(solution)/shard_map/ppermute | solution.py:22
  286.4 8.4 %collective-permute-start.2 = (f32[2,20,2,256]{3,2,1,0:T(2,128)S(1)}, f32[2,20,2,256]{3,2,1,0:T(2,128)S(1)}, u32[]{:S(2)}, u32[]{:S(2)}) collective-permute-start(f32[2,20,2,256]{3,2,1,0:T(2,128)S(1)} %get-tuple-element.32), channel_id=1, source_target_pairs={{0,1},{1,2},{2,3},{3,4},{4,5},{5,6},{6,7},{7,8},{8,9},{9,10},{10,1... | collective-permute-start | bytes 245768 | tf_op jit(solution)/shard_map/ppermute | solution.py:19
  297.3 7.7 %collective-permute-start.7 = (f32[5,20,2,256]{3,2,1,0:T(2,128)S(1)}, f32[5,20,2,256]{3,2,1,0:T(2,128)S(1)}, u32[]{:S(2)}, u32[]{:S(2)}) collective-permute-start(f32[5,20,2,256]{3,2,1,0:T(2,128)S(1)} %get-tuple-element.23), channel_id=1, source_target_pairs={{1,0},{2,1},{3,2},{4,3},{5,4},{6,5},{7,6},{8,7},{9,8},{10,9},{11,1... | collective-permute-start | bytes 614408 | tf_op jit(solution)/shard_map/ppermute | solution.py:22
  299.3 9.8 %collective-permute-start.6 = (f32[5,20,2,256]{3,2,1,0:T(2,128)S(1)}, f32[5,20,2,256]{3,2,1,0:T(2,128)S(1)}, u32[]{:S(2)}, u32[]{:S(2)}) collective-permute-start(f32[5,20,2,256]{3,2,1,0:T(2,128)S(1)} %get-tuple-element.22), channel_id=1, source_target_pairs={{0,1},{1,2},{2,3},{3,4},{4,5},{5,6},{6,7},{7,8},{8,9},{9,10},{10,1... | collective-permute-start | bytes 614408 | tf_op jit(solution)/shard_map/ppermute | solution.py:19
  325.5 35.7 %copy-start.42 = (s32[1024]{0:T(1024)S(1)}, s32[1024]{0:T(1024)}, u32[]{:S(2)}) copy-start(s32[1024]{0:T(1024)} %copy-done.41) | copy-start | bytes 12292
  331.7 41.0 %copy-start.40 = (s32[1024]{0:T(1024)S(1)}, s32[1024]{0:T(1024)}, u32[]{:S(2)}) copy-start(s32[1024]{0:T(1024)} %copy-done.39) | copy-start | bytes 12292
  332.4 33.9 %all-to-all-start.3 = ((f32[128,1,8]{2,1,0:T(1,128)}), f32[128,1,8]{2,1,0:T(1,128)S(1)}, u32[]{:S(2)}, u32[]{:S(2)}) async-start(f32[128,1,8]{2,1,0:T(1,128)} %bitcast.25), calls=%async_computation.3 | async-start | bytes 131072 | tf_op jit(solution)/shard_map/all_to_all | solution.py:185
  366.3 12.0 %all-to-all-start.19 = ((f32[16,8,128]{2,1,0:T(8,128)}), f32[16,8,128]{2,1,0:T(8,128)S(1)}, u32[]{:S(2)}, u32[]{:S(2)}) async-start(f32[16,8,128]{2,1,0:T(8,128)} %bitcast.112), calls=%async_computation.19 | async-start | bytes 131072 | tf_op jit(solution)/shard_map/all_to_all | solution.py:51
  378.3 18.6 %all-to-all-start.16 = ((f32[128,1,8]{2,1,0:T(1,128)}), f32[128,1,8]{2,1,0:T(1,128)S(1)}, u32[]{:S(2)}, u32[]{:S(2)}) async-start(f32[128,1,8]{2,1,0:T(1,128)} %bitcast.96), calls=%async_computation.16 | async-start | bytes 131072 | tf_op jit(solution)/shard_map/all_to_all | solution.py:201
  396.9 17.0 %all-to-all-start.17 = ((f32[16,1,1024]{2,1,0:T(1,128)}), f32[16,1,1024]{2,1,0:T(1,128)S(1)}, u32[]{:S(2)}, u32[]{:S(2)}) async-start(f32[16,1,1024]{2,1,0:T(1,128)} %bitcast.99), calls=%async_computation.17 | async-start | bytes 131072 | tf_op jit(solution)/shard_map/all_to_all | solution.py:51
  428.8 13.5 %all-to-all-start.20 = ((f32[16,1,1024]{2,1,0:T(1,128)}), f32[16,1,1024]{2,1,0:T(1,128)S(1)}, u32[]{:S(2)}, u32[]{:S(2)}) async-start(f32[16,1,1024]{2,1,0:T(1,128)} %broadcast_in_dim.112), calls=%async_computation.20 | async-start | bytes 131072 | tf_op jit(solution)/shard_map/all_to_all | solution.py:29
  442.3 11.1 %all-to-all-start.21 = ((f32[16,8,128]{2,1,0:T(8,128)}), f32[16,8,128]{2,1,0:T(8,128)S(1)}, u32[]{:S(2)}, u32[]{:S(2)}) async-start(f32[16,8,128]{2,1,0:T(8,128)} %bitcast.127), calls=%async_computation.21 | async-start | bytes 131072 | tf_op jit(solution)/shard_map/all_to_all | solution.py:51
  456.0 10.8 %all-to-all-start.22 = ((f32[16,1,2]{2,1,0:T(1,128)}), f32[16,1,2]{2,1,0:T(1,128)S(1)}, u32[]{:S(2)}, u32[]{:S(2)}) async-start(f32[16,1,2]{2,1,0:T(1,128)} %broadcast_in_dim.113), calls=%async_computation.22 | async-start | bytes 16384 | tf_op jit(solution)/shard_map/all_to_all | solution.py:29
  460.7 89.9 %collective-permute-start.9 = (f32[2,2,64,256]{3,2,1,0:T(8,128)}, f32[2,2,64,256]{3,2,1,0:T(8,128)S(1)}, u32[]{:S(2)}, u32[]{:S(2)}) collective-permute-start(f32[2,2,64,256]{3,2,1,0:T(8,128)} %get-tuple-element.35), channel_id=1, source_target_pairs={{16,0},{32,16},{48,32},{64,48},{80,64},{96,80},{112,96},{17,1},{33... | collective-permute-start | bytes 786440 | tf_op jit(solution)/shard_map/ppermute | solution.py:22
  469.4 11.5 %all-to-all-start.23 = ((f32[16,1,1024]{2,1,0:T(1,128)}), f32[16,1,1024]{2,1,0:T(1,128)S(1)}, u32[]{:S(2)}, u32[]{:S(2)}) async-start(f32[16,1,1024]{2,1,0:T(1,128)} %broadcast_in_dim.114), calls=%async_computation.23 | async-start | bytes 131072 | tf_op jit(solution)/shard_map/all_to_all | solution.py:29
  480.8 11.1 %all-to-all-start.24 = ((f32[16,8,128]{2,1,0:T(8,128)}), f32[16,8,128]{2,1,0:T(8,128)S(1)}, u32[]{:S(2)}, u32[]{:S(2)}) async-start(f32[16,8,128]{2,1,0:T(8,128)} %bitcast.145), calls=%async_computation.24 | async-start | bytes 131072 | tf_op jit(solution)/shard_map/all_to_all | solution.py:51
  494.5 10.8 %all-to-all-start.25 = ((f32[16,1,2]{2,1,0:T(1,128)}), f32[16,1,2]{2,1,0:T(1,128)S(1)}, u32[]{:S(2)}, u32[]{:S(2)}) async-start(f32[16,1,2]{2,1,0:T(1,128)} %broadcast_in_dim.115), calls=%async_computation.25 | async-start | bytes 16384 | tf_op jit(solution)/shard_map/all_to_all | solution.py:29
  499.3 51.4 %collective-permute-start.8 = (f32[2,2,64,256]{3,2,1,0:T(8,128)}, f32[2,2,64,256]{3,2,1,0:T(8,128)}, u32[]{:S(2)}, u32[]{:S(2)}) collective-permute-start(f32[2,2,64,256]{3,2,1,0:T(8,128)} %get-tuple-element.34), channel_id=1, source_target_pairs={{0,16},{16,32},{32,48},{48,64},{64,80},{80,96},{96,112},{1,17},{17... | collective-permute-start | bytes 786440 | tf_op jit(solution)/shard_map/ppermute | solution.py:19
  511.1 11.2 %all-to-all-start.26 = ((f32[16,1,1024]{2,1,0:T(1,128)}), f32[16,1,1024]{2,1,0:T(1,128)S(1)}, u32[]{:S(2)}, u32[]{:S(2)}) async-start(f32[16,1,1024]{2,1,0:T(1,128)} %broadcast_in_dim.216), calls=%async_computation.26 | async-start | bytes 131072 | tf_op jit(solution)/shard_map/all_to_all | solution.py:29
  522.3 11.1 %all-to-all-start.27 = ((f32[16,8,128]{2,1,0:T(8,128)}), f32[16,8,128]{2,1,0:T(8,128)S(1)}, u32[]{:S(2)}, u32[]{:S(2)}) async-start(f32[16,8,128]{2,1,0:T(8,128)} %bitcast.163), calls=%async_computation.27 | async-start | bytes 131072 | tf_op jit(solution)/shard_map/all_to_all | solution.py:51
  551.8 6.5 %collective-permute-start.11 = (f32[2,20,2,256]{3,2,1,0:T(2,128)S(1)}, f32[2,20,2,256]{3,2,1,0:T(2,128)S(1)}, u32[]{:S(2)}, u32[]{:S(2)}) collective-permute-start(f32[2,20,2,256]{3,2,1,0:T(2,128)S(1)} %get-tuple-element.31), channel_id=1, source_target_pairs={{1,0},{2,1},{3,2},{4,3},{5,4},{6,5},{7,6},{8,7},{9,8},{10,9},{11,1... | collective-permute-start | bytes 245768 | tf_op jit(solution)/shard_map/ppermute | solution.py:22
  555.8 8.4 %collective-permute-start.10 = (f32[2,20,2,256]{3,2,1,0:T(2,128)S(1)}, f32[2,20,2,256]{3,2,1,0:T(2,128)S(1)}, u32[]{:S(2)}, u32[]{:S(2)}) collective-permute-start(f32[2,20,2,256]{3,2,1,0:T(2,128)S(1)} %get-tuple-element.30), channel_id=1, source_target_pairs={{0,1},{1,2},{2,3},{3,4},{4,5},{5,6},{6,7},{7,8},{8,9},{9,10},{10,1... | collective-permute-start | bytes 245768 | tf_op jit(solution)/shard_map/ppermute | solution.py:19
  (45 other events, 442.3 us)

commit v2 on v1

v2 whole, which is shorter than its diff:
```python
import functools

import jax
import jax.numpy as jnp
from jax import lax
from jax.experimental import pallas as pl
from jax.experimental.pallas import tpu as pltpu
from jax.sharding import PartitionSpec as P

WEIGHT = 0.8
CAP = 8
LANES = 128
F32 = jnp.float32
BF16 = jnp.bfloat16
VMEM = pl.BlockSpec(memory_space=pltpu.VMEM)
SMEM = pl.BlockSpec(memory_space=pltpu.SMEM)
X, Y, Z, HI, LO, KAPPA, COLS = (CAP * i for i in range(7))


def shape(*dims, dtype=F32):
    return jax.ShapeDtypeStruct(dims, dtype)


def call(body, outs, in_specs, flops=1e6, nbytes=1e6, scratch=(), name=None, **more):
    return pl.pallas_call(
        body,
        out_shape=outs,
        in_specs=in_specs,
        scratch_shapes=scratch,
        compiler_params=pltpu.CompilerParams(vmem_limit_bytes=32 << 20),
        cost_estimate=pl.CostEstimate(
            flops=int(flops), bytes_accessed=int(nbytes), transcendentals=0
        ),
        name=name,
        **more,
    )


def iota(dims, dim):
    return lax.broadcasted_iota(jnp.int32, dims, dim)


def ones_where(mask):
    return jnp.where(mask, 1.0, 0.0).astype(BF16)


def split(v):
    top = v.astype(BF16)
    rest = v - top.astype(F32)
    middle = rest.astype(BF16)
    low = (rest - middle.astype(F32)).astype(BF16)
    return jnp.concatenate([top, middle, low], axis=1)


def pick(chosen, v):
    width = v.shape[1]
    out = jnp.dot(chosen, split(v), preferred_element_type=F32)
    return out[:, :width] + out[:, width : 2 * width] + out[:, 2 * width :]


def total(v):
    return jnp.sum(jnp.sum(v, axis=1, keepdims=True), axis=0, keepdims=True)


def row_sums(v):
    return jnp.sum(v.T, axis=0, keepdims=True)


def as_column(row):
    return jnp.broadcast_to(row, (LANES, LANES)).T


def pack_body(at, cols, owner_col, owner, cell, frac, kappa, x_own, send, slot_out, blocks):
    count = owner.shape[1]
    mine = at[0]
    own = owner[...]
    earlier = (owner_col[...] == own) & (iota((count, count), 0) < iota((count, count), 1))
    slot = jnp.sum(jnp.where(earlier, 1, 0), axis=0, keepdims=True)
    slot_out[...] = slot
    here = iota((CAP, count), 0) == slot
    c, f = cell[...], frac[...]
    k = kappa[...]
    top = k.astype(BF16).astype(F32)
    middle = (k - top).astype(BF16).astype(F32)
    low = k - top - middle
    whole = [c >> 14, (c >> 8) & 63, c & 255, f >> 7, f & 127]
    rows = [jnp.where(here, v.astype(F32), 0.0) for v in whole]
    rows = jnp.concatenate([*rows, jnp.where(here, top, 0.0), jnp.zeros((LANES - 6 * CAP, count), F32)], axis=0)
    chosen = ones_where(iota((LANES, count), 0) == own)
    nt = functools.partial(
        lax.dot_general,
        dimension_numbers=(((1,), (1,)), ((), ())),
        preferred_element_type=F32,
    )

    def kappas(v):
        return jnp.concatenate(
            [
                jnp.zeros((KAPPA, count), F32),
                jnp.where(here, v, 0.0),
                jnp.zeros((LANES - 6 * CAP, count), F32),
            ],
            axis=0,
        ).astype(BF16)

    message = nt(chosen, rows.astype(BF16)) + nt(chosen, kappas(middle)) + nt(chosen, kappas(low))
    lane = iota((1, LANES), 1)
    extra = jnp.zeros((1, LANES), F32)
    for t in range(cols.shape[1]):
        extra = jnp.where(lane == COLS + t, cols[mine, t].astype(F32), extra)
    blocks[...] = jnp.broadcast_to(x_own[pl.ds(mine, 1), :], (LANES, LANES))
    send[pl.ds(0, LANES, stride=2), :] = blocks[...]
    send[pl.ds(1, LANES, stride=2), :] = message + extra


def by_slot(message, k):
    x = message[:, X + k : X + k + 1].astype(jnp.int32)
    y = message[:, Y + k : Y + k + 1].astype(jnp.int32)
    z = message[:, Z + k : Z + k + 1].astype(jnp.int32)
    hi = message[:, HI + k : HI + k + 1].astype(jnp.int32)
    lo = message[:, LO + k : LO + k + 1].astype(jnp.int32)
    return x * 64 + y, z, hi, lo, message[:, KAPPA + k : KAPPA + k + 1]


def traces(message, pressure, gathered):
    rows, depth = pressure.shape
    chosen = jnp.concatenate(
        [ones_where(iota((LANES, rows), 1) == by_slot(message, k)[0]) for k in range(CAP)], axis=0
    )
    gathered[...] = pick(chosen, pressure)
    lane = iota((LANES, LANES), 1)
    out = jnp.zeros((LANES, LANES), F32)
    for k in range(CAP):
        z = by_slot(message, k)[1]
        part = gathered[k * LANES : (k + 1) * LANES, :]
        value = jnp.sum(jnp.where(iota((LANES, depth), 1) == z, part, 0.0), axis=1, keepdims=True)
        out = jnp.where(lane == k, value, out)
    return out


def at_mortar(message, x):
    chosen = jnp.concatenate(
        [ones_where(iota((LANES, LANES), 1) == by_slot(message, k)[2]) for k in range(CAP)], axis=0
    )
    found = pick(chosen, x)
    lane = iota((LANES, LANES), 1)
    out = jnp.zeros((LANES, LANES), F32)
    for k in range(CAP):
        part = found[k * LANES : (k + 1) * LANES, :]
        value = jnp.sum(jnp.where(lane == by_slot(message, k)[3], part, 0.0), axis=1, keepdims=True)
        out = jnp.where(lane == k, value, out)
    return out


def onto_fracture(message, *values):
    flipped = message.T
    hi = jnp.concatenate([flipped[HI + k : HI + k + 1, :] for k in range(CAP)], axis=1)
    chosen = ones_where(iota((LANES, CAP * LANES), 0) == hi.astype(jnp.int32))
    lane = iota((LANES, LANES), 1)
    wide = []
    for v in values:
        spread = [
            jnp.where(lane == by_slot(message, k)[3], v[:, k : k + 1], 0.0) for k in range(CAP)
        ]
        wide.append(jnp.concatenate(spread, axis=0))
    return [pick(chosen, v) for v in wide]


def kappa_of(message):
    lane = iota((LANES, LANES), 1)
    out = jnp.zeros((LANES, LANES), F32)
    for k in range(CAP):
        out = jnp.where(lane == k, message[:, KAPPA + k : KAPPA + k + 1], out)
    return out


def first_body(
    at, cols, got, pressure, tiles, diag, source, send, x_out, trace_out, flux_out, gathered, part
):
    mine, shard = at[0], at[1]
    groups = LANES // CAP
    for m in range(CAP):
        x_out[pl.ds(m, groups, stride=CAP), :] = got[
            pl.ds(2 * m * groups, groups, stride=2), :
        ]
    message = got[pl.ds(1, LANES, stride=2), :]
    trace = traces(message, pressure[...], gathered)
    kappa = kappa_of(message)
    flux = kappa * (trace - at_mortar(message, x_out[...]))
    load, weight = onto_fracture(message, flux, kappa)
    part[...] = load
    row = CAP * shard + mine
    x_row = x_out[pl.ds(row, 1), :]
    x_col = as_column(x_row)
    mixed = jnp.zeros((LANES, LANES), F32)
    for t in range(cols.shape[1]):
        tile = tiles[0, t]
        mixed += tile * x_out[pl.ds(cols[mine, t], 1), :]
        back = jnp.sum(tile * x_col, axis=0, keepdims=True)
        part[pl.ds(cols[mine, t], 1), :] -= 0.5 * back
    part[pl.ds(row, 1), :] += source[pl.ds(mine, 1), :] - (
        diag[pl.ds(mine, 1), :] * x_row + 0.5 * row_sums(mixed)
    )
    send[pl.ds(0, LANES, stride=2), :] = part[...]
    send[pl.ds(1, LANES, stride=2), :] = weight
    trace_out[...] = trace
    flux_out[...] = flux


def source_body(got, flux, base, rhs):
    message = got[pl.ds(1, LANES, stride=2), :]
    rows, depth = base.shape
    flipped = message.T
    cell_row = jnp.concatenate(
        [flipped[X + k : X + k + 1, :] * 64 + flipped[Y + k : Y + k + 1, :] for k in range(CAP)],
        axis=1,
    )
    chosen = ones_where(iota((rows, CAP * LANES), 0) == cell_row.astype(jnp.int32))
    spread = jnp.concatenate(
        [
            jnp.where(iota((LANES, depth), 1) == by_slot(message, k)[1], flux[:, k : k + 1], 0.0)
            for k in range(CAP)
        ],
        axis=0,
    )
    rhs[...] = base[...] + pick(chosen, spread)


def second_body(got, pressure, trace, trace_out, send, gathered):
    message = got[pl.ds(1, LANES, stride=2), :]
    now = traces(message, pressure[...], gathered)
    trace_out[...] = now
    [change] = onto_fracture(message, kappa_of(message) * (now - trace[...]))
    for m in range(send.shape[0] // LANES):
        send[m * LANES : (m + 1) * LANES, :] = change


def flux_body(got, trace, x, flux):
    message = got[pl.ds(1, LANES, stride=2), :]
    flux[...] = kappa_of(message) * (trace[...] - at_mortar(message, x[...]))


def home_body(got, owner, slot, flux):
    count = owner.shape[1]
    values = got[...].T[:CAP, :]
    chosen = ones_where(iota((LANES, count), 0) == owner[...])
    top = values.astype(BF16).astype(F32)
    middle = (values - top).astype(BF16).astype(F32)
    stacked = jnp.concatenate([top, middle, values - top - middle, jnp.zeros_like(top)], axis=0)
    found = jnp.dot(stacked.astype(BF16), chosen, preferred_element_type=F32)
    found = found[:CAP] + found[CAP : 2 * CAP] + found[2 * CAP : 3 * CAP]
    here = iota((CAP, count), 0) == slot[...]
    flux[...] = jnp.sum(jnp.where(here, found, 0.0), axis=0, keepdims=True)


def sum_body(got, send):
    for i in range(2):
        mine = jnp.sum(got[pl.ds(i, LANES, stride=2), :], axis=0, keepdims=True)
        send[pl.ds(i, LANES, stride=2), :] = jnp.broadcast_to(mine, (LANES, LANES))


def columns_body(got, chosen, *, shards, rows, tiles):
    flipped = got[pl.ds(1, LANES, stride=2), :].T[COLS : COLS + CAP, :]
    count = shards * rows * tiles
    tile = iota((LANES, count), 1)
    sender = (tile // tiles) % rows * shards + tile // (rows * tiles)
    moved = jnp.dot(
        jnp.concatenate([flipped, flipped], axis=0).astype(BF16),
        ones_where(iota((LANES, count), 0) == sender),
        preferred_element_type=F32,
    )[:CAP]
    here = iota((CAP, count), 0) == iota((CAP, count), 1) % tiles
    column = jnp.sum(jnp.where(here, moved, 0.0), axis=0, keepdims=True).astype(jnp.int32)
    chosen[...] = ones_where(iota((LANES, count), 0) == column)


def products(at, cols, d, tiles, diag, block):
    shard = at[1]
    rows, per_row = cols.shape
    for r in range(rows):
        d_row = d[pl.ds(CAP * shard + r, 1), :]
        d_col = as_column(d_row)
        mixed = jnp.zeros((LANES, LANES), F32)
        for t in range(per_row):
            tile = tiles[per_row * r + t]
            mixed += tile * d[pl.ds(cols[r, t], 1), :]
            back = jnp.sum(tile * d_col, axis=0, keepdims=True)
            block[rows + per_row * r + t : rows + per_row * r + t + 1, :] = 0.5 * back
        block[r : r + 1, :] = diag[r : r + 1, :] * d_row + 0.5 * row_sums(mixed)


def image_of(got, chosen, step, rows, tiles):
    shards = got.shape[0] // step
    own = jnp.concatenate([got[s * step : s * step + rows, :] for s in range(shards)], axis=0)
    back = jnp.concatenate(
        [got[s * step + rows : s * step + rows + tiles, :] for s in range(shards)], axis=0
    )
    return own + pick(chosen[...], back)


def start_body(at, cols, got, tiles, diag, r_out, weight_out, send, block):
    r_out[...] = got[pl.ds(0, LANES, stride=2), :]
    weight_out[...] = got[pl.ds(1, LANES, stride=2), :]
    products(at, cols, r_out, tiles, diag, block)
    size = block.shape[0]
    for s in range(send.shape[0] // size):
        send[s * size : (s + 1) * size, :] = block[...]


def step_body(at, cols, got, x, r, d, chosen, tiles, diag, *rest, ride, last):
    rows, per_row = cols.shape
    size = rows * (1 + per_row)
    shards = LANES // rows
    extra = list(rest)
    change = extra.pop(0) if ride == "reduce" else None
    x_before, weight = (extra.pop(0), extra.pop(0)) if ride == "next" else (None, None)
    x_out, r_out, d_out, send, block = extra
    got_step = got.shape[0] // shards
    image = image_of(got, chosen, got_step, rows, rows * per_row)
    old = d[...]
    norm = total(r[...] * r[...])
    alpha = norm / total(old * image)
    x_new = x[...] + alpha * old
    r_new = r[...] - alpha * image
    x_out[...] = x_new
    if ride == "next":
        moved = jnp.concatenate(
            [got[s * got_step + size : (s + 1) * got_step, :] for s in range(shards)], axis=0
        )
        r_new = r_new + moved - weight[...] * (x_new - x_before[...])
        d_out[...] = r_new
    else:
        d_out[...] = r_new + (total(r_new * r_new) / norm) * old
    r_out[...] = r_new
    if last:
        shard = at[1]
        lanes = jnp.zeros((1, LANES), F32)
        for i in range(rows):
            d_row = d_out[pl.ds(CAP * shard + i, 1), :]
            mixed = jnp.zeros((LANES, LANES), F32)
            for t in range(per_row):
                mixed += tiles[per_row * i + t] * d_out[pl.ds(cols[i, t], 1), :]
            lanes += diag[i : i + 1, :] * d_row * d_row
            lanes += jnp.sum(mixed * as_column(d_row), axis=0, keepdims=True)
        send[...] = jnp.broadcast_to(lanes, send.shape)
        return
    products(at, cols, d_out, tiles, diag, block)
    send_step = send.shape[0] // shards
    if ride == "gather":
        own = jnp.zeros((rows, LANES), F32)
        for s in range(shards):
            own += got[s * got_step + size : (s + 1) * got_step, :]
    if ride == "reduce":
        sums = jnp.zeros((LANES, LANES), F32)
        for m in range(change.shape[0] // LANES):
            sums += change[m * LANES : (m + 1) * LANES, :]
    for s in range(shards):
        send[s * send_step : s * send_step + size, :] = block[...]
        if ride == "gather":
            send[s * send_step + size : (s + 1) * send_step, :] = own
        if ride == "reduce":
            send[s * send_step + size : (s + 1) * send_step, :] = sums[
                s * rows : (s + 1) * rows, :
            ]


def final_body(at, got, x, r, d, out):
    alpha = total(r[...] * r[...]) / total(got[...])
    here = pl.ds(pl.multiple_of(CAP * at[1], CAP), CAP)
    out[...] = x[here, :] + alpha * d[here, :]


def edges_body(px0, px1, py0, py1, tx1, ty1, x_up, x_down, y_up, y_down):
    wide = px0.shape[1]
    x_up[:wide, :] = px1[0]
    x_up[wide:, :] = tx1[0, 0]
    x_down[...] = px0[0]
    deep = py0.shape[0]
    y_up[:deep, :] = py1[:, 7, :]
    y_up[deep:, :] = ty1[0, :, 7, :]
    y_down[...] = py0[:, 0, :]


def edges(pressure, trans):
    nx, ny, nz = pressure.shape
    y_last = ny // 8 - 1
    return pl.pallas_call(
        edges_body,
        grid=(1,),
        out_shape=(shape(2 * ny, nz), shape(ny, nz), shape(2 * nx, nz), shape(nx, nz)),
        in_specs=[
            pl.BlockSpec((1, ny, nz), lambda i: (0, 0, 0)),
            pl.BlockSpec((1, ny, nz), lambda i: (nx - 1, 0, 0)),
            pl.BlockSpec((nx, 8, nz), lambda i: (0, 0, 0)),
            pl.BlockSpec((nx, 8, nz), lambda i: (0, y_last, 0)),
            pl.BlockSpec((1, 1, ny, nz), lambda i: (0, nx - 1, 0, 0)),
            pl.BlockSpec((1, nx, 8, nz), lambda i: (1, 0, y_last, 0)),
        ],
        out_specs=(VMEM,) * 4,
        compiler_params=pltpu.CompilerParams(vmem_limit_bytes=16 << 20),
        name="edges",
    )(pressure, pressure, pressure, pressure, trans, trans)


def sweep_body(
    p, x_low, x_high, y_low, y_high, tx_low, ty_low, trans, cell, rhs, *rest, first, last
):
    rest = list(rest)
    weight = None if first else rest.pop(0)
    out = rest.pop(0)
    weight_out = rest.pop(0) if first else None
    carry, carry_t = rest.pop(), rest.pop()
    step = pl.program_id(0)
    many = out.shape[0]
    ny, nz = out.shape[1:]
    nx = p.shape[0]
    zero_row = iota((ny, nz), 0)
    lane = iota((ny, nz), 1)

    @pl.when(step == 0)
    def _():
        carry[...] = tx_low[...] * (x_low[...] - p[0])
        carry_t[...] = tx_low[...]

    for i in range(many):
        at = step * many + i
        here = p[at]
        after = jnp.where(at + 1 < nx, p[jnp.minimum(at + 1, nx - 1)], x_high[...])
        tx, ty, tz = trans[0, i], trans[1, i], trans[2, i]
        fx = tx * (here - after)
        y_next = jnp.where(zero_row == ny - 1, y_high[pl.ds(at, 1), :], pltpu.roll(here, ny - 1, 0))
        fy = ty * (here - y_next)
        ty_edge = ty_low[pl.ds(at, 1), :]
        fy_edge = ty_edge * (y_low[pl.ds(at, 1), :] - here[:1])
        fy_low = jnp.where(zero_row == 0, fy_edge, pltpu.roll(fy, 1, 0))
        z_next = jnp.where(lane == nz - 1, 0.0, pltpu.roll(here, nz - 1, 1))
        fz = tz * (here - z_next)
        fz_low = jnp.where(lane == 0, 0.0, pltpu.roll(fz, 1, 1))
        if first:
            ty_before = jnp.where(zero_row == 0, ty_edge, pltpu.roll(ty, 1, 0))
            tz_before = jnp.where(lane == 0, 0.0, pltpu.roll(tz, 1, 1))
            diagonal = cell[i] + tx + carry_t[...] + ty + ty_before + tz + tz_before
            w = WEIGHT / diagonal
            weight_out[i] = w
            carry_t[...] = tx
        else:
            w = weight[i]
        applied = cell[i] * here + fx - carry[...] + fy - fy_low + fz - fz_low
        carry[...] = fx
        out[i] = here + w * (rhs[i] - applied)
    if not last:
        x_up, x_down, y_up, y_down = rest

        @pl.when(step == 0)
        def _():
            x_down[...] = out[0]

        @pl.when(step == pl.num_programs(0) - 1)
        def _():
            x_up[...] = out[many - 1]

        for i in range(many):
            y_down[pl.ds(step * many + i, 1), :] = out[i, :1, :]
            y_up[pl.ds(step * many + i, 1), :] = out[i, ny - 1 :, :]


def sweep(p, halo, lows, trans, cell, rhs, weight=None, last=False, many=4):
    nx, ny, nz = p.shape
    whole = pl.BlockSpec((nx, ny, nz), lambda i: (0, 0, 0))
    part = pl.BlockSpec((many, ny, nz), lambda i: (i, 0, 0))
    x_face = pl.BlockSpec((ny, nz), lambda i: (0, 0))
    y_face = pl.BlockSpec((nx, nz), lambda i: (0, 0))
    first = weight is None
    out_shape, out_specs = [shape(nx, ny, nz)], [part]
    if first:
        out_shape.append(shape(nx, ny, nz))
        out_specs.append(part)
    if not last:
        out_shape += [shape(ny, nz)] * 2 + [shape(nx, nz)] * 2
        out_specs += [x_face, x_face, y_face, y_face]
    operands = [p, *halo, *lows, trans, cell, rhs] + ([] if first else [weight])
    return pl.pallas_call(
        functools.partial(sweep_body, first=first, last=last),
        grid=(nx // many,),
        out_shape=tuple(out_shape),
        in_specs=[whole, x_face, x_face, y_face, y_face, x_face, y_face]
        + [pl.BlockSpec((3, many, ny, nz), lambda i: (0, i, 0, 0)), part, part]
        + ([] if first else [part]),
        out_specs=tuple(out_specs),
        scratch_shapes=[pltpu.VMEM((ny, nz), F32)] * 2,
        compiler_params=pltpu.CompilerParams(vmem_limit_bytes=32 << 20),
        cost_estimate=pl.CostEstimate(flops=6_000_000, bytes_accessed=8 << 20, transcendentals=0),
        name="sweep",
    )(*operands)


def shifted(x_up, x_down, y_up, y_down, mats, shards):
    def move(v, axis, count, by):
        pairs = [(i, i + by) for i in range(count) if 0 <= i + by < count]
        return lax.ppermute(v, axis, pairs)

    return (
        move(x_up, "mat", mats, 1),
        move(x_down, "mat", mats, -1),
        move(y_up, "frac", shards, 1),
        move(y_down, "frac", shards, -1),
    )


def body(
    pressure_start,
    face_trans,
    cell_coef,
    matrix_source,
    mortar_owner,
    mortar_cell,
    mortar_frac,
    mortar_kappa,
    tiles,
    tile_cols,
    frac_diag,
    frac_source,
    fracture_start,
):
    nx, ny, nz = pressure_start.shape
    mats, shards = lax.axis_size("mat"), lax.axis_size("frac")
    rows, per_row = tile_cols.shape
    count = mortar_cell.shape[0]
    size = rows * (1 + per_row)
    at = jnp.stack([lax.axis_index("mat"), lax.axis_index("frac")]).astype(jnp.int32)
    everyone = functools.partial(
        lax.all_to_all, axis_name=("mat", "frac"), split_axis=0, concat_axis=0, tiled=True
    )
    over_frac = functools.partial(
        lax.all_to_all, axis_name="frac", split_axis=0, concat_axis=0, tiled=True
    )
    over_mat = functools.partial(
        lax.all_to_all, axis_name="mat", split_axis=0, concat_axis=0, tiled=True
    )
    square = shape(LANES, LANES)
    owner = mortar_owner.reshape(1, count)
    flat = (nx * ny, nz)
    tile_list = tiles.reshape(rows * per_row, LANES, LANES)
    diag = frac_diag.reshape(rows, LANES)
    square_scratch = pltpu.VMEM((LANES, LANES), F32)
    gathered = pltpu.VMEM((CAP * LANES, nz), F32)
    block = pltpu.VMEM((size, LANES), F32)

    send, slot = call(
        pack_body,
        (shape(2 * LANES, LANES), shape(1, count, dtype=jnp.int32)),
        [SMEM, SMEM] + [VMEM] * 6,
        scratch=[square_scratch],
        name="pack",
    )(
        at,
        tile_cols,
        mortar_owner,
        owner,
        mortar_cell.reshape(1, count),
        mortar_frac.reshape(1, count),
        mortar_kappa.reshape(1, count),
        fracture_start.reshape(rows, LANES),
    )
    got = everyone(send)

    x_low, x_high, y_low, y_high = shifted(
        *edges(pressure_start, face_trans), mats, shards
    )
    lows = (x_low[ny:], y_low[nx:])
    halo = (x_low[:ny], x_high, y_low[:nx], y_high)

    send, x_start, trace, flux = pl.pallas_call(
        first_body,
        out_shape=(shape(2 * LANES, LANES), square, square, square),
        grid_spec=pltpu.PrefetchScalarGridSpec(
            num_scalar_prefetch=2,
            grid=(1,),
            in_specs=[
                VMEM,
                VMEM,
                pl.BlockSpec(
                    (1, per_row, LANES, LANES), lambda i, at, cols: (at[0], 0, 0, 0)
                ),
                VMEM,
                VMEM,
            ],
            out_specs=(VMEM,) * 4,
            scratch_shapes=[gathered, square_scratch],
        ),
        compiler_params=pltpu.CompilerParams(vmem_limit_bytes=32 << 20),
        name="first",
    )(at, tile_cols, got, pressure_start.reshape(flat), tiles, diag, frac_source.reshape(rows, LANES))
    reduced = everyone(send)
    send = call(sum_body, shape(2 * LANES, LANES), [VMEM], name="sums")(reduced)
    residuals = everyone(send)

    base = matrix_source.reshape(flat)

    def with_source(flux):
        return call(source_body, shape(*flat), [VMEM] * 3, flops=2e9, nbytes=2 << 20, name="source")(
            got, flux, base
        ).reshape(nx, ny, nz)

    chosen = call(
        functools.partial(columns_body, shards=shards, rows=rows, tiles=per_row),
        shape(LANES, shards * rows * per_row, dtype=BF16),
        [VMEM],
        name="columns",
    )(got)
    rhs = with_source(flux)
    pressure, weight, *sides = sweep(
        pressure_start, halo, lows, face_trans, cell_coef, rhs
    )
    pressure, *sides = sweep(
        pressure, shifted(*sides, mats, shards), lows, face_trans, cell_coef, rhs, weight
    )
    halo = shifted(*sides, mats, shards)
    trace, send = call(
        second_body,
        (square, shape(mats * LANES, LANES)),
        [VMEM] * 3,
        flops=2e9,
        nbytes=2 << 20,
        scratch=[gathered],
        name="second",
    )(got, pressure.reshape(flat), trace)
    change = over_mat(send)

    r, sums, send = call(
        start_body,
        (square, square, shape(shards * size, LANES)),
        [SMEM, SMEM] + [VMEM] * 3,
        scratch=[block],
        name="start",
    )(at, tile_cols, residuals, tile_list, diag)
    x, d = x_start, r

    def step(arrived, x, r, d, *more, ride=None, last=False):
        length = LANES if last else shards * (size + (rows if ride in ("reduce", "gather") else 0))
        if last:
            length = shards
        return call(
            functools.partial(step_body, ride=ride, last=last),
            (square, square, square, shape(length, LANES)),
            [SMEM, SMEM] + [VMEM] * (7 + len(more)),
            scratch=[block],
            name="step",
        )(at, tile_cols, arrived, x, r, d, chosen, tile_list, diag, *more)

    x, r, d, send = step(over_frac(send), x, r, d, change, ride="reduce")
    x, r, d, send = step(over_frac(send), x, r, d, ride="gather")
    x, r, d, send = step(over_frac(send), x, r, d, x_start, sums, ride="next")

    flux = call(flux_body, square, [VMEM] * 3, name="flux")(got, trace, x)
    rhs = with_source(flux)
    pressure, *sides = sweep(pressure, halo, lows, face_trans, cell_coef, rhs, weight)
    [pressure] = sweep(
        pressure, shifted(*sides, mats, shards), lows, face_trans, cell_coef, rhs, weight, last=True
    )
    flux_out = call(home_body, shape(1, count), [VMEM] * 3, name="home")(
        everyone(flux), owner, slot
    )

    x, r, d, send = step(over_frac(send), x, r, d)
    x, r, d, send = step(over_frac(send), x, r, d, last=True)
    fracture = call(final_body, shape(rows, LANES), [SMEM] + [VMEM] * 4, name="final")(
        at, over_frac(send), x, r, d
    )
    return pressure, fracture.reshape(rows * LANES), flux_out.reshape(count)


def solution(mesh):
    in_specs = (
        P("mat", "frac", None),
        P(None, "mat", "frac", None),
        P("mat", "frac", None),
        P("mat", "frac", None),
        P(("mat", "frac"), None),
        P(("mat", "frac")),
        P(("mat", "frac")),
        P(("mat", "frac")),
        P("frac", None, None, None),
        P("frac", None),
        P("frac"),
        P("frac"),
        P("frac"),
    )
    out_specs = (P("mat", "frac", None), P("frac"), P(("mat", "frac")))
    return jax.shard_map(body, mesh=mesh, in_specs=in_specs, out_specs=out_specs, check_vma=False)
```

time: 587 us -> 250 us (0.43); the launches traced: 577 us -> 246 us
  waiting for transfers between devices: 103 us -> 17.6 us
  other arithmetic: 83.8 us -> 0.08 us
  starting transfers between devices: 188 us -> 108 us
  blocking collectives: 85.4 us -> 36.5 us
  Pallas kernels: 0 us -> 40.7 us
  local copies, waits for them, and re-layouts: 69.9 us -> 41.4 us
  matrix products: 25.7 us -> 0 us
  between operations: 21.5 us -> 1.37 us
    all_to_all x28 -> x8, starting transfers between devices: 158 us -> 62.2 us  [the longest x1 13.3 us: body(): residuals = everyone(send)]
    all_to_all x28 -> x8, waiting for transfers between devices: 85.7 us -> 16.1 us  [the longest x1 7.39 us: body(): x, r, d, send = step(over_frac(send), x, r, d, change, ride='reduce')]
    all_gather x2 -> x0, blocking collectives: 48.2 us -> none  [body(): fracture_whole = lax.all_gather(fracture, 'frac', axis=0, tiled=True)]
    pallas_call x0 -> x21, Pallas kernels: none -> 40.7 us  [the longest x4 12.7 us: sweep(): pl.pallas_call(functools.partial(sweep_body, first=first, last=last), gri...]
    scatter-add x12 -> x0, other arithmetic: 32.3 us -> none  [the longest x2 13.4 us: body(): jax.ops.segment_sum(arrived.reshape(-1), asked_safe.reshape(-1), num_segm...]
    unnamed x109 -> x146, local copies, waits for them, and re-layouts: 8.98 us -> 39.8 us
    gather x14 -> x0, local copies, waits for them, and re-layouts: 29.5 us -> none  [the longest x2 12.3 us: body(): local_values = pressure.reshape(-1)[asked_safe]]
    psum x2 -> x0, blocking collectives: 26.5 us -> none  [body(): load = lax.psum(rows_part, 'mat')]
  transfers between devices with their start and end apart: 40 -> 24, of which waited for: 25 -> 5; matrix products, arithmetic and copies ran while one was open for 26% -> 1% of each run, Pallas kernels for 0% -> 13%
where the time goes in v2:
time: 250 us; the launch traced here: 246 us
  starting transfers between devices  108 us (43%)
  local copies, waits for them, and re-layouts  41.4 us (17%)
  Pallas kernels  40.7 us (16%)
  blocking collectives  36.5 us (15%)
  waiting for transfers between devices  17.6 us (7%)
    ppermute x16, starting transfers between devices, move(): return lax.ppermute(v, axis, pairs)  46.3 us
    unnamed x146, local copies, waits for them, and re-layouts  39.8 us
    all_to_all x1, starting transfers between devices, body(): residuals = everyone(send)  13.3 us
    pallas_call x4, Pallas kernels, sweep(): pl.pallas_call(functools.partial(sweep_body, first=first, last=last), gri...  12.7 us
    all_to_all x1, blocking collectives, body(): x, r, d, send = step(over_frac(send), x, r, d, x_start, sums, ride='next')  12.2 us
    all_to_all x1, blocking collectives, body(): x, r, d, send = step(over_frac(send), x, r, d, ride='gather')  12.2 us
    all_to_all x1, blocking collectives, body(): x, r, d, send = step(over_frac(send), x, r, d)  12.1 us
    all_to_all x1, starting transfers between devices, body(): got = everyone(send)  9.93 us
  transfers between devices with their start and end apart: 24, of which 5 were waited for; matrix products, arithmetic and copies ran while one was open for 1% of the time, Pallas kernels for 13%

profile of v2, /device:TPU:32, one launch (start us, length us, event | category | flops | bytes accessed | tf_op | source)
XLA Modules:
  0.0 246.2 jit_solution(266002179602817589)
XLA Ops:
  0.6 1.9 copy-done
  5.8 3.5 %collective-permute-start.2 = (f32[32,256]{1,0:T(8,128)S(1)}, f32[32,256]{1,0:T(8,128)}, u32[]{:S(2)}, u32[]{:S(2)}) collective-permute-start(f32[32,256]{1,0:T(8,128)S(1)} %get-tuple-element.56), channel_id=1, source_target_pairs={{0,1},{1,2},{2,3},{3,4},{4,5},{5,6},{6,7},{7,8},{8,9},{9,10},{10,1... | collective-permute-start | bytes 98312 | tf_op jit(solution)/shard_map/ppermute | solution.py:500
  11.3 9.9 %all-to-all-start = ((f32[128,2,128]{2,1,0:T(2,128)}), f32[128,2,128]{2,1,0:T(2,128)S(1)}, u32[]{:S(2)}, u32[]{:S(2)}) async-start(f32[128,2,128]{2,1,0:T(2,128)} %bitcast.80), calls=%async_computation | async-start | bytes 262144 | tf_op jit(solution)/shard_map/all_to_all | solution.py:565
  21.2 2.7 %collective-permute-start = (f32[128,256]{1,0:T(8,128)}, f32[128,256]{1,0:T(8,128)}, u32[]{:S(2)}, u32[]{:S(2)}) collective-permute-start(f32[128,256]{1,0:T(8,128)} %copy-done.63), channel_id=1, source_target_pairs={{0,16},{16,32},{32,48},{48,64},{64,80},{80,96},{96,112},{1,17},{17... | collective-permute-start | bytes 393224 | tf_op jit(solution)/shard_map/ppermute | solution.py:500
  23.9 1.3 collective-permute-start.1
  25.2 4.5 %collective-permute-start.3 = (f32[16,256]{1,0:T(8,128)}, f32[16,256]{1,0:T(8,128)S(1)}, u32[]{:S(2)}, u32[]{:S(2)}) collective-permute-start(f32[16,256]{1,0:T(8,128)} %get-tuple-element.57), channel_id=1, source_target_pairs={{1,0},{2,1},{3,2},{4,3},{5,4},{6,5},{7,6},{8,7},{9,8},{10,9},{11,1... | collective-permute-start | bytes 49160 | tf_op jit(solution)/shard_map/ppermute | solution.py:500
  30.6 4.6 %first.1 = (f32[256,128]{1,0:T(8,128)}, f32[128,128]{1,0:T(8,128)S(1)}, f32[128,128]{1,0:T(8,128)S(1)}, f32[128,128]{1,0:T(8,128)S(1)}) custom-call(s32[2]{0:T(128)S(1)} %pad_add_fusion.at, s32[8,4]{1,0:T(8,128)S(1)} %copy.25.cols, f32[256,128]{1,0:T(8,128)S(1)} %bitcast.54, f32[1024,256]{1,0:T(8,128)S(1)} %bitcast.49, f32[8,4,128,128]{3,2,1,0:T(8,128)S(1)} %copy-done.2, ...), custom_call_target="tpu_custom_call" | custom-call | tf_op jit(solution)/shard_map/first/pallas_call | solution.py:573
  36.4 9.7 %all-to-all-start.1 = ((f32[128,2,128]{2,1,0:T(2,128)}), f32[128,2,128]{2,1,0:T(2,128)}, u32[]{:S(2)}, u32[]{:S(2)}) async-start(f32[128,2,128]{2,1,0:T(2,128)} %bitcast.15), calls=%async_computation.1 | async-start | bytes 262144 | tf_op jit(solution)/shard_map/all_to_all | solution.py:594
  48.2 2.1 source.2
  51.3 3.1 %sweep.4 = (f32[16,64,256]{2,1,0:T(8,128)S(1)}, f32[16,64,256]{2,1,0:T(8,128)S(1)}, f32[64,256]{1,0:T(8,128)S(1)}, f32[64,256]{1,0:T(8,128)S(1)}, f32[16,256]{1,0:T(8,128)S(1)}, /*index=5*/f32[16,256]{1,0:T(8,128)S(1)}) custom-call(f32[16,64,256]{2,1,0:T(8,128)S(1)} %copy-done.8, f32[64,256]{1,0:T(8,128)S(1)} %get-tuple-element.106.x_low, ...), custom_call_target="tpu_custom_call" | custom-call | flops 6000000 | bytes 8388608 | tf_op jit(solution)/shard_map/sweep/pallas_call | solution.py:482
  54.4 2.1 collective-permute-start.4
  56.5 1.3 collective-permute-start.5
  57.8 3.4 %collective-permute-start.6 = (f32[16,256]{1,0:T(8,128)S(1)}, f32[16,256]{1,0:T(8,128)S(1)}, u32[]{:S(2)}, u32[]{:S(2)}) collective-permute-start(f32[16,256]{1,0:T(8,128)S(1)} %get-tuple-element.63), channel_id=1, source_target_pairs={{0,1},{1,2},{2,3},{3,4},{4,5},{5,6},{6,7},{7,8},{8,9},{9,10},{10,1... | collective-permute-start | bytes 49160 | tf_op jit(solution)/shard_map/ppermute | solution.py:500
  61.2 4.5 %collective-permute-start.7 = (f32[16,256]{1,0:T(8,128)S(1)}, f32[16,256]{1,0:T(8,128)S(1)}, u32[]{:S(2)}, u32[]{:S(2)}) collective-permute-start(f32[16,256]{1,0:T(8,128)S(1)} %get-tuple-element.64), channel_id=1, source_target_pairs={{1,0},{2,1},{3,2},{4,3},{5,4},{6,5},{7,6},{8,7},{9,8},{10,9},{11,1... | collective-permute-start | bytes 49160 | tf_op jit(solution)/shard_map/ppermute | solution.py:500
  65.8 1.4 collective-permute-done.7.y_high
  67.2 2.4 sweep.5
  74.4 13.3 %all-to-all-start.2 = ((f32[128,2,128]{2,1,0:T(2,128)}), f32[128,2,128]{2,1,0:T(2,128)S(1)}, u32[]{:S(2)}, u32[]{:S(2)}) async-start(f32[128,2,128]{2,1,0:T(2,128)} %bitcast.66), calls=%async_computation.2 | async-start | bytes 262144 | tf_op jit(solution)/shard_map/all_to_all | solution.py:596
  89.7 2.8 %second.1 = (f32[128,128]{1,0:T(8,128)S(1)}, f32[1024,128]{1,0:T(8,128)S(1)}) custom-call(f32[256,128]{1,0:T(8,128)S(1)} %bitcast.56, f32[1024,256]{1,0:T(8,128)S(1)} %bitcast.63, f32[128,128]{1,0:T(8,128)S(1)} %copy-done.67), custom_call_target="tpu_custom_call" | custom-call | flops 2000000000 | bytes 2097152 | tf_op jit(solution)/shard_map/second/pallas_call | solution.py:619
  93.9 3.1 %all-to-all-done.2 = f32[128,2,128]{2,1,0:T(2,128)S(1)} async-done(((f32[128,2,128]{2,1,0:T(2,128)}), f32[128,2,128]{2,1,0:T(2,128)S(1)}, u32[]{:S(2)}, u32[]{:S(2)}) %all-to-all-start.2) | async-done | bytes 131104 | tf_op jit(solution)/shard_map/all_to_all | solution.py:596
  97.0 4.3 %all-to-all-start.4 = ((f32[8,128,128]{2,1,0:T(8,128)}), f32[8,128,128]{2,1,0:T(8,128)}, u32[]{:S(2)}, u32[]{:S(2)}) async-start(f32[8,128,128]{2,1,0:T(8,128)} %bitcast.65), calls=%async_computation.4 | async-start | bytes 1048576 | tf_op jit(solution)/shard_map/all_to_all | solution.py:628
  101.3 1.6 copy-done.3
  105.9 5.6 %all-to-all-done.4 = f32[8,128,128]{2,1,0:T(8,128)} async-done(((f32[8,128,128]{2,1,0:T(8,128)}), f32[8,128,128]{2,1,0:T(8,128)}, u32[]{:S(2)}, u32[]{:S(2)}) %all-to-all-start.4) | async-done | bytes 524320 | tf_op jit(solution)/shard_map/all_to_all | solution.py:628
  111.5 5.1 %all-to-all-start.3 = ((f32[16,40,128]{2,1,0:T(8,128)}), f32[16,40,128]{2,1,0:T(8,128)}, u32[]{:S(2)}, u32[]{:S(2)}) async-start(f32[16,40,128]{2,1,0:T(8,128)} %bitcast.70), calls=%async_computation.3 | async-start | bytes 655360 | tf_op jit(solution)/shard_map/all_to_all | solution.py:651
  116.8 7.4 %all-to-all-done.3 = f32[16,40,128]{2,1,0:T(8,128)} async-done(((f32[16,40,128]{2,1,0:T(8,128)}), f32[16,40,128]{2,1,0:T(8,128)}, u32[]{:S(2)}, u32[]{:S(2)}) %all-to-all-start.3) | async-done | bytes 327712 | tf_op jit(solution)/shard_map/all_to_all | solution.py:651
  124.2 1.6 copy-done.4
  127.5 2.0 step.5
  129.5 12.2 %all_to_all.121 = f32[16,48,128]{2,1,0:T(8,128)S(1)} all-to-all(f32[16,48,128]{2,1,0:T(8,128)S(1)} %bitcast.68), channel_id=1, replica_groups=mesh['mat'=8,'frac'=16] {'frac'}, dimensions={0} | all-to-all | bytes 786432 | tf_op jit(solution)/shard_map/all_to_all | solution.py:652
  141.7 1.4 step.6
  143.1 12.2 %all_to_all.122 = f32[16,48,128]{2,1,0:T(8,128)S(1)} all-to-all(f32[16,48,128]{2,1,0:T(8,128)S(1)} %bitcast.67), channel_id=1, replica_groups=mesh['mat'=8,'frac'=16] {'frac'}, dimensions={0} | all-to-all | bytes 786432 | tf_op jit(solution)/shard_map/all_to_all | solution.py:653
  155.4 1.3 step.7
  156.7 12.1 %all_to_all.123 = f32[16,40,128]{2,1,0:T(8,128)S(1)} all-to-all(f32[16,40,128]{2,1,0:T(8,128)S(1)} %bitcast.71), channel_id=1, replica_groups=mesh['mat'=8,'frac'=16] {'frac'}, dimensions={0} | all-to-all | bytes 655360 | tf_op jit(solution)/shard_map/all_to_all | solution.py:665
  168.8 1.4 step.8
  172.8 6.1 %all-to-all-start.8 = ((f32[16,40,128]{2,1,0:T(8,128)}), f32[16,40,128]{2,1,0:T(8,128)}, u32[]{:S(2)}, u32[]{:S(2)}) async-start(f32[16,40,128]{2,1,0:T(8,128)} %bitcast.69), calls=%async_computation.8 | async-start | bytes 655360 | tf_op jit(solution)/shard_map/all_to_all | solution.py:666
  178.9 1.9 collective-permute-start.8
  180.8 1.3 collective-permute-start.9
  182.1 3.4 %collective-permute-start.10 = (f32[16,256]{1,0:T(8,128)}, f32[16,256]{1,0:T(8,128)S(1)}, u32[]{:S(2)}, u32[]{:S(2)}) collective-permute-start(f32[16,256]{1,0:T(8,128)} %get-tuple-element.69), channel_id=1, source_target_pairs={{0,1},{1,2},{2,3},{3,4},{4,5},{5,6},{6,7},{7,8},{8,9},{9,10},{10,1... | collective-permute-start | bytes 49160 | tf_op jit(solution)/shard_map/ppermute | solution.py:500
  185.5 4.6 %collective-permute-start.11 = (f32[16,256]{1,0:T(8,128)S(1)}, f32[16,256]{1,0:T(8,128)S(1)}, u32[]{:S(2)}, u32[]{:S(2)}) collective-permute-start(f32[16,256]{1,0:T(8,128)S(1)} %get-tuple-element.70), channel_id=1, source_target_pairs={{1,0},{2,1},{3,2},{4,3},{5,4},{6,5},{7,6},{8,7},{9,8},{10,9},{11,1... | collective-permute-start | bytes 49160 | tf_op jit(solution)/shard_map/ppermute | solution.py:500
  191.7 1.3 flux.1
  193.7 8.3 %all-to-all-start.10 = ((f32[128,1,128]{2,1,0:T(1,128)}), f32[128,1,128]{2,1,0:T(1,128)}, u32[]{:S(2)}, u32[]{:S(2)}) async-start(f32[128,1,128]{2,1,0:T(1,128)} %bitcast.72), calls=%async_computation.10 | async-start | bytes 131072 | tf_op jit(solution)/shard_map/all_to_all | solution.py:662
  204.0 2.1 source.3
  206.3 3.7 %sweep.6 = (f32[16,64,256]{2,1,0:T(8,128)S(1)}, f32[64,256]{1,0:T(8,128)}, f32[64,256]{1,0:T(8,128)}, f32[16,256]{1,0:T(8,128)}, f32[16,256]{1,0:T(8,128)}) custom-call(f32[16,64,256]{2,1,0:T(8,128)S(1)} %copy-done.21, f32[64,256]{1,0:T(8,128)} %collective-permute-done.8.x_low, f32[64,256]{1,0:T(8,128)} %collective-permute-done.9.x_high, ...), custom_call_target="tpu_custom_call" | custom-call | flops 6000000 | bytes 8388608 | tf_op jit(solution)/shard_map/sweep/pallas_call | solution.py:482
  210.9 2.7 %collective-permute-start.12 = (f32[64,256]{1,0:T(8,128)}, f32[64,256]{1,0:T(8,128)}, u32[]{:S(2)}, u32[]{:S(2)}) collective-permute-start(f32[64,256]{1,0:T(8,128)} %get-tuple-element.89), channel_id=1, source_target_pairs={{0,16},{16,32},{32,48},{48,64},{64,80},{80,96},{96,112},{1,17},{17... | collective-permute-start | bytes 196616 | tf_op jit(solution)/shard_map/ppermute | solution.py:500
  214.9 3.4 %collective-permute-start.14 = (f32[16,256]{1,0:T(8,128)}, f32[16,256]{1,0:T(8,128)S(1)}, u32[]{:S(2)}, u32[]{:S(2)}) collective-permute-start(f32[16,256]{1,0:T(8,128)} %get-tuple-element.91), channel_id=1, source_target_pairs={{0,1},{1,2},{2,3},{3,4},{4,5},{5,6},{6,7},{7,8},{8,9},{9,10},{10,1... | collective-permute-start | bytes 49160 | tf_op jit(solution)/shard_map/ppermute | solution.py:500
  218.3 4.5 %collective-permute-start.15 = (f32[16,256]{1,0:T(8,128)}, f32[16,256]{1,0:T(8,128)S(1)}, u32[]{:S(2)}, u32[]{:S(2)}) collective-permute-start(f32[16,256]{1,0:T(8,128)} %get-tuple-element.92), channel_id=1, source_target_pairs={{1,0},{2,1},{3,2},{4,3},{5,4},{6,5},{7,6},{8,7},{9,8},{10,9},{11,1... | collective-permute-start | bytes 49160 | tf_op jit(solution)/shard_map/ppermute | solution.py:500
  222.9 2.3 step.9
  227.0 5.5 %all-to-all-start.9 = ((f32[16,1,128]{2,1,0:T(1,128)}), f32[16,1,128]{2,1,0:T(1,128)S(1)}, u32[]{:S(2)}, u32[]{:S(2)}) async-start(f32[16,1,128]{2,1,0:T(1,128)} %bitcast.34), calls=%async_computation.9 | async-start | bytes 16384 | tf_op jit(solution)/shard_map/all_to_all | solution.py:668
  233.2 1.6 home.1
  239.8 3.5 %sweep.7 = f32[16,64,256]{2,1,0:T(8,128)} custom-call(f32[16,64,256]{2,1,0:T(8,128)S(1)} %copy-done.18, f32[64,256]{1,0:T(8,128)} %collective-permute-done.12.x_low, f32[64,256]{1,0:T(8,128)} %collective-permute-done.13.x_high, f32[16,256]{1,0:T(8,128)S(1)} %collective-permute-done.14.y_low, f32[16,256]{1,0:T(8,128)S(1)} %collective-permute-done.15.y_high, ...), custom_call_target="tpu_custom_call" | custom-call | flops 6000000 | bytes 8388608 | tf_op jit(solution)/shard_map/sweep/pallas_call | solution.py:482
  (173 shorter events, 42.9 us)
Async XLA Ops:
  3.8 5.6 %copy-start.71 = (s32[8,4]{0,1:T(4,128)S(1)}, s32[8,4]{0,1:T(4,128)}, u32[]{:S(2)}) copy-start(s32[8,4]{0,1:T(4,128)} %param.22) | copy-start | bytes 388
  3.8 5.7 %copy-start.53 = (s32[512,1]{0,1:T(1,128)S(1)}, s32[512,1]{0,1:T(1,128)}, u32[]{:S(2)}) copy-start(s32[512,1]{0,1:T(1,128)} %param.17) | copy-start | bytes 6148
  3.8 5.8 %copy-start.54 = (f32[1024]{0:T(1024)S(1)}, f32[1024]{0:T(1024)}, u32[]{:S(2)}) copy-start(f32[1024]{0:T(1024)} %param.25) | copy-start | bytes 12292
  3.8 5.8 %copy-start.56 = (s32[512]{0:T(512)S(1)}, s32[512]{0:T(512)}, u32[]{:S(2)}) copy-start(s32[512]{0:T(512)} %param.18) | copy-start | bytes 6148
  3.8 5.8 %copy-start.57 = (s32[512]{0:T(512)S(1)}, s32[512]{0:T(512)}, u32[]{:S(2)}) copy-start(s32[512]{0:T(512)} %param.19) | copy-start | bytes 6148
  3.8 5.8 %copy-start.58 = (f32[512]{0:T(512)S(1)}, f32[512]{0:T(512)}, u32[]{:S(2)}) copy-start(f32[512]{0:T(512)} %param.20) | copy-start | bytes 6148
  3.8 26.8 %copy-start.2 = (f32[8,4,128,128]{3,2,1,0:T(8,128)S(1)}, f32[8,4,128,128]{3,2,1,0:T(8,128)}, u32[]{:S(2)}) copy-start(f32[8,4,128,128]{3,2,1,0:T(8,128)} %tiles.1) | copy-start | bytes 6291460
  3.8 26.8 %copy-start.7 = (f32[16,64,256]{2,1,0:T(8,128)S(1)}, f32[16,64,256]{2,1,0:T(8,128)}, u32[]{:S(2)}) copy-start(f32[16,64,256]{2,1,0:T(8,128)} %p.1) | copy-start | bytes 3145732
  3.8 26.8 %copy-start.35 = (f32[1024]{0:T(1024)S(1)}, f32[1024]{0:T(1024)}, u32[]{:S(2)}) copy-start(f32[1024]{0:T(1024)} %param.23) | copy-start | bytes 12292
  3.8 26.7 %copy-start.55 = (f32[1024]{0:T(1024)S(1)}, f32[1024]{0:T(1024)}, u32[]{:S(2)}) copy-start(f32[1024]{0:T(1024)} %param.24) | copy-start | bytes 12292
  5.8 24.0 %collective-permute-start.2 = (f32[32,256]{1,0:T(8,128)S(1)}, f32[32,256]{1,0:T(8,128)}, u32[]{:S(2)}, u32[]{:S(2)}) collective-permute-start(f32[32,256]{1,0:T(8,128)S(1)} %get-tuple-element.56), channel_id=1, source_target_pairs={{0,1},{1,2},{2,3},{3,4},{4,5},{5,6},{6,7},{7,8},{8,9},{9,10},{10,1... | collective-permute-start | bytes 98312 | tf_op jit(solution)/shard_map/ppermute | solution.py:500
  11.3 18.5 %copy-start.59 = (s32[1,512]{1,0:T(1,128)}, s32[1,512]{1,0:T(1,128)S(1)}, u32[]{:S(2)}) copy-start(s32[1,512]{1,0:T(1,128)S(1)} %get-tuple-element.104.slot) | copy-start | bytes 6148
  11.3 19.3 %all-to-all-start = ((f32[128,2,128]{2,1,0:T(2,128)}), f32[128,2,128]{2,1,0:T(2,128)S(1)}, u32[]{:S(2)}, u32[]{:S(2)}) async-start(f32[128,2,128]{2,1,0:T(2,128)} %bitcast.80), calls=%async_computation | async-start | bytes 262144 | tf_op jit(solution)/shard_map/all_to_all | solution.py:565
  21.2 29.1 %collective-permute-start = (f32[128,256]{1,0:T(8,128)}, f32[128,256]{1,0:T(8,128)}, u32[]{:S(2)}, u32[]{:S(2)}) collective-permute-start(f32[128,256]{1,0:T(8,128)} %copy-done.63), channel_id=1, source_target_pairs={{0,16},{16,32},{32,48},{48,64},{64,80},{80,96},{96,112},{1,17},{17... | collective-permute-start | bytes 393224 | tf_op jit(solution)/shard_map/ppermute | solution.py:500
  23.9 27.3 %collective-permute-start.1 = (f32[64,256]{1,0:T(8,128)}, f32[64,256]{1,0:T(8,128)}, u32[]{:S(2)}, u32[]{:S(2)}) collective-permute-start(f32[64,256]{1,0:T(8,128)} %copy-done.68), channel_id=1, source_target_pairs={{16,0},{32,16},{48,32},{64,48},{80,64},{96,80},{112,96},{17,1},{33... | collective-permute-start | bytes 196616 | tf_op jit(solution)/shard_map/ppermute | solution.py:500
  25.2 26.0 %collective-permute-start.3 = (f32[16,256]{1,0:T(8,128)}, f32[16,256]{1,0:T(8,128)S(1)}, u32[]{:S(2)}, u32[]{:S(2)}) collective-permute-start(f32[16,256]{1,0:T(8,128)} %get-tuple-element.57), channel_id=1, source_target_pairs={{1,0},{2,1},{3,2},{4,3},{5,4},{6,5},{7,6},{8,7},{9,8},{10,9},{11,1... | collective-permute-start | bytes 49160 | tf_op jit(solution)/shard_map/ppermute | solution.py:500
  36.4 9.7 %copy-start.26 = (f32[128,128]{1,0:T(8,128)}, f32[128,128]{1,0:T(8,128)S(1)}, u32[]{:S(2)}) copy-start(f32[128,128]{1,0:T(8,128)S(1)} %get-tuple-element.75.x.rest_0_) | copy-start | bytes 196612
  36.4 36.4 %all-to-all-start.1 = ((f32[128,2,128]{2,1,0:T(2,128)}), f32[128,2,128]{2,1,0:T(2,128)}, u32[]{:S(2)}, u32[]{:S(2)}) async-start(f32[128,2,128]{2,1,0:T(2,128)} %bitcast.15), calls=%async_computation.1 | async-start | bytes 262144 | tf_op jit(solution)/shard_map/all_to_all | solution.py:594
  48.2 3.0 %copy-start.1 = (f32[3,16,64,256]{3,2,1,0:T(8,128)S(1)}, f32[3,16,64,256]{3,2,1,0:T(8,128)}, u32[]{:S(2)}) copy-start(f32[3,16,64,256]{3,2,1,0:T(8,128)} %trans.7) | copy-start | bytes 9437188
  48.2 3.0 %copy-start.8 = (f32[16,64,256]{2,1,0:T(8,128)S(1)}, f32[16,64,256]{2,1,0:T(8,128)}, u32[]{:S(2)}) copy-start(f32[16,64,256]{2,1,0:T(8,128)} %p.1) | copy-start | bytes 3145732
  48.2 3.1 %copy-start.9 = (f32[16,64,256]{2,1,0:T(8,128)S(1)}, f32[16,64,256]{2,1,0:T(8,128)}, u32[]{:S(2)}) copy-start(f32[16,64,256]{2,1,0:T(8,128)} %cell.7) | copy-start | bytes 3145732
  54.4 12.8 %collective-permute-start.4 = (f32[64,256]{1,0:T(8,128)S(1)}, f32[64,256]{1,0:T(8,128)S(1)}, u32[]{:S(2)}, u32[]{:S(2)}) collective-permute-start(f32[64,256]{1,0:T(8,128)S(1)} %get-tuple-element.61), channel_id=1, source_target_pairs={{0,16},{16,32},{32,48},{48,64},{64,80},{80,96},{96,112},{1,17},{17... | collective-permute-start | bytes 196616 | tf_op jit(solution)/shard_map/ppermute | solution.py:500
  56.5 10.7 %collective-permute-start.5 = (f32[64,256]{1,0:T(8,128)S(1)}, f32[64,256]{1,0:T(8,128)S(1)}, u32[]{:S(2)}, u32[]{:S(2)}) collective-permute-start(f32[64,256]{1,0:T(8,128)S(1)} %get-tuple-element.62), channel_id=1, source_target_pairs={{16,0},{32,16},{48,32},{64,48},{80,64},{96,80},{112,96},{17,1},{33... | collective-permute-start | bytes 196616 | tf_op jit(solution)/shard_map/ppermute | solution.py:500
  57.8 8.0 %collective-permute-start.6 = (f32[16,256]{1,0:T(8,128)S(1)}, f32[16,256]{1,0:T(8,128)S(1)}, u32[]{:S(2)}, u32[]{:S(2)}) collective-permute-start(f32[16,256]{1,0:T(8,128)S(1)} %get-tuple-element.63), channel_id=1, source_target_pairs={{0,1},{1,2},{2,3},{3,4},{4,5},{5,6},{6,7},{7,8},{8,9},{9,10},{10,1... | collective-permute-start | bytes 49160 | tf_op jit(solution)/shard_map/ppermute | solution.py:500
  61.2 5.9 %collective-permute-start.7 = (f32[16,256]{1,0:T(8,128)S(1)}, f32[16,256]{1,0:T(8,128)S(1)}, u32[]{:S(2)}, u32[]{:S(2)}) collective-permute-start(f32[16,256]{1,0:T(8,128)S(1)} %get-tuple-element.64), channel_id=1, source_target_pairs={{1,0},{2,1},{3,2},{4,3},{5,4},{6,5},{7,6},{8,7},{9,8},{10,9},{11,1... | collective-permute-start | bytes 49160 | tf_op jit(solution)/shard_map/ppermute | solution.py:500
  74.4 22.6 %all-to-all-start.2 = ((f32[128,2,128]{2,1,0:T(2,128)}), f32[128,2,128]{2,1,0:T(2,128)S(1)}, u32[]{:S(2)}, u32[]{:S(2)}) async-start(f32[128,2,128]{2,1,0:T(2,128)} %bitcast.66), calls=%async_computation.2 | async-start | bytes 262144 | tf_op jit(solution)/shard_map/all_to_all | solution.py:596
  97.0 14.5 %all-to-all-start.4 = ((f32[8,128,128]{2,1,0:T(8,128)}), f32[8,128,128]{2,1,0:T(8,128)}, u32[]{:S(2)}, u32[]{:S(2)}) async-start(f32[8,128,128]{2,1,0:T(8,128)} %bitcast.65), calls=%async_computation.4 | async-start | bytes 1048576 | tf_op jit(solution)/shard_map/all_to_all | solution.py:628
  111.5 12.7 %all-to-all-start.3 = ((f32[16,40,128]{2,1,0:T(8,128)}), f32[16,40,128]{2,1,0:T(8,128)}, u32[]{:S(2)}, u32[]{:S(2)}) async-start(f32[16,40,128]{2,1,0:T(8,128)} %bitcast.70), calls=%async_computation.3 | async-start | bytes 655360 | tf_op jit(solution)/shard_map/all_to_all | solution.py:651
  127.5 27.9 %copy-start.28 = (f32[128,128]{1,0:T(8,128)S(1)}, f32[128,128]{1,0:T(8,128)}, u32[]{:S(2)}) copy-start(f32[128,128]{1,0:T(8,128)} %copy-done.26) | copy-start | bytes 196612
  127.5 27.9 %copy-start.52 = (f32[128,128]{1,0:T(8,128)S(1)}, f32[128,128]{1,0:T(8,128)}, u32[]{:S(2)}) copy-start(f32[128,128]{1,0:T(8,128)} %copy-done.51) | copy-start | bytes 196612
  156.7 13.5 %copy-start.29 = (f32[128,128]{1,0:T(8,128)}, f32[128,128]{1,0:T(8,128)S(1)}, u32[]{:S(2)}) copy-start(f32[128,128]{1,0:T(8,128)S(1)} %get-tuple-element.87.x) | copy-start | bytes 196612
  172.8 20.8 %all-to-all-start.8 = ((f32[16,40,128]{2,1,0:T(8,128)}), f32[16,40,128]{2,1,0:T(8,128)}, u32[]{:S(2)}, u32[]{:S(2)}) async-start(f32[16,40,128]{2,1,0:T(8,128)} %bitcast.69), calls=%async_computation.8 | async-start | bytes 655360 | tf_op jit(solution)/shard_map/all_to_all | solution.py:666
  178.9 27.3 %collective-permute-start.8 = (f32[64,256]{1,0:T(8,128)}, f32[64,256]{1,0:T(8,128)}, u32[]{:S(2)}, u32[]{:S(2)}) collective-permute-start(f32[64,256]{1,0:T(8,128)} %copy-done.65), channel_id=1, source_target_pairs={{0,16},{16,32},{32,48},{48,64},{64,80},{80,96},{96,112},{1,17},{17... | collective-permute-start | bytes 196616 | tf_op jit(solution)/shard_map/ppermute | solution.py:500
  180.8 25.4 %collective-permute-start.9 = (f32[64,256]{1,0:T(8,128)}, f32[64,256]{1,0:T(8,128)}, u32[]{:S(2)}, u32[]{:S(2)}) collective-permute-start(f32[64,256]{1,0:T(8,128)} %copy-done.64), channel_id=1, source_target_pairs={{16,0},{32,16},{48,32},{64,48},{80,64},{96,80},{112,96},{17,1},{33... | collective-permute-start | bytes 196616 | tf_op jit(solution)/shard_map/ppermute | solution.py:500
  182.1 24.1 %collective-permute-start.10 = (f32[16,256]{1,0:T(8,128)}, f32[16,256]{1,0:T(8,128)S(1)}, u32[]{:S(2)}, u32[]{:S(2)}) collective-permute-start(f32[16,256]{1,0:T(8,128)} %get-tuple-element.69), channel_id=1, source_target_pairs={{0,1},{1,2},{2,3},{3,4},{4,5},{5,6},{6,7},{7,8},{8,9},{9,10},{10,1... | collective-permute-start | bytes 49160 | tf_op jit(solution)/shard_map/ppermute | solution.py:500
  185.5 20.7 %collective-permute-start.11 = (f32[16,256]{1,0:T(8,128)S(1)}, f32[16,256]{1,0:T(8,128)S(1)}, u32[]{:S(2)}, u32[]{:S(2)}) collective-permute-start(f32[16,256]{1,0:T(8,128)S(1)} %get-tuple-element.70), channel_id=1, source_target_pairs={{1,0},{2,1},{3,2},{4,3},{5,4},{6,5},{7,6},{8,7},{9,8},{10,9},{11,1... | collective-permute-start | bytes 49160 | tf_op jit(solution)/shard_map/ppermute | solution.py:500
  193.7 33.4 %all-to-all-start.10 = ((f32[128,1,128]{2,1,0:T(1,128)}), f32[128,1,128]{2,1,0:T(1,128)}, u32[]{:S(2)}, u32[]{:S(2)}) async-start(f32[128,1,128]{2,1,0:T(1,128)} %bitcast.72), calls=%async_computation.10 | async-start | bytes 131072 | tf_op jit(solution)/shard_map/all_to_all | solution.py:662
  206.1 3.8 %copy-start.15 = (f32[1024,256]{1,0:T(8,128)}, f32[1024,256]{1,0:T(8,128)S(1)}, u32[]{:S(2)}) copy-start(f32[1024,256]{1,0:T(8,128)S(1)} %source.3) | copy-start | bytes 3145732
  206.2 16.6 %copy-start.5 = (f32[8,4,128,128]{3,2,1,0:T(8,128)S(1)}, f32[8,4,128,128]{3,2,1,0:T(8,128)}, u32[]{:S(2)}) copy-start(f32[8,4,128,128]{3,2,1,0:T(8,128)} %tiles.1) | copy-start | bytes 6291460
  206.2 16.6 %copy-start.40 = (f32[128,128]{1,0:T(8,128)S(1)}, f32[128,128]{1,0:T(8,128)}, u32[]{:S(2)}) copy-start(f32[128,128]{1,0:T(8,128)} %copy-done.39) | copy-start | bytes 196612
  206.3 16.6 %copy-start.42 = (f32[128,128]{1,0:T(8,128)S(1)}, f32[128,128]{1,0:T(8,128)}, u32[]{:S(2)}) copy-start(f32[128,128]{1,0:T(8,128)} %copy-done.41) | copy-start | bytes 196612
  206.3 16.6 %copy-start.44 = (f32[128,128]{1,0:T(8,128)S(1)}, f32[128,128]{1,0:T(8,128)}, u32[]{:S(2)}) copy-start(f32[128,128]{1,0:T(8,128)} %copy-done.43) | copy-start | bytes 196612
  210.9 23.9 %collective-permute-start.12 = (f32[64,256]{1,0:T(8,128)}, f32[64,256]{1,0:T(8,128)}, u32[]{:S(2)}, u32[]{:S(2)}) collective-permute-start(f32[64,256]{1,0:T(8,128)} %get-tuple-element.89), channel_id=1, source_target_pairs={{0,16},{16,32},{32,48},{48,64},{64,80},{80,96},{96,112},{1,17},{17... | collective-permute-start | bytes 196616 | tf_op jit(solution)/shard_map/ppermute | solution.py:500
  213.6 21.3 %collective-permute-start.13 = (f32[64,256]{1,0:T(8,128)}, f32[64,256]{1,0:T(8,128)}, u32[]{:S(2)}, u32[]{:S(2)}) collective-permute-start(f32[64,256]{1,0:T(8,128)} %get-tuple-element.90), channel_id=1, source_target_pairs={{16,0},{32,16},{48,32},{64,48},{80,64},{96,80},{112,96},{17,1},{33... | collective-permute-start | bytes 196616 | tf_op jit(solution)/shard_map/ppermute | solution.py:500
  214.9 20.0 %collective-permute-start.14 = (f32[16,256]{1,0:T(8,128)}, f32[16,256]{1,0:T(8,128)S(1)}, u32[]{:S(2)}, u32[]{:S(2)}) collective-permute-start(f32[16,256]{1,0:T(8,128)} %get-tuple-element.91), channel_id=1, source_target_pairs={{0,1},{1,2},{2,3},{3,4},{4,5},{5,6},{6,7},{7,8},{8,9},{9,10},{10,1... | collective-permute-start | bytes 49160 | tf_op jit(solution)/shard_map/ppermute | solution.py:500
  218.3 16.6 %collective-permute-start.15 = (f32[16,256]{1,0:T(8,128)}, f32[16,256]{1,0:T(8,128)S(1)}, u32[]{:S(2)}, u32[]{:S(2)}) collective-permute-start(f32[16,256]{1,0:T(8,128)} %get-tuple-element.92), channel_id=1, source_target_pairs={{1,0},{2,1},{3,2},{4,3},{5,4},{6,5},{7,6},{8,7},{9,8},{10,9},{11,1... | collective-permute-start | bytes 49160 | tf_op jit(solution)/shard_map/ppermute | solution.py:500
  227.0 16.3 %all-to-all-start.9 = ((f32[16,1,128]{2,1,0:T(1,128)}), f32[16,1,128]{2,1,0:T(1,128)S(1)}, u32[]{:S(2)}, u32[]{:S(2)}) async-start(f32[16,1,128]{2,1,0:T(1,128)} %bitcast.34), calls=%async_computation.9 | async-start | bytes 16384 | tf_op jit(solution)/shard_map/all_to_all | solution.py:668
  239.8 3.5 %copy-start.46 = (f32[128,128]{1,0:T(8,128)S(1)}, f32[128,128]{1,0:T(8,128)}, u32[]{:S(2)}) copy-start(f32[128,128]{1,0:T(8,128)} %copy-done.45) | copy-start | bytes 196612
  (48 other events, 46.2 us)

commit v3 on v2

--- a/solution.py
+++ b/solution.py
@@ -12,28 +12,46 @@
 LANES = 128
 F32 = jnp.float32
 BF16 = jnp.bfloat16
-VMEM = pl.BlockSpec(memory_space=pltpu.VMEM)
 SMEM = pl.BlockSpec(memory_space=pltpu.SMEM)
+RAW = pl.BlockSpec(memory_space=pltpu.HBM)
 X, Y, Z, HI, LO, KAPPA, COLS = (CAP * i for i in range(7))
 
 
 def shape(*dims, dtype=F32):
-    return jax.ShapeDtypeStruct(dims, dtype)
-
-
-def call(body, outs, in_specs, flops=1e6, nbytes=1e6, scratch=(), name=None, **more):
-    return pl.pallas_call(
+    return pltpu.HBM(dims, dtype)
+
+
+def in_hbm(x):
+    return pltpu.with_memory_space_constraint(x, pltpu.HBM)
+
+
+def whole(dims):
+    return pl.BlockSpec(dims, lambda i: (0,) * len(dims), pipeline_mode=pl.Buffered(1))
+
+
+def params():
+    return pltpu.CompilerParams(vmem_limit_bytes=32 << 20)
+
+
+def call(body, outs, *operands, scalars=(), raw=(), scratch=(), flops=1e6, nbytes=1e6, name=None):
+    single = not isinstance(outs, tuple)
+    outs = (outs,) if single else outs
+    result = pl.pallas_call(
         body,
+        grid=(1,),
         out_shape=outs,
-        in_specs=in_specs,
+        in_specs=[SMEM] * len(scalars) + [RAW] * len(raw) + [whole(v.shape) for v in operands],
+        out_specs=tuple(
+            pl.BlockSpec(v.shape, lambda i, n=len(v.shape): (0,) * n) for v in outs
+        ),
         scratch_shapes=scratch,
-        compiler_params=pltpu.CompilerParams(vmem_limit_bytes=32 << 20),
+        compiler_params=params(),
         cost_estimate=pl.CostEstimate(
             flops=int(flops), bytes_accessed=int(nbytes), transcendentals=0
         ),
         name=name,
-        **more,
-    )
+    )(*scalars, *(in_hbm(v) for v in (*raw, *operands)))
+    return result[0] if single else result
 
 
 def iota(dims, dim):
@@ -175,9 +193,26 @@
 
 
 def first_body(
-    at, cols, got, pressure, tiles, diag, source, send, x_out, trace_out, flux_out, gathered, part
+    at,
+    cols,
+    tiles_all,
+    got,
+    pressure,
+    diag,
+    source,
+    send,
+    x_out,
+    trace_out,
+    flux_out,
+    gathered,
+    part,
+    tiles,
+    arrived,
 ):
     mine, shard = at[0], at[1]
+    per_row = cols.shape[1]
+    fetch = pltpu.make_async_copy(tiles_all.at[pl.ds(per_row * mine, per_row)], tiles, arrived)
+    fetch.start()
     groups = LANES // CAP
     for m in range(CAP):
         x_out[pl.ds(m, groups, stride=CAP), :] = got[
@@ -193,8 +228,9 @@
     x_row = x_out[pl.ds(row, 1), :]
     x_col = as_column(x_row)
     mixed = jnp.zeros((LANES, LANES), F32)
-    for t in range(cols.shape[1]):
-        tile = tiles[0, t]
+    fetch.wait()
+    for t in range(per_row):
+        tile = tiles[t]
         mixed += tile * x_out[pl.ds(cols[mine, t], 1), :]
         back = jnp.sum(tile * x_col, axis=0, keepdims=True)
         part[pl.ds(cols[mine, t], 1), :] -= 0.5 * back
@@ -226,6 +262,12 @@
     rhs[...] = base[...] + pick(chosen, spread)
 
 
+def second_source_body(got, trace, x, base, rhs):
+    message = got[pl.ds(1, LANES, stride=2), :]
+    flux = kappa_of(message) * (trace[...] - at_mortar(message, x[...]))
+    source_body(got, flux, base, rhs)
+
+
 def second_body(got, pressure, trace, trace_out, send, gathered):
     message = got[pl.ds(1, LANES, stride=2), :]
     now = traces(message, pressure[...], gathered)
@@ -235,22 +277,27 @@
         send[m * LANES : (m + 1) * LANES, :] = change
 
 
-def flux_body(got, trace, x, flux):
-    message = got[pl.ds(1, LANES, stride=2), :]
-    flux[...] = kappa_of(message) * (trace[...] - at_mortar(message, x[...]))
-
-
-def home_body(got, owner, slot, flux):
+def home_body(got, owner, slot, frac, kappa, x, flux):
     count = owner.shape[1]
-    values = got[...].T[:CAP, :]
-    chosen = ones_where(iota((LANES, count), 0) == owner[...])
-    top = values.astype(BF16).astype(F32)
-    middle = (values - top).astype(BF16).astype(F32)
-    stacked = jnp.concatenate([top, middle, values - top - middle, jnp.zeros_like(top)], axis=0)
-    found = jnp.dot(stacked.astype(BF16), chosen, preferred_element_type=F32)
-    found = found[:CAP] + found[CAP : 2 * CAP] + found[2 * CAP : 3 * CAP]
+
+    def found(values, chosen):
+        top = values.astype(BF16).astype(F32)
+        middle = (values - top).astype(BF16).astype(F32)
+        parts = jnp.concatenate([top, middle, values - top - middle], axis=0)
+        if parts.shape[0] % 16:
+            parts = jnp.concatenate([parts, jnp.zeros_like(top)], axis=0)
+        out = jnp.dot(parts.astype(BF16), chosen, preferred_element_type=F32)
+        n = values.shape[0]
+        return out[:n] + out[n : 2 * n] + out[2 * n : 3 * n]
+
+    traces_all = found(got[...].T[:CAP, :], ones_where(iota((LANES, count), 0) == owner[...]))
     here = iota((CAP, count), 0) == slot[...]
-    flux[...] = jnp.sum(jnp.where(here, found, 0.0), axis=0, keepdims=True)
+    trace = jnp.sum(jnp.where(here, traces_all, 0.0), axis=0, keepdims=True)
+    f = frac[...]
+    x_all = found(x[...].T, ones_where(iota((LANES, count), 0) == f >> 7))
+    here = iota((LANES, count), 0) == (f & 127)
+    x_there = jnp.sum(jnp.where(here, x_all, 0.0), axis=0, keepdims=True)
+    flux[...] = kappa[...] * (trace - x_there)
 
 
 def sum_body(got, send):
@@ -298,23 +345,28 @@
     return own + pick(chosen[...], back)
 
 
-def start_body(at, cols, got, tiles, diag, r_out, weight_out, send, block):
+def start_body(at, cols, tiles_all, got, diag, r_out, weight_out, send, block, tiles, arrived):
+    fetch = pltpu.make_async_copy(tiles_all, tiles, arrived)
+    fetch.start()
     r_out[...] = got[pl.ds(0, LANES, stride=2), :]
     weight_out[...] = got[pl.ds(1, LANES, stride=2), :]
+    fetch.wait()
     products(at, cols, r_out, tiles, diag, block)
     size = block.shape[0]
     for s in range(send.shape[0] // size):
         send[s * size : (s + 1) * size, :] = block[...]
 
 
-def step_body(at, cols, got, x, r, d, chosen, tiles, diag, *rest, ride, last):
+def step_body(at, cols, tiles_all, got, x, r, d, chosen, diag, *rest, ride, last):
     rows, per_row = cols.shape
     size = rows * (1 + per_row)
     shards = LANES // rows
     extra = list(rest)
     change = extra.pop(0) if ride == "reduce" else None
     x_before, weight = (extra.pop(0), extra.pop(0)) if ride == "next" else (None, None)
-    x_out, r_out, d_out, send, block = extra
+    x_out, r_out, d_out, send, block, tiles, arrived = extra
+    fetch = pltpu.make_async_copy(tiles_all, tiles, arrived)
+    fetch.start()
     got_step = got.shape[0] // shards
     image = image_of(got, chosen, got_step, rows, rows * per_row)
     old = d[...]
@@ -332,6 +384,7 @@
     else:
         d_out[...] = r_new + (total(r_new * r_new) / norm) * old
     r_out[...] = r_new
+    fetch.wait()
     if last:
         shard = at[1]
         lanes = jnp.zeros((1, LANES), F32)
@@ -370,25 +423,35 @@
     out[...] = x[here, :] + alpha * d[here, :]
 
 
-def edges_body(px0, px1, py0, py1, tx1, ty1, x_up, x_down, y_up, y_down):
-    wide = px0.shape[1]
-    x_up[:wide, :] = px1[0]
-    x_up[wide:, :] = tx1[0, 0]
-    x_down[...] = px0[0]
-    deep = py0.shape[0]
-    y_up[:deep, :] = py1[:, 7, :]
-    y_up[deep:, :] = ty1[0, :, 7, :]
-    y_down[...] = py0[:, 0, :]
-
-
-def edges(pressure, trans):
+def even(at, dim):
+    return (at[dim] & 1) == 0
+
+
+def edges_body(at, px0, px1, py0, py1, tx1, ty1, xa, xb, ya, yb):
+    wide, deep = px0.shape[1], py0.shape[0]
+    low, high = px0[0], px1[0]
+    xa[:wide, :] = jnp.where(even(at, 0), high, low)
+    xb[:wide, :] = jnp.where(even(at, 0), low, high)
+    xa[wide:, :] = tx1[0, 0]
+    xb[wide:, :] = tx1[0, 0]
+    low, high = py0[:, 0, :], py1[:, 7, :]
+    ya[:deep, :] = jnp.where(even(at, 1), high, low)
+    yb[:deep, :] = jnp.where(even(at, 1), low, high)
+    ya[deep:, :] = ty1[0, :, 7, :]
+    yb[deep:, :] = ty1[0, :, 7, :]
+
+
+def edges(at, pressure, trans):
     nx, ny, nz = pressure.shape
     y_last = ny // 8 - 1
+    out = [(2 * ny, nz)] * 2 + [(2 * nx, nz)] * 2
+    pressure, trans = in_hbm(pressure), in_hbm(trans)
     return pl.pallas_call(
         edges_body,
         grid=(1,),
-        out_shape=(shape(2 * ny, nz), shape(ny, nz), shape(2 * nx, nz), shape(nx, nz)),
+        out_shape=tuple(shape(*v) for v in out),
         in_specs=[
+            SMEM,
             pl.BlockSpec((1, ny, nz), lambda i: (0, 0, 0)),
             pl.BlockSpec((1, ny, nz), lambda i: (nx - 1, 0, 0)),
             pl.BlockSpec((nx, 8, nz), lambda i: (0, 0, 0)),
@@ -396,48 +459,59 @@
             pl.BlockSpec((1, 1, ny, nz), lambda i: (0, nx - 1, 0, 0)),
             pl.BlockSpec((1, nx, 8, nz), lambda i: (1, 0, y_last, 0)),
         ],
-        out_specs=(VMEM,) * 4,
-        compiler_params=pltpu.CompilerParams(vmem_limit_bytes=16 << 20),
+        out_specs=tuple(pl.BlockSpec(v, lambda i: (0, 0)) for v in out),
+        compiler_params=params(),
         name="edges",
-    )(pressure, pressure, pressure, pressure, trans, trans)
+    )(at, pressure, pressure, pressure, pressure, trans, trans)
 
 
 def sweep_body(
-    p, x_low, x_high, y_low, y_high, tx_low, ty_low, trans, cell, rhs, *rest, first, last
+    at, p, xa, xb, ya, yb, cxa, cxb, cya, cyb, trans, cell, rhs, *rest, first, last
 ):
     rest = list(rest)
     weight = None if first else rest.pop(0)
     out = rest.pop(0)
     weight_out = rest.pop(0) if first else None
-    carry, carry_t = rest.pop(), rest.pop()
+    carry_t = rest.pop() if first else None
+    carry = rest.pop()
     step = pl.program_id(0)
-    many = out.shape[0]
-    ny, nz = out.shape[1:]
+    steps = pl.num_programs(0)
+    many, ny, nz = out.shape
     nx = p.shape[0]
-    zero_row = iota((ny, nz), 0)
+    row = iota((ny, nz), 0)
     lane = iota((ny, nz), 1)
+    x_even, y_even = even(at, 0), even(at, 1)
 
     @pl.when(step == 0)
     def _():
-        carry[...] = tx_low[...] * (x_low[...] - p[0])
-        carry_t[...] = tx_low[...]
+        tx_low = jnp.where(x_even, cxb[ny:, :], cxa[ny:, :])
+        carry[...] = tx_low * (jnp.where(x_even, xb[:ny, :], xa[:ny, :]) - p[0])
+        if first:
+            carry_t[...] = tx_low
 
     for i in range(many):
-        at = step * many + i
-        here = p[at]
-        after = jnp.where(at + 1 < nx, p[jnp.minimum(at + 1, nx - 1)], x_high[...])
+        here_at = step * many + i
+        here = p[here_at]
+        if i + 1 < many:
+            after = p[here_at + 1]
+        else:
+            x_high = jnp.where(x_even, xa[:ny, :], xb[:ny, :])
+            after = jnp.where(step + 1 < steps, p[jnp.minimum(here_at + 1, nx - 1)], x_high)
+        one = pl.ds(here_at, 1)
+        edge = pl.ds(nx + here_at, 1)
+        y_low = jnp.where(y_even, yb[one, :], ya[one, :])
+        y_high = jnp.where(y_even, ya[one, :], yb[one, :])
+        ty_edge = jnp.where(y_even, cyb[edge, :], cya[edge, :])
         tx, ty, tz = trans[0, i], trans[1, i], trans[2, i]
         fx = tx * (here - after)
-        y_next = jnp.where(zero_row == ny - 1, y_high[pl.ds(at, 1), :], pltpu.roll(here, ny - 1, 0))
+        y_next = jnp.where(row == ny - 1, y_high, pltpu.roll(here, ny - 1, 0))
         fy = ty * (here - y_next)
-        ty_edge = ty_low[pl.ds(at, 1), :]
-        fy_edge = ty_edge * (y_low[pl.ds(at, 1), :] - here[:1])
-        fy_low = jnp.where(zero_row == 0, fy_edge, pltpu.roll(fy, 1, 0))
+        fy_low = jnp.where(row == 0, ty_edge * (y_low - here[:1]), pltpu.roll(fy, 1, 0))
         z_next = jnp.where(lane == nz - 1, 0.0, pltpu.roll(here, nz - 1, 1))
         fz = tz * (here - z_next)
         fz_low = jnp.where(lane == 0, 0.0, pltpu.roll(fz, 1, 1))
         if first:
-            ty_before = jnp.where(zero_row == 0, ty_edge, pltpu.roll(ty, 1, 0))
+            ty_before = jnp.where(row == 0, ty_edge, pltpu.roll(ty, 1, 0))
             tz_before = jnp.where(lane == 0, 0.0, pltpu.roll(tz, 1, 1))
             diagonal = cell[i] + tx + carry_t[...] + ty + ty_before + tz + tz_before
             w = WEIGHT / diagonal
@@ -448,25 +522,36 @@
         applied = cell[i] * here + fx - carry[...] + fy - fy_low + fz - fz_low
         carry[...] = fx
         out[i] = here + w * (rhs[i] - applied)
-    if not last:
-        x_up, x_down, y_up, y_down = rest
-
-        @pl.when(step == 0)
-        def _():
-            x_down[...] = out[0]
-
-        @pl.when(step == pl.num_programs(0) - 1)
-        def _():
-            x_up[...] = out[many - 1]
-
-        for i in range(many):
-            y_down[pl.ds(step * many + i, 1), :] = out[i, :1, :]
-            y_up[pl.ds(step * many + i, 1), :] = out[i, ny - 1 :, :]
-
-
-def sweep(p, halo, lows, trans, cell, rhs, weight=None, last=False, many=4):
+    if last:
+        return
+    xa_out, xb_out, ya_out, yb_out = rest
+    start, end = step == 0, step == steps - 1
+
+    @pl.when(start & x_even)
+    def _():
+        xb_out[...] = out[0]
+
+    @pl.when(start & ~x_even)
+    def _():
+        xa_out[...] = out[0]
+
+    @pl.when(end & x_even)
+    def _():
+        xa_out[...] = out[many - 1]
+
+    @pl.when(end & ~x_even)
+    def _():
+        xb_out[...] = out[many - 1]
+
+    for i in range(many):
+        one = pl.ds(step * many + i, 1)
+        low, high = out[i, :1, :], out[i, ny - 1 :, :]
+        ya_out[one, :] = jnp.where(y_even, high, low)
+        yb_out[one, :] = jnp.where(y_even, low, high)
+
+
+def sweep(at, p, halo, faces, trans, cell, rhs, weight=None, last=False, many=4):
     nx, ny, nz = p.shape
-    whole = pl.BlockSpec((nx, ny, nz), lambda i: (0, 0, 0))
     part = pl.BlockSpec((many, ny, nz), lambda i: (i, 0, 0))
     x_face = pl.BlockSpec((ny, nz), lambda i: (0, 0))
     y_face = pl.BlockSpec((nx, nz), lambda i: (0, 0))
@@ -478,32 +563,33 @@
     if not last:
         out_shape += [shape(ny, nz)] * 2 + [shape(nx, nz)] * 2
         out_specs += [x_face, x_face, y_face, y_face]
-    operands = [p, *halo, *lows, trans, cell, rhs] + ([] if first else [weight])
+    operands = [p, *halo, *faces, trans, cell, rhs] + ([] if first else [weight])
     return pl.pallas_call(
         functools.partial(sweep_body, first=first, last=last),
         grid=(nx // many,),
         out_shape=tuple(out_shape),
-        in_specs=[whole, x_face, x_face, y_face, y_face, x_face, y_face]
+        in_specs=[SMEM]
+        + [whole(v.shape) for v in (p, *halo, *faces)]
         + [pl.BlockSpec((3, many, ny, nz), lambda i: (0, i, 0, 0)), part, part]
         + ([] if first else [part]),
         out_specs=tuple(out_specs),
-        scratch_shapes=[pltpu.VMEM((ny, nz), F32)] * 2,
-        compiler_params=pltpu.CompilerParams(vmem_limit_bytes=32 << 20),
+        scratch_shapes=[pltpu.VMEM((ny, nz), F32)] * (2 if first else 1),
+        compiler_params=params(),
         cost_estimate=pl.CostEstimate(flops=6_000_000, bytes_accessed=8 << 20, transcendentals=0),
         name="sweep",
-    )(*operands)
-
-
-def shifted(x_up, x_down, y_up, y_down, mats, shards):
-    def move(v, axis, count, by):
-        pairs = [(i, i + by) for i in range(count) if 0 <= i + by < count]
-        return lax.ppermute(v, axis, pairs)
+    )(at, *(in_hbm(v) for v in operands))
+
+
+def swapped(xa, xb, ya, yb, mats, shards):
+    def swap(v, axis, count, low):
+        pairs = [(i, i + 1) for i in range(low, count - 1, 2)]
+        return lax.ppermute(v, axis, pairs + [(b, a) for a, b in pairs])
 
     return (
-        move(x_up, "mat", mats, 1),
-        move(x_down, "mat", mats, -1),
-        move(y_up, "frac", shards, 1),
-        move(y_down, "frac", shards, -1),
+        swap(xa, "mat", mats, 0),
+        swap(xb, "mat", mats, 1),
+        swap(ya, "frac", shards, 0),
+        swap(yb, "frac", shards, 1),
     )
 
 
@@ -539,135 +625,153 @@
     )
     square = shape(LANES, LANES)
     owner = mortar_owner.reshape(1, count)
+    frac, kappa = mortar_frac.reshape(1, count), mortar_kappa.reshape(1, count)
     flat = (nx * ny, nz)
     tile_list = tiles.reshape(rows * per_row, LANES, LANES)
     diag = frac_diag.reshape(rows, LANES)
     square_scratch = pltpu.VMEM((LANES, LANES), F32)
     gathered = pltpu.VMEM((CAP * LANES, nz), F32)
     block = pltpu.VMEM((size, LANES), F32)
+    tile_scratch = [
+        pltpu.VMEM((rows * per_row, LANES, LANES), F32),
+        pltpu.SemaphoreType.DMA(()),
+    ]
+    scalars = (at, tile_cols)
 
     send, slot = call(
         pack_body,
         (shape(2 * LANES, LANES), shape(1, count, dtype=jnp.int32)),
-        [SMEM, SMEM] + [VMEM] * 6,
-        scratch=[square_scratch],
-        name="pack",
-    )(
-        at,
-        tile_cols,
         mortar_owner,
         owner,
         mortar_cell.reshape(1, count),
-        mortar_frac.reshape(1, count),
-        mortar_kappa.reshape(1, count),
+        frac,
+        kappa,
         fracture_start.reshape(rows, LANES),
+        scalars=scalars,
+        scratch=[square_scratch],
+        name="pack",
     )
     got = everyone(send)
 
-    x_low, x_high, y_low, y_high = shifted(
-        *edges(pressure_start, face_trans), mats, shards
-    )
-    lows = (x_low[ny:], y_low[nx:])
-    halo = (x_low[:ny], x_high, y_low[:nx], y_high)
-
-    send, x_start, trace, flux = pl.pallas_call(
+    faces = swapped(*edges(at, pressure_start, face_trans), mats, shards)
+
+    send, x_start, trace, flux = call(
         first_body,
-        out_shape=(shape(2 * LANES, LANES), square, square, square),
-        grid_spec=pltpu.PrefetchScalarGridSpec(
-            num_scalar_prefetch=2,
-            grid=(1,),
-            in_specs=[
-                VMEM,
-                VMEM,
-                pl.BlockSpec(
-                    (1, per_row, LANES, LANES), lambda i, at, cols: (at[0], 0, 0, 0)
-                ),
-                VMEM,
-                VMEM,
-            ],
-            out_specs=(VMEM,) * 4,
-            scratch_shapes=[gathered, square_scratch],
-        ),
-        compiler_params=pltpu.CompilerParams(vmem_limit_bytes=32 << 20),
+        (shape(2 * LANES, LANES), square, square, square),
+        got,
+        pressure_start.reshape(flat),
+        diag,
+        frac_source.reshape(rows, LANES),
+        scalars=scalars,
+        raw=(tile_list,),
+        scratch=[
+            gathered,
+            square_scratch,
+            pltpu.VMEM((per_row, LANES, LANES), F32),
+            pltpu.SemaphoreType.DMA(()),
+        ],
+        flops=2e9,
         name="first",
-    )(at, tile_cols, got, pressure_start.reshape(flat), tiles, diag, frac_source.reshape(rows, LANES))
+    )
     reduced = everyone(send)
-    send = call(sum_body, shape(2 * LANES, LANES), [VMEM], name="sums")(reduced)
+    base = matrix_source.reshape(flat)
+    rhs = call(source_body, shape(*flat), got, flux, base, flops=2e9, name="source")
+    rhs = rhs.reshape(nx, ny, nz)
+    pressure, weight, *sides = sweep(
+        at, pressure_start, faces, faces, face_trans, cell_coef, rhs
+    )
+    sides = swapped(*sides, mats, shards)
+
+    send = call(sum_body, shape(2 * LANES, LANES), reduced, name="sums")
+    send, pressure = lax.optimization_barrier((send, pressure))
     residuals = everyone(send)
-
-    base = matrix_source.reshape(flat)
-
-    def with_source(flux):
-        return call(source_body, shape(*flat), [VMEM] * 3, flops=2e9, nbytes=2 << 20, name="source")(
-            got, flux, base
-        ).reshape(nx, ny, nz)
-
     chosen = call(
         functools.partial(columns_body, shards=shards, rows=rows, tiles=per_row),
         shape(LANES, shards * rows * per_row, dtype=BF16),
-        [VMEM],
+        got,
         name="columns",
-    )(got)
-    rhs = with_source(flux)
-    pressure, weight, *sides = sweep(
-        pressure_start, halo, lows, face_trans, cell_coef, rhs
-    )
-    pressure, *sides = sweep(
-        pressure, shifted(*sides, mats, shards), lows, face_trans, cell_coef, rhs, weight
-    )
-    halo = shifted(*sides, mats, shards)
-    trace, send = call(
-        second_body,
-        (square, shape(mats * LANES, LANES)),
-        [VMEM] * 3,
-        flops=2e9,
-        nbytes=2 << 20,
-        scratch=[gathered],
-        name="second",
-    )(got, pressure.reshape(flat), trace)
-    change = over_mat(send)
+    )
+    pressure, *sides = sweep(at, pressure, sides, faces, face_trans, cell_coef, rhs, weight)
 
     r, sums, send = call(
         start_body,
         (square, square, shape(shards * size, LANES)),
-        [SMEM, SMEM] + [VMEM] * 3,
-        scratch=[block],
+        residuals,
+        diag,
+        scalars=scalars,
+        raw=(tile_list,),
+        scratch=[block, *tile_scratch],
         name="start",
-    )(at, tile_cols, residuals, tile_list, diag)
+    )
     x, d = x_start, r
+    send, pressure = lax.optimization_barrier((send, pressure))
+    arrived = over_frac(send)
+    trace, change = call(
+        second_body,
+        (square, shape(mats * LANES, LANES)),
+        got,
+        pressure.reshape(flat),
+        trace,
+        scratch=[gathered],
+        flops=2e9,
+        name="second",
+    )
+    change = over_mat(change)
 
     def step(arrived, x, r, d, *more, ride=None, last=False):
-        length = LANES if last else shards * (size + (rows if ride in ("reduce", "gather") else 0))
-        if last:
-            length = shards
+        length = shards * (size + (rows if ride in ("reduce", "gather") else 0))
         return call(
             functools.partial(step_body, ride=ride, last=last),
-            (square, square, square, shape(length, LANES)),
-            [SMEM, SMEM] + [VMEM] * (7 + len(more)),
-            scratch=[block],
+            (square, square, square, shape(shards if last else length, LANES)),
+            arrived,
+            x,
+            r,
+            d,
+            chosen,
+            diag,
+            *more,
+            scalars=scalars,
+            raw=(tile_list,),
+            scratch=[block, *tile_scratch],
             name="step",
-        )(at, tile_cols, arrived, x, r, d, chosen, tile_list, diag, *more)
-
-    x, r, d, send = step(over_frac(send), x, r, d, change, ride="reduce")
-    x, r, d, send = step(over_frac(send), x, r, d, ride="gather")
-    x, r, d, send = step(over_frac(send), x, r, d, x_start, sums, ride="next")
-
-    flux = call(flux_body, square, [VMEM] * 3, name="flux")(got, trace, x)
-    rhs = with_source(flux)
-    pressure, *sides = sweep(pressure, halo, lows, face_trans, cell_coef, rhs, weight)
+        )
+
+    x, r, d, send = step(arrived, x, r, d, change, ride="reduce")
+    send, trace, sides = lax.optimization_barrier((send, trace, sides))
+    arrived = over_frac(send)
+    sides = swapped(*sides, mats, shards)
+
+    x, r, d, send = step(arrived, x, r, d, ride="gather")
+    send, home = lax.optimization_barrier((send, trace))
+    arrived = over_frac(send)
+    home = everyone(home)
+
+    x, r, d, send = step(arrived, x, r, d, x_start, sums, ride="next")
+    x_flux = x
+    arrived = over_frac(send)
+    rhs = call(
+        second_source_body, shape(*flat), got, trace, x_flux, base, flops=2e9, name="source"
+    ).reshape(nx, ny, nz)
+    pressure, *sides = sweep(at, pressure, sides, faces, face_trans, cell_coef, rhs, weight)
+
+    x, r, d, send = step(arrived, x, r, d)
+    send, sides, home = lax.optimization_barrier((send, sides, home))
+    arrived = over_frac(send)
+    sides = swapped(*sides, mats, shards)
+    flux = call(
+        home_body, shape(1, count), home, owner, slot, frac, kappa, x_flux, name="home"
+    )
+
+    x, r, d, send = step(arrived, x, r, d, last=True)
+    send, pressure, flux = lax.optimization_barrier((send, pressure, flux))
+    arrived = over_frac(send)
     [pressure] = sweep(
-        pressure, shifted(*sides, mats, shards), lows, face_trans, cell_coef, rhs, weight, last=True
-    )
-    flux_out = call(home_body, shape(1, count), [VMEM] * 3, name="home")(
-        everyone(flux), owner, slot
-    )
-
-    x, r, d, send = step(over_frac(send), x, r, d)
-    x, r, d, send = step(over_frac(send), x, r, d, last=True)
-    fracture = call(final_body, shape(rows, LANES), [SMEM] + [VMEM] * 4, name="final")(
-        at, over_frac(send), x, r, d
-    )
-    return pressure, fracture.reshape(rows * LANES), flux_out.reshape(count)
+        at, pressure, sides, faces, face_trans, cell_coef, rhs, weight, last=True
+    )
+    fracture = call(
+        final_body, shape(rows, LANES), arrived, x, r, d, scalars=(at,), name="final"
+    )
+    return pressure, fracture.reshape(rows * LANES), flux.reshape(count)
 
 
 def solution(mesh):

time: 250 us -> 232 us (0.928)
  the two profiles are of different devices: /device:TPU:32 before, /device:TPU:1 now
where the time goes in v3:
time: 232 us; the launch traced here: 230 us
  starting transfers between devices  98.5 us (42%)
  Pallas kernels  76.6 us (33%)
  blocking collectives  26 us (11%)
  waiting for transfers between devices  18.2 us (8%)
  local copies, waits for them, and re-layouts  9.54 us (4%)
    pallas_call x15, Pallas kernels, call(): pl.pallas_call(body, grid=(1,), out_shape=outs, in_specs=[SMEM] * len(sca...  51.9 us
    all_to_all x4, starting transfers between devices, body(): arrived = over_frac(send)  29.1 us
    all_to_all x2, blocking collectives, body(): arrived = over_frac(send)  26 us
    ppermute x16, starting transfers between devices, swap(): return lax.ppermute(v, axis, pairs + [(b, a) for a, b in pairs])  24.7 us
    pallas_call x4, Pallas kernels, sweep(): pl.pallas_call(functools.partial(sweep_body, first=first, last=last), gri...  22.8 us
    all_to_all x1, starting transfers between devices, body(): got = everyone(send)  11.5 us
    all_to_all x1, starting transfers between devices, body(): home = everyone(home)  10.1 us
    all_to_all x1, starting transfers between devices, body(): residuals = everyone(send)  9.76 us
  transfers between devices with their start and end apart: 25, of which 7 were waited for; matrix products, arithmetic and copies ran while one was open for 0% of the time, Pallas kernels for 24%

profile of v3, /device:TPU:1, one launch (start us, length us, event | category | flops | bytes accessed | tf_op | source)
XLA Modules:
  0.0 230.1 jit_solution(1555832089742904461)
XLA Ops:
  1.4 1.5 copy.26.owner_col
  3.0 2.0 pack.1
  5.0 11.5 %all-to-all-start = ((f32[128,2,128]{2,1,0:T(2,128)}), f32[128,2,128]{2,1,0:T(2,128)S(1)}, u32[]{:S(2)}, u32[]{:S(2)}) async-start(f32[128,2,128]{2,1,0:T(2,128)} %bitcast.85), calls=%async_computation | async-start | bytes 262144 | tf_op jit(solution)/shard_map/all_to_all | solution.py:654
  16.5 1.9 edges.1
  18.4 1.1 collective-permute-start
  19.5 2.6 %collective-permute-start.1 = (f32[128,256]{1,0:T(8,128)}, f32[128,256]{1,0:T(8,128)S(1)}, u32[]{:S(2)}, u32[]{:S(2)}) collective-permute-start(f32[128,256]{1,0:T(8,128)} %get-tuple-element.78), channel_id=1, source_target_pairs={{16,32},{48,64},{80,96},{32,16},{64,48},{96,80},{17,33},{49,65},{8... | collective-permute-start | bytes 393224 | tf_op jit(solution)/shard_map/ppermute | solution.py:586
  22.1 1.3 collective-permute-start.2
  24.1 2.7 %all-to-all-done = f32[128,2,128]{2,1,0:T(2,128)S(1)} async-done(((f32[128,2,128]{2,1,0:T(2,128)}), f32[128,2,128]{2,1,0:T(2,128)S(1)}, u32[]{:S(2)}, u32[]{:S(2)}) %all-to-all-start) | async-done | bytes 131104 | tf_op jit(solution)/shard_map/all_to_all | solution.py:654
  27.4 5.4 %first.1 = (f32[256,128]{1,0:T(8,128)}, f32[128,128]{1,0:T(8,128)}, f32[128,128]{1,0:T(8,128)}, f32[128,128]{1,0:T(8,128)}) custom-call(s32[2]{0:T(128)S(1)} %pad_add_fusion.at, s32[8,4]{1,0:T(8,128)S(1)} %copy.34.cols, f32[32,128,128]{2,1,0:T(8,128)} %bitcast.43, f32[256,128]{1,0:T(8,128)} %bitcast.64, f32[1024,256]{1,0:T(8,128)} %bitcast.50, ...), custom_call_target="tpu_custom_call" | custom-call | flops 2000000000 | bytes 1000000 | tf_op jit(solution)/shard_map/first/pallas_call | solution.py:39
  32.8 8.6 %all-to-all-start.1 = ((f32[128,2,128]{2,1,0:T(2,128)}), f32[128,2,128]{2,1,0:T(2,128)S(1)}, u32[]{:S(2)}, u32[]{:S(2)}) async-start(f32[128,2,128]{2,1,0:T(2,128)} %bitcast.84), calls=%async_computation.1 | async-start | bytes 262144 | tf_op jit(solution)/shard_map/all_to_all | solution.py:676
  41.3 4.4 %source.2 = f32[1024,256]{1,0:T(8,128)} custom-call(f32[256,128]{1,0:T(8,128)} %bitcast.65, f32[128,128]{1,0:T(8,128)} %get-tuple-element.81.flux, f32[1024,256]{1,0:T(8,128)} %bitcast.98), custom_call_target="tpu_custom_call" | custom-call | flops 2000000000 | bytes 1000000 | tf_op jit(solution)/shard_map/source/pallas_call | solution.py:39
  46.5 6.2 %sweep.4 = (f32[16,64,256]{2,1,0:T(8,128)}, f32[16,64,256]{2,1,0:T(8,128)}, f32[64,256]{1,0:T(8,128)}, f32[64,256]{1,0:T(8,128)}, f32[16,256]{1,0:T(8,128)}, /*index=5*/f32[16,256]{1,0:T(8,128)}) custom-call(s32[2]{0:T(128)S(1)} %pad_add_fusion.at, f32[16,64,256]{2,1,0:T(8,128)} %p.1, f32[128,256]{1,0:T(8,128)} %copy-done, f32[128,256]{1,0:T(8,128)} %copy-done.1, ...), custom_call_target="tpu_custom_call" | custom-call | flops 6000000 | bytes 8388608 | tf_op jit(solution)/shard_map/sweep/pallas_call | solution.py:567
  53.4 1.6 sums.1
  55.0 9.8 %all-to-all-start.2 = ((f32[128,2,128]{2,1,0:T(2,128)}), f32[128,2,128]{2,1,0:T(2,128)S(1)}, u32[]{:S(2)}, u32[]{:S(2)}) async-start(f32[128,2,128]{2,1,0:T(2,128)} %bitcast.69), calls=%async_computation.2 | async-start | bytes 262144 | tf_op jit(solution)/shard_map/all_to_all | solution.py:687
  64.7 1.1 collective-permute-start.4
  65.9 2.6 %collective-permute-start.5 = (f32[64,256]{1,0:T(8,128)}, f32[64,256]{1,0:T(8,128)S(1)}, u32[]{:S(2)}, u32[]{:S(2)}) collective-permute-start(f32[64,256]{1,0:T(8,128)} %get-tuple-element.87), channel_id=1, source_target_pairs={{16,32},{48,64},{80,96},{32,16},{64,48},{96,80},{17,33},{49,65},{8... | collective-permute-start | bytes 196616 | tf_op jit(solution)/shard_map/ppermute | solution.py:586
  68.5 1.3 collective-permute-start.6
  70.4 1.2 collective-permute-done.6.ya
  72.6 5.6 %sweep.5 = (f32[16,64,256]{2,1,0:T(8,128)}, f32[64,256]{1,0:T(8,128)}, f32[64,256]{1,0:T(8,128)}, f32[16,256]{1,0:T(8,128)}, f32[16,256]{1,0:T(8,128)}) custom-call(s32[2]{0:T(128)S(1)} %pad_add_fusion.at, f32[16,64,256]{2,1,0:T(8,128)} %get-tuple-element.85.p, f32[64,256]{1,0:T(8,128)} %copy-done.16, f32[64,256]{1,0:T(8,128)} %copy-done.17, ...), custom_call_target="tpu_custom_call" | custom-call | flops 6000000 | bytes 8388608 | tf_op jit(solution)/shard_map/sweep/pallas_call | solution.py:567
  78.8 3.6 %start.1 = (f32[128,128]{1,0:T(8,128)}, f32[128,128]{1,0:T(8,128)}, f32[640,128]{1,0:T(8,128)}) custom-call(s32[2]{0:T(128)S(1)} %pad_add_fusion.at, s32[8,4]{1,0:T(8,128)S(1)} %copy.34.cols, f32[32,128,128]{2,1,0:T(8,128)} %bitcast.44, f32[256,128]{1,0:T(8,128)} %bitcast.62, f32[8,128]{1,0:T(8,128)} %bitcast.78), custom_call_target="tpu_custom_call" | custom-call | flops 1000000 | bytes 1000000 | tf_op jit(solution)/shard_map/start/pallas_call | solution.py:39
  82.5 10.8 %all-to-all-start.3 = ((f32[16,40,128]{2,1,0:T(8,128)}), f32[16,40,128]{2,1,0:T(8,128)S(1)}, u32[]{:S(2)}, u32[]{:S(2)}) async-start(f32[16,40,128]{2,1,0:T(8,128)} %bitcast.75), calls=%async_computation.3 | async-start | bytes 655360 | tf_op jit(solution)/shard_map/all_to_all | solution.py:708
  93.2 4.8 %second.1 = (f32[128,128]{1,0:T(8,128)}, f32[1024,128]{1,0:T(8,128)}) custom-call(f32[256,128]{1,0:T(8,128)} %bitcast.66, f32[1024,256]{1,0:T(8,128)} %bitcast.61, f32[128,128]{1,0:T(8,128)} %get-tuple-element.96.trace), custom_call_target="tpu_custom_call" | custom-call | flops 2000000000 | bytes 1000000 | tf_op jit(solution)/shard_map/second/pallas_call | solution.py:39
  98.0 4.9 %all-to-all-done.3 = f32[16,40,128]{2,1,0:T(8,128)S(1)} async-done(((f32[16,40,128]{2,1,0:T(8,128)}), f32[16,40,128]{2,1,0:T(8,128)S(1)}, u32[]{:S(2)}, u32[]{:S(2)}) %all-to-all-start.3) | async-done | bytes 327712 | tf_op jit(solution)/shard_map/all_to_all | solution.py:708
  102.9 4.8 %all-to-all-start.4 = ((f32[8,128,128]{2,1,0:T(8,128)}), f32[8,128,128]{2,1,0:T(8,128)S(1)}, u32[]{:S(2)}, u32[]{:S(2)}) async-start(f32[8,128,128]{2,1,0:T(8,128)} %bitcast.63), calls=%async_computation.4 | async-start | bytes 1048576 | tf_op jit(solution)/shard_map/all_to_all | solution.py:719
  107.7 1.8 columns.1.chosen
  109.5 7.7 %all-to-all-done.4 = f32[8,128,128]{2,1,0:T(8,128)S(1)} async-done(((f32[8,128,128]{2,1,0:T(8,128)}), f32[8,128,128]{2,1,0:T(8,128)S(1)}, u32[]{:S(2)}, u32[]{:S(2)}) %all-to-all-start.4) | async-done | bytes 524320 | tf_op jit(solution)/shard_map/all_to_all | solution.py:719
  118.0 4.1 %step.5 = (f32[128,128]{1,0:T(8,128)}, f32[128,128]{1,0:T(8,128)}, f32[128,128]{1,0:T(8,128)}, f32[768,128]{1,0:T(8,128)}) custom-call(s32[2]{0:T(128)S(1)} %pad_add_fusion.at, s32[8,4]{1,0:T(8,128)S(1)} %copy.34.cols, f32[32,128,128]{2,1,0:T(8,128)} %bitcast.45, f32[640,128]{1,0:T(8,128)} %bitcast.60, f32[128,128]{1,0:T(8,128)} %get-tuple-element.93.x.rest_0_, ...), custom_call_target="tpu_custom_call" | custom-call | flops 1000000 | bytes 1000000 | tf_op jit(solution)/shard_map/step/pallas_call | solution.py:39
  122.1 13.5 %all_to_all.122 = f32[16,48,128]{2,1,0:T(8,128)} all-to-all(f32[16,48,128]{2,1,0:T(8,128)} %bitcast.71), channel_id=1, replica_groups=mesh['mat'=8,'frac'=16] {'frac'}, dimensions={0} | all-to-all | bytes 786432 | tf_op jit(solution)/shard_map/all_to_all | solution.py:741
  135.6 3.9 %step.6 = (f32[128,128]{1,0:T(8,128)}, f32[128,128]{1,0:T(8,128)}, f32[128,128]{1,0:T(8,128)}, f32[768,128]{1,0:T(8,128)}) custom-call(s32[2]{0:T(128)S(1)} %pad_add_fusion.at, s32[8,4]{1,0:T(8,128)S(1)} %copy.34.cols, f32[32,128,128]{2,1,0:T(8,128)} %bitcast.46, f32[768,128]{1,0:T(8,128)} %bitcast.57, f32[128,128]{1,0:T(8,128)} %get-tuple-element.105.x, ...), custom_call_target="tpu_custom_call" | custom-call | flops 1000000 | bytes 1000000 | tf_op jit(solution)/shard_map/step/pallas_call | solution.py:39
  139.5 12.5 %all_to_all.123 = f32[16,48,128]{2,1,0:T(8,128)} all-to-all(f32[16,48,128]{2,1,0:T(8,128)} %bitcast.72), channel_id=1, replica_groups=mesh['mat'=8,'frac'=16] {'frac'}, dimensions={0} | all-to-all | bytes 786432 | tf_op jit(solution)/shard_map/all_to_all | solution.py:746
  152.0 3.9 %step.7 = (f32[128,128]{1,0:T(8,128)}, f32[128,128]{1,0:T(8,128)}, f32[128,128]{1,0:T(8,128)}, f32[640,128]{1,0:T(8,128)}) custom-call(s32[2]{0:T(128)S(1)} %pad_add_fusion.at, s32[8,4]{1,0:T(8,128)S(1)} %copy.34.cols, f32[32,128,128]{2,1,0:T(8,128)} %bitcast.47, f32[768,128]{1,0:T(8,128)} %bitcast.56, f32[128,128]{1,0:T(8,128)} %get-tuple-element.111.x, ...), custom_call_target="tpu_custom_call" | custom-call | flops 1000000 | bytes 1000000 | tf_op jit(solution)/shard_map/step/pallas_call | solution.py:39
  155.9 3.6 %all-to-all-start.7 = ((f32[16,40,128]{2,1,0:T(8,128)}), f32[16,40,128]{2,1,0:T(8,128)S(1)}, u32[]{:S(2)}, u32[]{:S(2)}) async-start(f32[16,40,128]{2,1,0:T(8,128)} %bitcast.74), calls=%async_computation.7 | async-start | bytes 655360 | tf_op jit(solution)/shard_map/all_to_all | solution.py:751
  159.4 2.9 %collective-permute-start.8 = (f32[64,256]{1,0:T(8,128)S(1)}, f32[64,256]{1,0:T(8,128)S(1)}, u32[]{:S(2)}, u32[]{:S(2)}) collective-permute-start(f32[64,256]{1,0:T(8,128)S(1)} %copy-done.26), channel_id=1, source_target_pairs={{0,16},{32,48},{64,80},{96,112},{16,0},{48,32},{80,64},{112,96},{1... | collective-permute-start | bytes 196616 | tf_op jit(solution)/shard_map/ppermute | solution.py:586
  162.4 2.1 collective-permute-start.9
  164.5 1.6 collective-permute-start.10
  167.4 10.1 %all-to-all-start.8 = ((f32[128,1,128]{2,1,0:T(1,128)}), f32[128,1,128]{2,1,0:T(1,128)S(1)}, u32[]{:S(2)}, u32[]{:S(2)}) async-start(f32[128,1,128]{2,1,0:T(1,128)} %bitcast.32), calls=%async_computation.8 | async-start | bytes 131072 | tf_op jit(solution)/shard_map/all_to_all | solution.py:747
  177.5 5.6 %source.3 = f32[1024,256]{1,0:T(8,128)} custom-call(f32[256,128]{1,0:T(8,128)} %bitcast.68, f32[128,128]{1,0:T(8,128)} %get-tuple-element.128.trace, f32[128,128]{1,0:T(8,128)} %get-tuple-element.116.x, f32[1024,256]{1,0:T(8,128)} %bitcast.99), custom_call_target="tpu_custom_call" | custom-call | flops 2000000000 | bytes 1000000 | tf_op jit(solution)/shard_map/source/pallas_call | solution.py:39
  183.7 5.6 %sweep.6 = (f32[16,64,256]{2,1,0:T(8,128)}, f32[64,256]{1,0:T(8,128)}, f32[64,256]{1,0:T(8,128)}, f32[16,256]{1,0:T(8,128)}, f32[16,256]{1,0:T(8,128)}) custom-call(s32[2]{0:T(128)S(1)} %pad_add_fusion.at, f32[16,64,256]{2,1,0:T(8,128)} %get-tuple-element.95.p, f32[64,256]{1,0:T(8,128)} %copy-done.14, f32[64,256]{1,0:T(8,128)} %copy-done.15, ...), custom_call_target="tpu_custom_call" | custom-call | flops 6000000 | bytes 8388608 | tf_op jit(solution)/shard_map/sweep/pallas_call | solution.py:567
  189.3 3.9 %step.8 = (f32[128,128]{1,0:T(8,128)}, f32[128,128]{1,0:T(8,128)}, f32[128,128]{1,0:T(8,128)}, f32[640,128]{1,0:T(8,128)}) custom-call(s32[2]{0:T(128)S(1)} %pad_add_fusion.at, s32[8,4]{1,0:T(8,128)S(1)} %copy.34.cols, f32[32,128,128]{2,1,0:T(8,128)} %bitcast.48, f32[640,128]{1,0:T(8,128)} %bitcast.58, f32[128,128]{1,0:T(8,128)} %get-tuple-element.116.x, ...), custom_call_target="tpu_custom_call" | custom-call | flops 1000000 | bytes 1000000 | tf_op jit(solution)/shard_map/step/pallas_call | solution.py:39
  193.2 7.2 %all-to-all-start.9 = ((f32[16,40,128]{2,1,0:T(8,128)}), f32[16,40,128]{2,1,0:T(8,128)S(1)}, u32[]{:S(2)}, u32[]{:S(2)}) async-start(f32[16,40,128]{2,1,0:T(8,128)} %bitcast.73), calls=%async_computation.9 | async-start | bytes 655360 | tf_op jit(solution)/shard_map/all_to_all | solution.py:759
  201.2 3.0 %collective-permute-start.13 = (f32[64,256]{1,0:T(8,128)S(1)}, f32[64,256]{1,0:T(8,128)S(1)}, u32[]{:S(2)}, u32[]{:S(2)}) collective-permute-start(f32[64,256]{1,0:T(8,128)S(1)} %copy-done.27), channel_id=1, source_target_pairs={{16,32},{48,64},{80,96},{32,16},{64,48},{96,80},{17,33},{49,65},{8... | collective-permute-start | bytes 196616 | tf_op jit(solution)/shard_map/ppermute | solution.py:586
  204.2 1.7 collective-permute-start.14
  206.6 1.9 home.1
  208.5 0.8 all-to-all-done.9
  210.0 3.6 %step.9 = (f32[128,128]{1,0:T(8,128)}, f32[128,128]{1,0:T(8,128)}, f32[128,128]{1,0:T(8,128)}, f32[16,128]{1,0:T(8,128)}) custom-call(s32[2]{0:T(128)S(1)} %pad_add_fusion.at, s32[8,4]{1,0:T(8,128)S(1)} %copy.34.cols, f32[32,128,128]{2,1,0:T(8,128)} %bitcast.49, f32[640,128]{1,0:T(8,128)} %bitcast.59, f32[128,128]{1,0:T(8,128)} %get-tuple-element.130.x, ...), custom_call_target="tpu_custom_call" | custom-call | flops 1000000 | bytes 1000000 | tf_op jit(solution)/shard_map/step/pallas_call | solution.py:39
  213.6 7.5 %all-to-all-start.10 = ((f32[16,1,128]{2,1,0:T(1,128)}), f32[16,1,128]{2,1,0:T(1,128)S(1)}, u32[]{:S(2)}, u32[]{:S(2)}) async-start(f32[16,1,128]{2,1,0:T(1,128)} %bitcast.93), calls=%async_computation.10 | async-start | bytes 16384 | tf_op jit(solution)/shard_map/all_to_all | solution.py:767
  222.4 5.4 %sweep.7 = f32[16,64,256]{2,1,0:T(8,128)} custom-call(s32[2]{0:T(128)S(1)} %pad_add_fusion.at, f32[16,64,256]{2,1,0:T(8,128)} %get-tuple-element.137.p, f32[64,256]{1,0:T(8,128)} %copy-done.12, f32[64,256]{1,0:T(8,128)} %copy-done.13, f32[16,256]{1,0:T(8,128)} %copy-done.19, f32[16,256]{1,0:T(8,128)} %copy-done.20, f32[128,256]{1,0:T(8,128)} %copy-done, ...), custom_call_target="tpu_custom_call" | custom-call | flops 6000000 | bytes 8388608 | tf_op jit(solution)/shard_map/sweep/pallas_call | solution.py:567
  228.4 1.6 final.1
  (93 shorter events, 12.3 us)
Async XLA Ops:
  5.0 21.7 %all-to-all-start = ((f32[128,2,128]{2,1,0:T(2,128)}), f32[128,2,128]{2,1,0:T(2,128)S(1)}, u32[]{:S(2)}, u32[]{:S(2)}) async-start(f32[128,2,128]{2,1,0:T(2,128)} %bitcast.85), calls=%async_computation | async-start | bytes 262144 | tf_op jit(solution)/shard_map/all_to_all | solution.py:654
  18.4 27.3 %collective-permute-start = (f32[128,256]{1,0:T(8,128)}, f32[128,256]{1,0:T(8,128)S(1)}, u32[]{:S(2)}, u32[]{:S(2)}) collective-permute-start(f32[128,256]{1,0:T(8,128)} %get-tuple-element.77), channel_id=1, source_target_pairs={{0,16},{32,48},{64,80},{96,112},{16,0},{48,32},{80,64},{112,96},{1... | collective-permute-start | bytes 393224 | tf_op jit(solution)/shard_map/ppermute | solution.py:586
  19.5 26.3 %collective-permute-start.1 = (f32[128,256]{1,0:T(8,128)}, f32[128,256]{1,0:T(8,128)S(1)}, u32[]{:S(2)}, u32[]{:S(2)}) collective-permute-start(f32[128,256]{1,0:T(8,128)} %get-tuple-element.78), channel_id=1, source_target_pairs={{16,32},{48,64},{80,96},{32,16},{64,48},{96,80},{17,33},{49,65},{8... | collective-permute-start | bytes 393224 | tf_op jit(solution)/shard_map/ppermute | solution.py:586
  22.1 23.6 %collective-permute-start.2 = (f32[32,256]{1,0:T(8,128)}, f32[32,256]{1,0:T(8,128)S(1)}, u32[]{:S(2)}, u32[]{:S(2)}) collective-permute-start(f32[32,256]{1,0:T(8,128)} %get-tuple-element.79), channel_id=1, source_target_pairs={{0,1},{2,3},{4,5},{6,7},{8,9},{10,11},{12,13},{14,15},{1,0},{3,2},... | collective-permute-start | bytes 98312 | tf_op jit(solution)/shard_map/ppermute | solution.py:586
  23.4 22.4 %collective-permute-start.3 = (f32[32,256]{1,0:T(8,128)}, f32[32,256]{1,0:T(8,128)S(1)}, u32[]{:S(2)}, u32[]{:S(2)}) collective-permute-start(f32[32,256]{1,0:T(8,128)} %get-tuple-element.80), channel_id=1, source_target_pairs={{1,2},{3,4},{5,6},{7,8},{9,10},{11,12},{13,14},{2,1},{4,3},{6,5},{... | collective-permute-start | bytes 98312 | tf_op jit(solution)/shard_map/ppermute | solution.py:586
  26.8 0.7 copy-start.9
  32.8 20.0 %all-to-all-start.1 = ((f32[128,2,128]{2,1,0:T(2,128)}), f32[128,2,128]{2,1,0:T(2,128)S(1)}, u32[]{:S(2)}, u32[]{:S(2)}) async-start(f32[128,2,128]{2,1,0:T(2,128)} %bitcast.84), calls=%async_computation.1 | async-start | bytes 262144 | tf_op jit(solution)/shard_map/all_to_all | solution.py:676
  45.8 0.7 copy-start
  45.8 0.7 copy-start.1
  52.7 0.7 copy-start.10
  55.0 23.2 %all-to-all-start.2 = ((f32[128,2,128]{2,1,0:T(2,128)}), f32[128,2,128]{2,1,0:T(2,128)S(1)}, u32[]{:S(2)}, u32[]{:S(2)}) async-start(f32[128,2,128]{2,1,0:T(2,128)} %bitcast.69), calls=%async_computation.2 | async-start | bytes 262144 | tf_op jit(solution)/shard_map/all_to_all | solution.py:687
  64.7 6.9 %collective-permute-start.4 = (f32[64,256]{1,0:T(8,128)}, f32[64,256]{1,0:T(8,128)S(1)}, u32[]{:S(2)}, u32[]{:S(2)}) collective-permute-start(f32[64,256]{1,0:T(8,128)} %get-tuple-element.86), channel_id=1, source_target_pairs={{0,16},{32,48},{64,80},{96,112},{16,0},{48,32},{80,64},{112,96},{1... | collective-permute-start | bytes 196616 | tf_op jit(solution)/shard_map/ppermute | solution.py:586
  65.9 6.1 %collective-permute-start.5 = (f32[64,256]{1,0:T(8,128)}, f32[64,256]{1,0:T(8,128)S(1)}, u32[]{:S(2)}, u32[]{:S(2)}) collective-permute-start(f32[64,256]{1,0:T(8,128)} %get-tuple-element.87), channel_id=1, source_target_pairs={{16,32},{48,64},{80,96},{32,16},{64,48},{96,80},{17,33},{49,65},{8... | collective-permute-start | bytes 196616 | tf_op jit(solution)/shard_map/ppermute | solution.py:586
  68.5 3.2 %collective-permute-start.6 = (f32[16,256]{1,0:T(8,128)}, f32[16,256]{1,0:T(8,128)S(1)}, u32[]{:S(2)}, u32[]{:S(2)}) collective-permute-start(f32[16,256]{1,0:T(8,128)} %get-tuple-element.88), channel_id=1, source_target_pairs={{0,1},{2,3},{4,5},{6,7},{8,9},{10,11},{12,13},{14,15},{1,0},{3,2},... | collective-permute-start | bytes 49160 | tf_op jit(solution)/shard_map/ppermute | solution.py:586
  69.8 1.9 collective-permute-start.7
  71.7 0.6 copy-start.16
  72.0 0.6 copy-start.17
  78.2 0.7 copy-start.8
  82.5 20.4 %all-to-all-start.3 = ((f32[16,40,128]{2,1,0:T(8,128)}), f32[16,40,128]{2,1,0:T(8,128)S(1)}, u32[]{:S(2)}, u32[]{:S(2)}) async-start(f32[16,40,128]{2,1,0:T(8,128)} %bitcast.75), calls=%async_computation.3 | async-start | bytes 655360 | tf_op jit(solution)/shard_map/all_to_all | solution.py:708
  102.9 14.3 %copy-start.5 = (f32[16,40,128]{2,1,0:T(8,128)}, f32[16,40,128]{2,1,0:T(8,128)S(1)}, u32[]{:S(2)}) copy-start(f32[16,40,128]{2,1,0:T(8,128)S(1)} %all-to-all-done.3) | copy-start | bytes 983044
  102.9 14.3 %all-to-all-start.4 = ((f32[8,128,128]{2,1,0:T(8,128)}), f32[8,128,128]{2,1,0:T(8,128)S(1)}, u32[]{:S(2)}, u32[]{:S(2)}) async-start(f32[8,128,128]{2,1,0:T(8,128)} %bitcast.63), calls=%async_computation.4 | async-start | bytes 1048576 | tf_op jit(solution)/shard_map/all_to_all | solution.py:719
  117.2 0.8 copy-start.2
  135.6 23.9 %copy-start.26 = (f32[64,256]{1,0:T(8,128)S(1)}, f32[64,256]{1,0:T(8,128)}, u32[]{:S(2)}) copy-start(f32[64,256]{1,0:T(8,128)} %get-tuple-element.120) | copy-start | bytes 196612
  135.6 26.8 %copy-start.25 = (f32[64,256]{1,0:T(8,128)S(1)}, f32[64,256]{1,0:T(8,128)}, u32[]{:S(2)}) copy-start(f32[64,256]{1,0:T(8,128)} %get-tuple-element.121) | copy-start | bytes 196612
  135.6 28.9 %copy-start.30 = (f32[16,256]{1,0:T(8,128)S(1)}, f32[16,256]{1,0:T(8,128)}, u32[]{:S(2)}) copy-start(f32[16,256]{1,0:T(8,128)} %get-tuple-element.122) | copy-start | bytes 49156
  135.6 30.5 %copy-start.29 = (f32[16,256]{1,0:T(8,128)S(1)}, f32[16,256]{1,0:T(8,128)}, u32[]{:S(2)}) copy-start(f32[16,256]{1,0:T(8,128)} %get-tuple-element.123) | copy-start | bytes 49156
  155.9 11.5 %all-to-all-start.7 = ((f32[16,40,128]{2,1,0:T(8,128)}), f32[16,40,128]{2,1,0:T(8,128)S(1)}, u32[]{:S(2)}, u32[]{:S(2)}) async-start(f32[16,40,128]{2,1,0:T(8,128)} %bitcast.74), calls=%async_computation.7 | async-start | bytes 655360 | tf_op jit(solution)/shard_map/all_to_all | solution.py:751
  159.4 23.6 %collective-permute-start.8 = (f32[64,256]{1,0:T(8,128)S(1)}, f32[64,256]{1,0:T(8,128)S(1)}, u32[]{:S(2)}, u32[]{:S(2)}) collective-permute-start(f32[64,256]{1,0:T(8,128)S(1)} %copy-done.26), channel_id=1, source_target_pairs={{0,16},{32,48},{64,80},{96,112},{16,0},{48,32},{80,64},{112,96},{1... | collective-permute-start | bytes 196616 | tf_op jit(solution)/shard_map/ppermute | solution.py:586
  162.4 20.7 %collective-permute-start.9 = (f32[64,256]{1,0:T(8,128)S(1)}, f32[64,256]{1,0:T(8,128)S(1)}, u32[]{:S(2)}, u32[]{:S(2)}) collective-permute-start(f32[64,256]{1,0:T(8,128)S(1)} %copy-done.25), channel_id=1, source_target_pairs={{16,32},{48,64},{80,96},{32,16},{64,48},{96,80},{17,33},{49,65},{8... | collective-permute-start | bytes 196616 | tf_op jit(solution)/shard_map/ppermute | solution.py:586
  164.5 18.6 %collective-permute-start.10 = (f32[16,256]{1,0:T(8,128)S(1)}, f32[16,256]{1,0:T(8,128)S(1)}, u32[]{:S(2)}, u32[]{:S(2)}) collective-permute-start(f32[16,256]{1,0:T(8,128)S(1)} %copy-done.30), channel_id=1, source_target_pairs={{0,1},{2,3},{4,5},{6,7},{8,9},{10,11},{12,13},{14,15},{1,0},{3,2},... | collective-permute-start | bytes 49160 | tf_op jit(solution)/shard_map/ppermute | solution.py:586
  166.1 17.0 %collective-permute-start.11 = (f32[16,256]{1,0:T(8,128)S(1)}, f32[16,256]{1,0:T(8,128)S(1)}, u32[]{:S(2)}, u32[]{:S(2)}) collective-permute-start(f32[16,256]{1,0:T(8,128)S(1)} %copy-done.29), channel_id=1, source_target_pairs={{1,2},{3,4},{5,6},{7,8},{9,10},{11,12},{13,14},{2,1},{4,3},{6,5},{... | collective-permute-start | bytes 49160 | tf_op jit(solution)/shard_map/ppermute | solution.py:586
  167.3 15.7 %copy-start.3 = (f32[16,40,128]{2,1,0:T(8,128)}, f32[16,40,128]{2,1,0:T(8,128)S(1)}, u32[]{:S(2)}) copy-start(f32[16,40,128]{2,1,0:T(8,128)S(1)} %all-to-all-done.7) | copy-start | bytes 983044
  167.4 25.9 %all-to-all-start.8 = ((f32[128,1,128]{2,1,0:T(1,128)}), f32[128,1,128]{2,1,0:T(1,128)S(1)}, u32[]{:S(2)}, u32[]{:S(2)}) async-start(f32[128,1,128]{2,1,0:T(1,128)} %bitcast.32), calls=%async_computation.8 | async-start | bytes 131072 | tf_op jit(solution)/shard_map/all_to_all | solution.py:747
  183.1 0.6 copy-start.14
  183.1 0.6 copy-start.15
  189.3 11.2 %copy-start.28 = (f32[64,256]{1,0:T(8,128)S(1)}, f32[64,256]{1,0:T(8,128)}, u32[]{:S(2)}) copy-start(f32[64,256]{1,0:T(8,128)} %get-tuple-element.138) | copy-start | bytes 196612
  189.3 11.9 %copy-start.27 = (f32[64,256]{1,0:T(8,128)S(1)}, f32[64,256]{1,0:T(8,128)}, u32[]{:S(2)}) copy-start(f32[64,256]{1,0:T(8,128)} %get-tuple-element.139) | copy-start | bytes 196612
  189.3 14.9 %copy-start.32 = (f32[16,256]{1,0:T(8,128)S(1)}, f32[16,256]{1,0:T(8,128)}, u32[]{:S(2)}) copy-start(f32[16,256]{1,0:T(8,128)} %get-tuple-element.140) | copy-start | bytes 49156
  189.3 16.6 %copy-start.31 = (f32[16,256]{1,0:T(8,128)S(1)}, f32[16,256]{1,0:T(8,128)}, u32[]{:S(2)}) copy-start(f32[16,256]{1,0:T(8,128)} %get-tuple-element.141) | copy-start | bytes 49156
  193.2 13.4 %copy-start.11 = (f32[128,1,128]{2,1,0:T(1,128)}, f32[128,1,128]{2,1,0:T(1,128)S(1)}, u32[]{:S(2)}) copy-start(f32[128,1,128]{2,1,0:T(1,128)S(1)} %all-to-all-done.8) | copy-start | bytes 196612
  193.2 16.1 %all-to-all-start.9 = ((f32[16,40,128]{2,1,0:T(8,128)}), f32[16,40,128]{2,1,0:T(8,128)S(1)}, u32[]{:S(2)}, u32[]{:S(2)}) async-start(f32[16,40,128]{2,1,0:T(8,128)} %bitcast.73), calls=%async_computation.9 | async-start | bytes 655360 | tf_op jit(solution)/shard_map/all_to_all | solution.py:759
  200.5 20.7 %collective-permute-start.12 = (f32[64,256]{1,0:T(8,128)S(1)}, f32[64,256]{1,0:T(8,128)S(1)}, u32[]{:S(2)}, u32[]{:S(2)}) collective-permute-start(f32[64,256]{1,0:T(8,128)S(1)} %copy-done.28), channel_id=1, source_target_pairs={{0,16},{32,48},{64,80},{96,112},{16,0},{48,32},{80,64},{112,96},{1... | collective-permute-start | bytes 196616 | tf_op jit(solution)/shard_map/ppermute | solution.py:586
  201.2 20.0 %collective-permute-start.13 = (f32[64,256]{1,0:T(8,128)S(1)}, f32[64,256]{1,0:T(8,128)S(1)}, u32[]{:S(2)}, u32[]{:S(2)}) collective-permute-start(f32[64,256]{1,0:T(8,128)S(1)} %copy-done.27), channel_id=1, source_target_pairs={{16,32},{48,64},{80,96},{32,16},{64,48},{96,80},{17,33},{49,65},{8... | collective-permute-start | bytes 196616 | tf_op jit(solution)/shard_map/ppermute | solution.py:586
  204.2 16.9 %collective-permute-start.14 = (f32[16,256]{1,0:T(8,128)S(1)}, f32[16,256]{1,0:T(8,128)S(1)}, u32[]{:S(2)}, u32[]{:S(2)}) collective-permute-start(f32[16,256]{1,0:T(8,128)S(1)} %copy-done.32), channel_id=1, source_target_pairs={{0,1},{2,3},{4,5},{6,7},{8,9},{10,11},{12,13},{14,15},{1,0},{3,2},... | collective-permute-start | bytes 49160 | tf_op jit(solution)/shard_map/ppermute | solution.py:586
  205.9 15.2 %collective-permute-start.15 = (f32[16,256]{1,0:T(8,128)S(1)}, f32[16,256]{1,0:T(8,128)S(1)}, u32[]{:S(2)}, u32[]{:S(2)}) collective-permute-start(f32[16,256]{1,0:T(8,128)S(1)} %copy-done.31), channel_id=1, source_target_pairs={{1,2},{3,4},{5,6},{7,8},{9,10},{11,12},{13,14},{2,1},{4,3},{6,5},{... | collective-permute-start | bytes 49160 | tf_op jit(solution)/shard_map/ppermute | solution.py:586
  209.3 0.7 copy-start.4
  213.6 14.3 %all-to-all-start.10 = ((f32[16,1,128]{2,1,0:T(1,128)}), f32[16,1,128]{2,1,0:T(1,128)S(1)}, u32[]{:S(2)}, u32[]{:S(2)}) async-start(f32[16,1,128]{2,1,0:T(1,128)} %bitcast.93), calls=%async_computation.10 | async-start | bytes 16384 | tf_op jit(solution)/shard_map/all_to_all | solution.py:767
  221.2 0.6 copy-start.12
  (10 other events, 6.0 us)

commit v4 on v3

--- a/solution.py
+++ b/solution.py
@@ -1,4 +1,5 @@
 import functools
+import math
 
 import jax
 import jax.numpy as jnp
@@ -10,19 +11,33 @@
 WEIGHT = 0.8
 CAP = 8
 LANES = 128
+LARGE = 1 << 18
 F32 = jnp.float32
 BF16 = jnp.bfloat16
 SMEM = pl.BlockSpec(memory_space=pltpu.SMEM)
+VMEM = pl.BlockSpec(memory_space=pltpu.VMEM)
 RAW = pl.BlockSpec(memory_space=pltpu.HBM)
 X, Y, Z, HI, LO, KAPPA, COLS = (CAP * i for i in range(7))
 
 
 def shape(*dims, dtype=F32):
-    return pltpu.HBM(dims, dtype)
-
-
-def in_hbm(x):
+    if math.prod(dims) >= LARGE:
+        return pltpu.HBM(dims, dtype)
+    return jax.ShapeDtypeStruct(dims, dtype)
+
+
+def sent(*dims):
+    return pltpu.HBM(dims, F32)
+
+
+def in_hbm(x, least=LARGE):
+    if x.size < least:
+        return x
     return pltpu.with_memory_space_constraint(x, pltpu.HBM)
+
+
+def on_chip(v):
+    return isinstance(v, jax.ShapeDtypeStruct) and math.prod(v.shape) < LARGE
 
 
 def whole(dims):
@@ -33,16 +48,20 @@
     return pltpu.CompilerParams(vmem_limit_bytes=32 << 20)
 
 
-def call(body, outs, *operands, scalars=(), raw=(), scratch=(), flops=1e6, nbytes=1e6, name=None):
+def call(
+    body, outs, *operands, scalars=(), raw=(), resident=(), side=(), scratch=(), flops=1e6, nbytes=1e6, name=None, least=LARGE
+):
     single = not isinstance(outs, tuple)
     outs = (outs,) if single else outs
     result = pl.pallas_call(
         body,
         grid=(1,),
         out_shape=outs,
-        in_specs=[SMEM] * len(scalars) + [RAW] * len(raw) + [whole(v.shape) for v in operands],
+        in_specs=[SMEM] * len(scalars) + [RAW] * len(raw) + [VMEM] * len(resident) + [VMEM if v.size < least else whole(v.shape) for v in operands]
+        + [whole(v.shape) for v in side],
         out_specs=tuple(
-            pl.BlockSpec(v.shape, lambda i, n=len(v.shape): (0,) * n) for v in outs
+            VMEM if on_chip(v) else pl.BlockSpec(v.shape, lambda i, n=len(v.shape): (0,) * n)
+            for v in outs
         ),
         scratch_shapes=scratch,
         compiler_params=params(),
@@ -50,7 +69,13 @@
             flops=int(flops), bytes_accessed=int(nbytes), transcendentals=0
         ),
         name=name,
-    )(*scalars, *(in_hbm(v) for v in (*raw, *operands)))
+    )(
+        *scalars,
+        *(in_hbm(v, least) for v in raw),
+        *resident,
+        *(in_hbm(v, least) for v in operands),
+        *(in_hbm(v, 1) for v in side),
+    )
     return result[0] if single else result
 
 
@@ -60,6 +85,17 @@
 
 def ones_where(mask):
     return jnp.where(mask, 1.0, 0.0).astype(BF16)
+
+
+def halves(v):
+    top = v.astype(BF16)
+    return jnp.concatenate([top, (v - top.astype(F32)).astype(BF16)], axis=1)
+
+
+def pick_rounded(chosen, v):
+    width = v.shape[1]
+    out = jnp.dot(chosen, halves(v), preferred_element_type=F32)
+    return out[:, :width] + out[:, width:]
 
 
 def split(v):
@@ -88,12 +124,16 @@
     return jnp.broadcast_to(row, (LANES, LANES)).T
 
 
-def pack_body(at, cols, owner_col, owner, cell, frac, kappa, x_own, send, slot_out, blocks):
+def pack_body(at, cols, owner, cell, frac, kappa, x_own, send, slot_out, blocks):
     count = owner.shape[1]
     mine = at[0]
     own = owner[...]
-    earlier = (owner_col[...] == own) & (iota((count, count), 0) < iota((count, count), 1))
-    slot = jnp.sum(jnp.where(earlier, 1, 0), axis=0, keepdims=True)
+    slot = jnp.zeros((1, count), jnp.int32)
+    for first in range(0, count, LANES):
+        column = jnp.broadcast_to(own[:, first : first + LANES], (LANES, LANES)).T
+        column = jnp.concatenate([column] * (count // LANES), axis=1)
+        before = iota((LANES, count), 0) + first < iota((LANES, count), 1)
+        slot += jnp.sum(jnp.where((column == own) & before, 1, 0), axis=0, keepdims=True)
     slot_out[...] = slot
     here = iota((CAP, count), 0) == slot
     c, f = cell[...], frac[...]
@@ -124,8 +164,8 @@
     message = nt(chosen, rows.astype(BF16)) + nt(chosen, kappas(middle)) + nt(chosen, kappas(low))
     lane = iota((1, LANES), 1)
     extra = jnp.zeros((1, LANES), F32)
-    for t in range(cols.shape[1]):
-        extra = jnp.where(lane == COLS + t, cols[mine, t].astype(F32), extra)
+    for t in range(cols.shape[0]):
+        extra = jnp.where(lane == COLS + t, cols[t, mine].astype(F32), extra)
     blocks[...] = jnp.broadcast_to(x_own[pl.ds(mine, 1), :], (LANES, LANES))
     send[pl.ds(0, LANES, stride=2), :] = blocks[...]
     send[pl.ds(1, LANES, stride=2), :] = message + extra
@@ -140,12 +180,28 @@
     return x * 64 + y, z, hi, lo, message[:, KAPPA + k : KAPPA + k + 1]
 
 
-def traces(message, pressure, gathered):
+def in_parts(source, target, arrived):
+    parts = arrived.shape[0]
+    each = source.shape[0] // parts
+    copies = []
+    for i in range(parts):
+        part = pl.ds(i * each, each)
+        copies.append(
+            pltpu.make_async_copy(source.at[part], target.at[part], arrived.at[i])
+        )
+        copies[-1].start()
+    return copies
+
+
+def traces(message, pressure_all, pressure, here, gathered):
+    copies = in_parts(pressure_all, pressure, here)
     rows, depth = pressure.shape
     chosen = jnp.concatenate(
         [ones_where(iota((LANES, rows), 1) == by_slot(message, k)[0]) for k in range(CAP)], axis=0
     )
-    gathered[...] = pick(chosen, pressure)
+    for copy in copies:
+        copy.wait()
+    gathered[...] = pick_rounded(chosen, pressure[...])
     lane = iota((LANES, LANES), 1)
     out = jnp.zeros((LANES, LANES), F32)
     for k in range(CAP):
@@ -196,21 +252,24 @@
     at,
     cols,
     tiles_all,
+    pressure_all,
     got,
-    pressure,
     diag,
     source,
     send,
     x_out,
     trace_out,
     flux_out,
+    message_out,
     gathered,
     part,
     tiles,
     arrived,
+    pressure,
+    here,
 ):
     mine, shard = at[0], at[1]
-    per_row = cols.shape[1]
+    per_row = cols.shape[0]
     fetch = pltpu.make_async_copy(tiles_all.at[pl.ds(per_row * mine, per_row)], tiles, arrived)
     fetch.start()
     groups = LANES // CAP
@@ -219,7 +278,8 @@
             pl.ds(2 * m * groups, groups, stride=2), :
         ]
     message = got[pl.ds(1, LANES, stride=2), :]
-    trace = traces(message, pressure[...], gathered)
+    message_out[...] = message
+    trace = traces(message, pressure_all, pressure, here, gathered)
     kappa = kappa_of(message)
     flux = kappa * (trace - at_mortar(message, x_out[...]))
     load, weight = onto_fracture(message, flux, kappa)
@@ -231,9 +291,9 @@
     fetch.wait()
     for t in range(per_row):
         tile = tiles[t]
-        mixed += tile * x_out[pl.ds(cols[mine, t], 1), :]
+        mixed += tile * x_out[pl.ds(cols[t, mine], 1), :]
         back = jnp.sum(tile * x_col, axis=0, keepdims=True)
-        part[pl.ds(cols[mine, t], 1), :] -= 0.5 * back
+        part[pl.ds(cols[t, mine], 1), :] -= 0.5 * back
     part[pl.ds(row, 1), :] += source[pl.ds(mine, 1), :] - (
         diag[pl.ds(mine, 1), :] * x_row + 0.5 * row_sums(mixed)
     )
@@ -243,41 +303,39 @@
     flux_out[...] = flux
 
 
-def source_body(got, flux, base, rhs):
-    message = got[pl.ds(1, LANES, stride=2), :]
-    rows, depth = base.shape
+def spread_flux(message, values, spread, cell_row, depth):
     flipped = message.T
-    cell_row = jnp.concatenate(
-        [flipped[X + k : X + k + 1, :] * 64 + flipped[Y + k : Y + k + 1, :] for k in range(CAP)],
-        axis=1,
-    )
-    chosen = ones_where(iota((rows, CAP * LANES), 0) == cell_row.astype(jnp.int32))
-    spread = jnp.concatenate(
-        [
-            jnp.where(iota((LANES, depth), 1) == by_slot(message, k)[1], flux[:, k : k + 1], 0.0)
-            for k in range(CAP)
-        ],
-        axis=0,
-    )
-    rhs[...] = base[...] + pick(chosen, spread)
-
-
-def second_source_body(got, trace, x, base, rhs):
-    message = got[pl.ds(1, LANES, stride=2), :]
-    flux = kappa_of(message) * (trace[...] - at_mortar(message, x[...]))
-    source_body(got, flux, base, rhs)
-
-
-def second_body(got, pressure, trace, trace_out, send, gathered):
-    message = got[pl.ds(1, LANES, stride=2), :]
-    now = traces(message, pressure[...], gathered)
+    for k in range(CAP):
+        z = by_slot(message, k)[1]
+        placed = jnp.where(iota((LANES, depth), 1) == z, values[:, k : k + 1], 0.0)
+        spread[k * LANES : (k + 1) * LANES, :] = halves(placed)
+        cell_row[:, k * LANES : (k + 1) * LANES] = (
+            flipped[X + k : X + k + 1, :] * 64 + flipped[Y + k : Y + k + 1, :]
+        ).astype(jnp.int32)
+
+
+def sources(rows, step, spread, cell_row):
+    depth = spread.shape[1] // 2
+    row = iota((rows, CAP * LANES), 0) + step * rows
+    chosen = ones_where(row == cell_row[...])
+    out = jnp.dot(chosen, spread[...], preferred_element_type=F32)
+    return out[:, :depth] + out[:, depth:]
+
+
+def second_body(pressure_all, message, trace, trace_out, send, gathered, pressure, here, change):
+    message = message[...]
+    now = traces(message, pressure_all, pressure, here, gathered)
     trace_out[...] = now
-    [change] = onto_fracture(message, kappa_of(message) * (now - trace[...]))
-    for m in range(send.shape[0] // LANES):
-        send[m * LANES : (m + 1) * LANES, :] = change
-
-
-def home_body(got, owner, slot, frac, kappa, x, flux):
+    change[...] = onto_fracture(message, kappa_of(message) * (now - trace[...]))[0]
+    mats = CAP
+    each = LANES // mats
+    for m in range(mats):
+        part = slice(m * each, (m + 1) * each)
+        send[2 * m * each : (2 * m + 1) * each, :] = change[part, :]
+        send[(2 * m + 1) * each : (2 * m + 2) * each, :] = now[part, :]
+
+
+def home_body(got, owner, slot, frac, kappa, x, flux, *, mats):
     count = owner.shape[1]
 
     def found(values, chosen):
@@ -290,7 +348,10 @@
         n = values.shape[0]
         return out[:n] + out[n : 2 * n] + out[2 * n : 3 * n]
 
-    traces_all = found(got[...].T[:CAP, :], ones_where(iota((LANES, count), 0) == owner[...]))
+    shards = LANES // mats
+    own = owner[...]
+    source = (own & (shards - 1)) * mats + own // shards
+    traces_all = found(got[...].T[:CAP, :], ones_where(iota((LANES, count), 0) == source))
     here = iota((CAP, count), 0) == slot[...]
     trace = jnp.sum(jnp.where(here, traces_all, 0.0), axis=0, keepdims=True)
     f = frac[...]
@@ -323,14 +384,14 @@
 
 def products(at, cols, d, tiles, diag, block):
     shard = at[1]
-    rows, per_row = cols.shape
+    per_row, rows = cols.shape
     for r in range(rows):
         d_row = d[pl.ds(CAP * shard + r, 1), :]
         d_col = as_column(d_row)
         mixed = jnp.zeros((LANES, LANES), F32)
         for t in range(per_row):
             tile = tiles[per_row * r + t]
-            mixed += tile * d[pl.ds(cols[r, t], 1), :]
+            mixed += tile * d[pl.ds(cols[t, r], 1), :]
             back = jnp.sum(tile * d_col, axis=0, keepdims=True)
             block[rows + per_row * r + t : rows + per_row * r + t + 1, :] = 0.5 * back
         block[r : r + 1, :] = diag[r : r + 1, :] * d_row + 0.5 * row_sums(mixed)
@@ -345,29 +406,33 @@
     return own + pick(chosen[...], back)
 
 
-def start_body(at, cols, tiles_all, got, diag, r_out, weight_out, send, block, tiles, arrived):
-    fetch = pltpu.make_async_copy(tiles_all, tiles, arrived)
-    fetch.start()
+def start_body(at, cols, tiles, got, diag, r_out, weight_out, send, block):
     r_out[...] = got[pl.ds(0, LANES, stride=2), :]
     weight_out[...] = got[pl.ds(1, LANES, stride=2), :]
-    fetch.wait()
     products(at, cols, r_out, tiles, diag, block)
     size = block.shape[0]
     for s in range(send.shape[0] // size):
         send[s * size : (s + 1) * size, :] = block[...]
 
 
-def step_body(at, cols, tiles_all, got, x, r, d, chosen, diag, *rest, ride, last):
-    rows, per_row = cols.shape
+def step_body(
+    at, cols, tiles, got, x, r, d, chosen, diag, *rest, ride, last, faces_in, faces_out
+):
+    per_row, rows = cols.shape
     size = rows * (1 + per_row)
     shards = LANES // rows
+    mats = rows
     extra = list(rest)
     change = extra.pop(0) if ride == "reduce" else None
+    parts = [extra.pop(0) for _ in range(4)] if ride == "next" else None
     x_before, weight = (extra.pop(0), extra.pop(0)) if ride == "next" else (None, None)
-    x_out, r_out, d_out, send, block, tiles, arrived = extra
-    fetch = pltpu.make_async_copy(tiles_all, tiles, arrived)
-    fetch.start()
+    y_faces = (extra.pop(0), extra.pop(0)) if faces_out else None
+    x_out, r_out, d_out, send = (extra.pop(0) for _ in range(4))
+    change_out, home = (extra.pop(0), extra.pop(0)) if ride == "gather" else (None, None)
+    y_halo = (extra.pop(0), extra.pop(0)) if faces_in else None
+    block = extra.pop()
     got_step = got.shape[0] // shards
+    shard = at[1]
     image = image_of(got, chosen, got_step, rows, rows * per_row)
     old = d[...]
     norm = total(r[...] * r[...])
@@ -376,45 +441,69 @@
     r_new = r[...] - alpha * image
     x_out[...] = x_new
     if ride == "next":
-        moved = jnp.concatenate(
-            [got[s * got_step + size : (s + 1) * got_step, :] for s in range(shards)], axis=0
-        )
-        r_new = r_new + moved - weight[...] * (x_new - x_before[...])
+        [whole_change] = extra
+        k = 0
+        for part in parts:
+            for i in range(part.shape[0] // shards):
+                place = pl.multiple_of((at[0] ^ k) * shards, shards)
+                whole_change[pl.ds(place, shards), :] = part[i * shards : (i + 1) * shards, :]
+                k += 1
+        r_new = r_new + whole_change[...] - weight[...] * (x_new - x_before[...])
         d_out[...] = r_new
     else:
         d_out[...] = r_new + (total(r_new * r_new) / norm) * old
     r_out[...] = r_new
-    fetch.wait()
     if last:
-        shard = at[1]
         lanes = jnp.zeros((1, LANES), F32)
         for i in range(rows):
             d_row = d_out[pl.ds(CAP * shard + i, 1), :]
             mixed = jnp.zeros((LANES, LANES), F32)
             for t in range(per_row):
-                mixed += tiles[per_row * i + t] * d_out[pl.ds(cols[i, t], 1), :]
+                mixed += tiles[per_row * i + t] * d_out[pl.ds(cols[t, i], 1), :]
             lanes += diag[i : i + 1, :] * d_row * d_row
             lanes += jnp.sum(mixed * as_column(d_row), axis=0, keepdims=True)
         send[...] = jnp.broadcast_to(lanes, send.shape)
-        return
-    products(at, cols, d_out, tiles, diag, block)
-    send_step = send.shape[0] // shards
+    else:
+        products(at, cols, d_out, tiles, diag, block)
+        send_step = send.shape[0] // shards
+        if ride == "reduce":
+            found = change[:shards, :]
+            for m in range(1, mats):
+                found = found + change[2 * m * shards : (2 * m + 1) * shards, :]
+        for s in range(shards):
+            first = s * send_step
+            send[first : first + size, :] = block[...]
+            first += size
+            if ride == "reduce":
+                send[first : first + shards, :] = found
+                for m in range(mats):
+                    row = (2 * m + 1) * shards + s
+                    send[first + shards + m : first + shards + m + 1, :] = change[row : row + 1, :]
+                first += shards + mats
+            if faces_out:
+                face = jnp.where(shard < s, y_faces[1][...], y_faces[0][...])
+                deep = face.shape[0]
+                send[first : first + deep, :] = face[:, :LANES]
+                send[first + deep : first + 2 * deep, :] = face[:, LANES:]
+    first = size
     if ride == "gather":
-        own = jnp.zeros((rows, LANES), F32)
+        found = jnp.zeros((shards, LANES), F32)
         for s in range(shards):
-            own += got[s * got_step + size : (s + 1) * got_step, :]
-    if ride == "reduce":
-        sums = jnp.zeros((LANES, LANES), F32)
-        for m in range(change.shape[0] // LANES):
-            sums += change[m * LANES : (m + 1) * LANES, :]
-    for s in range(shards):
-        send[s * send_step : s * send_step + size, :] = block[...]
-        if ride == "gather":
-            send[s * send_step + size : (s + 1) * send_step, :] = own
-        if ride == "reduce":
-            send[s * send_step + size : (s + 1) * send_step, :] = sums[
-                s * rows : (s + 1) * rows, :
-            ]
+            row = s * got_step + size
+            found += got[row : row + shards, :]
+            home[s * mats : (s + 1) * mats, :] = got[row + shards : row + shards + mats, :]
+        change_out[...] = found
+        first += shards + mats
+    if faces_in:
+        deep = y_halo[0].shape[0]
+        for halo, other, there in (
+            (y_halo[0], jnp.maximum(shard - 1, 0), shard > 0),
+            (y_halo[1], jnp.minimum(shard + 1, shards - 1), shard < shards - 1),
+        ):
+            row = pl.multiple_of(other * got_step + first, 8)
+            for half in range(2):
+                values = got[pl.ds(row + half * deep, deep), :]
+                halo[:, half * LANES : (half + 1) * LANES] = jnp.where(there, values, 0.0)
 
 
 def final_body(at, got, x, r, d, out):
@@ -449,7 +538,7 @@
     return pl.pallas_call(
         edges_body,
         grid=(1,),
-        out_shape=tuple(shape(*v) for v in out),
+        out_shape=tuple(sent(*v) for v in out),
         in_specs=[
             SMEM,
             pl.BlockSpec((1, ny, nz), lambda i: (0, 0, 0)),
@@ -466,41 +555,59 @@
 
 
 def sweep_body(
-    at, p, xa, xb, ya, yb, cxa, cxb, cya, cyb, trans, cell, rhs, *rest, first, last
+    at, xa, xb, ya, yb, cxa, cxb, cya, cyb, p, p_after, trans, cell, rhs, *rest, first, last, fluxes, y_in, y_out
 ):
     rest = list(rest)
     weight = None if first else rest.pop(0)
+    if fluxes:
+        got, values = rest.pop(0), [rest.pop(0) for _ in range(fluxes)]
     out = rest.pop(0)
     weight_out = rest.pop(0) if first else None
+    rhs_out = rest.pop(0) if fluxes else None
+    if fluxes:
+        found, spread, cell_row = rest.pop(), rest.pop(), rest.pop()
     carry_t = rest.pop() if first else None
     carry = rest.pop()
     step = pl.program_id(0)
     steps = pl.num_programs(0)
     many, ny, nz = out.shape
-    nx = p.shape[0]
+    nx = ya.shape[0] if not first else ya.shape[0] // 2
     row = iota((ny, nz), 0)
     lane = iota((ny, nz), 1)
     x_even, y_even = even(at, 0), even(at, 1)
 
     @pl.when(step == 0)
     def _():
+        if fluxes == 1:
+            spread_flux(got[...], values[0][...], spread, cell_row, nz)
+        if fluxes == 2:
+            message = got[...]
+            flux = values[0][...] - at_mortar(message, values[1][...])
+            spread_flux(message, kappa_of(message) * flux, spread, cell_row, nz)
         tx_low = jnp.where(x_even, cxb[ny:, :], cxa[ny:, :])
         carry[...] = tx_low * (jnp.where(x_even, xb[:ny, :], xa[:ny, :]) - p[0])
         if first:
             carry_t[...] = tx_low
 
+    if fluxes:
+        found[...] = sources(many * ny, step, spread, cell_row)
     for i in range(many):
         here_at = step * many + i
-        here = p[here_at]
+        right = rhs[i]
+        if fluxes:
+            right = right + found[i * ny : (i + 1) * ny, :]
+            rhs_out[i] = right
+        here = p[i]
         if i + 1 < many:
-            after = p[here_at + 1]
+            after = p[i + 1]
         else:
             x_high = jnp.where(x_even, xa[:ny, :], xb[:ny, :])
-            after = jnp.where(step + 1 < steps, p[jnp.minimum(here_at + 1, nx - 1)], x_high)
+            after = jnp.where(step + 1 < steps, p_after[0], x_high)
         one = pl.ds(here_at, 1)
         edge = pl.ds(nx + here_at, 1)
-        y_low = jnp.where(y_even, yb[one, :], ya[one, :])
-        y_high = jnp.where(y_even, ya[one, :], yb[one, :])
+        y_low, y_high = ya[one, :], yb[one, :]
+        if not y_in:
+            y_low, y_high = jnp.where(y_even, y_high, y_low), jnp.where(y_even, y_low, y_high)
         ty_edge = jnp.where(y_even, cyb[edge, :], cya[edge, :])
         tx, ty, tz = trans[0, i], trans[1, i], trans[2, i]
         fx = tx * (here - after)
@@ -521,7 +628,7 @@
             w = weight[i]
         applied = cell[i] * here + fx - carry[...] + fy - fy_low + fz - fz_low
         carry[...] = fx
-        out[i] = here + w * (rhs[i] - applied)
+        out[i] = here + w * (right - applied)
     if last:
         return
     xa_out, xb_out, ya_out, yb_out = rest
@@ -546,11 +653,13 @@
     for i in range(many):
         one = pl.ds(step * many + i, 1)
         low, high = out[i, :1, :], out[i, ny - 1 :, :]
-        ya_out[one, :] = jnp.where(y_even, high, low)
-        yb_out[one, :] = jnp.where(y_even, low, high)
-
-
-def sweep(at, p, halo, faces, trans, cell, rhs, weight=None, last=False, many=4):
+        if not y_out:
+            low, high = jnp.where(y_even, high, low), jnp.where(y_even, low, high)
+        ya_out[one, :] = low
+        yb_out[one, :] = high
+
+
+def sweep(at, p, halo, faces, trans, cell, rhs, weight=None, last=False, got=None, values=(), y_in=False, y_out=False, many=4):
     nx, ny, nz = p.shape
     part = pl.BlockSpec((many, ny, nz), lambda i: (i, 0, 0))
     x_face = pl.BlockSpec((ny, nz), lambda i: (0, 0))
@@ -560,31 +669,47 @@
     if first:
         out_shape.append(shape(nx, ny, nz))
         out_specs.append(part)
+    scratch = [pltpu.VMEM((ny, nz), F32)] * (2 if first else 1)
+    if values:
+        out_shape.append(shape(nx, ny, nz))
+        out_specs.append(part)
+        scratch += [
+            pltpu.VMEM((1, CAP * LANES), jnp.int32),
+            pltpu.VMEM((CAP * LANES, 2 * nz), BF16),
+            pltpu.VMEM((many * ny, nz), F32),
+        ]
     if not last:
-        out_shape += [shape(ny, nz)] * 2 + [shape(nx, nz)] * 2
+        out_shape += [sent(ny, nz)] * 2 + [sent(nx, nz)] * 2
         out_specs += [x_face, x_face, y_face, y_face]
-    operands = [p, *halo, *faces, trans, cell, rhs] + ([] if first else [weight])
+    after = pl.BlockSpec(
+        (1, ny, nz), lambda i: (jnp.minimum((i + 1) * many, nx - 1), 0, 0)
+    )
+    operands = [*halo, *faces, p, p, trans, cell, rhs] + ([] if first else [weight])
+    operands += [got, *values] if values else []
     return pl.pallas_call(
-        functools.partial(sweep_body, first=first, last=last),
+        functools.partial(sweep_body, first=first, last=last, fluxes=len(values), y_in=y_in, y_out=y_out),
         grid=(nx // many,),
         out_shape=tuple(out_shape),
         in_specs=[SMEM]
-        + [whole(v.shape) for v in (p, *halo, *faces)]
+        + [whole(v.shape) for v in (*halo, *faces)]
+        + [part, after]
         + [pl.BlockSpec((3, many, ny, nz), lambda i: (0, i, 0, 0)), part, part]
-        + ([] if first else [part]),
+        + ([] if first else [part])
+        + ([whole(v.shape) for v in (got, *values)] if values else []),
         out_specs=tuple(out_specs),
-        scratch_shapes=[pltpu.VMEM((ny, nz), F32)] * (2 if first else 1),
+        scratch_shapes=scratch,
         compiler_params=params(),
         cost_estimate=pl.CostEstimate(flops=6_000_000, bytes_accessed=8 << 20, transcendentals=0),
         name="sweep",
     )(at, *(in_hbm(v) for v in operands))
 
 
+def swap(v, axis, count, low):
+    pairs = [(i, i + 1) for i in range(low, count - 1, 2)]
+    return lax.ppermute(v, axis, pairs + [(b, a) for a, b in pairs])
+
+
 def swapped(xa, xb, ya, yb, mats, shards):
-    def swap(v, axis, count, low):
-        pairs = [(i, i + 1) for i in range(low, count - 1, 2)]
-        return lax.ppermute(v, axis, pairs + [(b, a) for a, b in pairs])
-
     return (
         swap(xa, "mat", mats, 0),
         swap(xb, "mat", mats, 1),
@@ -632,16 +757,12 @@
     square_scratch = pltpu.VMEM((LANES, LANES), F32)
     gathered = pltpu.VMEM((CAP * LANES, nz), F32)
     block = pltpu.VMEM((size, LANES), F32)
-    tile_scratch = [
-        pltpu.VMEM((rows * per_row, LANES, LANES), F32),
-        pltpu.SemaphoreType.DMA(()),
-    ]
-    scalars = (at, tile_cols)
+    scalars = (at, tile_cols.T)
+    fetch_scratch = [pltpu.VMEM(flat, F32), pltpu.SemaphoreType.DMA((8,))]
 
     send, slot = call(
         pack_body,
-        (shape(2 * LANES, LANES), shape(1, count, dtype=jnp.int32)),
-        mortar_owner,
+        (sent(2 * LANES, LANES), pltpu.HBM((1, count), jnp.int32)),
         owner,
         mortar_cell.reshape(1, count),
         frac,
@@ -650,39 +771,39 @@
         scalars=scalars,
         scratch=[square_scratch],
         name="pack",
-    )
+        least=1,
+    )
+    send, edges_at = lax.optimization_barrier((send, at))
     got = everyone(send)
 
-    faces = swapped(*edges(at, pressure_start, face_trans), mats, shards)
-
-    send, x_start, trace, flux = call(
+    faces = swapped(*edges(edges_at, pressure_start, face_trans), mats, shards)
+    got, *faces = lax.optimization_barrier((got, *faces))
+
+    send, x_start, trace, flux, message = call(
         first_body,
-        (shape(2 * LANES, LANES), square, square, square),
+        (sent(2 * LANES, LANES), square, *[sent(LANES, LANES)] * 3),
         got,
-        pressure_start.reshape(flat),
         diag,
         frac_source.reshape(rows, LANES),
         scalars=scalars,
-        raw=(tile_list,),
+        raw=(tile_list, pressure_start.reshape(flat)),
         scratch=[
             gathered,
             square_scratch,
             pltpu.VMEM((per_row, LANES, LANES), F32),
             pltpu.SemaphoreType.DMA(()),
+            *fetch_scratch,
         ],
         flops=2e9,
         name="first",
     )
     reduced = everyone(send)
-    base = matrix_source.reshape(flat)
-    rhs = call(source_body, shape(*flat), got, flux, base, flops=2e9, name="source")
-    rhs = rhs.reshape(nx, ny, nz)
-    pressure, weight, *sides = sweep(
-        at, pressure_start, faces, faces, face_trans, cell_coef, rhs
+    pressure, weight, rhs, *sides = sweep(
+        at, pressure_start, faces, faces, face_trans, cell_coef, matrix_source, got=message, values=(flux,)
     )
     sides = swapped(*sides, mats, shards)
 
-    send = call(sum_body, shape(2 * LANES, LANES), reduced, name="sums")
+    send = call(sum_body, sent(2 * LANES, LANES), reduced, name="sums")
     send, pressure = lax.optimization_barrier((send, pressure))
     residuals = everyone(send)
     chosen = call(
@@ -691,16 +812,18 @@
         got,
         name="columns",
     )
-    pressure, *sides = sweep(at, pressure, sides, faces, face_trans, cell_coef, rhs, weight)
+    pressure, *sides = sweep(
+        at, pressure, sides, faces, face_trans, cell_coef, rhs, weight, y_out=True
+    )
 
     r, sums, send = call(
         start_body,
-        (square, square, shape(shards * size, LANES)),
+        (square, sent(LANES, LANES), sent(shards * size, LANES)),
         residuals,
         diag,
         scalars=scalars,
-        raw=(tile_list,),
-        scratch=[block, *tile_scratch],
+        resident=(tile_list,),
+        scratch=[block],
         name="start",
     )
     x, d = x_start, r
@@ -708,21 +831,30 @@
     arrived = over_frac(send)
     trace, change = call(
         second_body,
-        (square, shape(mats * LANES, LANES)),
-        got,
-        pressure.reshape(flat),
-        trace,
-        scratch=[gathered],
+        (sent(LANES, LANES), sent(2 * LANES, LANES)),
+        side=(message, trace),
+        raw=(pressure.reshape(flat),),
+        scratch=[gathered, *fetch_scratch, square_scratch],
         flops=2e9,
         name="second",
     )
+
+    arrived, change = lax.optimization_barrier((arrived, change))
     change = over_mat(change)
-
-    def step(arrived, x, r, d, *more, ride=None, last=False):
-        length = shards * (size + (rows if ride in ("reduce", "gather") else 0))
+    arrived, change = lax.optimization_barrier((arrived, change))
+
+    def step(arrived, x, r, d, *more, ride=None, last=False, faces_in=False, faces=(), side=()):
+        length = size + (shards + mats if ride == "reduce" else 0) + (2 * nx if faces else 0)
+        outs = [square, square, square, sent(shards * (1 if last else length), LANES)]
+        if ride == "gather":
+            outs += [sent(shards, LANES), sent(LANES, LANES)]
+        if faces_in:
+            outs += [sent(nx, nz)] * 2
         return call(
-            functools.partial(step_body, ride=ride, last=last),
-            (square, square, square, shape(shards if last else length, LANES)),
+            functools.partial(
+                step_body, ride=ride, last=last, faces_in=faces_in, faces_out=bool(faces)
+            ),
+            tuple(outs),
             arrived,
             x,
             r,
@@ -730,43 +862,73 @@
             chosen,
             diag,
             *more,
+            side=(*side, *faces),
             scalars=scalars,
-            raw=(tile_list,),
-            scratch=[block, *tile_scratch],
+            resident=(tile_list,),
+            scratch=([square_scratch] if ride == "next" else []) + [block],
             name="step",
         )
 
+    def swapped_mat(xa, xb):
+        return swap(xa, "mat", mats, 0), swap(xb, "mat", mats, 1)
+
     x, r, d, send = step(arrived, x, r, d, change, ride="reduce")
-    send, trace, sides = lax.optimization_barrier((send, trace, sides))
+    send, trace, *x_sides = lax.optimization_barrier((send, trace, *sides[:2]))
     arrived = over_frac(send)
-    sides = swapped(*sides, mats, shards)
-
-    x, r, d, send = step(arrived, x, r, d, ride="gather")
-    send, home = lax.optimization_barrier((send, trace))
+    x_sides = swapped_mat(*x_sides)
+    arrived, *x_sides = lax.optimization_barrier((arrived, *x_sides))
+
+    x, r, d, send, change, home = step(arrived, x, r, d, ride="gather", faces=sides[2:])
     arrived = over_frac(send)
-    home = everyone(home)
-
-    x, r, d, send = step(arrived, x, r, d, x_start, sums, ride="next")
+    parts = [change]
+    for hop in (1, 2, 4):
+        mine = jnp.concatenate(parts, axis=0) if hop > 1 else change
+        parts.append(lax.ppermute(mine, "mat", [(i, i ^ hop) for i in range(mats)]))
+
+    x, r, d, send, *y_sides = step(
+        arrived, x, r, d, faces_in=True, ride="next", side=(*parts, x_start, sums))
     x_flux = x
     arrived = over_frac(send)
-    rhs = call(
-        second_source_body, shape(*flat), got, trace, x_flux, base, flops=2e9, name="source"
-    ).reshape(nx, ny, nz)
-    pressure, *sides = sweep(at, pressure, sides, faces, face_trans, cell_coef, rhs, weight)
-
-    x, r, d, send = step(arrived, x, r, d)
-    send, sides, home = lax.optimization_barrier((send, sides, home))
+    pressure, rhs, *sides = sweep(
+        at,
+        pressure,
+        (*x_sides, *y_sides),
+        faces,
+        face_trans,
+        cell_coef,
+        matrix_source,
+        weight,
+        got=message,
+        values=(trace, x_flux),
+        y_in=True,
+        y_out=True,
+    )
+    arrived, pressure, *sides = lax.optimization_barrier((arrived, pressure, *sides))
+    x, r, d, send = step(arrived, x, r, d, faces=sides[2:])
+    send, home, *sides = lax.optimization_barrier((send, home, *sides[:2]))
     arrived = over_frac(send)
-    sides = swapped(*sides, mats, shards)
+    x_sides = swapped_mat(*sides)
     flux = call(
-        home_body, shape(1, count), home, owner, slot, frac, kappa, x_flux, name="home"
-    )
-
-    x, r, d, send = step(arrived, x, r, d, last=True)
+        functools.partial(home_body, mats=mats),
+        shape(1, count),
+        side=(home, owner, slot, frac, kappa, x_flux),
+        name="home",
+    )
+    arrived, flux, *x_sides = lax.optimization_barrier((arrived, flux, *x_sides))
+    x, r, d, send, *y_sides = step(arrived, x, r, d, last=True, faces_in=True)
     send, pressure, flux = lax.optimization_barrier((send, pressure, flux))
     arrived = over_frac(send)
     [pressure] = sweep(
-        at, pressure, sides, faces, face_trans, cell_coef, rhs, weight, last=True
+        at,
+        pressure,
+        (*x_sides, *y_sides),
+        faces,
+        face_trans,
+        cell_coef,
+        rhs,
+        weight,
+        last=True,
+        y_in=True,
     )
     fracture = call(
         final_body, shape(rows, LANES), arrived, x, r, d, scalars=(at,), name="final"

time: 232 us -> 204 us (0.88)
  the two profiles are of different devices: /device:TPU:1 before, /device:TPU:32 now
where the time goes in v4:
time: 204 us; the launch traced here: 201 us
  starting transfers between devices  87.9 us (43%)
  Pallas kernels  56.1 us (28%)
  waiting for transfers between devices  42.4 us (21%)
  local copies, waits for them, and re-layouts  12.4 us (6%)
    all_to_all x6, starting transfers between devices, body(): arrived = over_frac(send)  38.1 us
    pallas_call x13, Pallas kernels, call(): pl.pallas_call(body, grid=(1,), out_shape=outs, in_specs=[SMEM] * len(sca...  29.4 us
    pallas_call x4, Pallas kernels, sweep(): pl.pallas_call(functools.partial(sweep_body, first=first, last=last, flux...  24.8 us
    all_to_all x6, waiting for transfers between devices, body(): arrived = over_frac(send)  17.1 us
    ppermute x12, starting transfers between devices, swap(): return lax.ppermute(v, axis, pairs + [(b, a) for a, b in pairs])  13.7 us
    all_to_all x1, starting transfers between devices, body(): got = everyone(send)  12.4 us
    unnamed x66, local copies, waits for them, and re-layouts  12.4 us
    ppermute x12, waiting for transfers between devices, swap(): return lax.ppermute(v, axis, pairs + [(b, a) for a, b in pairs])  9.26 us
  transfers between devices with their start and end apart: 25, of which 11 were waited for; matrix products, arithmetic and copies ran while one was open for 1% of the time, Pallas kernels for 16%

profile of v4, /device:TPU:32, one launch (start us, length us, event | category | flops | bytes accessed | tf_op | source)
XLA Modules:
  0.0 201.2 jit_solution(2108843867366824249)
XLA Ops:
  1.4 1.8 pack.1
  3.2 1.9 edges.1
  5.8 12.4 %all-to-all-start = ((f32[128,2,128]{2,1,0:T(2,128)}), f32[128,2,128]{2,1,0:T(2,128)S(1)}, u32[]{:S(2)}, u32[]{:S(2)}) async-start(f32[128,2,128]{2,1,0:T(2,128)} %bitcast.10), calls=%async_computation | async-start | bytes 262144 | tf_op jit(solution)/shard_map/all_to_all | solution.py:777
  18.2 1.6 collective-permute-start.2
  19.8 3.8 %collective-permute-start.3 = (f32[32,256]{1,0:T(8,128)}, f32[32,256]{1,0:T(8,128)S(1)}, u32[]{:S(2)}, u32[]{:S(2)}) collective-permute-start(f32[32,256]{1,0:T(8,128)} %get-tuple-element.108), channel_id=1, source_target_pairs={{1,2},{3,4},{5,6},{7,8},{9,10},{11,12},{13,14},{2,1},{4,3},{6,5},{... | collective-permute-start | bytes 98312 | tf_op jit(solution)/shard_map/ppermute | solution.py:709
  23.6 4.3 %collective-permute-done.3.yb.cyb = f32[32,256]{1,0:T(8,128)S(1)} collective-permute-done((f32[32,256]{1,0:T(8,128)}, f32[32,256]{1,0:T(8,128)S(1)}, u32[]{:S(2)}, u32[]{:S(2)}) %collective-permute-start.3) | collective-permute-done | bytes 32800 | tf_op jit(solution)/shard_map/ppermute | solution.py:709
  28.0 5.6 %first.1 = (f32[256,128]{1,0:T(8,128)}, f32[128,128]{1,0:T(8,128)S(1)}, f32[128,128]{1,0:T(8,128)}, f32[128,128]{1,0:T(8,128)}, f32[128,128]{1,0:T(8,128)}) custom-call(s32[2]{0:T(128)S(1)} %pad_add_fusion.at, s32[4,8]{1,0:T(4,128)S(1)} %bitcast.62, f32[32,128,128]{2,1,0:T(8,128)} %bitcast.37, f32[1024,256]{1,0:T(8,128)} %bitcast.71, ...), custom_call_target="tpu_custom_call" | custom-call | flops 2000000000 | bytes 1000000 | tf_op jit(solution)/shard_map/first/pallas_call | solution.py:56
  33.5 8.8 %all-to-all-start.1 = ((f32[128,2,128]{2,1,0:T(2,128)}), f32[128,2,128]{2,1,0:T(2,128)S(1)}, u32[]{:S(2)}, u32[]{:S(2)}) async-start(f32[128,2,128]{2,1,0:T(2,128)} %bitcast.79), calls=%async_computation.1 | async-start | bytes 262144 | tf_op jit(solution)/shard_map/all_to_all | solution.py:800
  42.4 0.8 copy-done.2
  43.2 0.8 copy-done.9
  44.0 6.5 %sweep.4 = (f32[16,64,256]{2,1,0:T(8,128)}, f32[16,64,256]{2,1,0:T(8,128)}, f32[16,64,256]{2,1,0:T(8,128)}, f32[64,256]{1,0:T(8,128)}, f32[64,256]{1,0:T(8,128)}, /*index=5*/f32[16,256]{1,0:T(8,128)}, f32[16,256]{1,0:T(8,128)}) custom-call(s32[2]{0:T(128)S(1)} %pad_add_fusion.at, f32[128,256]{1,0:T(8,128)S(1)} %collective-permute-done.xa.cxa, ...), custom_call_target="tpu_custom_call" | custom-call | flops 6000000 | bytes 8388608 | tf_op jit(solution)/shard_map/sweep/pallas_call | solution.py:689
  50.6 1.1 all-to-all-done.1
  52.4 8.6 %all-to-all-start.2 = ((f32[128,2,128]{2,1,0:T(2,128)}), f32[128,2,128]{2,1,0:T(2,128)S(1)}, u32[]{:S(2)}, u32[]{:S(2)}) async-start(f32[128,2,128]{2,1,0:T(2,128)} %bitcast.76), calls=%async_computation.2 | async-start | bytes 262144 | tf_op jit(solution)/shard_map/all_to_all | solution.py:808
  61.9 1.6 collective-permute-start.6
  63.5 3.8 %collective-permute-start.7 = (f32[16,256]{1,0:T(8,128)}, f32[16,256]{1,0:T(8,128)S(1)}, u32[]{:S(2)}, u32[]{:S(2)}) collective-permute-start(f32[16,256]{1,0:T(8,128)} %get-tuple-element.123), channel_id=1, source_target_pairs={{1,2},{3,4},{5,6},{7,8},{9,10},{11,12},{13,14},{2,1},{4,3},{6,5},{... | collective-permute-start | bytes 49160 | tf_op jit(solution)/shard_map/ppermute | solution.py:709
  67.3 4.1 %collective-permute-done.7.yb = f32[16,256]{1,0:T(8,128)S(1)} collective-permute-done((f32[16,256]{1,0:T(8,128)}, f32[16,256]{1,0:T(8,128)S(1)}, u32[]{:S(2)}, u32[]{:S(2)}) %collective-permute-start.7) | collective-permute-done | bytes 16416 | tf_op jit(solution)/shard_map/ppermute | solution.py:709
  71.5 5.5 %sweep.5 = (f32[16,64,256]{2,1,0:T(8,128)}, f32[64,256]{1,0:T(8,128)}, f32[64,256]{1,0:T(8,128)}, f32[16,256]{1,0:T(8,128)}, f32[16,256]{1,0:T(8,128)}) custom-call(s32[2]{0:T(128)S(1)} %pad_add_fusion.at, f32[64,256]{1,0:T(8,128)S(1)} %collective-permute-done.4.xa, f32[64,256]{1,0:T(8,128)S(1)} %collective-permute-done.5.xb, ...), custom_call_target="tpu_custom_call" | custom-call | flops 6000000 | bytes 8388608 | tf_op jit(solution)/shard_map/sweep/pallas_call | solution.py:689
  77.0 1.7 start.1
  78.7 6.7 %all-to-all-start.3 = ((f32[16,40,128]{2,1,0:T(8,128)}), f32[16,40,128]{2,1,0:T(8,128)S(1)}, u32[]{:S(2)}, u32[]{:S(2)}) async-start(f32[16,40,128]{2,1,0:T(8,128)} %bitcast.78), calls=%async_computation.3 | async-start | bytes 655360 | tf_op jit(solution)/shard_map/all_to_all | solution.py:831
  85.4 5.0 %second.1 = (f32[128,128]{1,0:T(8,128)}, f32[256,128]{1,0:T(8,128)}) custom-call(f32[1024,256]{1,0:T(8,128)} %bitcast.72, f32[128,128]{1,0:T(8,128)} %get-tuple-element.115.rest_0_.message.rest_1_, f32[128,128]{1,0:T(8,128)} %get-tuple-element.130.trace), custom_call_target="tpu_custom_call" | custom-call | flops 2000000000 | bytes 1000000 | tf_op jit(solution)/shard_map/second/pallas_call | solution.py:56
  90.4 3.6 %all-to-all-done.3 = f32[16,40,128]{2,1,0:T(8,128)S(1)} async-done(((f32[16,40,128]{2,1,0:T(8,128)}), f32[16,40,128]{2,1,0:T(8,128)S(1)}, u32[]{:S(2)}, u32[]{:S(2)}) %all-to-all-start.3) | async-done | bytes 327712 | tf_op jit(solution)/shard_map/all_to_all | solution.py:831
  94.0 4.6 %all-to-all-start.4 = ((f32[8,32,128]{2,1,0:T(8,128)}), f32[8,32,128]{2,1,0:T(8,128)S(1)}, u32[]{:S(2)}, u32[]{:S(2)}) async-start(f32[8,32,128]{2,1,0:T(8,128)} %bitcast.80), calls=%async_computation.4 | async-start | bytes 262144 | tf_op jit(solution)/shard_map/all_to_all | solution.py:843
  98.8 5.9 %all-to-all-done.4 = f32[8,32,128]{2,1,0:T(8,128)S(1)} async-done(((f32[8,32,128]{2,1,0:T(8,128)}), f32[8,32,128]{2,1,0:T(8,128)S(1)}, u32[]{:S(2)}, u32[]{:S(2)}) %all-to-all-start.4) | async-done | bytes 131104 | tf_op jit(solution)/shard_map/all_to_all | solution.py:843
  104.7 2.2 %step.5 = (f32[128,128]{1,0:T(8,128)S(1)}, f32[128,128]{1,0:T(8,128)S(1)}, f32[128,128]{1,0:T(8,128)S(1)}, f32[1024,128]{1,0:T(8,128)}) custom-call(s32[2]{0:T(128)S(1)} %pad_add_fusion.at, s32[4,8]{1,0:T(4,128)S(1)} %bitcast.64, f32[32,128,128]{2,1,0:T(8,128)S(1)} %bitcast.39, f32[640,128]{1,0:T(8,128)S(1)} %bitcast.47, ...), custom_call_target="tpu_custom_call" | custom-call | flops 1000000 | bytes 1000000 | tf_op jit(solution)/shard_map/step/pallas_call | solution.py:56
  107.6 5.4 %all-to-all-start.5 = ((f32[16,64,128]{2,1,0:T(8,128)}), f32[16,64,128]{2,1,0:T(8,128)S(1)}, u32[]{:S(2)}, u32[]{:S(2)}) async-start(f32[16,64,128]{2,1,0:T(8,128)} %bitcast.75), calls=%async_computation.5 | async-start | bytes 1048576 | tf_op jit(solution)/shard_map/all_to_all | solution.py:877
  113.6 0.8 collective-permute-done.8.xa
  114.4 7.6 %all-to-all-done.5 = f32[16,64,128]{2,1,0:T(8,128)S(1)} async-done(((f32[16,64,128]{2,1,0:T(8,128)}), f32[16,64,128]{2,1,0:T(8,128)S(1)}, u32[]{:S(2)}, u32[]{:S(2)}) %all-to-all-start.5) | async-done | bytes 524320 | tf_op jit(solution)/shard_map/all_to_all | solution.py:877
  122.1 0.8 copy-done.15
  122.9 0.8 copy-done.17
  123.8 2.4 %step.6 = (f32[128,128]{1,0:T(8,128)S(1)}, f32[128,128]{1,0:T(8,128)S(1)}, f32[128,128]{1,0:T(8,128)S(1)}, f32[1152,128]{1,0:T(8,128)}, f32[16,128]{1,0:T(8,128)}, /*index=5*/f32[128,128]{1,0:T(8,128)}) custom-call(s32[2]{0:T(128)S(1)} %pad_add_fusion.at, s32[4,8]{1,0:T(4,128)S(1)} %bitcast.65, f32[32,128,128]{2,1,0:T(8,128)S(1)} %bitcast.40, ...), custom_call_target="tpu_custom_call" | custom-call | flops 1000000 | bytes 1000000 | tf_op jit(solution)/shard_map/step/pallas_call | solution.py:56
  126.8 6.2 %all-to-all-start.6 = ((f32[16,72,128]{2,1,0:T(8,128)}), f32[16,72,128]{2,1,0:T(8,128)S(1)}, u32[]{:S(2)}, u32[]{:S(2)}) async-start(f32[16,72,128]{2,1,0:T(8,128)} %bitcast.73), calls=%async_computation.6 | async-start | bytes 1179648 | tf_op jit(solution)/shard_map/all_to_all | solution.py:882
  133.0 1.4 collective-permute-done.10.rest_1_
  135.7 3.2 %collective-permute-done.11.rest_2_ = f32[32,128]{1,0:T(8,128)S(1)} collective-permute-done((f32[32,128]{1,0:T(8,128)S(1)}, f32[32,128]{1,0:T(8,128)S(1)}, u32[]{:S(2)}, u32[]{:S(2)}) %collective-permute-start.11) | collective-permute-done | bytes 16416 | tf_op jit(solution)/shard_map/ppermute | solution.py:886
  139.5 1.0 collective-permute-start.12
  140.6 4.5 %collective-permute-done.12.rest_3_ = f32[64,128]{1,0:T(8,128)} collective-permute-done((f32[64,128]{1,0:T(8,128)S(1)}, f32[64,128]{1,0:T(8,128)}, u32[]{:S(2)}, u32[]{:S(2)}) %collective-permute-start.12) | collective-permute-done | bytes 32800 | tf_op jit(solution)/shard_map/ppermute | solution.py:886
  145.1 0.8 copy-done.11
  145.9 0.8 copy-done.13
  146.8 2.4 %step.7 = (f32[128,128]{1,0:T(8,128)S(1)}, f32[128,128]{1,0:T(8,128)S(1)}, f32[128,128]{1,0:T(8,128)S(1)}, f32[640,128]{1,0:T(8,128)}, f32[16,256]{1,0:T(8,128)}, /*index=5*/f32[16,256]{1,0:T(8,128)}) custom-call(s32[2]{0:T(128)S(1)} %pad_add_fusion.at, s32[4,8]{1,0:T(4,128)S(1)} %bitcast.66, f32[32,128,128]{2,1,0:T(8,128)S(1)} %bitcast.41, ...), custom_call_target="tpu_custom_call" | custom-call | flops 1000000 | bytes 1000000 | tf_op jit(solution)/shard_map/step/pallas_call | solution.py:56
  150.4 7.3 %all-to-all-start.7 = ((f32[16,40,128]{2,1,0:T(8,128)}), f32[16,40,128]{2,1,0:T(8,128)S(1)}, u32[]{:S(2)}, u32[]{:S(2)}) async-start(f32[16,40,128]{2,1,0:T(8,128)} %bitcast.77), calls=%async_computation.7 | async-start | bytes 655360 | tf_op jit(solution)/shard_map/all_to_all | solution.py:891
  159.1 7.6 %sweep.6 = (f32[16,64,256]{2,1,0:T(8,128)}, f32[16,64,256]{2,1,0:T(8,128)}, f32[64,256]{1,0:T(8,128)}, f32[64,256]{1,0:T(8,128)}, f32[16,256]{1,0:T(8,128)}, /*index=5*/f32[16,256]{1,0:T(8,128)}) custom-call(s32[2]{0:T(128)S(1)} %pad_add_fusion.at, f32[64,256]{1,0:T(8,128)S(1)} %collective-permute-done.8.xa, f32[64,256]{1,0:T(8,128)S(1)} %collective-permute-done.9.xb, ...), custom_call_target="tpu_custom_call" | custom-call | flops 6000000 | bytes 8388608 | tf_op jit(solution)/shard_map/sweep/pallas_call | solution.py:689
  166.8 2.4 %step.8 = (f32[128,128]{1,0:T(8,128)S(1)}, f32[128,128]{1,0:T(8,128)S(1)}, f32[128,128]{1,0:T(8,128)S(1)}, f32[1152,128]{1,0:T(8,128)}) custom-call(s32[2]{0:T(128)S(1)} %pad_add_fusion.at, s32[4,8]{1,0:T(4,128)S(1)} %bitcast.67, f32[32,128,128]{2,1,0:T(8,128)S(1)} %bitcast.42, f32[640,128]{1,0:T(8,128)S(1)} %bitcast.48, ...), custom_call_target="tpu_custom_call" | custom-call | flops 1000000 | bytes 1000000 | tf_op jit(solution)/shard_map/step/pallas_call | solution.py:56
  169.2 7.2 %all-to-all-start.8 = ((f32[16,72,128]{2,1,0:T(8,128)}), f32[16,72,128]{2,1,0:T(8,128)S(1)}, u32[]{:S(2)}, u32[]{:S(2)}) async-start(f32[16,72,128]{2,1,0:T(8,128)} %bitcast.74), calls=%async_computation.8 | async-start | bytes 1179648 | tf_op jit(solution)/shard_map/all_to_all | solution.py:909
  177.1 1.9 home.1
  179.0 5.9 %all-to-all-done.8 = f32[16,72,128]{2,1,0:T(8,128)S(1)} async-done(((f32[16,72,128]{2,1,0:T(8,128)}), f32[16,72,128]{2,1,0:T(8,128)S(1)}, u32[]{:S(2)}, u32[]{:S(2)}) %all-to-all-start.8) | async-done | bytes 589856 | tf_op jit(solution)/shard_map/all_to_all | solution.py:909
  184.8 1.8 step.9
  187.9 5.4 %all-to-all-start.9 = ((f32[16,1,128]{2,1,0:T(1,128)}), f32[16,1,128]{2,1,0:T(1,128)S(1)}, u32[]{:S(2)}, u32[]{:S(2)}) async-start(f32[16,1,128]{2,1,0:T(1,128)} %bitcast.87), calls=%async_computation.9 | async-start | bytes 16384 | tf_op jit(solution)/shard_map/all_to_all | solution.py:920
  194.8 5.2 %sweep.7 = f32[16,64,256]{2,1,0:T(8,128)} custom-call(s32[2]{0:T(128)S(1)} %pad_add_fusion.at, f32[64,256]{1,0:T(8,128)S(1)} %collective-permute-done.13.xa, f32[64,256]{1,0:T(8,128)S(1)} %collective-permute-done.14.xb, f32[16,256]{1,0:T(8,128)S(1)} %copy-done.28, f32[16,256]{1,0:T(8,128)S(1)} %copy-done.29, f32[128,256]{1,0:T(8,128)S(1)} %collective-permute-done.xa.cxa, ...), custom_call_target="tpu_custom_call" | custom-call | flops 6000000 | bytes 8388608 | tf_op jit(solution)/shard_map/sweep/pallas_call | solution.py:689
  200.0 1.2 final.1
  (89 shorter events, 13.2 us)
Async XLA Ops:
  3.2 24.7 %copy-start.5 = (f32[1024]{0:T(1024)S(1)}, f32[1024]{0:T(1024)}, u32[]{:S(2)}) copy-start(f32[1024]{0:T(1024)} %param.23) | copy-start | bytes 12292
  3.2 24.7 %copy-start.7 = (s32[8,4]{0,1:T(4,128)S(1)}, s32[8,4]{0,1:T(4,128)}, u32[]{:S(2)}) copy-start(s32[8,4]{0,1:T(4,128)} %param.22) | copy-start | bytes 388
  3.2 24.7 %copy-start.30 = (f32[1024]{0:T(1024)S(1)}, f32[1024]{0:T(1024)}, u32[]{:S(2)}) copy-start(f32[1024]{0:T(1024)} %param.24) | copy-start | bytes 12292
  5.1 22.8 %collective-permute-start = (f32[128,256]{1,0:T(8,128)}, f32[128,256]{1,0:T(8,128)S(1)}, u32[]{:S(2)}, u32[]{:S(2)}) collective-permute-start(f32[128,256]{1,0:T(8,128)} %get-tuple-element.105), channel_id=1, source_target_pairs={{0,16},{32,48},{64,80},{96,112},{16,0},{48,32},{80,64},{112,96},{1... | collective-permute-start | bytes 393224 | tf_op jit(solution)/shard_map/ppermute | solution.py:709
  5.1 22.8 %collective-permute-start.1 = (f32[128,256]{1,0:T(8,128)}, f32[128,256]{1,0:T(8,128)S(1)}, u32[]{:S(2)}, u32[]{:S(2)}) collective-permute-start(f32[128,256]{1,0:T(8,128)} %get-tuple-element.106), channel_id=1, source_target_pairs={{16,32},{48,64},{80,96},{32,16},{64,48},{96,80},{17,33},{49,65},{8... | collective-permute-start | bytes 393224 | tf_op jit(solution)/shard_map/ppermute | solution.py:709
  5.8 22.1 %all-to-all-start = ((f32[128,2,128]{2,1,0:T(2,128)}), f32[128,2,128]{2,1,0:T(2,128)S(1)}, u32[]{:S(2)}, u32[]{:S(2)}) async-start(f32[128,2,128]{2,1,0:T(2,128)} %bitcast.10), calls=%async_computation | async-start | bytes 262144 | tf_op jit(solution)/shard_map/all_to_all | solution.py:777
  18.2 5.4 %collective-permute-start.2 = (f32[32,256]{1,0:T(8,128)}, f32[32,256]{1,0:T(8,128)S(1)}, u32[]{:S(2)}, u32[]{:S(2)}) collective-permute-start(f32[32,256]{1,0:T(8,128)} %get-tuple-element.107), channel_id=1, source_target_pairs={{0,1},{2,3},{4,5},{6,7},{8,9},{10,11},{12,13},{14,15},{1,0},{3,2},... | collective-permute-start | bytes 98312 | tf_op jit(solution)/shard_map/ppermute | solution.py:709
  19.8 8.1 %collective-permute-start.3 = (f32[32,256]{1,0:T(8,128)}, f32[32,256]{1,0:T(8,128)S(1)}, u32[]{:S(2)}, u32[]{:S(2)}) collective-permute-start(f32[32,256]{1,0:T(8,128)} %get-tuple-element.108), channel_id=1, source_target_pairs={{1,2},{3,4},{5,6},{7,8},{9,10},{11,12},{13,14},{2,1},{4,3},{6,5},{... | collective-permute-start | bytes 98312 | tf_op jit(solution)/shard_map/ppermute | solution.py:709
  33.5 71.2 %copy-start.4 = (f32[128,128]{1,0:T(8,128)}, f32[128,128]{1,0:T(8,128)S(1)}, u32[]{:S(2)}) copy-start(f32[128,128]{1,0:T(8,128)S(1)} %get-tuple-element.135.x.rest_4_) | copy-start | bytes 196612
  33.5 18.2 %all-to-all-start.1 = ((f32[128,2,128]{2,1,0:T(2,128)}), f32[128,2,128]{2,1,0:T(2,128)S(1)}, u32[]{:S(2)}, u32[]{:S(2)}) async-start(f32[128,2,128]{2,1,0:T(2,128)} %bitcast.79), calls=%async_computation.1 | async-start | bytes 262144 | tf_op jit(solution)/shard_map/all_to_all | solution.py:800
  42.4 0.8 copy-start.2
  43.2 0.8 copy-start.9
  52.4 24.6 %all-to-all-start.2 = ((f32[128,2,128]{2,1,0:T(2,128)}), f32[128,2,128]{2,1,0:T(2,128)S(1)}, u32[]{:S(2)}, u32[]{:S(2)}) async-start(f32[128,2,128]{2,1,0:T(2,128)} %bitcast.76), calls=%async_computation.2 | async-start | bytes 262144 | tf_op jit(solution)/shard_map/all_to_all | solution.py:808
  61.0 10.4 %collective-permute-start.4 = (f32[64,256]{1,0:T(8,128)}, f32[64,256]{1,0:T(8,128)S(1)}, u32[]{:S(2)}, u32[]{:S(2)}) collective-permute-start(f32[64,256]{1,0:T(8,128)} %get-tuple-element.120), channel_id=1, source_target_pairs={{0,16},{32,48},{64,80},{96,112},{16,0},{48,32},{80,64},{112,96},{1... | collective-permute-start | bytes 196616 | tf_op jit(solution)/shard_map/ppermute | solution.py:709
  61.3 10.2 %collective-permute-start.5 = (f32[64,256]{1,0:T(8,128)}, f32[64,256]{1,0:T(8,128)S(1)}, u32[]{:S(2)}, u32[]{:S(2)}) collective-permute-start(f32[64,256]{1,0:T(8,128)} %get-tuple-element.121), channel_id=1, source_target_pairs={{16,32},{48,64},{80,96},{32,16},{64,48},{96,80},{17,33},{49,65},{8... | collective-permute-start | bytes 196616 | tf_op jit(solution)/shard_map/ppermute | solution.py:709
  61.9 5.4 %collective-permute-start.6 = (f32[16,256]{1,0:T(8,128)}, f32[16,256]{1,0:T(8,128)S(1)}, u32[]{:S(2)}, u32[]{:S(2)}) collective-permute-start(f32[16,256]{1,0:T(8,128)} %get-tuple-element.122), channel_id=1, source_target_pairs={{0,1},{2,3},{4,5},{6,7},{8,9},{10,11},{12,13},{14,15},{1,0},{3,2},... | collective-permute-start | bytes 49160 | tf_op jit(solution)/shard_map/ppermute | solution.py:709
  63.5 7.9 %collective-permute-start.7 = (f32[16,256]{1,0:T(8,128)}, f32[16,256]{1,0:T(8,128)S(1)}, u32[]{:S(2)}, u32[]{:S(2)}) collective-permute-start(f32[16,256]{1,0:T(8,128)} %get-tuple-element.123), channel_id=1, source_target_pairs={{1,2},{3,4},{5,6},{7,8},{9,10},{11,12},{13,14},{2,1},{4,3},{6,5},{... | collective-permute-start | bytes 49160 | tf_op jit(solution)/shard_map/ppermute | solution.py:709
  71.5 5.5 %copy-start = (f32[8,4,128,128]{3,2,1,0:T(8,128)S(1)}, f32[8,4,128,128]{3,2,1,0:T(8,128)}, u32[]{:S(2)}) copy-start(f32[8,4,128,128]{3,2,1,0:T(8,128)} %param.21) | copy-start | bytes 6291460
  78.7 15.2 %all-to-all-start.3 = ((f32[16,40,128]{2,1,0:T(8,128)}), f32[16,40,128]{2,1,0:T(8,128)S(1)}, u32[]{:S(2)}, u32[]{:S(2)}) async-start(f32[16,40,128]{2,1,0:T(8,128)} %bitcast.78), calls=%async_computation.3 | async-start | bytes 655360 | tf_op jit(solution)/shard_map/all_to_all | solution.py:831
  94.0 10.8 %all-to-all-start.4 = ((f32[8,32,128]{2,1,0:T(8,128)}), f32[8,32,128]{2,1,0:T(8,128)S(1)}, u32[]{:S(2)}, u32[]{:S(2)}) async-start(f32[8,32,128]{2,1,0:T(8,128)} %bitcast.80), calls=%async_computation.4 | async-start | bytes 262144 | tf_op jit(solution)/shard_map/all_to_all | solution.py:843
  107.6 14.5 %copy-start.16 = (f32[128,128]{1,0:T(8,128)}, f32[128,128]{1,0:T(8,128)S(1)}, u32[]{:S(2)}) copy-start(f32[128,128]{1,0:T(8,128)S(1)} %get-tuple-element.148.d) | copy-start | bytes 196612
  107.6 14.5 %all-to-all-start.5 = ((f32[16,64,128]{2,1,0:T(8,128)}), f32[16,64,128]{2,1,0:T(8,128)S(1)}, u32[]{:S(2)}, u32[]{:S(2)}) async-start(f32[16,64,128]{2,1,0:T(8,128)} %bitcast.75), calls=%async_computation.5 | async-start | bytes 1048576 | tf_op jit(solution)/shard_map/all_to_all | solution.py:877
  113.0 1.5 collective-permute-start.8
  113.0 1.5 collective-permute-start.9
  122.1 0.8 copy-start.15
  122.9 0.8 copy-start.17
  126.8 18.3 %copy-start.12 = (f32[128,128]{1,0:T(8,128)}, f32[128,128]{1,0:T(8,128)S(1)}, u32[]{:S(2)}) copy-start(f32[128,128]{1,0:T(8,128)S(1)} %get-tuple-element.154.d) | copy-start | bytes 196612
  126.8 30.9 %copy-start.3 = (f32[128,128]{1,0:T(8,128)S(1)}, f32[128,128]{1,0:T(8,128)}, u32[]{:S(2)}) copy-start(f32[128,128]{1,0:T(8,128)} %get-tuple-element.115.rest_0_.message.rest_1_) | copy-start | bytes 196612
  126.8 30.9 %copy-start.8 = (f32[128,128]{1,0:T(8,128)S(1)}, f32[128,128]{1,0:T(8,128)}, u32[]{:S(2)}) copy-start(f32[128,128]{1,0:T(8,128)} %get-tuple-element.162.rest_2_) | copy-start | bytes 196612
  126.8 18.3 %all-to-all-start.6 = ((f32[16,72,128]{2,1,0:T(8,128)}), f32[16,72,128]{2,1,0:T(8,128)S(1)}, u32[]{:S(2)}, u32[]{:S(2)}) async-start(f32[16,72,128]{2,1,0:T(8,128)} %bitcast.73), calls=%async_computation.6 | async-start | bytes 1179648 | tf_op jit(solution)/shard_map/all_to_all | solution.py:882
  133.0 1.4 collective-permute-start.10
  134.4 6.2 %copy-start.31 = (f32[16,128]{1,0:T(8,128)}, f32[16,128]{1,0:T(8,128)S(1)}, u32[]{:S(2)}) copy-start(f32[16,128]{1,0:T(8,128)S(1)} %collective-permute-done.10.rest_1_) | copy-start | bytes 24580
  135.1 3.7 %collective-permute-start.11 = (f32[32,128]{1,0:T(8,128)S(1)}, f32[32,128]{1,0:T(8,128)S(1)}, u32[]{:S(2)}, u32[]{:S(2)}) collective-permute-start(f32[32,128]{1,0:T(8,128)S(1)} %pad_maximum_fusion.1), channel_id=1, source_target_pairs={{0,32},{16,48},{32,0},{48,16},{64,96},{80,112},{96,64},{112,80},{1... | collective-permute-start | bytes 49160 | tf_op jit(solution)/shard_map/ppermute | solution.py:886
  138.8 1.8 copy-start.32
  139.5 5.5 %collective-permute-start.12 = (f32[64,128]{1,0:T(8,128)S(1)}, f32[64,128]{1,0:T(8,128)}, u32[]{:S(2)}, u32[]{:S(2)}) collective-permute-start(f32[64,128]{1,0:T(8,128)S(1)} %pad_maximum_fusion), channel_id=1, source_target_pairs={{0,64},{16,80},{32,96},{48,112},{64,0},{80,16},{96,32},{112,48},{1... | collective-permute-start | bytes 98312 | tf_op jit(solution)/shard_map/ppermute | solution.py:886
  145.1 0.8 copy-start.11
  145.9 0.8 copy-start.13
  150.4 16.3 %copy-start.1 = (f32[128,128]{1,0:T(8,128)}, f32[128,128]{1,0:T(8,128)S(1)}, u32[]{:S(2)}) copy-start(f32[128,128]{1,0:T(8,128)S(1)} %get-tuple-element.163.rest_3_.x) | copy-start | bytes 196612
  150.4 16.3 %all-to-all-start.7 = ((f32[16,40,128]{2,1,0:T(8,128)}), f32[16,40,128]{2,1,0:T(8,128)S(1)}, u32[]{:S(2)}, u32[]{:S(2)}) async-start(f32[16,40,128]{2,1,0:T(8,128)} %bitcast.77), calls=%async_computation.7 | async-start | bytes 655360 | tf_op jit(solution)/shard_map/all_to_all | solution.py:891
  157.7 0.7 copy-start.26
  159.1 7.6 %copy-start.23 = (f32[128,128]{1,0:T(8,128)S(1)}, f32[128,128]{1,0:T(8,128)}, u32[]{:S(2)}) copy-start(f32[128,128]{1,0:T(8,128)} %copy-done.22) | copy-start | bytes 196612
  159.1 7.6 %copy-start.25 = (f32[128,128]{1,0:T(8,128)S(1)}, f32[128,128]{1,0:T(8,128)}, u32[]{:S(2)}) copy-start(f32[128,128]{1,0:T(8,128)} %copy-done.24) | copy-start | bytes 196612
  169.2 15.7 %all-to-all-start.8 = ((f32[16,72,128]{2,1,0:T(8,128)}), f32[16,72,128]{2,1,0:T(8,128)S(1)}, u32[]{:S(2)}, u32[]{:S(2)}) async-start(f32[16,72,128]{2,1,0:T(8,128)} %bitcast.74), calls=%async_computation.8 | async-start | bytes 1179648 | tf_op jit(solution)/shard_map/all_to_all | solution.py:909
  176.4 2.6 %collective-permute-start.13 = (f32[64,256]{1,0:T(8,128)}, f32[64,256]{1,0:T(8,128)S(1)}, u32[]{:S(2)}, u32[]{:S(2)}) collective-permute-start(f32[64,256]{1,0:T(8,128)} %get-tuple-element.181), channel_id=1, source_target_pairs={{0,16},{32,48},{64,80},{96,112},{16,0},{48,32},{80,64},{112,96},{1... | collective-permute-start | bytes 196616 | tf_op jit(solution)/shard_map/ppermute | solution.py:709
  176.4 2.5 %collective-permute-start.14 = (f32[64,256]{1,0:T(8,128)}, f32[64,256]{1,0:T(8,128)S(1)}, u32[]{:S(2)}, u32[]{:S(2)}) collective-permute-start(f32[64,256]{1,0:T(8,128)} %get-tuple-element.182), channel_id=1, source_target_pairs={{16,32},{48,64},{80,96},{32,16},{64,48},{96,80},{17,33},{49,65},{8... | collective-permute-start | bytes 196616 | tf_op jit(solution)/shard_map/ppermute | solution.py:709
  187.9 12.1 %all-to-all-start.9 = ((f32[16,1,128]{2,1,0:T(1,128)}), f32[16,1,128]{2,1,0:T(1,128)S(1)}, u32[]{:S(2)}, u32[]{:S(2)}) async-start(f32[16,1,128]{2,1,0:T(1,128)} %bitcast.87), calls=%async_computation.9 | async-start | bytes 16384 | tf_op jit(solution)/shard_map/all_to_all | solution.py:920
  194.7 5.2 %copy-start.19 = (f32[128,128]{1,0:T(8,128)S(1)}, f32[128,128]{1,0:T(8,128)}, u32[]{:S(2)}) copy-start(f32[128,128]{1,0:T(8,128)} %copy-done.18) | copy-start | bytes 196612
  194.8 5.2 %copy-start.21 = (f32[128,128]{1,0:T(8,128)S(1)}, f32[128,128]{1,0:T(8,128)}, u32[]{:S(2)}) copy-start(f32[128,128]{1,0:T(8,128)} %copy-done.20) | copy-start | bytes 196612
  (10 other events, 6.6 us)

commit v5 on v4

--- a/solution.py
+++ b/solution.py
@@ -416,7 +416,7 @@
 
 
 def step_body(
-    at, cols, tiles, got, x, r, d, chosen, diag, *rest, ride, last, faces_in, faces_out
+    at, cols, tiles, got, chosen, diag, *rest, ride, last, faces_in, faces_out
 ):
     per_row, rows = cols.shape
     size = rows * (1 + per_row)
@@ -424,7 +424,10 @@
     mats = rows
     extra = list(rest)
     change = extra.pop(0) if ride == "reduce" else None
-    parts = [extra.pop(0) for _ in range(4)] if ride == "next" else None
+    parts = [extra.pop(0) for _ in range(3)] if ride == "next" else None
+    x, r, d = (extra.pop(0) for _ in range(3))
+    if ride == "next":
+        parts.insert(0, extra.pop(0))
     x_before, weight = (extra.pop(0), extra.pop(0)) if ride == "next" else (None, None)
     y_faces = (extra.pop(0), extra.pop(0)) if faces_out else None
     x_out, r_out, d_out, send = (extra.pop(0) for _ in range(4))
@@ -684,8 +687,10 @@
     after = pl.BlockSpec(
         (1, ny, nz), lambda i: (jnp.minimum((i + 1) * many, nx - 1), 0, 0)
     )
+    if y_in:
+        halo = (*halo[:2], *(in_hbm(v, 1) for v in halo[2:]))
     operands = [*halo, *faces, p, p, trans, cell, rhs] + ([] if first else [weight])
-    operands += [got, *values] if values else []
+    operands += [in_hbm(v, 1) for v in (got, *values)] if values else []
     return pl.pallas_call(
         functools.partial(sweep_body, first=first, last=last, fluxes=len(values), y_in=y_in, y_out=y_out),
         grid=(nx // many,),
@@ -777,11 +782,10 @@
     got = everyone(send)
 
     faces = swapped(*edges(edges_at, pressure_start, face_trans), mats, shards)
-    got, *faces = lax.optimization_barrier((got, *faces))
 
     send, x_start, trace, flux, message = call(
         first_body,
-        (sent(2 * LANES, LANES), square, *[sent(LANES, LANES)] * 3),
+        (sent(2 * LANES, LANES), *[sent(LANES, LANES)] * 4),
         got,
         diag,
         frac_source.reshape(rows, LANES),
@@ -797,6 +801,7 @@
         flops=2e9,
         name="first",
     )
+    send, *faces = lax.optimization_barrier((send, *faces))
     reduced = everyone(send)
     pressure, weight, rhs, *sides = sweep(
         at, pressure_start, faces, faces, face_trans, cell_coef, matrix_source, got=message, values=(flux,)
@@ -818,7 +823,7 @@
 
     r, sums, send = call(
         start_body,
-        (square, sent(LANES, LANES), sent(shards * size, LANES)),
+        (*[sent(LANES, LANES)] * 2, sent(shards * size, LANES)),
         residuals,
         diag,
         scalars=scalars,
@@ -845,7 +850,7 @@
 
     def step(arrived, x, r, d, *more, ride=None, last=False, faces_in=False, faces=(), side=()):
         length = size + (shards + mats if ride == "reduce" else 0) + (2 * nx if faces else 0)
-        outs = [square, square, square, sent(shards * (1 if last else length), LANES)]
+        outs = [*[sent(LANES, LANES)] * 3, sent(shards * (1 if last else length), LANES)]
         if ride == "gather":
             outs += [sent(shards, LANES), sent(LANES, LANES)]
         if faces_in:
@@ -856,13 +861,10 @@
             ),
             tuple(outs),
             arrived,
-            x,
-            r,
-            d,
             chosen,
             diag,
             *more,
-            side=(*side, *faces),
+            side=(x, r, d, *side, *faces),
             scalars=scalars,
             resident=(tile_list,),
             scratch=([square_scratch] if ride == "next" else []) + [block],
@@ -886,7 +888,8 @@
         parts.append(lax.ppermute(mine, "mat", [(i, i ^ hop) for i in range(mats)]))
 
     x, r, d, send, *y_sides = step(
-        arrived, x, r, d, faces_in=True, ride="next", side=(*parts, x_start, sums))
+        arrived, x, r, d, *parts[1:], faces_in=True, ride="next", side=(change, x_start, sums)
+    )
     x_flux = x
     arrived = over_frac(send)
     pressure, rhs, *sides = sweep(
@@ -931,7 +934,7 @@
         y_in=True,
     )
     fracture = call(
-        final_body, shape(rows, LANES), arrived, x, r, d, scalars=(at,), name="final"
+        final_body, shape(rows, LANES), arrived, side=(x, r, d), scalars=(at,), name="final"
     )
     return pressure, fracture.reshape(rows * LANES), flux.reshape(count)
 

time: 204 us -> 191 us (0.936)
  local copies, waits for them, and re-layouts: 12.4 us -> 0.72 us
  starting transfers between devices: 87.9 us -> 85 us
    unnamed x66 -> x18, local copies, waits for them, and re-layouts: 12.4 us -> 0.72 us
    ppermute x12, waiting for transfers between devices: 9.26 us -> 4.73 us  [swap(): return lax.ppermute(v, axis, pairs + [(b, a) for a, b in pairs])]
    all_to_all x1, starting transfers between devices: 12.4 us -> 10.2 us  [body(): got = everyone(send)]
  transfers between devices with their start and end apart: 25 -> 25, of which waited for: 11 -> 12; matrix products, arithmetic and copies ran while one was open for 1% -> 1% of each run, Pallas kernels for 16% -> 21%
where the time goes in v5:
time: 191 us; the launch traced here: 188 us
  starting transfers between devices  85 us (45%)
  Pallas kernels  58 us (30%)
  waiting for transfers between devices  41.7 us (22%)
    all_to_all x6, starting transfers between devices, body(): arrived = over_frac(send)  38 us
    pallas_call x13, Pallas kernels, call(): pl.pallas_call(body, grid=(1,), out_shape=outs, in_specs=[SMEM] * len(sca...  31.3 us
    pallas_call x4, Pallas kernels, sweep(): pl.pallas_call(functools.partial(sweep_body, first=first, last=last, flux...  24.9 us
    all_to_all x6, waiting for transfers between devices, body(): arrived = over_frac(send)  18 us
    ppermute x12, starting transfers between devices, swap(): return lax.ppermute(v, axis, pairs + [(b, a) for a, b in pairs])  13.8 us
    all_to_all x1, starting transfers between devices, body(): got = everyone(send)  10.2 us
    all_to_all x1, starting transfers between devices, body(): reduced = everyone(send)  9.68 us
    ppermute x3, waiting for transfers between devices, body(): parts.append(lax.ppermute(mine, 'mat', [(i, i ^ hop) for i in range(mats)]))  8.92 us
  transfers between devices with their start and end apart: 25, of which 12 were waited for; matrix products, arithmetic and copies ran while one was open for 1% of the time, Pallas kernels for 21%

profile of v5, /device:TPU:32, one launch (start us, length us, event | category | flops | bytes accessed | tf_op | source)
XLA Modules:
  0.0 187.9 jit_solution(17207062049889516426)
XLA Ops:
  0.7 0.7 copy-done.2
  1.4 1.8 pack.1
  3.2 10.2 %all-to-all-start = ((f32[128,2,128]{2,1,0:T(2,128)}), f32[128,2,128]{2,1,0:T(2,128)S(1)}, u32[]{:S(2)}, u32[]{:S(2)}) async-start(f32[128,2,128]{2,1,0:T(2,128)} %bitcast.80), calls=%async_computation | async-start | bytes 262144 | tf_op jit(solution)/shard_map/all_to_all | solution.py:782
  13.5 1.9 edges.1
  15.3 1.5 collective-permute-start.2
  16.9 3.8 %collective-permute-start.3 = (f32[32,256]{1,0:T(8,128)}, f32[32,256]{1,0:T(8,128)S(1)}, u32[]{:S(2)}, u32[]{:S(2)}) collective-permute-start(f32[32,256]{1,0:T(8,128)} %get-tuple-element.109), channel_id=1, source_target_pairs={{1,2},{3,4},{5,6},{7,8},{9,10},{11,12},{13,14},{2,1},{4,3},{6,5},{... | collective-permute-start | bytes 98312 | tf_op jit(solution)/shard_map/ppermute | solution.py:714
  20.8 0.7 collective-permute-start.1
  21.4 1.4 all-to-all-done
  22.8 5.9 %first.1 = (f32[256,128]{1,0:T(8,128)}, f32[128,128]{1,0:T(8,128)}, f32[128,128]{1,0:T(8,128)}, f32[128,128]{1,0:T(8,128)}, f32[128,128]{1,0:T(8,128)}) custom-call(s32[2]{0:T(128)S(1)} %pad_add_fusion.at, s32[4,8]{1,0:T(4,128)S(1)} %bitcast.62, f32[32,128,128]{2,1,0:T(8,128)} %bitcast.37, f32[1024,256]{1,0:T(8,128)} %bitcast.71, f32[256,128]{1,0:T(8,128)S(1)} %bitcast.51, ...), custom_call_target="tpu_custom_call" | custom-call | flops 2000000000 | bytes 1000000 | tf_op jit(solution)/shard_map/first/pallas_call | solution.py:56
  28.8 9.7 %all-to-all-start.1 = ((f32[128,2,128]{2,1,0:T(2,128)}), f32[128,2,128]{2,1,0:T(2,128)S(1)}, u32[]{:S(2)}, u32[]{:S(2)}) async-start(f32[128,2,128]{2,1,0:T(2,128)} %bitcast.79), calls=%async_computation.1 | async-start | bytes 262144 | tf_op jit(solution)/shard_map/all_to_all | solution.py:805
  38.5 6.5 %sweep.4 = (f32[16,64,256]{2,1,0:T(8,128)}, f32[16,64,256]{2,1,0:T(8,128)}, f32[16,64,256]{2,1,0:T(8,128)}, f32[64,256]{1,0:T(8,128)}, f32[64,256]{1,0:T(8,128)}, /*index=5*/f32[16,256]{1,0:T(8,128)}, f32[16,256]{1,0:T(8,128)}) custom-call(s32[2]{0:T(128)S(1)} %pad_add_fusion.at, f32[128,256]{1,0:T(8,128)S(1)} %collective-permute-done.xa.cxa, ...), custom_call_target="tpu_custom_call" | custom-call | flops 6000000 | bytes 8388608 | tf_op jit(solution)/shard_map/sweep/pallas_call | solution.py:694
  45.0 2.8 %all-to-all-done.1 = f32[128,2,128]{2,1,0:T(2,128)S(1)} async-done(((f32[128,2,128]{2,1,0:T(2,128)}), f32[128,2,128]{2,1,0:T(2,128)S(1)}, u32[]{:S(2)}, u32[]{:S(2)}) %all-to-all-start.1) | async-done | bytes 131104 | tf_op jit(solution)/shard_map/all_to_all | solution.py:805
  47.8 0.7 sums.1
  48.5 7.0 %all-to-all-start.2 = ((f32[128,2,128]{2,1,0:T(2,128)}), f32[128,2,128]{2,1,0:T(2,128)S(1)}, u32[]{:S(2)}, u32[]{:S(2)}) async-start(f32[128,2,128]{2,1,0:T(2,128)} %bitcast.76), calls=%async_computation.2 | async-start | bytes 262144 | tf_op jit(solution)/shard_map/all_to_all | solution.py:813
  56.4 1.6 collective-permute-start.6
  58.0 3.8 %collective-permute-start.7 = (f32[16,256]{1,0:T(8,128)}, f32[16,256]{1,0:T(8,128)S(1)}, u32[]{:S(2)}, u32[]{:S(2)}) collective-permute-start(f32[16,256]{1,0:T(8,128)} %get-tuple-element.123), channel_id=1, source_target_pairs={{1,2},{3,4},{5,6},{7,8},{9,10},{11,12},{13,14},{2,1},{4,3},{6,5},{... | collective-permute-start | bytes 49160 | tf_op jit(solution)/shard_map/ppermute | solution.py:714
  61.8 4.1 %collective-permute-done.7.yb = f32[16,256]{1,0:T(8,128)S(1)} collective-permute-done((f32[16,256]{1,0:T(8,128)}, f32[16,256]{1,0:T(8,128)S(1)}, u32[]{:S(2)}, u32[]{:S(2)}) %collective-permute-start.7) | collective-permute-done | bytes 16416 | tf_op jit(solution)/shard_map/ppermute | solution.py:714
  65.9 5.5 %sweep.5 = (f32[16,64,256]{2,1,0:T(8,128)}, f32[64,256]{1,0:T(8,128)}, f32[64,256]{1,0:T(8,128)}, f32[16,256]{1,0:T(8,128)}, f32[16,256]{1,0:T(8,128)}) custom-call(s32[2]{0:T(128)S(1)} %pad_add_fusion.at, f32[64,256]{1,0:T(8,128)S(1)} %collective-permute-done.4.xa, f32[64,256]{1,0:T(8,128)S(1)} %collective-permute-done.5.xb, ...), custom_call_target="tpu_custom_call" | custom-call | flops 6000000 | bytes 8388608 | tf_op jit(solution)/shard_map/sweep/pallas_call | solution.py:694
  71.5 1.7 start.1
  73.2 6.7 %all-to-all-start.3 = ((f32[16,40,128]{2,1,0:T(8,128)}), f32[16,40,128]{2,1,0:T(8,128)S(1)}, u32[]{:S(2)}, u32[]{:S(2)}) async-start(f32[16,40,128]{2,1,0:T(8,128)} %bitcast.78), calls=%async_computation.3 | async-start | bytes 655360 | tf_op jit(solution)/shard_map/all_to_all | solution.py:836
  79.8 5.0 %second.1 = (f32[128,128]{1,0:T(8,128)}, f32[256,128]{1,0:T(8,128)}) custom-call(f32[1024,256]{1,0:T(8,128)} %bitcast.72, f32[128,128]{1,0:T(8,128)} %get-tuple-element.115.rest_0_.message.rest_1_, f32[128,128]{1,0:T(8,128)} %get-tuple-element.130.trace), custom_call_target="tpu_custom_call" | custom-call | flops 2000000000 | bytes 1000000 | tf_op jit(solution)/shard_map/second/pallas_call | solution.py:56
  84.8 3.5 %all-to-all-done.3 = f32[16,40,128]{2,1,0:T(8,128)S(1)} async-done(((f32[16,40,128]{2,1,0:T(8,128)}), f32[16,40,128]{2,1,0:T(8,128)S(1)}, u32[]{:S(2)}, u32[]{:S(2)}) %all-to-all-start.3) | async-done | bytes 327712 | tf_op jit(solution)/shard_map/all_to_all | solution.py:836
  88.4 4.6 %all-to-all-start.4 = ((f32[8,32,128]{2,1,0:T(8,128)}), f32[8,32,128]{2,1,0:T(8,128)S(1)}, u32[]{:S(2)}, u32[]{:S(2)}) async-start(f32[8,32,128]{2,1,0:T(8,128)} %bitcast.81), calls=%async_computation.4 | async-start | bytes 262144 | tf_op jit(solution)/shard_map/all_to_all | solution.py:848
  93.3 5.9 %all-to-all-done.4 = f32[8,32,128]{2,1,0:T(8,128)S(1)} async-done(((f32[8,32,128]{2,1,0:T(8,128)}), f32[8,32,128]{2,1,0:T(8,128)S(1)}, u32[]{:S(2)}, u32[]{:S(2)}) %all-to-all-start.4) | async-done | bytes 131104 | tf_op jit(solution)/shard_map/all_to_all | solution.py:848
  99.2 2.6 %step.5 = (f32[128,128]{1,0:T(8,128)}, f32[128,128]{1,0:T(8,128)}, f32[128,128]{1,0:T(8,128)}, f32[1024,128]{1,0:T(8,128)}) custom-call(s32[2]{0:T(128)S(1)} %pad_add_fusion.at, s32[4,8]{1,0:T(4,128)S(1)} %bitcast.64, f32[32,128,128]{2,1,0:T(8,128)S(1)} %bitcast.39, f32[640,128]{1,0:T(8,128)S(1)} %bitcast.47, bf16[128,512]{1,0:T(8,128)(2,1)S(1)} %columns.1.chosen, ...), custom_call_target="tpu_custom_call" | custom-call | flops 1000000 | bytes 1000000 | tf_op jit(solution)/shard_map/step/pallas_call | solution.py:56
  101.8 5.4 %all-to-all-start.5 = ((f32[16,64,128]{2,1,0:T(8,128)}), f32[16,64,128]{2,1,0:T(8,128)S(1)}, u32[]{:S(2)}, u32[]{:S(2)}) async-start(f32[16,64,128]{2,1,0:T(8,128)} %bitcast.75), calls=%async_computation.5 | async-start | bytes 1048576 | tf_op jit(solution)/shard_map/all_to_all | solution.py:879
  107.2 0.7 collective-permute-start.9
  108.5 7.8 %all-to-all-done.5 = f32[16,64,128]{2,1,0:T(8,128)S(1)} async-done(((f32[16,64,128]{2,1,0:T(8,128)}), f32[16,64,128]{2,1,0:T(8,128)S(1)}, u32[]{:S(2)}, u32[]{:S(2)}) %all-to-all-start.5) | async-done | bytes 524320 | tf_op jit(solution)/shard_map/all_to_all | solution.py:879
  116.2 2.6 %step.6 = (f32[128,128]{1,0:T(8,128)}, f32[128,128]{1,0:T(8,128)}, f32[128,128]{1,0:T(8,128)}, f32[1152,128]{1,0:T(8,128)}, f32[16,128]{1,0:T(8,128)}, /*index=5*/f32[128,128]{1,0:T(8,128)}) custom-call(s32[2]{0:T(128)S(1)} %pad_add_fusion.at, s32[4,8]{1,0:T(4,128)S(1)} %bitcast.65, f32[32,128,128]{2,1,0:T(8,128)S(1)} %bitcast.40, f32[1024,128]{1,0:T(8,128)S(1)} %bitcast.46, ...), custom_call_target="tpu_custom_call" | custom-call | flops 1000000 | bytes 1000000 | tf_op jit(solution)/shard_map/step/pallas_call | solution.py:56
  118.8 6.1 %all-to-all-start.6 = ((f32[16,72,128]{2,1,0:T(8,128)}), f32[16,72,128]{2,1,0:T(8,128)S(1)}, u32[]{:S(2)}, u32[]{:S(2)}) async-start(f32[16,72,128]{2,1,0:T(8,128)} %bitcast.73), calls=%async_computation.6 | async-start | bytes 1179648 | tf_op jit(solution)/shard_map/all_to_all | solution.py:884
  124.9 1.4 collective-permute-done.10.rest_0_
  126.3 0.7 pad_maximum_fusion.1
  127.5 3.2 %collective-permute-done.11.rest_1_ = f32[32,128]{1,0:T(8,128)S(1)} collective-permute-done((f32[32,128]{1,0:T(8,128)S(1)}, f32[32,128]{1,0:T(8,128)S(1)}, u32[]{:S(2)}, u32[]{:S(2)}) %collective-permute-start.11) | collective-permute-done | bytes 16416 | tf_op jit(solution)/shard_map/ppermute | solution.py:888
  130.7 0.7 pad_maximum_fusion
  131.4 1.0 collective-permute-start.12
  132.5 4.4 %collective-permute-done.12.rest_2_ = f32[64,128]{1,0:T(8,128)S(1)} collective-permute-done((f32[64,128]{1,0:T(8,128)S(1)}, f32[64,128]{1,0:T(8,128)S(1)}, u32[]{:S(2)}, u32[]{:S(2)}) %collective-permute-start.12) | collective-permute-done | bytes 32800 | tf_op jit(solution)/shard_map/ppermute | solution.py:888
  136.8 2.5 %step.7 = (f32[128,128]{1,0:T(8,128)}, f32[128,128]{1,0:T(8,128)}, f32[128,128]{1,0:T(8,128)}, f32[640,128]{1,0:T(8,128)}, f32[16,256]{1,0:T(8,128)}, /*index=5*/f32[16,256]{1,0:T(8,128)}) custom-call(s32[2]{0:T(128)S(1)} %pad_add_fusion.at, s32[4,8]{1,0:T(4,128)S(1)} %bitcast.66, f32[32,128,128]{2,1,0:T(8,128)S(1)} %bitcast.41, f32[1152,128]{1,0:T(8,128)S(1)} %bitcast.44, ...), custom_call_target="tpu_custom_call" | custom-call | flops 1000000 | bytes 1000000 | tf_op jit(solution)/shard_map/step/pallas_call | solution.py:56
  139.3 7.3 %all-to-all-start.7 = ((f32[16,40,128]{2,1,0:T(8,128)}), f32[16,40,128]{2,1,0:T(8,128)S(1)}, u32[]{:S(2)}, u32[]{:S(2)}) async-start(f32[16,40,128]{2,1,0:T(8,128)} %bitcast.77), calls=%async_computation.7 | async-start | bytes 655360 | tf_op jit(solution)/shard_map/all_to_all | solution.py:894
  146.6 7.6 %sweep.6 = (f32[16,64,256]{2,1,0:T(8,128)}, f32[16,64,256]{2,1,0:T(8,128)}, f32[64,256]{1,0:T(8,128)}, f32[64,256]{1,0:T(8,128)}, f32[16,256]{1,0:T(8,128)}, /*index=5*/f32[16,256]{1,0:T(8,128)}) custom-call(s32[2]{0:T(128)S(1)} %pad_add_fusion.at, f32[64,256]{1,0:T(8,128)S(1)} %collective-permute-done.8.xa, f32[64,256]{1,0:T(8,128)S(1)} %collective-permute-done.9.xb, ...), custom_call_target="tpu_custom_call" | custom-call | flops 6000000 | bytes 8388608 | tf_op jit(solution)/shard_map/sweep/pallas_call | solution.py:694
  154.2 2.6 %step.8 = (f32[128,128]{1,0:T(8,128)}, f32[128,128]{1,0:T(8,128)}, f32[128,128]{1,0:T(8,128)}, f32[1152,128]{1,0:T(8,128)}) custom-call(s32[2]{0:T(128)S(1)} %pad_add_fusion.at, s32[4,8]{1,0:T(4,128)S(1)} %bitcast.67, f32[32,128,128]{2,1,0:T(8,128)S(1)} %bitcast.42, f32[640,128]{1,0:T(8,128)S(1)} %bitcast.48, bf16[128,512]{1,0:T(8,128)(2,1)S(1)} %columns.1.chosen, ...), custom_call_target="tpu_custom_call" | custom-call | flops 1000000 | bytes 1000000 | tf_op jit(solution)/shard_map/step/pallas_call | solution.py:56
  156.8 7.2 %all-to-all-start.8 = ((f32[16,72,128]{2,1,0:T(8,128)}), f32[16,72,128]{2,1,0:T(8,128)S(1)}, u32[]{:S(2)}, u32[]{:S(2)}) async-start(f32[16,72,128]{2,1,0:T(8,128)} %bitcast.74), calls=%async_computation.8 | async-start | bytes 1179648 | tf_op jit(solution)/shard_map/all_to_all | solution.py:912
  164.8 1.9 home.1
  166.7 5.8 %all-to-all-done.8 = f32[16,72,128]{2,1,0:T(8,128)S(1)} async-done(((f32[16,72,128]{2,1,0:T(8,128)}), f32[16,72,128]{2,1,0:T(8,128)S(1)}, u32[]{:S(2)}, u32[]{:S(2)}) %all-to-all-start.8) | async-done | bytes 589856 | tf_op jit(solution)/shard_map/all_to_all | solution.py:912
  172.5 2.2 %step.9 = (f32[128,128]{1,0:T(8,128)}, f32[128,128]{1,0:T(8,128)}, f32[128,128]{1,0:T(8,128)}, f32[16,128]{1,0:T(8,128)}, f32[16,256]{1,0:T(8,128)}, /*index=5*/f32[16,256]{1,0:T(8,128)}) custom-call(s32[2]{0:T(128)S(1)} %pad_add_fusion.at, s32[4,8]{1,0:T(4,128)S(1)} %bitcast.68, f32[32,128,128]{2,1,0:T(8,128)S(1)} %bitcast.43, f32[1152,128]{1,0:T(8,128)S(1)} %bitcast.45, ...), custom_call_target="tpu_custom_call" | custom-call | flops 1000000 | bytes 1000000 | tf_op jit(solution)/shard_map/step/pallas_call | solution.py:56
  174.7 5.4 %all-to-all-start.9 = ((f32[16,1,128]{2,1,0:T(1,128)}), f32[16,1,128]{2,1,0:T(1,128)S(1)}, u32[]{:S(2)}, u32[]{:S(2)}) async-start(f32[16,1,128]{2,1,0:T(1,128)} %bitcast.88), calls=%async_computation.9 | async-start | bytes 16384 | tf_op jit(solution)/shard_map/all_to_all | solution.py:923
  180.1 5.2 %sweep.7 = f32[16,64,256]{2,1,0:T(8,128)} custom-call(s32[2]{0:T(128)S(1)} %pad_add_fusion.at, f32[64,256]{1,0:T(8,128)S(1)} %collective-permute-done.13.xa, f32[64,256]{1,0:T(8,128)S(1)} %collective-permute-done.14.xb, f32[16,256]{1,0:T(8,128)} %get-tuple-element.189.ya, f32[16,256]{1,0:T(8,128)} %get-tuple-element.190.yb, ...), custom_call_target="tpu_custom_call" | custom-call | flops 6000000 | bytes 8388608 | tf_op jit(solution)/shard_map/sweep/pallas_call | solution.py:694
  185.4 0.9 all-to-all-done.9
  186.2 1.6 final.1
  (41 shorter events, 3.3 us)
Async XLA Ops:
  0.7 0.7 copy-start.2
  3.2 19.6 %all-to-all-start = ((f32[128,2,128]{2,1,0:T(2,128)}), f32[128,2,128]{2,1,0:T(2,128)S(1)}, u32[]{:S(2)}, u32[]{:S(2)}) async-start(f32[128,2,128]{2,1,0:T(2,128)} %bitcast.80), calls=%async_computation | async-start | bytes 262144 | tf_op jit(solution)/shard_map/all_to_all | solution.py:782
  13.4 9.4 %copy-start.1 = (f32[1024]{0:T(1024)S(1)}, f32[1024]{0:T(1024)}, u32[]{:S(2)}) copy-start(f32[1024]{0:T(1024)} %param.23) | copy-start | bytes 12292
  13.4 9.4 %copy-start.3 = (s32[8,4]{0,1:T(4,128)S(1)}, s32[8,4]{0,1:T(4,128)}, u32[]{:S(2)}) copy-start(s32[8,4]{0,1:T(4,128)} %param.22) | copy-start | bytes 388
  13.5 9.4 %copy-start.4 = (f32[1024]{0:T(1024)S(1)}, f32[1024]{0:T(1024)}, u32[]{:S(2)}) copy-start(f32[1024]{0:T(1024)} %param.24) | copy-start | bytes 12292
  15.3 13.4 %collective-permute-start.2 = (f32[32,256]{1,0:T(8,128)}, f32[32,256]{1,0:T(8,128)S(1)}, u32[]{:S(2)}, u32[]{:S(2)}) collective-permute-start(f32[32,256]{1,0:T(8,128)} %get-tuple-element.108), channel_id=1, source_target_pairs={{0,1},{2,3},{4,5},{6,7},{8,9},{10,11},{12,13},{14,15},{1,0},{3,2},... | collective-permute-start | bytes 98312 | tf_op jit(solution)/shard_map/ppermute | solution.py:714
  16.9 11.9 %collective-permute-start.3 = (f32[32,256]{1,0:T(8,128)}, f32[32,256]{1,0:T(8,128)S(1)}, u32[]{:S(2)}, u32[]{:S(2)}) collective-permute-start(f32[32,256]{1,0:T(8,128)} %get-tuple-element.109), channel_id=1, source_target_pairs={{1,2},{3,4},{5,6},{7,8},{9,10},{11,12},{13,14},{2,1},{4,3},{6,5},{... | collective-permute-start | bytes 98312 | tf_op jit(solution)/shard_map/ppermute | solution.py:714
  20.7 8.1 %collective-permute-start = (f32[128,256]{1,0:T(8,128)}, f32[128,256]{1,0:T(8,128)S(1)}, u32[]{:S(2)}, u32[]{:S(2)}) collective-permute-start(f32[128,256]{1,0:T(8,128)} %get-tuple-element.106), channel_id=1, source_target_pairs={{0,16},{32,48},{64,80},{96,112},{16,0},{48,32},{80,64},{112,96},{1... | collective-permute-start | bytes 393224 | tf_op jit(solution)/shard_map/ppermute | solution.py:714
  20.8 8.0 %collective-permute-start.1 = (f32[128,256]{1,0:T(8,128)}, f32[128,256]{1,0:T(8,128)S(1)}, u32[]{:S(2)}, u32[]{:S(2)}) collective-permute-start(f32[128,256]{1,0:T(8,128)} %get-tuple-element.107), channel_id=1, source_target_pairs={{16,32},{48,64},{80,96},{32,16},{64,48},{96,80},{17,33},{49,65},{8... | collective-permute-start | bytes 393224 | tf_op jit(solution)/shard_map/ppermute | solution.py:714
  28.8 19.0 %all-to-all-start.1 = ((f32[128,2,128]{2,1,0:T(2,128)}), f32[128,2,128]{2,1,0:T(2,128)S(1)}, u32[]{:S(2)}, u32[]{:S(2)}) async-start(f32[128,2,128]{2,1,0:T(2,128)} %bitcast.79), calls=%async_computation.1 | async-start | bytes 262144 | tf_op jit(solution)/shard_map/all_to_all | solution.py:805
  48.5 23.0 %all-to-all-start.2 = ((f32[128,2,128]{2,1,0:T(2,128)}), f32[128,2,128]{2,1,0:T(2,128)S(1)}, u32[]{:S(2)}, u32[]{:S(2)}) async-start(f32[128,2,128]{2,1,0:T(2,128)} %bitcast.76), calls=%async_computation.2 | async-start | bytes 262144 | tf_op jit(solution)/shard_map/all_to_all | solution.py:813
  55.5 10.4 %collective-permute-start.4 = (f32[64,256]{1,0:T(8,128)}, f32[64,256]{1,0:T(8,128)S(1)}, u32[]{:S(2)}, u32[]{:S(2)}) collective-permute-start(f32[64,256]{1,0:T(8,128)} %get-tuple-element.120), channel_id=1, source_target_pairs={{0,16},{32,48},{64,80},{96,112},{16,0},{48,32},{80,64},{112,96},{1... | collective-permute-start | bytes 196616 | tf_op jit(solution)/shard_map/ppermute | solution.py:714
  55.7 10.2 %collective-permute-start.5 = (f32[64,256]{1,0:T(8,128)}, f32[64,256]{1,0:T(8,128)S(1)}, u32[]{:S(2)}, u32[]{:S(2)}) collective-permute-start(f32[64,256]{1,0:T(8,128)} %get-tuple-element.121), channel_id=1, source_target_pairs={{16,32},{48,64},{80,96},{32,16},{64,48},{96,80},{17,33},{49,65},{8... | collective-permute-start | bytes 196616 | tf_op jit(solution)/shard_map/ppermute | solution.py:714
  56.4 5.4 %collective-permute-start.6 = (f32[16,256]{1,0:T(8,128)}, f32[16,256]{1,0:T(8,128)S(1)}, u32[]{:S(2)}, u32[]{:S(2)}) collective-permute-start(f32[16,256]{1,0:T(8,128)} %get-tuple-element.122), channel_id=1, source_target_pairs={{0,1},{2,3},{4,5},{6,7},{8,9},{10,11},{12,13},{14,15},{1,0},{3,2},... | collective-permute-start | bytes 49160 | tf_op jit(solution)/shard_map/ppermute | solution.py:714
  58.0 7.9 %collective-permute-start.7 = (f32[16,256]{1,0:T(8,128)}, f32[16,256]{1,0:T(8,128)S(1)}, u32[]{:S(2)}, u32[]{:S(2)}) collective-permute-start(f32[16,256]{1,0:T(8,128)} %get-tuple-element.123), channel_id=1, source_target_pairs={{1,2},{3,4},{5,6},{7,8},{9,10},{11,12},{13,14},{2,1},{4,3},{6,5},{... | collective-permute-start | bytes 49160 | tf_op jit(solution)/shard_map/ppermute | solution.py:714
  65.9 5.5 %copy-start = (f32[8,4,128,128]{3,2,1,0:T(8,128)S(1)}, f32[8,4,128,128]{3,2,1,0:T(8,128)}, u32[]{:S(2)}) copy-start(f32[8,4,128,128]{3,2,1,0:T(8,128)} %param.21) | copy-start | bytes 6291460
  73.2 15.2 %all-to-all-start.3 = ((f32[16,40,128]{2,1,0:T(8,128)}), f32[16,40,128]{2,1,0:T(8,128)S(1)}, u32[]{:S(2)}, u32[]{:S(2)}) async-start(f32[16,40,128]{2,1,0:T(8,128)} %bitcast.78), calls=%async_computation.3 | async-start | bytes 655360 | tf_op jit(solution)/shard_map/all_to_all | solution.py:836
  84.8 22.3 %copy-start.6 = (f32[64,256]{1,0:T(8,128)S(1)}, f32[64,256]{1,0:T(8,128)}, u32[]{:S(2)}) copy-start(f32[64,256]{1,0:T(8,128)} %get-tuple-element.143) | copy-start | bytes 196612
  84.8 22.4 %copy-start.5 = (f32[64,256]{1,0:T(8,128)S(1)}, f32[64,256]{1,0:T(8,128)}, u32[]{:S(2)}) copy-start(f32[64,256]{1,0:T(8,128)} %get-tuple-element.144) | copy-start | bytes 196612
  88.4 10.8 %all-to-all-start.4 = ((f32[8,32,128]{2,1,0:T(8,128)}), f32[8,32,128]{2,1,0:T(8,128)S(1)}, u32[]{:S(2)}, u32[]{:S(2)}) async-start(f32[8,32,128]{2,1,0:T(8,128)} %bitcast.81), calls=%async_computation.4 | async-start | bytes 262144 | tf_op jit(solution)/shard_map/all_to_all | solution.py:848
  101.8 14.5 %all-to-all-start.5 = ((f32[16,64,128]{2,1,0:T(8,128)}), f32[16,64,128]{2,1,0:T(8,128)S(1)}, u32[]{:S(2)}, u32[]{:S(2)}) async-start(f32[16,64,128]{2,1,0:T(8,128)} %bitcast.75), calls=%async_computation.5 | async-start | bytes 1048576 | tf_op jit(solution)/shard_map/all_to_all | solution.py:879
  107.1 1.3 collective-permute-start.8
  107.2 1.2 collective-permute-start.9
  118.8 18.0 %all-to-all-start.6 = ((f32[16,72,128]{2,1,0:T(8,128)}), f32[16,72,128]{2,1,0:T(8,128)S(1)}, u32[]{:S(2)}, u32[]{:S(2)}) async-start(f32[16,72,128]{2,1,0:T(8,128)} %bitcast.73), calls=%async_computation.6 | async-start | bytes 1179648 | tf_op jit(solution)/shard_map/all_to_all | solution.py:884
  124.9 1.4 collective-permute-start.10
  127.0 3.7 %collective-permute-start.11 = (f32[32,128]{1,0:T(8,128)S(1)}, f32[32,128]{1,0:T(8,128)S(1)}, u32[]{:S(2)}, u32[]{:S(2)}) collective-permute-start(f32[32,128]{1,0:T(8,128)S(1)} %pad_maximum_fusion.1), channel_id=1, source_target_pairs={{0,32},{16,48},{32,0},{48,16},{64,96},{80,112},{96,64},{112,80},{1... | collective-permute-start | bytes 49160 | tf_op jit(solution)/shard_map/ppermute | solution.py:888
  131.4 5.4 %collective-permute-start.12 = (f32[64,128]{1,0:T(8,128)S(1)}, f32[64,128]{1,0:T(8,128)S(1)}, u32[]{:S(2)}, u32[]{:S(2)}) collective-permute-start(f32[64,128]{1,0:T(8,128)S(1)} %pad_maximum_fusion), channel_id=1, source_target_pairs={{0,64},{16,80},{32,96},{48,112},{64,0},{80,16},{96,32},{112,48},{1... | collective-permute-start | bytes 98312 | tf_op jit(solution)/shard_map/ppermute | solution.py:888
  139.3 14.9 %all-to-all-start.7 = ((f32[16,40,128]{2,1,0:T(8,128)}), f32[16,40,128]{2,1,0:T(8,128)S(1)}, u32[]{:S(2)}, u32[]{:S(2)}) async-start(f32[16,40,128]{2,1,0:T(8,128)} %bitcast.77), calls=%async_computation.7 | async-start | bytes 655360 | tf_op jit(solution)/shard_map/all_to_all | solution.py:894
  154.2 9.9 %copy-start.8 = (f32[64,256]{1,0:T(8,128)S(1)}, f32[64,256]{1,0:T(8,128)}, u32[]{:S(2)}) copy-start(f32[64,256]{1,0:T(8,128)} %get-tuple-element.181) | copy-start | bytes 196612
  154.2 10.0 %copy-start.7 = (f32[64,256]{1,0:T(8,128)S(1)}, f32[64,256]{1,0:T(8,128)}, u32[]{:S(2)}) copy-start(f32[64,256]{1,0:T(8,128)} %get-tuple-element.182) | copy-start | bytes 196612
  156.8 15.7 %all-to-all-start.8 = ((f32[16,72,128]{2,1,0:T(8,128)}), f32[16,72,128]{2,1,0:T(8,128)S(1)}, u32[]{:S(2)}, u32[]{:S(2)}) async-start(f32[16,72,128]{2,1,0:T(8,128)} %bitcast.74), calls=%async_computation.8 | async-start | bytes 1179648 | tf_op jit(solution)/shard_map/all_to_all | solution.py:912
  164.1 2.6 %collective-permute-start.13 = (f32[64,256]{1,0:T(8,128)S(1)}, f32[64,256]{1,0:T(8,128)S(1)}, u32[]{:S(2)}, u32[]{:S(2)}) collective-permute-start(f32[64,256]{1,0:T(8,128)S(1)} %copy-done.8), channel_id=1, source_target_pairs={{0,16},{32,48},{64,80},{96,112},{16,0},{48,32},{80,64},{112,96},{1... | collective-permute-start | bytes 196616 | tf_op jit(solution)/shard_map/ppermute | solution.py:714
  164.2 2.5 %collective-permute-start.14 = (f32[64,256]{1,0:T(8,128)S(1)}, f32[64,256]{1,0:T(8,128)S(1)}, u32[]{:S(2)}, u32[]{:S(2)}) collective-permute-start(f32[64,256]{1,0:T(8,128)S(1)} %copy-done.7), channel_id=1, source_target_pairs={{16,32},{48,64},{80,96},{32,16},{64,48},{96,80},{17,33},{49,65},{8... | collective-permute-start | bytes 196616 | tf_op jit(solution)/shard_map/ppermute | solution.py:714
  174.7 11.5 %all-to-all-start.9 = ((f32[16,1,128]{2,1,0:T(1,128)}), f32[16,1,128]{2,1,0:T(1,128)S(1)}, u32[]{:S(2)}, u32[]{:S(2)}) async-start(f32[16,1,128]{2,1,0:T(1,128)} %bitcast.88), calls=%async_computation.9 | async-start | bytes 16384 | tf_op jit(solution)/shard_map/all_to_all | solution.py:923

commit v6 on v5

--- a/solution.py
+++ b/solution.py
@@ -202,6 +202,11 @@
     for copy in copies:
         copy.wait()
     gathered[...] = pick_rounded(chosen, pressure[...])
+    return at_depth(message, gathered)
+
+
+def at_depth(message, gathered):
+    depth = gathered.shape[1]
     lane = iota((LANES, LANES), 1)
     out = jnp.zeros((LANES, LANES), F32)
     for k in range(CAP):
@@ -322,11 +327,10 @@
     return out[:, :depth] + out[:, depth:]
 
 
-def second_body(pressure_all, message, trace, trace_out, send, gathered, pressure, here, change):
-    message = message[...]
-    now = traces(message, pressure_all, pressure, here, gathered)
+def second_traces(message, trace, gathered, trace_out, send):
+    now = at_depth(message, gathered)
     trace_out[...] = now
-    change[...] = onto_fracture(message, kappa_of(message) * (now - trace[...]))[0]
+    [change] = onto_fracture(message, kappa_of(message) * (now - trace))
     mats = CAP
     each = LANES // mats
     for m in range(mats):
@@ -424,7 +428,7 @@
     mats = rows
     extra = list(rest)
     change = extra.pop(0) if ride == "reduce" else None
-    parts = [extra.pop(0) for _ in range(3)] if ride == "next" else None
+    parts = [extra.pop(0) for _ in range(mats // 2)] if ride == "next" else None
     x, r, d = (extra.pop(0) for _ in range(3))
     if ride == "next":
         parts.insert(0, extra.pop(0))
@@ -558,15 +562,37 @@
 
 
 def sweep_body(
-    at, xa, xb, ya, yb, cxa, cxb, cya, cyb, p, p_after, trans, cell, rhs, *rest, first, last, fluxes, y_in, y_out
+    at,
+    xa,
+    xb,
+    ya,
+    yb,
+    cxa,
+    cxb,
+    cya,
+    cyb,
+    p,
+    p_after,
+    trans,
+    rhs,
+    *rest,
+    first,
+    last,
+    fluxes,
+    gather,
+    y_in,
+    y_out,
 ):
     rest = list(rest)
+    cell = rest.pop(0) if first else None
     weight = None if first else rest.pop(0)
-    if fluxes:
-        got, values = rest.pop(0), [rest.pop(0) for _ in range(fluxes)]
+    if fluxes or gather:
+        got, values = rest.pop(0), [rest.pop(0) for _ in range(fluxes + gather)]
     out = rest.pop(0)
     weight_out = rest.pop(0) if first else None
     rhs_out = rest.pop(0) if fluxes else None
+    trace_out, cuts = (rest.pop(0), rest.pop(0)) if gather else (None, None)
+    gathered = rest.pop() if gather else None
     if fluxes:
         found, spread, cell_row = rest.pop(), rest.pop(), rest.pop()
     carry_t = rest.pop() if first else None
@@ -588,7 +614,7 @@
             flux = values[0][...] - at_mortar(message, values[1][...])
             spread_flux(message, kappa_of(message) * flux, spread, cell_row, nz)
         tx_low = jnp.where(x_even, cxb[ny:, :], cxa[ny:, :])
-        carry[...] = tx_low * (jnp.where(x_even, xb[:ny, :], xa[:ny, :]) - p[0])
+        carry[...] = tx_low * jnp.where(x_even, xb[:ny, :], xa[:ny, :])
         if first:
             carry_t[...] = tx_low
 
@@ -613,13 +639,10 @@
             y_low, y_high = jnp.where(y_even, y_high, y_low), jnp.where(y_even, y_low, y_high)
         ty_edge = jnp.where(y_even, cyb[edge, :], cya[edge, :])
         tx, ty, tz = trans[0, i], trans[1, i], trans[2, i]
-        fx = tx * (here - after)
         y_next = jnp.where(row == ny - 1, y_high, pltpu.roll(here, ny - 1, 0))
-        fy = ty * (here - y_next)
-        fy_low = jnp.where(row == 0, ty_edge * (y_low - here[:1]), pltpu.roll(fy, 1, 0))
+        y_prev = jnp.where(row == 0, ty_edge * y_low, pltpu.roll(ty * here, 1, 0))
         z_next = jnp.where(lane == nz - 1, 0.0, pltpu.roll(here, nz - 1, 1))
-        fz = tz * (here - z_next)
-        fz_low = jnp.where(lane == 0, 0.0, pltpu.roll(fz, 1, 1))
+        z_prev = jnp.where(lane == 0, 0.0, pltpu.roll(tz * here, 1, 1))
         if first:
             ty_before = jnp.where(row == 0, ty_edge, pltpu.roll(ty, 1, 0))
             tz_before = jnp.where(lane == 0, 0.0, pltpu.roll(tz, 1, 1))
@@ -629,9 +652,30 @@
             carry_t[...] = tx
         else:
             w = weight[i]
-        applied = cell[i] * here + fx - carry[...] + fy - fy_low + fz - fz_low
-        carry[...] = fx
-        out[i] = here + w * (right - applied)
+        around = (tx * after + carry[...]) + (ty * y_next + y_prev) + (tz * z_next + z_prev)
+        carry[...] = tx * here
+        out[i] = (1.0 - WEIGHT) * here + w * (right + around)
+    if gather:
+        message = got[...]
+        rows = iota((LANES, many * ny), 1) + step * (many * ny)
+        chosen = jnp.concatenate(
+            [ones_where(rows == by_slot(message, k)[0]) for k in range(CAP)], axis=0
+        )
+        planes = jnp.concatenate([out[i] for i in range(many)], axis=0)
+        found = pick_rounded(chosen, planes)
+
+        @pl.when(step == 0)
+        def _():
+            gathered[...] = found
+
+        @pl.when(step > 0)
+        def _():
+            gathered[...] += found
+
+        @pl.when(step == steps - 1)
+        def _():
+            second_traces(message, values[0][...], gathered, trace_out, cuts)
+
     if last:
         return
     xa_out, xb_out, ya_out, yb_out = rest
@@ -662,7 +706,23 @@
         yb_out[one, :] = high
 
 
-def sweep(at, p, halo, faces, trans, cell, rhs, weight=None, last=False, got=None, values=(), y_in=False, y_out=False, many=4):
+def sweep(
+    at,
+    p,
+    halo,
+    faces,
+    trans,
+    rhs,
+    cell=None,
+    weight=None,
+    last=False,
+    got=None,
+    values=(),
+    gather=False,
+    y_in=False,
+    y_out=False,
+    many=4,
+):
     nx, ny, nz = p.shape
     part = pl.BlockSpec((many, ny, nz), lambda i: (i, 0, 0))
     x_face = pl.BlockSpec((ny, nz), lambda i: (0, 0))
@@ -673,7 +733,11 @@
         out_shape.append(shape(nx, ny, nz))
         out_specs.append(part)
     scratch = [pltpu.VMEM((ny, nz), F32)] * (2 if first else 1)
-    if values:
+    if gather:
+        out_shape += [sent(LANES, LANES), sent(2 * LANES, LANES)]
+        out_specs += [whole((LANES, LANES)), whole((2 * LANES, LANES))]
+        scratch.append(pltpu.VMEM((CAP * LANES, nz), F32))
+    elif values:
         out_shape.append(shape(nx, ny, nz))
         out_specs.append(part)
         scratch += [
@@ -689,17 +753,24 @@
     )
     if y_in:
         halo = (*halo[:2], *(in_hbm(v, 1) for v in halo[2:]))
-    operands = [*halo, *faces, p, p, trans, cell, rhs] + ([] if first else [weight])
+    operands = [*halo, *faces, p, p, trans, rhs, cell if first else weight]
     operands += [in_hbm(v, 1) for v in (got, *values)] if values else []
     return pl.pallas_call(
-        functools.partial(sweep_body, first=first, last=last, fluxes=len(values), y_in=y_in, y_out=y_out),
+        functools.partial(
+            sweep_body,
+            first=first,
+            last=last,
+            fluxes=0 if gather else len(values),
+            gather=gather,
+            y_in=y_in,
+            y_out=y_out,
+        ),
         grid=(nx // many,),
         out_shape=tuple(out_shape),
         in_specs=[SMEM]
         + [whole(v.shape) for v in (*halo, *faces)]
         + [part, after]
         + [pl.BlockSpec((3, many, ny, nz), lambda i: (0, i, 0, 0)), part, part]
-        + ([] if first else [part])
         + ([whole(v.shape) for v in (got, *values)] if values else []),
         out_specs=tuple(out_specs),
         scratch_shapes=scratch,
@@ -804,7 +875,7 @@
     send, *faces = lax.optimization_barrier((send, *faces))
     reduced = everyone(send)
     pressure, weight, rhs, *sides = sweep(
-        at, pressure_start, faces, faces, face_trans, cell_coef, matrix_source, got=message, values=(flux,)
+        at, pressure_start, faces, faces, face_trans, matrix_source, cell_coef, got=message, values=(flux,)
     )
     sides = swapped(*sides, mats, shards)
 
@@ -817,10 +888,6 @@
         got,
         name="columns",
     )
-    pressure, *sides = sweep(
-        at, pressure, sides, faces, face_trans, cell_coef, rhs, weight, y_out=True
-    )
-
     r, sums, send = call(
         start_body,
         (*[sent(LANES, LANES)] * 2, sent(shards * size, LANES)),
@@ -832,16 +899,20 @@
         name="start",
     )
     x, d = x_start, r
-    send, pressure = lax.optimization_barrier((send, pressure))
+    send, pressure, *sides = lax.optimization_barrier((send, pressure, *sides))
     arrived = over_frac(send)
-    trace, change = call(
-        second_body,
-        (sent(LANES, LANES), sent(2 * LANES, LANES)),
-        side=(message, trace),
-        raw=(pressure.reshape(flat),),
-        scratch=[gathered, *fetch_scratch, square_scratch],
-        flops=2e9,
-        name="second",
+    pressure, trace, change, *sides = sweep(
+        at,
+        pressure,
+        sides,
+        faces,
+        face_trans,
+        rhs,
+        weight=weight,
+        got=message,
+        values=(trace,),
+        gather=True,
+        y_out=True,
     )
 
     arrived, change = lax.optimization_barrier((arrived, change))
@@ -882,10 +953,10 @@
 
     x, r, d, send, change, home = step(arrived, x, r, d, ride="gather", faces=sides[2:])
     arrived = over_frac(send)
-    parts = [change]
-    for hop in (1, 2, 4):
-        mine = jnp.concatenate(parts, axis=0) if hop > 1 else change
-        parts.append(lax.ppermute(mine, "mat", [(i, i ^ hop) for i in range(mats)]))
+    parts = [change, lax.ppermute(change, "mat", [(i, i ^ 1) for i in range(mats)])]
+    pair = jnp.concatenate(parts, axis=0)
+    for hop in range(2, mats, 2):
+        parts.append(lax.ppermute(pair, "mat", [(i, i ^ hop) for i in range(mats)]))
 
     x, r, d, send, *y_sides = step(
         arrived, x, r, d, *parts[1:], faces_in=True, ride="next", side=(change, x_start, sums)
@@ -898,9 +969,8 @@
         (*x_sides, *y_sides),
         faces,
         face_trans,
-        cell_coef,
         matrix_source,
-        weight,
+        weight=weight,
         got=message,
         values=(trace, x_flux),
         y_in=True,
@@ -927,9 +997,8 @@
         (*x_sides, *y_sides),
         faces,
         face_trans,
-        cell_coef,
         rhs,
-        weight,
+        weight=weight,
         last=True,
         y_in=True,
     )

time: 191 us -> 183 us (0.958)
  waiting for transfers between devices: 41.7 us -> 32.6 us
  starting transfers between devices: 85 us -> 89 us
  Pallas kernels: 58 us -> 55.4 us
    ppermute x3 -> x4, waiting for transfers between devices: 8.92 us -> 2.99 us  [the longest x3 2.32 us: body(): parts.append(lax.ppermute(pair, 'mat', [(i, i ^ hop) for i in range(mats)]))]
    pallas_call x13 -> x12, Pallas kernels: 31.3 us -> 26.3 us  [call(): pl.pallas_call(body, grid=(1,), out_shape=outs, in_specs=[SMEM] * len(sca...]
    ppermute x12, waiting for transfers between devices: 4.73 us -> 0.59 us  [swap(): return lax.ppermute(v, axis, pairs + [(b, a) for a, b in pairs])]
    all_to_all x1, waiting for transfers between devices: 0.01 us -> 3.06 us  [body(): residuals = everyone(send)]
    ppermute x3 -> x4, starting transfers between devices: 1.61 us -> 4.1 us  [the longest x3 4.09 us: body(): parts.append(lax.ppermute(pair, 'mat', [(i, i ^ hop) for i in range(mats)]))]
    pallas_call x4, Pallas kernels: 24.9 us -> 27.3 us  [sweep(): pl.pallas_call(functools.partial(sweep_body, first=first, last=last, flux...]
  transfers between devices with their start and end apart: 25 -> 26, of which waited for: 12 -> 13; matrix products, arithmetic and copies ran while one was open for 1% -> 0% of each run, Pallas kernels for 21% -> 22%
where the time goes in v6:
time: 183 us; the launch traced here: 179 us
  starting transfers between devices  89 us (49%)
  Pallas kernels  55.4 us (30%)
  waiting for transfers between devices  32.6 us (18%)
    all_to_all x6, starting transfers between devices, body(): arrived = over_frac(send)  38 us
    pallas_call x4, Pallas kernels, sweep(): pl.pallas_call(functools.partial(sweep_body, first=first, last=last, flux...  27.3 us
    pallas_call x12, Pallas kernels, call(): pl.pallas_call(body, grid=(1,), out_shape=outs, in_specs=[SMEM] * len(sca...  26.3 us
    all_to_all x6, waiting for transfers between devices, body(): arrived = over_frac(send)  16.2 us
    ppermute x12, starting transfers between devices, swap(): return lax.ppermute(v, axis, pairs + [(b, a) for a, b in pairs])  13.8 us
    all_to_all x1, starting transfers between devices, body(): got = everyone(send)  10.2 us
    all_to_all x1, starting transfers between devices, body(): reduced = everyone(send)  9.68 us
    all_to_all x1, starting transfers between devices, body(): residuals = everyone(send)  7.24 us
  transfers between devices with their start and end apart: 26, of which 13 were waited for; matrix products, arithmetic and copies ran while one was open for 0% of the time, Pallas kernels for 22%

profile of v6, /device:TPU:32, one launch (start us, length us, event | category | flops | bytes accessed | tf_op | source)
XLA Modules:
  0.0 179.5 jit_solution(13149756202849781672)
XLA Ops:
  0.7 0.7 copy-done.2
  1.4 1.8 %pack.1 = (f32[256,128]{1,0:T(8,128)}, s32[1,512]{1,0:T(1,128)}) custom-call(s32[2]{0:T(128)S(1)} %pad_add_fusion.at, s32[4,8]{1,0:T(4,128)S(1)} %bitcast.60, s32[1,512]{1,0:T(1,128)} %bitcast.80, s32[1,512]{1,0:T(1,128)} %bitcast.90, s32[1,512]{1,0:T(1,128)} %bitcast.82, f32[1,512]{1,0:T(1,128)} %bitcast.84, f32[8,128]{1,0:T(8,128)} %bitcast.88), custom_call_target="tpu_custom_call" | custom-call | flops 1000000 | bytes 1000000 | tf_op jit(solution)/shard_map/pack/pallas_call | solution.py:56
  3.2 10.2 %all-to-all-start = ((f32[128,2,128]{2,1,0:T(2,128)}), f32[128,2,128]{2,1,0:T(2,128)S(1)}, u32[]{:S(2)}, u32[]{:S(2)}) async-start(f32[128,2,128]{2,1,0:T(2,128)} %bitcast.78), calls=%async_computation | async-start | bytes 262144 | tf_op jit(solution)/shard_map/all_to_all | solution.py:853
  13.5 1.9 %edges.1 = (f32[128,256]{1,0:T(8,128)}, f32[128,256]{1,0:T(8,128)}, f32[32,256]{1,0:T(8,128)}, f32[32,256]{1,0:T(8,128)}) custom-call(s32[2]{0:T(128)S(1)} %pad_add_fusion.at, f32[16,64,256]{2,1,0:T(8,128)} %p_after.1, f32[16,64,256]{2,1,0:T(8,128)} %p_after.1, f32[16,64,256]{2,1,0:T(8,128)} %p_after.1, f32[16,64,256]{2,1,0:T(8,128)} %p_after.1, ...), custom_call_target="tpu_custom_call" | custom-call | tf_op jit(solution)/shard_map/edges/pallas_call | solution.py:545
  15.3 1.5 collective-permute-start.2
  16.9 3.8 %collective-permute-start.3 = (f32[32,256]{1,0:T(8,128)}, f32[32,256]{1,0:T(8,128)S(1)}, u32[]{:S(2)}, u32[]{:S(2)}) collective-permute-start(f32[32,256]{1,0:T(8,128)} %get-tuple-element.113), channel_id=1, source_target_pairs={{1,2},{3,4},{5,6},{7,8},{9,10},{11,12},{13,14},{2,1},{4,3},{6,5},{... | collective-permute-start | bytes 98312 | tf_op jit(solution)/shard_map/ppermute | solution.py:785
  20.8 0.7 collective-permute-start.1
  21.4 1.4 all-to-all-done
  22.8 5.9 %first.1 = (f32[256,128]{1,0:T(8,128)}, f32[128,128]{1,0:T(8,128)}, f32[128,128]{1,0:T(8,128)}, f32[128,128]{1,0:T(8,128)}, f32[128,128]{1,0:T(8,128)}) custom-call(s32[2]{0:T(128)S(1)} %pad_add_fusion.at, s32[4,8]{1,0:T(4,128)S(1)} %bitcast.61, f32[32,128,128]{2,1,0:T(8,128)} %bitcast.36, f32[1024,256]{1,0:T(8,128)} %bitcast.70, f32[256,128]{1,0:T(8,128)S(1)} %bitcast.50, ...), custom_call_target="tpu_custom_call" | custom-call | flops 2000000000 | bytes 1000000 | tf_op jit(solution)/shard_map/first/pallas_call | solution.py:56
  28.8 9.7 %all-to-all-start.1 = ((f32[128,2,128]{2,1,0:T(2,128)}), f32[128,2,128]{2,1,0:T(2,128)S(1)}, u32[]{:S(2)}, u32[]{:S(2)}) async-start(f32[128,2,128]{2,1,0:T(2,128)} %bitcast.77), calls=%async_computation.1 | async-start | bytes 262144 | tf_op jit(solution)/shard_map/all_to_all | solution.py:876
  38.5 6.8 %sweep.4 = (f32[16,64,256]{2,1,0:T(8,128)}, f32[16,64,256]{2,1,0:T(8,128)}, f32[16,64,256]{2,1,0:T(8,128)}, f32[64,256]{1,0:T(8,128)}, f32[64,256]{1,0:T(8,128)}, /*index=5*/f32[16,256]{1,0:T(8,128)}, f32[16,256]{1,0:T(8,128)}) custom-call(s32[2]{0:T(128)S(1)} %pad_add_fusion.at, f32[128,256]{1,0:T(8,128)S(1)} %collective-permute-done.xa.cxa, ...), custom_call_target="tpu_custom_call" | custom-call | flops 6000000 | bytes 8388608 | tf_op jit(solution)/shard_map/sweep/pallas_call | solution.py:758
  45.3 2.5 %all-to-all-done.1 = f32[128,2,128]{2,1,0:T(2,128)S(1)} async-done(((f32[128,2,128]{2,1,0:T(2,128)}), f32[128,2,128]{2,1,0:T(2,128)S(1)}, u32[]{:S(2)}, u32[]{:S(2)}) %all-to-all-start.1) | async-done | bytes 131104 | tf_op jit(solution)/shard_map/all_to_all | solution.py:876
  47.8 0.7 sums.1
  48.5 7.2 %all-to-all-start.2 = ((f32[128,2,128]{2,1,0:T(2,128)}), f32[128,2,128]{2,1,0:T(2,128)S(1)}, u32[]{:S(2)}, u32[]{:S(2)}) async-start(f32[128,2,128]{2,1,0:T(2,128)} %bitcast.74), calls=%async_computation.2 | async-start | bytes 262144 | tf_op jit(solution)/shard_map/all_to_all | solution.py:884
  56.6 1.6 collective-permute-start.6
  58.2 3.8 %collective-permute-start.7 = (f32[16,256]{1,0:T(8,128)}, f32[16,256]{1,0:T(8,128)S(1)}, u32[]{:S(2)}, u32[]{:S(2)}) collective-permute-start(f32[16,256]{1,0:T(8,128)} %get-tuple-element.128), channel_id=1, source_target_pairs={{1,2},{3,4},{5,6},{7,8},{9,10},{11,12},{13,14},{2,1},{4,3},{6,5},{... | collective-permute-start | bytes 49160 | tf_op jit(solution)/shard_map/ppermute | solution.py:785
  62.0 3.1 %all-to-all-done.2 = f32[128,2,128]{2,1,0:T(2,128)S(1)} async-done(((f32[128,2,128]{2,1,0:T(2,128)}), f32[128,2,128]{2,1,0:T(2,128)S(1)}, u32[]{:S(2)}, u32[]{:S(2)}) %all-to-all-start.2) | async-done | bytes 131104 | tf_op jit(solution)/shard_map/all_to_all | solution.py:884
  65.1 1.7 start.1
  66.8 6.1 %all-to-all-start.3 = ((f32[16,40,128]{2,1,0:T(8,128)}), f32[16,40,128]{2,1,0:T(8,128)S(1)}, u32[]{:S(2)}, u32[]{:S(2)}) async-start(f32[16,40,128]{2,1,0:T(8,128)} %bitcast.75), calls=%async_computation.3 | async-start | bytes 655360 | tf_op jit(solution)/shard_map/all_to_all | solution.py:903
  72.8 8.2 %sweep.5 = (f32[16,64,256]{2,1,0:T(8,128)}, f32[128,128]{1,0:T(8,128)}, f32[256,128]{1,0:T(8,128)}, f32[64,256]{1,0:T(8,128)}, f32[64,256]{1,0:T(8,128)}, /*index=5*/f32[16,256]{1,0:T(8,128)}, f32[16,256]{1,0:T(8,128)}) custom-call(s32[2]{0:T(128)S(1)} %pad_add_fusion.at, f32[64,256]{1,0:T(8,128)S(1)} %collective-permute-done.4.xa, ...), custom_call_target="tpu_custom_call" | custom-call | flops 6000000 | bytes 8388608 | tf_op jit(solution)/shard_map/sweep/pallas_call | solution.py:758
  81.4 5.9 %all-to-all-start.4 = ((f32[8,32,128]{2,1,0:T(8,128)}), f32[8,32,128]{2,1,0:T(8,128)S(1)}, u32[]{:S(2)}, u32[]{:S(2)}) async-start(f32[8,32,128]{2,1,0:T(8,128)} %bitcast.79), calls=%async_computation.4 | async-start | bytes 262144 | tf_op jit(solution)/shard_map/all_to_all | solution.py:919
  87.5 5.9 %all-to-all-done.4 = f32[8,32,128]{2,1,0:T(8,128)S(1)} async-done(((f32[8,32,128]{2,1,0:T(8,128)}), f32[8,32,128]{2,1,0:T(8,128)S(1)}, u32[]{:S(2)}, u32[]{:S(2)}) %all-to-all-start.4) | async-done | bytes 131104 | tf_op jit(solution)/shard_map/all_to_all | solution.py:919
  93.4 2.6 %step.5 = (f32[128,128]{1,0:T(8,128)}, f32[128,128]{1,0:T(8,128)}, f32[128,128]{1,0:T(8,128)}, f32[1024,128]{1,0:T(8,128)}) custom-call(s32[2]{0:T(128)S(1)} %pad_add_fusion.at, s32[4,8]{1,0:T(4,128)S(1)} %bitcast.63, f32[32,128,128]{2,1,0:T(8,128)S(1)} %bitcast.38, f32[640,128]{1,0:T(8,128)S(1)} %bitcast.46, bf16[128,512]{1,0:T(8,128)(2,1)S(1)} %columns.1.chosen, ...), custom_call_target="tpu_custom_call" | custom-call | flops 1000000 | bytes 1000000 | tf_op jit(solution)/shard_map/step/pallas_call | solution.py:56
  96.0 7.2 %all-to-all-start.5 = ((f32[16,64,128]{2,1,0:T(8,128)}), f32[16,64,128]{2,1,0:T(8,128)S(1)}, u32[]{:S(2)}, u32[]{:S(2)}) async-start(f32[16,64,128]{2,1,0:T(8,128)} %bitcast.73), calls=%async_computation.5 | async-start | bytes 1048576 | tf_op jit(solution)/shard_map/all_to_all | solution.py:950
  103.4 0.7 collective-permute-start.9
  104.6 7.5 %all-to-all-done.5 = f32[16,64,128]{2,1,0:T(8,128)S(1)} async-done(((f32[16,64,128]{2,1,0:T(8,128)}), f32[16,64,128]{2,1,0:T(8,128)S(1)}, u32[]{:S(2)}, u32[]{:S(2)}) %all-to-all-start.5) | async-done | bytes 524320 | tf_op jit(solution)/shard_map/all_to_all | solution.py:950
  112.0 2.6 %step.6 = (f32[128,128]{1,0:T(8,128)}, f32[128,128]{1,0:T(8,128)}, f32[128,128]{1,0:T(8,128)}, f32[1152,128]{1,0:T(8,128)}, f32[16,128]{1,0:T(8,128)}, /*index=5*/f32[128,128]{1,0:T(8,128)}) custom-call(s32[2]{0:T(128)S(1)} %pad_add_fusion.at, s32[4,8]{1,0:T(4,128)S(1)} %bitcast.64, f32[32,128,128]{2,1,0:T(8,128)S(1)} %bitcast.39, f32[1024,128]{1,0:T(8,128)S(1)} %bitcast.45, ...), custom_call_target="tpu_custom_call" | custom-call | flops 1000000 | bytes 1000000 | tf_op jit(solution)/shard_map/step/pallas_call | solution.py:56
  114.6 6.0 %all-to-all-start.6 = ((f32[16,72,128]{2,1,0:T(8,128)}), f32[16,72,128]{2,1,0:T(8,128)S(1)}, u32[]{:S(2)}, u32[]{:S(2)}) async-start(f32[16,72,128]{2,1,0:T(8,128)} %bitcast.71), calls=%async_computation.6 | async-start | bytes 1179648 | tf_op jit(solution)/shard_map/all_to_all | solution.py:955
  120.7 0.7 constant_dynamic-update-slice_fusion.1
  121.4 0.7 collective-permute-done.10.rest_0_
  122.1 1.2 collective-permute-start.13
  123.2 1.5 collective-permute-start.12
  124.7 1.5 collective-permute-start.11
  126.1 0.9 collective-permute-done.13.rest_3_
  127.0 1.5 collective-permute-done.12.rest_2_
  128.5 1.2 all-to-all-done.6
  129.7 2.5 %step.7 = (f32[128,128]{1,0:T(8,128)}, f32[128,128]{1,0:T(8,128)}, f32[128,128]{1,0:T(8,128)}, f32[640,128]{1,0:T(8,128)}, f32[16,256]{1,0:T(8,128)}, /*index=5*/f32[16,256]{1,0:T(8,128)}) custom-call(s32[2]{0:T(128)S(1)} %pad_add_fusion.at, s32[4,8]{1,0:T(4,128)S(1)} %bitcast.65, f32[32,128,128]{2,1,0:T(8,128)S(1)} %bitcast.40, f32[1152,128]{1,0:T(8,128)S(1)} %bitcast.43, ...), custom_call_target="tpu_custom_call" | custom-call | flops 1000000 | bytes 1000000 | tf_op jit(solution)/shard_map/step/pallas_call | solution.py:56
  132.1 6.1 %all-to-all-start.7 = ((f32[16,40,128]{2,1,0:T(8,128)}), f32[16,40,128]{2,1,0:T(8,128)S(1)}, u32[]{:S(2)}, u32[]{:S(2)}) async-start(f32[16,40,128]{2,1,0:T(8,128)} %bitcast.76), calls=%async_computation.7 | async-start | bytes 655360 | tf_op jit(solution)/shard_map/all_to_all | solution.py:965
  138.2 7.4 %sweep.6 = (f32[16,64,256]{2,1,0:T(8,128)}, f32[16,64,256]{2,1,0:T(8,128)}, f32[64,256]{1,0:T(8,128)}, f32[64,256]{1,0:T(8,128)}, f32[16,256]{1,0:T(8,128)}, /*index=5*/f32[16,256]{1,0:T(8,128)}) custom-call(s32[2]{0:T(128)S(1)} %pad_add_fusion.at, f32[64,256]{1,0:T(8,128)S(1)} %collective-permute-done.8.xa, f32[64,256]{1,0:T(8,128)S(1)} %collective-permute-done.9.xb, ...), custom_call_target="tpu_custom_call" | custom-call | flops 6000000 | bytes 8388608 | tf_op jit(solution)/shard_map/sweep/pallas_call | solution.py:758
  145.7 2.6 %step.8 = (f32[128,128]{1,0:T(8,128)}, f32[128,128]{1,0:T(8,128)}, f32[128,128]{1,0:T(8,128)}, f32[1152,128]{1,0:T(8,128)}) custom-call(s32[2]{0:T(128)S(1)} %pad_add_fusion.at, s32[4,8]{1,0:T(4,128)S(1)} %bitcast.66, f32[32,128,128]{2,1,0:T(8,128)S(1)} %bitcast.41, f32[640,128]{1,0:T(8,128)S(1)} %bitcast.47, bf16[128,512]{1,0:T(8,128)(2,1)S(1)} %columns.1.chosen, ...), custom_call_target="tpu_custom_call" | custom-call | flops 1000000 | bytes 1000000 | tf_op jit(solution)/shard_map/step/pallas_call | solution.py:56
  148.3 7.2 %all-to-all-start.8 = ((f32[16,72,128]{2,1,0:T(8,128)}), f32[16,72,128]{2,1,0:T(8,128)S(1)}, u32[]{:S(2)}, u32[]{:S(2)}) async-start(f32[16,72,128]{2,1,0:T(8,128)} %bitcast.72), calls=%async_computation.8 | async-start | bytes 1179648 | tf_op jit(solution)/shard_map/all_to_all | solution.py:982
  156.3 1.9 %home.1 = f32[1,512]{1,0:T(1,128)} custom-call(f32[128,128]{1,0:T(8,128)} %get-tuple-element.187.got, s32[1,512]{1,0:T(1,128)} %bitcast.81, s32[1,512]{1,0:T(1,128)} %get-tuple-element.188.slot, s32[1,512]{1,0:T(1,128)} %bitcast.83, f32[1,512]{1,0:T(1,128)} %bitcast.85, f32[128,128]{1,0:T(8,128)} %get-tuple-element.171.rest_3_.rest_0_.x), custom_call_target="tpu_custom_call" | custom-call | flops 1000000 | bytes 1000000 | tf_op jit(solution)/shard_map/home/pallas_call | solution.py:56
  158.2 5.9 %all-to-all-done.8 = f32[16,72,128]{2,1,0:T(8,128)S(1)} async-done(((f32[16,72,128]{2,1,0:T(8,128)}), f32[16,72,128]{2,1,0:T(8,128)S(1)}, u32[]{:S(2)}, u32[]{:S(2)}) %all-to-all-start.8) | async-done | bytes 589856 | tf_op jit(solution)/shard_map/all_to_all | solution.py:982
  164.1 2.2 %step.9 = (f32[128,128]{1,0:T(8,128)}, f32[128,128]{1,0:T(8,128)}, f32[128,128]{1,0:T(8,128)}, f32[16,128]{1,0:T(8,128)}, f32[16,256]{1,0:T(8,128)}, /*index=5*/f32[16,256]{1,0:T(8,128)}) custom-call(s32[2]{0:T(128)S(1)} %pad_add_fusion.at, s32[4,8]{1,0:T(4,128)S(1)} %bitcast.67, f32[32,128,128]{2,1,0:T(8,128)S(1)} %bitcast.42, f32[1152,128]{1,0:T(8,128)S(1)} %bitcast.44, ...), custom_call_target="tpu_custom_call" | custom-call | flops 1000000 | bytes 1000000 | tf_op jit(solution)/shard_map/step/pallas_call | solution.py:56
  166.3 5.4 %all-to-all-start.9 = ((f32[16,1,128]{2,1,0:T(1,128)}), f32[16,1,128]{2,1,0:T(1,128)S(1)}, u32[]{:S(2)}, u32[]{:S(2)}) async-start(f32[16,1,128]{2,1,0:T(1,128)} %bitcast.86), calls=%async_computation.9 | async-start | bytes 16384 | tf_op jit(solution)/shard_map/all_to_all | solution.py:993
  171.7 4.8 %sweep.7 = f32[16,64,256]{2,1,0:T(8,128)} custom-call(s32[2]{0:T(128)S(1)} %pad_add_fusion.at, f32[64,256]{1,0:T(8,128)S(1)} %collective-permute-done.14.xa, f32[64,256]{1,0:T(8,128)S(1)} %collective-permute-done.15.xb, f32[16,256]{1,0:T(8,128)} %get-tuple-element.197.ya, f32[16,256]{1,0:T(8,128)} %get-tuple-element.198.yb, ...), custom_call_target="tpu_custom_call" | custom-call | flops 6000000 | bytes 8388608 | tf_op jit(solution)/shard_map/sweep/pallas_call | solution.py:758
  176.6 1.3 all-to-all-done.9
  177.9 1.6 final.1
  (42 shorter events, 3.1 us)
Async XLA Ops:
  0.7 0.7 copy-start.2
  3.2 19.6 %all-to-all-start = ((f32[128,2,128]{2,1,0:T(2,128)}), f32[128,2,128]{2,1,0:T(2,128)S(1)}, u32[]{:S(2)}, u32[]{:S(2)}) async-start(f32[128,2,128]{2,1,0:T(2,128)} %bitcast.78), calls=%async_computation | async-start | bytes 262144 | tf_op jit(solution)/shard_map/all_to_all | solution.py:853
  13.4 9.4 %copy-start.1 = (f32[1024]{0:T(1024)S(1)}, f32[1024]{0:T(1024)}, u32[]{:S(2)}) copy-start(f32[1024]{0:T(1024)} %param.23) | copy-start | bytes 12292
  13.4 9.4 %copy-start.3 = (s32[8,4]{0,1:T(4,128)S(1)}, s32[8,4]{0,1:T(4,128)}, u32[]{:S(2)}) copy-start(s32[8,4]{0,1:T(4,128)} %param.22) | copy-start | bytes 388
  13.5 9.4 %copy-start.4 = (f32[1024]{0:T(1024)S(1)}, f32[1024]{0:T(1024)}, u32[]{:S(2)}) copy-start(f32[1024]{0:T(1024)} %param.24) | copy-start | bytes 12292
  15.3 13.4 %collective-permute-start.2 = (f32[32,256]{1,0:T(8,128)}, f32[32,256]{1,0:T(8,128)S(1)}, u32[]{:S(2)}, u32[]{:S(2)}) collective-permute-start(f32[32,256]{1,0:T(8,128)} %get-tuple-element.112), channel_id=1, source_target_pairs={{0,1},{2,3},{4,5},{6,7},{8,9},{10,11},{12,13},{14,15},{1,0},{3,2},... | collective-permute-start | bytes 98312 | tf_op jit(solution)/shard_map/ppermute | solution.py:785
  16.9 11.9 %collective-permute-start.3 = (f32[32,256]{1,0:T(8,128)}, f32[32,256]{1,0:T(8,128)S(1)}, u32[]{:S(2)}, u32[]{:S(2)}) collective-permute-start(f32[32,256]{1,0:T(8,128)} %get-tuple-element.113), channel_id=1, source_target_pairs={{1,2},{3,4},{5,6},{7,8},{9,10},{11,12},{13,14},{2,1},{4,3},{6,5},{... | collective-permute-start | bytes 98312 | tf_op jit(solution)/shard_map/ppermute | solution.py:785
  20.7 8.1 %collective-permute-start = (f32[128,256]{1,0:T(8,128)}, f32[128,256]{1,0:T(8,128)S(1)}, u32[]{:S(2)}, u32[]{:S(2)}) collective-permute-start(f32[128,256]{1,0:T(8,128)} %get-tuple-element.110), channel_id=1, source_target_pairs={{0,16},{32,48},{64,80},{96,112},{16,0},{48,32},{80,64},{112,96},{1... | collective-permute-start | bytes 393224 | tf_op jit(solution)/shard_map/ppermute | solution.py:785
  20.8 8.0 %collective-permute-start.1 = (f32[128,256]{1,0:T(8,128)}, f32[128,256]{1,0:T(8,128)S(1)}, u32[]{:S(2)}, u32[]{:S(2)}) collective-permute-start(f32[128,256]{1,0:T(8,128)} %get-tuple-element.111), channel_id=1, source_target_pairs={{16,32},{48,64},{80,96},{32,16},{64,48},{96,80},{17,33},{49,65},{8... | collective-permute-start | bytes 393224 | tf_op jit(solution)/shard_map/ppermute | solution.py:785
  28.8 19.0 %all-to-all-start.1 = ((f32[128,2,128]{2,1,0:T(2,128)}), f32[128,2,128]{2,1,0:T(2,128)S(1)}, u32[]{:S(2)}, u32[]{:S(2)}) async-start(f32[128,2,128]{2,1,0:T(2,128)} %bitcast.77), calls=%async_computation.1 | async-start | bytes 262144 | tf_op jit(solution)/shard_map/all_to_all | solution.py:876
  38.5 26.6 %copy-start = (f32[8,4,128,128]{3,2,1,0:T(8,128)S(1)}, f32[8,4,128,128]{3,2,1,0:T(8,128)}, u32[]{:S(2)}) copy-start(f32[8,4,128,128]{3,2,1,0:T(8,128)} %param.21) | copy-start | bytes 6291460
  48.5 16.6 %all-to-all-start.2 = ((f32[128,2,128]{2,1,0:T(2,128)}), f32[128,2,128]{2,1,0:T(2,128)S(1)}, u32[]{:S(2)}, u32[]{:S(2)}) async-start(f32[128,2,128]{2,1,0:T(2,128)} %bitcast.74), calls=%async_computation.2 | async-start | bytes 262144 | tf_op jit(solution)/shard_map/all_to_all | solution.py:884
  55.7 11.0 %collective-permute-start.4 = (f32[64,256]{1,0:T(8,128)}, f32[64,256]{1,0:T(8,128)S(1)}, u32[]{:S(2)}, u32[]{:S(2)}) collective-permute-start(f32[64,256]{1,0:T(8,128)} %get-tuple-element.125), channel_id=1, source_target_pairs={{0,16},{32,48},{64,80},{96,112},{16,0},{48,32},{80,64},{112,96},{1... | collective-permute-start | bytes 196616 | tf_op jit(solution)/shard_map/ppermute | solution.py:785
  56.0 10.8 %collective-permute-start.5 = (f32[64,256]{1,0:T(8,128)}, f32[64,256]{1,0:T(8,128)S(1)}, u32[]{:S(2)}, u32[]{:S(2)}) collective-permute-start(f32[64,256]{1,0:T(8,128)} %get-tuple-element.126), channel_id=1, source_target_pairs={{16,32},{48,64},{80,96},{32,16},{64,48},{96,80},{17,33},{49,65},{8... | collective-permute-start | bytes 196616 | tf_op jit(solution)/shard_map/ppermute | solution.py:785
  56.6 10.1 %collective-permute-start.6 = (f32[16,256]{1,0:T(8,128)}, f32[16,256]{1,0:T(8,128)S(1)}, u32[]{:S(2)}, u32[]{:S(2)}) collective-permute-start(f32[16,256]{1,0:T(8,128)} %get-tuple-element.127), channel_id=1, source_target_pairs={{0,1},{2,3},{4,5},{6,7},{8,9},{10,11},{12,13},{14,15},{1,0},{3,2},... | collective-permute-start | bytes 49160 | tf_op jit(solution)/shard_map/ppermute | solution.py:785
  58.2 8.5 %collective-permute-start.7 = (f32[16,256]{1,0:T(8,128)}, f32[16,256]{1,0:T(8,128)S(1)}, u32[]{:S(2)}, u32[]{:S(2)}) collective-permute-start(f32[16,256]{1,0:T(8,128)} %get-tuple-element.128), channel_id=1, source_target_pairs={{1,2},{3,4},{5,6},{7,8},{9,10},{11,12},{13,14},{2,1},{4,3},{6,5},{... | collective-permute-start | bytes 49160 | tf_op jit(solution)/shard_map/ppermute | solution.py:785
  66.8 14.6 %all-to-all-start.3 = ((f32[16,40,128]{2,1,0:T(8,128)}), f32[16,40,128]{2,1,0:T(8,128)S(1)}, u32[]{:S(2)}, u32[]{:S(2)}) async-start(f32[16,40,128]{2,1,0:T(8,128)} %bitcast.75), calls=%async_computation.3 | async-start | bytes 655360 | tf_op jit(solution)/shard_map/all_to_all | solution.py:903
  81.1 22.2 %copy-start.6 = (f32[64,256]{1,0:T(8,128)S(1)}, f32[64,256]{1,0:T(8,128)}, u32[]{:S(2)}) copy-start(f32[64,256]{1,0:T(8,128)} %get-tuple-element.150) | copy-start | bytes 196612
  81.1 22.3 %copy-start.5 = (f32[64,256]{1,0:T(8,128)S(1)}, f32[64,256]{1,0:T(8,128)}, u32[]{:S(2)}) copy-start(f32[64,256]{1,0:T(8,128)} %get-tuple-element.151) | copy-start | bytes 196612
  81.4 12.0 %all-to-all-start.4 = ((f32[8,32,128]{2,1,0:T(8,128)}), f32[8,32,128]{2,1,0:T(8,128)S(1)}, u32[]{:S(2)}, u32[]{:S(2)}) async-start(f32[8,32,128]{2,1,0:T(8,128)} %bitcast.79), calls=%async_computation.4 | async-start | bytes 262144 | tf_op jit(solution)/shard_map/all_to_all | solution.py:919
  96.0 16.0 %all-to-all-start.5 = ((f32[16,64,128]{2,1,0:T(8,128)}), f32[16,64,128]{2,1,0:T(8,128)S(1)}, u32[]{:S(2)}, u32[]{:S(2)}) async-start(f32[16,64,128]{2,1,0:T(8,128)} %bitcast.73), calls=%async_computation.5 | async-start | bytes 1048576 | tf_op jit(solution)/shard_map/all_to_all | solution.py:950
  103.2 1.3 collective-permute-start.8
  103.4 1.2 collective-permute-start.9
  114.6 15.0 %all-to-all-start.6 = ((f32[16,72,128]{2,1,0:T(8,128)}), f32[16,72,128]{2,1,0:T(8,128)S(1)}, u32[]{:S(2)}, u32[]{:S(2)}) async-start(f32[16,72,128]{2,1,0:T(8,128)} %bitcast.71), calls=%async_computation.6 | async-start | bytes 1179648 | tf_op jit(solution)/shard_map/all_to_all | solution.py:955
  120.7 1.4 collective-permute-start.10
  122.1 4.9 %collective-permute-start.13 = (f32[32,128]{1,0:T(8,128)S(1)}, f32[32,128]{1,0:T(8,128)S(1)}, u32[]{:S(2)}, u32[]{:S(2)}) collective-permute-start(f32[32,128]{1,0:T(8,128)S(1)} %constant_dynamic-update-slice_fusion), channel_id=1, source_target_pairs={{0,96},{16,112},{32,64},{48,80},{64,32},{80,48},{96,0},{112,16},{1... | collective-permute-start | bytes 49160 | tf_op jit(solution)/shard_map/ppermute | solution.py:959
  123.2 5.2 %collective-permute-start.12 = (f32[32,128]{1,0:T(8,128)S(1)}, f32[32,128]{1,0:T(8,128)S(1)}, u32[]{:S(2)}, u32[]{:S(2)}) collective-permute-start(f32[32,128]{1,0:T(8,128)S(1)} %constant_dynamic-update-slice_fusion), channel_id=1, source_target_pairs={{0,64},{16,80},{32,96},{48,112},{64,0},{80,16},{96,32},{112,48},{1... | collective-permute-start | bytes 49160 | tf_op jit(solution)/shard_map/ppermute | solution.py:959
  124.7 3.8 %collective-permute-start.11 = (f32[32,128]{1,0:T(8,128)S(1)}, f32[32,128]{1,0:T(8,128)S(1)}, u32[]{:S(2)}, u32[]{:S(2)}) collective-permute-start(f32[32,128]{1,0:T(8,128)S(1)} %constant_dynamic-update-slice_fusion), channel_id=1, source_target_pairs={{0,32},{16,48},{32,0},{48,16},{64,96},{80,112},{96,64},{112,80},{1... | collective-permute-start | bytes 49160 | tf_op jit(solution)/shard_map/ppermute | solution.py:959
  132.1 13.5 %all-to-all-start.7 = ((f32[16,40,128]{2,1,0:T(8,128)}), f32[16,40,128]{2,1,0:T(8,128)S(1)}, u32[]{:S(2)}, u32[]{:S(2)}) async-start(f32[16,40,128]{2,1,0:T(8,128)} %bitcast.76), calls=%async_computation.7 | async-start | bytes 655360 | tf_op jit(solution)/shard_map/all_to_all | solution.py:965
  145.6 9.9 %copy-start.8 = (f32[64,256]{1,0:T(8,128)S(1)}, f32[64,256]{1,0:T(8,128)}, u32[]{:S(2)}) copy-start(f32[64,256]{1,0:T(8,128)} %get-tuple-element.189) | copy-start | bytes 196612
  145.6 10.0 %copy-start.7 = (f32[64,256]{1,0:T(8,128)S(1)}, f32[64,256]{1,0:T(8,128)}, u32[]{:S(2)}) copy-start(f32[64,256]{1,0:T(8,128)} %get-tuple-element.190) | copy-start | bytes 196612
  148.3 15.8 %all-to-all-start.8 = ((f32[16,72,128]{2,1,0:T(8,128)}), f32[16,72,128]{2,1,0:T(8,128)S(1)}, u32[]{:S(2)}, u32[]{:S(2)}) async-start(f32[16,72,128]{2,1,0:T(8,128)} %bitcast.72), calls=%async_computation.8 | async-start | bytes 1179648 | tf_op jit(solution)/shard_map/all_to_all | solution.py:982
  155.5 2.6 %collective-permute-start.14 = (f32[64,256]{1,0:T(8,128)S(1)}, f32[64,256]{1,0:T(8,128)S(1)}, u32[]{:S(2)}, u32[]{:S(2)}) collective-permute-start(f32[64,256]{1,0:T(8,128)S(1)} %copy-done.8), channel_id=1, source_target_pairs={{0,16},{32,48},{64,80},{96,112},{16,0},{48,32},{80,64},{112,96},{1... | collective-permute-start | bytes 196616 | tf_op jit(solution)/shard_map/ppermute | solution.py:785
  155.6 2.5 %collective-permute-start.15 = (f32[64,256]{1,0:T(8,128)S(1)}, f32[64,256]{1,0:T(8,128)S(1)}, u32[]{:S(2)}, u32[]{:S(2)}) collective-permute-start(f32[64,256]{1,0:T(8,128)S(1)} %copy-done.7), channel_id=1, source_target_pairs={{16,32},{48,64},{80,96},{32,16},{64,48},{96,80},{17,33},{49,65},{8... | collective-permute-start | bytes 196616 | tf_op jit(solution)/shard_map/ppermute | solution.py:785
  166.3 11.5 %all-to-all-start.9 = ((f32[16,1,128]{2,1,0:T(1,128)}), f32[16,1,128]{2,1,0:T(1,128)S(1)}, u32[]{:S(2)}, u32[]{:S(2)}) async-start(f32[16,1,128]{2,1,0:T(1,128)} %bitcast.86), calls=%async_computation.9 | async-start | bytes 16384 | tf_op jit(solution)/shard_map/all_to_all | solution.py:993

commit v7 on v6

--- a/solution.py
+++ b/solution.py
@@ -165,7 +165,9 @@
     lane = iota((1, LANES), 1)
     extra = jnp.zeros((1, LANES), F32)
     for t in range(cols.shape[0]):
-        extra = jnp.where(lane == COLS + t, cols[t, mine].astype(F32), extra)
+        column = jnp.where(iota((1, cols.shape[1]), 1) == mine, cols[t : t + 1, :], 0)
+        column = jnp.sum(column, axis=1, keepdims=True).astype(F32)
+        extra = jnp.where(lane == COLS + t, column, extra)
     blocks[...] = jnp.broadcast_to(x_own[pl.ds(mine, 1), :], (LANES, LANES))
     send[pl.ds(0, LANES, stride=2), :] = blocks[...]
     send[pl.ds(1, LANES, stride=2), :] = message + extra
@@ -721,7 +723,7 @@
     gather=False,
     y_in=False,
     y_out=False,
-    many=4,
+    many=8,
 ):
     nx, ny, nz = p.shape
     part = pl.BlockSpec((many, ny, nz), lambda i: (i, 0, 0))
@@ -839,12 +841,13 @@
     send, slot = call(
         pack_body,
         (sent(2 * LANES, LANES), pltpu.HBM((1, count), jnp.int32)),
+        tile_cols.T,
         owner,
         mortar_cell.reshape(1, count),
         frac,
         kappa,
         fracture_start.reshape(rows, LANES),
-        scalars=scalars,
+        scalars=(at,),
         scratch=[square_scratch],
         name="pack",
         least=1,

time: 183 us -> 179 us (0.978)
  Pallas kernels: 55.4 us -> 52.1 us
  waiting for transfers between devices: 32.6 us -> 35.7 us
  starting transfers between devices: 89 us -> 86.9 us
    pallas_call x4, Pallas kernels: 27.3 us -> 24 us  [sweep(): pl.pallas_call(functools.partial(sweep_body, first=first, last=last, flux...]
    all_to_all x6, waiting for transfers between devices: 16.2 us -> 18.5 us  [body(): arrived = over_frac(send)]
  transfers between devices with their start and end apart: 26 -> 26, of which waited for: 13 -> 14; matrix products, arithmetic and copies ran while one was open for 0% -> 0% of each run, Pallas kernels for 22% -> 20%
where the time goes in v7:
time: 179 us; the launch traced here: 176 us
  starting transfers between devices  86.9 us (49%)
  Pallas kernels  52.1 us (29%)
  waiting for transfers between devices  35.7 us (20%)
    all_to_all x6, starting transfers between devices, body(): arrived = over_frac(send)  37.7 us
    pallas_call x12, Pallas kernels, call(): pl.pallas_call(body, grid=(1,), out_shape=outs, in_specs=[SMEM] * len(sca...  26.2 us
    pallas_call x4, Pallas kernels, sweep(): pl.pallas_call(functools.partial(sweep_body, first=first, last=last, flux...  24 us
    all_to_all x6, waiting for transfers between devices, body(): arrived = over_frac(send)  18.5 us
    ppermute x12, starting transfers between devices, swap(): return lax.ppermute(v, axis, pairs + [(b, a) for a, b in pairs])  13.8 us
    all_to_all x1, starting transfers between devices, body(): got = everyone(send)  10.2 us
    all_to_all x1, starting transfers between devices, body(): reduced = everyone(send)  9.68 us
    all_to_all x1, starting transfers between devices, body(): residuals = everyone(send)  6.6 us
  transfers between devices with their start and end apart: 26, of which 14 were waited for; matrix products, arithmetic and copies ran while one was open for 0% of the time, Pallas kernels for 20%

profile of v7, /device:TPU:32, one launch (start us, length us, event | category | flops | bytes accessed | tf_op | source)
XLA Modules:
  0.0 176.3 jit_solution(14346330066994300408)
XLA Ops:
  0.7 1.8 %pack.1 = (f32[256,128]{1,0:T(8,128)}, s32[1,512]{1,0:T(1,128)}) custom-call(s32[2]{0:T(128)S(1)} %pad_add_fusion.at, s32[4,8]{1,0:T(4,128)} %bitcast.60, s32[1,512]{1,0:T(1,128)} %bitcast.80, s32[1,512]{1,0:T(1,128)} %bitcast.90, s32[1,512]{1,0:T(1,128)} %bitcast.82, f32[1,512]{1,0:T(1,128)} %bitcast.84, f32[8,128]{1,0:T(8,128)} %bitcast.88), custom_call_target="tpu_custom_call" | custom-call | flops 1000000 | bytes 1000000 | tf_op jit(solution)/shard_map/pack/pallas_call | solution.py:56
  2.5 10.2 %all-to-all-start = ((f32[128,2,128]{2,1,0:T(2,128)}), f32[128,2,128]{2,1,0:T(2,128)S(1)}, u32[]{:S(2)}, u32[]{:S(2)}) async-start(f32[128,2,128]{2,1,0:T(2,128)} %bitcast.78), calls=%async_computation | async-start | bytes 262144 | tf_op jit(solution)/shard_map/all_to_all | solution.py:856
  12.8 1.9 %edges.1 = (f32[128,256]{1,0:T(8,128)}, f32[128,256]{1,0:T(8,128)}, f32[32,256]{1,0:T(8,128)}, f32[32,256]{1,0:T(8,128)}) custom-call(s32[2]{0:T(128)S(1)} %pad_add_fusion.at, f32[16,64,256]{2,1,0:T(8,128)} %p_after.1, f32[16,64,256]{2,1,0:T(8,128)} %p_after.1, f32[16,64,256]{2,1,0:T(8,128)} %p_after.1, f32[16,64,256]{2,1,0:T(8,128)} %p_after.1, ...), custom_call_target="tpu_custom_call" | custom-call | tf_op jit(solution)/shard_map/edges/pallas_call | solution.py:547
  14.7 1.5 collective-permute-start.2
  16.2 3.8 %collective-permute-start.3 = (f32[32,256]{1,0:T(8,128)}, f32[32,256]{1,0:T(8,128)S(1)}, u32[]{:S(2)}, u32[]{:S(2)}) collective-permute-start(f32[32,256]{1,0:T(8,128)} %get-tuple-element.113), channel_id=1, source_target_pairs={{1,2},{3,4},{5,6},{7,8},{9,10},{11,12},{13,14},{2,1},{4,3},{6,5},{... | collective-permute-start | bytes 98312 | tf_op jit(solution)/shard_map/ppermute | solution.py:787
  20.1 0.7 collective-permute-start.1
  20.8 1.4 all-to-all-done
  22.2 5.9 %first.1 = (f32[256,128]{1,0:T(8,128)}, f32[128,128]{1,0:T(8,128)}, f32[128,128]{1,0:T(8,128)}, f32[128,128]{1,0:T(8,128)}, f32[128,128]{1,0:T(8,128)}) custom-call(s32[2]{0:T(128)S(1)} %pad_add_fusion.at, s32[4,8]{1,0:T(4,128)S(1)} %bitcast.61, f32[32,128,128]{2,1,0:T(8,128)} %bitcast.36, f32[1024,256]{1,0:T(8,128)} %bitcast.70, f32[256,128]{1,0:T(8,128)S(1)} %bitcast.50, ...), custom_call_target="tpu_custom_call" | custom-call | flops 2000000000 | bytes 1000000 | tf_op jit(solution)/shard_map/first/pallas_call | solution.py:56
  28.1 9.7 %all-to-all-start.1 = ((f32[128,2,128]{2,1,0:T(2,128)}), f32[128,2,128]{2,1,0:T(2,128)S(1)}, u32[]{:S(2)}, u32[]{:S(2)}) async-start(f32[128,2,128]{2,1,0:T(2,128)} %bitcast.77), calls=%async_computation.1 | async-start | bytes 262144 | tf_op jit(solution)/shard_map/all_to_all | solution.py:879
  37.8 6.2 %sweep.4 = (f32[16,64,256]{2,1,0:T(8,128)}, f32[16,64,256]{2,1,0:T(8,128)}, f32[16,64,256]{2,1,0:T(8,128)}, f32[64,256]{1,0:T(8,128)}, f32[64,256]{1,0:T(8,128)}, /*index=5*/f32[16,256]{1,0:T(8,128)}, f32[16,256]{1,0:T(8,128)}) custom-call(s32[2]{0:T(128)S(1)} %pad_add_fusion.at, f32[128,256]{1,0:T(8,128)S(1)} %collective-permute-done.xa.cxa, ...), custom_call_target="tpu_custom_call" | custom-call | flops 6000000 | bytes 8388608 | tf_op jit(solution)/shard_map/sweep/pallas_call | solution.py:760
  44.0 3.2 %all-to-all-done.1 = f32[128,2,128]{2,1,0:T(2,128)S(1)} async-done(((f32[128,2,128]{2,1,0:T(2,128)}), f32[128,2,128]{2,1,0:T(2,128)S(1)}, u32[]{:S(2)}, u32[]{:S(2)}) %all-to-all-start.1) | async-done | bytes 131104 | tf_op jit(solution)/shard_map/all_to_all | solution.py:879
  47.1 0.7 sums.1
  47.8 6.6 %all-to-all-start.2 = ((f32[128,2,128]{2,1,0:T(2,128)}), f32[128,2,128]{2,1,0:T(2,128)S(1)}, u32[]{:S(2)}, u32[]{:S(2)}) async-start(f32[128,2,128]{2,1,0:T(2,128)} %bitcast.74), calls=%async_computation.2 | async-start | bytes 262144 | tf_op jit(solution)/shard_map/all_to_all | solution.py:887
  55.3 1.6 collective-permute-start.6
  56.9 3.8 %collective-permute-start.7 = (f32[16,256]{1,0:T(8,128)}, f32[16,256]{1,0:T(8,128)S(1)}, u32[]{:S(2)}, u32[]{:S(2)}) collective-permute-start(f32[16,256]{1,0:T(8,128)} %get-tuple-element.128), channel_id=1, source_target_pairs={{1,2},{3,4},{5,6},{7,8},{9,10},{11,12},{13,14},{2,1},{4,3},{6,5},{... | collective-permute-start | bytes 49160 | tf_op jit(solution)/shard_map/ppermute | solution.py:787
  60.7 3.1 %all-to-all-done.2 = f32[128,2,128]{2,1,0:T(2,128)S(1)} async-done(((f32[128,2,128]{2,1,0:T(2,128)}), f32[128,2,128]{2,1,0:T(2,128)S(1)}, u32[]{:S(2)}, u32[]{:S(2)}) %all-to-all-start.2) | async-done | bytes 131104 | tf_op jit(solution)/shard_map/all_to_all | solution.py:887
  63.8 1.7 start.1
  65.5 6.1 %all-to-all-start.3 = ((f32[16,40,128]{2,1,0:T(8,128)}), f32[16,40,128]{2,1,0:T(8,128)S(1)}, u32[]{:S(2)}, u32[]{:S(2)}) async-start(f32[16,40,128]{2,1,0:T(8,128)} %bitcast.75), calls=%async_computation.3 | async-start | bytes 655360 | tf_op jit(solution)/shard_map/all_to_all | solution.py:906
  71.5 7.0 %sweep.5 = (f32[16,64,256]{2,1,0:T(8,128)}, f32[128,128]{1,0:T(8,128)}, f32[256,128]{1,0:T(8,128)}, f32[64,256]{1,0:T(8,128)}, f32[64,256]{1,0:T(8,128)}, /*index=5*/f32[16,256]{1,0:T(8,128)}, f32[16,256]{1,0:T(8,128)}) custom-call(s32[2]{0:T(128)S(1)} %pad_add_fusion.at, f32[64,256]{1,0:T(8,128)S(1)} %collective-permute-done.4.xa, ...), custom_call_target="tpu_custom_call" | custom-call | flops 6000000 | bytes 8388608 | tf_op jit(solution)/shard_map/sweep/pallas_call | solution.py:760
  78.6 1.5 all-to-all-done.3
  80.1 4.7 %all-to-all-start.4 = ((f32[8,32,128]{2,1,0:T(8,128)}), f32[8,32,128]{2,1,0:T(8,128)S(1)}, u32[]{:S(2)}, u32[]{:S(2)}) async-start(f32[8,32,128]{2,1,0:T(8,128)} %bitcast.79), calls=%async_computation.4 | async-start | bytes 262144 | tf_op jit(solution)/shard_map/all_to_all | solution.py:922
  85.0 5.9 %all-to-all-done.4 = f32[8,32,128]{2,1,0:T(8,128)S(1)} async-done(((f32[8,32,128]{2,1,0:T(8,128)}), f32[8,32,128]{2,1,0:T(8,128)S(1)}, u32[]{:S(2)}, u32[]{:S(2)}) %all-to-all-start.4) | async-done | bytes 131104 | tf_op jit(solution)/shard_map/all_to_all | solution.py:922
  91.0 2.6 %step.5 = (f32[128,128]{1,0:T(8,128)}, f32[128,128]{1,0:T(8,128)}, f32[128,128]{1,0:T(8,128)}, f32[1024,128]{1,0:T(8,128)}) custom-call(s32[2]{0:T(128)S(1)} %pad_add_fusion.at, s32[4,8]{1,0:T(4,128)S(1)} %bitcast.63, f32[32,128,128]{2,1,0:T(8,128)S(1)} %bitcast.38, f32[640,128]{1,0:T(8,128)S(1)} %bitcast.46, bf16[128,512]{1,0:T(8,128)(2,1)S(1)} %columns.1.chosen, ...), custom_call_target="tpu_custom_call" | custom-call | flops 1000000 | bytes 1000000 | tf_op jit(solution)/shard_map/step/pallas_call | solution.py:56
  93.5 7.2 %all-to-all-start.5 = ((f32[16,64,128]{2,1,0:T(8,128)}), f32[16,64,128]{2,1,0:T(8,128)S(1)}, u32[]{:S(2)}, u32[]{:S(2)}) async-start(f32[16,64,128]{2,1,0:T(8,128)} %bitcast.73), calls=%async_computation.5 | async-start | bytes 1048576 | tf_op jit(solution)/shard_map/all_to_all | solution.py:953
  102.1 7.5 %all-to-all-done.5 = f32[16,64,128]{2,1,0:T(8,128)S(1)} async-done(((f32[16,64,128]{2,1,0:T(8,128)}), f32[16,64,128]{2,1,0:T(8,128)S(1)}, u32[]{:S(2)}, u32[]{:S(2)}) %all-to-all-start.5) | async-done | bytes 524320 | tf_op jit(solution)/shard_map/all_to_all | solution.py:953
  109.6 2.6 %step.6 = (f32[128,128]{1,0:T(8,128)}, f32[128,128]{1,0:T(8,128)}, f32[128,128]{1,0:T(8,128)}, f32[1152,128]{1,0:T(8,128)}, f32[16,128]{1,0:T(8,128)}, /*index=5*/f32[128,128]{1,0:T(8,128)}) custom-call(s32[2]{0:T(128)S(1)} %pad_add_fusion.at, s32[4,8]{1,0:T(4,128)S(1)} %bitcast.64, f32[32,128,128]{2,1,0:T(8,128)S(1)} %bitcast.39, f32[1024,128]{1,0:T(8,128)S(1)} %bitcast.45, ...), custom_call_target="tpu_custom_call" | custom-call | flops 1000000 | bytes 1000000 | tf_op jit(solution)/shard_map/step/pallas_call | solution.py:56
  112.2 6.0 %all-to-all-start.6 = ((f32[16,72,128]{2,1,0:T(8,128)}), f32[16,72,128]{2,1,0:T(8,128)S(1)}, u32[]{:S(2)}, u32[]{:S(2)}) async-start(f32[16,72,128]{2,1,0:T(8,128)} %bitcast.71), calls=%async_computation.6 | async-start | bytes 1179648 | tf_op jit(solution)/shard_map/all_to_all | solution.py:958
  118.2 0.7 constant_dynamic-update-slice_fusion.1
  118.9 0.7 collective-permute-done.10.rest_0_
  119.6 1.2 collective-permute-start.13
  120.7 1.5 collective-permute-start.12
  122.2 1.5 collective-permute-start.11
  123.7 0.9 collective-permute-done.13.rest_3_
  124.5 1.5 collective-permute-done.12.rest_2_
  126.0 1.2 all-to-all-done.6
  127.2 2.5 %step.7 = (f32[128,128]{1,0:T(8,128)}, f32[128,128]{1,0:T(8,128)}, f32[128,128]{1,0:T(8,128)}, f32[640,128]{1,0:T(8,128)}, f32[16,256]{1,0:T(8,128)}, /*index=5*/f32[16,256]{1,0:T(8,128)}) custom-call(s32[2]{0:T(128)S(1)} %pad_add_fusion.at, s32[4,8]{1,0:T(4,128)S(1)} %bitcast.65, f32[32,128,128]{2,1,0:T(8,128)S(1)} %bitcast.40, f32[1152,128]{1,0:T(8,128)S(1)} %bitcast.43, ...), custom_call_target="tpu_custom_call" | custom-call | flops 1000000 | bytes 1000000 | tf_op jit(solution)/shard_map/step/pallas_call | solution.py:56
  129.7 6.1 %all-to-all-start.7 = ((f32[16,40,128]{2,1,0:T(8,128)}), f32[16,40,128]{2,1,0:T(8,128)S(1)}, u32[]{:S(2)}, u32[]{:S(2)}) async-start(f32[16,40,128]{2,1,0:T(8,128)} %bitcast.76), calls=%async_computation.7 | async-start | bytes 655360 | tf_op jit(solution)/shard_map/all_to_all | solution.py:968
  135.7 6.6 %sweep.6 = (f32[16,64,256]{2,1,0:T(8,128)}, f32[16,64,256]{2,1,0:T(8,128)}, f32[64,256]{1,0:T(8,128)}, f32[64,256]{1,0:T(8,128)}, f32[16,256]{1,0:T(8,128)}, /*index=5*/f32[16,256]{1,0:T(8,128)}) custom-call(s32[2]{0:T(128)S(1)} %pad_add_fusion.at, f32[64,256]{1,0:T(8,128)S(1)} %collective-permute-done.8.xa, f32[64,256]{1,0:T(8,128)S(1)} %collective-permute-done.9.xb, ...), custom_call_target="tpu_custom_call" | custom-call | flops 6000000 | bytes 8388608 | tf_op jit(solution)/shard_map/sweep/pallas_call | solution.py:760
  142.8 2.6 %step.8 = (f32[128,128]{1,0:T(8,128)}, f32[128,128]{1,0:T(8,128)}, f32[128,128]{1,0:T(8,128)}, f32[1152,128]{1,0:T(8,128)}) custom-call(s32[2]{0:T(128)S(1)} %pad_add_fusion.at, s32[4,8]{1,0:T(4,128)S(1)} %bitcast.66, f32[32,128,128]{2,1,0:T(8,128)S(1)} %bitcast.41, f32[640,128]{1,0:T(8,128)S(1)} %bitcast.47, bf16[128,512]{1,0:T(8,128)(2,1)S(1)} %columns.1.chosen, ...), custom_call_target="tpu_custom_call" | custom-call | flops 1000000 | bytes 1000000 | tf_op jit(solution)/shard_map/step/pallas_call | solution.py:56
  145.3 6.9 %all-to-all-start.8 = ((f32[16,72,128]{2,1,0:T(8,128)}), f32[16,72,128]{2,1,0:T(8,128)S(1)}, u32[]{:S(2)}, u32[]{:S(2)}) async-start(f32[16,72,128]{2,1,0:T(8,128)} %bitcast.72), calls=%async_computation.8 | async-start | bytes 1179648 | tf_op jit(solution)/shard_map/all_to_all | solution.py:985
  152.4 0.7 collective-permute-start.15
  153.1 1.9 %home.1 = f32[1,512]{1,0:T(1,128)} custom-call(f32[128,128]{1,0:T(8,128)} %get-tuple-element.187.got, s32[1,512]{1,0:T(1,128)} %bitcast.81, s32[1,512]{1,0:T(1,128)} %get-tuple-element.188.slot, s32[1,512]{1,0:T(1,128)} %bitcast.83, f32[1,512]{1,0:T(1,128)} %bitcast.85, f32[128,128]{1,0:T(8,128)} %get-tuple-element.171.rest_3_.rest_0_.x), custom_call_target="tpu_custom_call" | custom-call | flops 1000000 | bytes 1000000 | tf_op jit(solution)/shard_map/home/pallas_call | solution.py:56
  154.9 5.9 %all-to-all-done.8 = f32[16,72,128]{2,1,0:T(8,128)S(1)} async-done(((f32[16,72,128]{2,1,0:T(8,128)}), f32[16,72,128]{2,1,0:T(8,128)S(1)}, u32[]{:S(2)}, u32[]{:S(2)}) %all-to-all-start.8) | async-done | bytes 589856 | tf_op jit(solution)/shard_map/all_to_all | solution.py:985
  160.9 2.2 %step.9 = (f32[128,128]{1,0:T(8,128)}, f32[128,128]{1,0:T(8,128)}, f32[128,128]{1,0:T(8,128)}, f32[16,128]{1,0:T(8,128)}, f32[16,256]{1,0:T(8,128)}, /*index=5*/f32[16,256]{1,0:T(8,128)}) custom-call(s32[2]{0:T(128)S(1)} %pad_add_fusion.at, s32[4,8]{1,0:T(4,128)S(1)} %bitcast.67, f32[32,128,128]{2,1,0:T(8,128)S(1)} %bitcast.42, f32[1152,128]{1,0:T(8,128)S(1)} %bitcast.44, ...), custom_call_target="tpu_custom_call" | custom-call | flops 1000000 | bytes 1000000 | tf_op jit(solution)/shard_map/step/pallas_call | solution.py:56
  163.1 5.4 %all-to-all-start.9 = ((f32[16,1,128]{2,1,0:T(1,128)}), f32[16,1,128]{2,1,0:T(1,128)S(1)}, u32[]{:S(2)}, u32[]{:S(2)}) async-start(f32[16,1,128]{2,1,0:T(1,128)} %bitcast.86), calls=%async_computation.9 | async-start | bytes 16384 | tf_op jit(solution)/shard_map/all_to_all | solution.py:996
  168.5 4.2 %sweep.7 = f32[16,64,256]{2,1,0:T(8,128)} custom-call(s32[2]{0:T(128)S(1)} %pad_add_fusion.at, f32[64,256]{1,0:T(8,128)S(1)} %collective-permute-done.14.xa, f32[64,256]{1,0:T(8,128)S(1)} %collective-permute-done.15.xb, f32[16,256]{1,0:T(8,128)} %get-tuple-element.197.ya, f32[16,256]{1,0:T(8,128)} %get-tuple-element.198.yb, ...), custom_call_target="tpu_custom_call" | custom-call | flops 6000000 | bytes 8388608 | tf_op jit(solution)/shard_map/sweep/pallas_call | solution.py:760
  172.6 2.1 %all-to-all-done.9 = f32[16,1,128]{2,1,0:T(1,128)S(1)} async-done(((f32[16,1,128]{2,1,0:T(1,128)}), f32[16,1,128]{2,1,0:T(1,128)S(1)}, u32[]{:S(2)}, u32[]{:S(2)}) %all-to-all-start.9) | async-done | bytes 8224 | tf_op jit(solution)/shard_map/all_to_all | solution.py:996
  174.7 1.6 final.1
  (40 shorter events, 3.1 us)
Async XLA Ops:
  2.5 19.6 %all-to-all-start = ((f32[128,2,128]{2,1,0:T(2,128)}), f32[128,2,128]{2,1,0:T(2,128)S(1)}, u32[]{:S(2)}, u32[]{:S(2)}) async-start(f32[128,2,128]{2,1,0:T(2,128)} %bitcast.78), calls=%async_computation | async-start | bytes 262144 | tf_op jit(solution)/shard_map/all_to_all | solution.py:856
  12.8 9.4 %copy-start.1 = (f32[1024]{0:T(1024)S(1)}, f32[1024]{0:T(1024)}, u32[]{:S(2)}) copy-start(f32[1024]{0:T(1024)} %param.23) | copy-start | bytes 12292
  12.8 9.4 %copy-start.2 = (s32[8,4]{0,1:T(4,128)S(1)}, s32[8,4]{0,1:T(4,128)}, u32[]{:S(2)}) copy-start(s32[8,4]{0,1:T(4,128)} %param.22) | copy-start | bytes 388
  12.8 9.4 %copy-start.3 = (f32[1024]{0:T(1024)S(1)}, f32[1024]{0:T(1024)}, u32[]{:S(2)}) copy-start(f32[1024]{0:T(1024)} %param.24) | copy-start | bytes 12292
  14.7 13.4 %collective-permute-start.2 = (f32[32,256]{1,0:T(8,128)}, f32[32,256]{1,0:T(8,128)S(1)}, u32[]{:S(2)}, u32[]{:S(2)}) collective-permute-start(f32[32,256]{1,0:T(8,128)} %get-tuple-element.112), channel_id=1, source_target_pairs={{0,1},{2,3},{4,5},{6,7},{8,9},{10,11},{12,13},{14,15},{1,0},{3,2},... | collective-permute-start | bytes 98312 | tf_op jit(solution)/shard_map/ppermute | solution.py:787
  16.2 11.9 %collective-permute-start.3 = (f32[32,256]{1,0:T(8,128)}, f32[32,256]{1,0:T(8,128)S(1)}, u32[]{:S(2)}, u32[]{:S(2)}) collective-permute-start(f32[32,256]{1,0:T(8,128)} %get-tuple-element.113), channel_id=1, source_target_pairs={{1,2},{3,4},{5,6},{7,8},{9,10},{11,12},{13,14},{2,1},{4,3},{6,5},{... | collective-permute-start | bytes 98312 | tf_op jit(solution)/shard_map/ppermute | solution.py:787
  20.0 8.1 %collective-permute-start = (f32[128,256]{1,0:T(8,128)}, f32[128,256]{1,0:T(8,128)S(1)}, u32[]{:S(2)}, u32[]{:S(2)}) collective-permute-start(f32[128,256]{1,0:T(8,128)} %get-tuple-element.110), channel_id=1, source_target_pairs={{0,16},{32,48},{64,80},{96,112},{16,0},{48,32},{80,64},{112,96},{1... | collective-permute-start | bytes 393224 | tf_op jit(solution)/shard_map/ppermute | solution.py:787
  20.1 8.0 %collective-permute-start.1 = (f32[128,256]{1,0:T(8,128)}, f32[128,256]{1,0:T(8,128)S(1)}, u32[]{:S(2)}, u32[]{:S(2)}) collective-permute-start(f32[128,256]{1,0:T(8,128)} %get-tuple-element.111), channel_id=1, source_target_pairs={{16,32},{48,64},{80,96},{32,16},{64,48},{96,80},{17,33},{49,65},{8... | collective-permute-start | bytes 393224 | tf_op jit(solution)/shard_map/ppermute | solution.py:787
  28.1 19.0 %all-to-all-start.1 = ((f32[128,2,128]{2,1,0:T(2,128)}), f32[128,2,128]{2,1,0:T(2,128)S(1)}, u32[]{:S(2)}, u32[]{:S(2)}) async-start(f32[128,2,128]{2,1,0:T(2,128)} %bitcast.77), calls=%async_computation.1 | async-start | bytes 262144 | tf_op jit(solution)/shard_map/all_to_all | solution.py:879
  37.8 26.0 %copy-start = (f32[8,4,128,128]{3,2,1,0:T(8,128)S(1)}, f32[8,4,128,128]{3,2,1,0:T(8,128)}, u32[]{:S(2)}) copy-start(f32[8,4,128,128]{3,2,1,0:T(8,128)} %param.21) | copy-start | bytes 6291460
  47.8 16.0 %all-to-all-start.2 = ((f32[128,2,128]{2,1,0:T(2,128)}), f32[128,2,128]{2,1,0:T(2,128)S(1)}, u32[]{:S(2)}, u32[]{:S(2)}) async-start(f32[128,2,128]{2,1,0:T(2,128)} %bitcast.74), calls=%async_computation.2 | async-start | bytes 262144 | tf_op jit(solution)/shard_map/all_to_all | solution.py:887
  54.4 11.0 %collective-permute-start.4 = (f32[64,256]{1,0:T(8,128)}, f32[64,256]{1,0:T(8,128)S(1)}, u32[]{:S(2)}, u32[]{:S(2)}) collective-permute-start(f32[64,256]{1,0:T(8,128)} %get-tuple-element.125), channel_id=1, source_target_pairs={{0,16},{32,48},{64,80},{96,112},{16,0},{48,32},{80,64},{112,96},{1... | collective-permute-start | bytes 196616 | tf_op jit(solution)/shard_map/ppermute | solution.py:787
  54.7 10.8 %collective-permute-start.5 = (f32[64,256]{1,0:T(8,128)}, f32[64,256]{1,0:T(8,128)S(1)}, u32[]{:S(2)}, u32[]{:S(2)}) collective-permute-start(f32[64,256]{1,0:T(8,128)} %get-tuple-element.126), channel_id=1, source_target_pairs={{16,32},{48,64},{80,96},{32,16},{64,48},{96,80},{17,33},{49,65},{8... | collective-permute-start | bytes 196616 | tf_op jit(solution)/shard_map/ppermute | solution.py:787
  55.3 10.1 %collective-permute-start.6 = (f32[16,256]{1,0:T(8,128)}, f32[16,256]{1,0:T(8,128)S(1)}, u32[]{:S(2)}, u32[]{:S(2)}) collective-permute-start(f32[16,256]{1,0:T(8,128)} %get-tuple-element.127), channel_id=1, source_target_pairs={{0,1},{2,3},{4,5},{6,7},{8,9},{10,11},{12,13},{14,15},{1,0},{3,2},... | collective-permute-start | bytes 49160 | tf_op jit(solution)/shard_map/ppermute | solution.py:787
  56.9 8.5 %collective-permute-start.7 = (f32[16,256]{1,0:T(8,128)}, f32[16,256]{1,0:T(8,128)S(1)}, u32[]{:S(2)}, u32[]{:S(2)}) collective-permute-start(f32[16,256]{1,0:T(8,128)} %get-tuple-element.128), channel_id=1, source_target_pairs={{1,2},{3,4},{5,6},{7,8},{9,10},{11,12},{13,14},{2,1},{4,3},{6,5},{... | collective-permute-start | bytes 49160 | tf_op jit(solution)/shard_map/ppermute | solution.py:787
  65.5 14.6 %all-to-all-start.3 = ((f32[16,40,128]{2,1,0:T(8,128)}), f32[16,40,128]{2,1,0:T(8,128)S(1)}, u32[]{:S(2)}, u32[]{:S(2)}) async-start(f32[16,40,128]{2,1,0:T(8,128)} %bitcast.75), calls=%async_computation.3 | async-start | bytes 655360 | tf_op jit(solution)/shard_map/all_to_all | solution.py:906
  78.6 22.2 %copy-start.5 = (f32[64,256]{1,0:T(8,128)S(1)}, f32[64,256]{1,0:T(8,128)}, u32[]{:S(2)}) copy-start(f32[64,256]{1,0:T(8,128)} %get-tuple-element.150) | copy-start | bytes 196612
  78.6 22.3 %copy-start.4 = (f32[64,256]{1,0:T(8,128)S(1)}, f32[64,256]{1,0:T(8,128)}, u32[]{:S(2)}) copy-start(f32[64,256]{1,0:T(8,128)} %get-tuple-element.151) | copy-start | bytes 196612
  80.1 10.8 %all-to-all-start.4 = ((f32[8,32,128]{2,1,0:T(8,128)}), f32[8,32,128]{2,1,0:T(8,128)S(1)}, u32[]{:S(2)}, u32[]{:S(2)}) async-start(f32[8,32,128]{2,1,0:T(8,128)} %bitcast.79), calls=%async_computation.4 | async-start | bytes 262144 | tf_op jit(solution)/shard_map/all_to_all | solution.py:922
  93.5 16.0 %all-to-all-start.5 = ((f32[16,64,128]{2,1,0:T(8,128)}), f32[16,64,128]{2,1,0:T(8,128)S(1)}, u32[]{:S(2)}, u32[]{:S(2)}) async-start(f32[16,64,128]{2,1,0:T(8,128)} %bitcast.73), calls=%async_computation.5 | async-start | bytes 1048576 | tf_op jit(solution)/shard_map/all_to_all | solution.py:953
  100.8 1.3 collective-permute-start.8
  100.9 1.2 collective-permute-start.9
  112.2 15.0 %all-to-all-start.6 = ((f32[16,72,128]{2,1,0:T(8,128)}), f32[16,72,128]{2,1,0:T(8,128)S(1)}, u32[]{:S(2)}, u32[]{:S(2)}) async-start(f32[16,72,128]{2,1,0:T(8,128)} %bitcast.71), calls=%async_computation.6 | async-start | bytes 1179648 | tf_op jit(solution)/shard_map/all_to_all | solution.py:958
  118.2 1.4 collective-permute-start.10
  119.6 4.9 %collective-permute-start.13 = (f32[32,128]{1,0:T(8,128)S(1)}, f32[32,128]{1,0:T(8,128)S(1)}, u32[]{:S(2)}, u32[]{:S(2)}) collective-permute-start(f32[32,128]{1,0:T(8,128)S(1)} %constant_dynamic-update-slice_fusion), channel_id=1, source_target_pairs={{0,96},{16,112},{32,64},{48,80},{64,32},{80,48},{96,0},{112,16},{1... | collective-permute-start | bytes 49160 | tf_op jit(solution)/shard_map/ppermute | solution.py:962
  120.7 5.2 %collective-permute-start.12 = (f32[32,128]{1,0:T(8,128)S(1)}, f32[32,128]{1,0:T(8,128)S(1)}, u32[]{:S(2)}, u32[]{:S(2)}) collective-permute-start(f32[32,128]{1,0:T(8,128)S(1)} %constant_dynamic-update-slice_fusion), channel_id=1, source_target_pairs={{0,64},{16,80},{32,96},{48,112},{64,0},{80,16},{96,32},{112,48},{1... | collective-permute-start | bytes 49160 | tf_op jit(solution)/shard_map/ppermute | solution.py:962
  122.2 3.8 %collective-permute-start.11 = (f32[32,128]{1,0:T(8,128)S(1)}, f32[32,128]{1,0:T(8,128)S(1)}, u32[]{:S(2)}, u32[]{:S(2)}) collective-permute-start(f32[32,128]{1,0:T(8,128)S(1)} %constant_dynamic-update-slice_fusion), channel_id=1, source_target_pairs={{0,32},{16,48},{32,0},{48,16},{64,96},{80,112},{96,64},{112,80},{1... | collective-permute-start | bytes 49160 | tf_op jit(solution)/shard_map/ppermute | solution.py:962
  129.7 13.1 %all-to-all-start.7 = ((f32[16,40,128]{2,1,0:T(8,128)}), f32[16,40,128]{2,1,0:T(8,128)S(1)}, u32[]{:S(2)}, u32[]{:S(2)}) async-start(f32[16,40,128]{2,1,0:T(8,128)} %bitcast.76), calls=%async_computation.7 | async-start | bytes 655360 | tf_op jit(solution)/shard_map/all_to_all | solution.py:968
  142.4 9.9 %copy-start.7 = (f32[64,256]{1,0:T(8,128)S(1)}, f32[64,256]{1,0:T(8,128)}, u32[]{:S(2)}) copy-start(f32[64,256]{1,0:T(8,128)} %get-tuple-element.189) | copy-start | bytes 196612
  142.4 10.0 %copy-start.6 = (f32[64,256]{1,0:T(8,128)S(1)}, f32[64,256]{1,0:T(8,128)}, u32[]{:S(2)}) copy-start(f32[64,256]{1,0:T(8,128)} %get-tuple-element.190) | copy-start | bytes 196612
  145.3 15.5 %all-to-all-start.8 = ((f32[16,72,128]{2,1,0:T(8,128)}), f32[16,72,128]{2,1,0:T(8,128)S(1)}, u32[]{:S(2)}, u32[]{:S(2)}) async-start(f32[16,72,128]{2,1,0:T(8,128)} %bitcast.72), calls=%async_computation.8 | async-start | bytes 1179648 | tf_op jit(solution)/shard_map/all_to_all | solution.py:985
  152.3 2.6 %collective-permute-start.14 = (f32[64,256]{1,0:T(8,128)S(1)}, f32[64,256]{1,0:T(8,128)S(1)}, u32[]{:S(2)}, u32[]{:S(2)}) collective-permute-start(f32[64,256]{1,0:T(8,128)S(1)} %copy-done.7), channel_id=1, source_target_pairs={{0,16},{32,48},{64,80},{96,112},{16,0},{48,32},{80,64},{112,96},{1... | collective-permute-start | bytes 196616 | tf_op jit(solution)/shard_map/ppermute | solution.py:787
  152.4 2.5 %collective-permute-start.15 = (f32[64,256]{1,0:T(8,128)S(1)}, f32[64,256]{1,0:T(8,128)S(1)}, u32[]{:S(2)}, u32[]{:S(2)}) collective-permute-start(f32[64,256]{1,0:T(8,128)S(1)} %copy-done.6), channel_id=1, source_target_pairs={{16,32},{48,64},{80,96},{32,16},{64,48},{96,80},{17,33},{49,65},{8... | collective-permute-start | bytes 196616 | tf_op jit(solution)/shard_map/ppermute | solution.py:787
  163.1 11.7 %all-to-all-start.9 = ((f32[16,1,128]{2,1,0:T(1,128)}), f32[16,1,128]{2,1,0:T(1,128)S(1)}, u32[]{:S(2)}, u32[]{:S(2)}) async-start(f32[16,1,128]{2,1,0:T(1,128)} %bitcast.86), calls=%async_computation.9 | async-start | bytes 16384 | tf_op jit(solution)/shard_map/all_to_all | solution.py:996

commit v8 on v7

--- a/solution.py
+++ b/solution.py
@@ -98,20 +98,6 @@
     return out[:, :width] + out[:, width:]
 
 
-def split(v):
-    top = v.astype(BF16)
-    rest = v - top.astype(F32)
-    middle = rest.astype(BF16)
-    low = (rest - middle.astype(F32)).astype(BF16)
-    return jnp.concatenate([top, middle, low], axis=1)
-
-
-def pick(chosen, v):
-    width = v.shape[1]
-    out = jnp.dot(chosen, split(v), preferred_element_type=F32)
-    return out[:, :width] + out[:, width : 2 * width] + out[:, 2 * width :]
-
-
 def total(v):
     return jnp.sum(jnp.sum(v, axis=1, keepdims=True), axis=0, keepdims=True)
 
@@ -223,7 +209,7 @@
     chosen = jnp.concatenate(
         [ones_where(iota((LANES, LANES), 1) == by_slot(message, k)[2]) for k in range(CAP)], axis=0
     )
-    found = pick(chosen, x)
+    found = pick_rounded(chosen, x)
     lane = iota((LANES, LANES), 1)
     out = jnp.zeros((LANES, LANES), F32)
     for k in range(CAP):
@@ -244,7 +230,7 @@
             jnp.where(lane == by_slot(message, k)[3], v[:, k : k + 1], 0.0) for k in range(CAP)
         ]
         wide.append(jnp.concatenate(spread, axis=0))
-    return [pick(chosen, v) for v in wide]
+    return [pick_rounded(chosen, v) for v in wide]
 
 
 def kappa_of(message):
@@ -409,7 +395,7 @@
     back = jnp.concatenate(
         [got[s * step + rows : s * step + rows + tiles, :] for s in range(shards)], axis=0
     )
-    return own + pick(chosen[...], back)
+    return own + pick_rounded(chosen[...], back)
 
 
 def start_body(at, cols, tiles, got, diag, r_out, weight_out, send, block):

time: 179 us -> 178 us (level)
  no operation moved by 1% of the time
where the time goes in v8:
time: 178 us; the launch traced here: 176 us
  starting transfers between devices  86.7 us (49%)
  Pallas kernels  51.3 us (29%)
  waiting for transfers between devices  35.8 us (20%)
    all_to_all x6, starting transfers between devices, body(): arrived = over_frac(send)  37.6 us
    pallas_call x12, Pallas kernels, call(): pl.pallas_call(body, grid=(1,), out_shape=outs, in_specs=[SMEM] * len(sca...  25.5 us
    pallas_call x4, Pallas kernels, sweep(): pl.pallas_call(functools.partial(sweep_body, first=first, last=last, flux...  23.9 us
    all_to_all x6, waiting for transfers between devices, body(): arrived = over_frac(send)  18.7 us
    ppermute x12, starting transfers between devices, swap(): return lax.ppermute(v, axis, pairs + [(b, a) for a, b in pairs])  13.8 us
    all_to_all x1, starting transfers between devices, body(): got = everyone(send)  10.2 us
    all_to_all x1, starting transfers between devices, body(): reduced = everyone(send)  9.67 us
    all_to_all x1, starting transfers between devices, body(): residuals = everyone(send)  6.6 us
  transfers between devices with their start and end apart: 26, of which 14 were waited for; matrix products, arithmetic and copies ran while one was open for 0% of the time, Pallas kernels for 20%

profile of v8, /device:TPU:32, one launch (start us, length us, event | category | flops | bytes accessed | tf_op | source)
XLA Modules:
  0.0 175.5 jit_solution(4938703054572261727)
XLA Ops:
  0.7 1.8 %pack.1 = (f32[256,128]{1,0:T(8,128)}, s32[1,512]{1,0:T(1,128)}) custom-call(s32[2]{0:T(128)S(1)} %pad_add_fusion.at, s32[4,8]{1,0:T(4,128)} %bitcast.60, s32[1,512]{1,0:T(1,128)} %bitcast.80, s32[1,512]{1,0:T(1,128)} %bitcast.90, s32[1,512]{1,0:T(1,128)} %bitcast.82, f32[1,512]{1,0:T(1,128)} %bitcast.84, f32[8,128]{1,0:T(8,128)} %bitcast.88), custom_call_target="tpu_custom_call" | custom-call | flops 1000000 | bytes 1000000 | tf_op jit(solution)/shard_map/pack/pallas_call | solution.py:56
  2.5 10.2 %all-to-all-start = ((f32[128,2,128]{2,1,0:T(2,128)}), f32[128,2,128]{2,1,0:T(2,128)S(1)}, u32[]{:S(2)}, u32[]{:S(2)}) async-start(f32[128,2,128]{2,1,0:T(2,128)} %bitcast.78), calls=%async_computation | async-start | bytes 262144 | tf_op jit(solution)/shard_map/all_to_all | solution.py:842
  12.8 1.9 %edges.1 = (f32[128,256]{1,0:T(8,128)}, f32[128,256]{1,0:T(8,128)}, f32[32,256]{1,0:T(8,128)}, f32[32,256]{1,0:T(8,128)}) custom-call(s32[2]{0:T(128)S(1)} %pad_add_fusion.at, f32[16,64,256]{2,1,0:T(8,128)} %p_after.1, f32[16,64,256]{2,1,0:T(8,128)} %p_after.1, f32[16,64,256]{2,1,0:T(8,128)} %p_after.1, f32[16,64,256]{2,1,0:T(8,128)} %p_after.1, ...), custom_call_target="tpu_custom_call" | custom-call | tf_op jit(solution)/shard_map/edges/pallas_call | solution.py:533
  14.7 1.5 collective-permute-start.2
  16.2 3.8 %collective-permute-start.3 = (f32[32,256]{1,0:T(8,128)}, f32[32,256]{1,0:T(8,128)S(1)}, u32[]{:S(2)}, u32[]{:S(2)}) collective-permute-start(f32[32,256]{1,0:T(8,128)} %get-tuple-element.113), channel_id=1, source_target_pairs={{1,2},{3,4},{5,6},{7,8},{9,10},{11,12},{13,14},{2,1},{4,3},{6,5},{... | collective-permute-start | bytes 98312 | tf_op jit(solution)/shard_map/ppermute | solution.py:773
  20.1 0.7 collective-permute-start.1
  20.8 1.4 all-to-all-done
  22.2 5.4 %first.1 = (f32[256,128]{1,0:T(8,128)}, f32[128,128]{1,0:T(8,128)}, f32[128,128]{1,0:T(8,128)}, f32[128,128]{1,0:T(8,128)}, f32[128,128]{1,0:T(8,128)}) custom-call(s32[2]{0:T(128)S(1)} %pad_add_fusion.at, s32[4,8]{1,0:T(4,128)S(1)} %bitcast.61, f32[32,128,128]{2,1,0:T(8,128)} %bitcast.36, f32[1024,256]{1,0:T(8,128)} %bitcast.70, f32[256,128]{1,0:T(8,128)S(1)} %bitcast.50, ...), custom_call_target="tpu_custom_call" | custom-call | flops 2000000000 | bytes 1000000 | tf_op jit(solution)/shard_map/first/pallas_call | solution.py:56
  27.6 9.7 %all-to-all-start.1 = ((f32[128,2,128]{2,1,0:T(2,128)}), f32[128,2,128]{2,1,0:T(2,128)S(1)}, u32[]{:S(2)}, u32[]{:S(2)}) async-start(f32[128,2,128]{2,1,0:T(2,128)} %bitcast.77), calls=%async_computation.1 | async-start | bytes 262144 | tf_op jit(solution)/shard_map/all_to_all | solution.py:865
  37.3 6.2 %sweep.4 = (f32[16,64,256]{2,1,0:T(8,128)}, f32[16,64,256]{2,1,0:T(8,128)}, f32[16,64,256]{2,1,0:T(8,128)}, f32[64,256]{1,0:T(8,128)}, f32[64,256]{1,0:T(8,128)}, /*index=5*/f32[16,256]{1,0:T(8,128)}, f32[16,256]{1,0:T(8,128)}) custom-call(s32[2]{0:T(128)S(1)} %pad_add_fusion.at, f32[128,256]{1,0:T(8,128)S(1)} %collective-permute-done.xa.cxa, ...), custom_call_target="tpu_custom_call" | custom-call | flops 6000000 | bytes 8388608 | tf_op jit(solution)/shard_map/sweep/pallas_call | solution.py:746
  43.5 3.2 %all-to-all-done.1 = f32[128,2,128]{2,1,0:T(2,128)S(1)} async-done(((f32[128,2,128]{2,1,0:T(2,128)}), f32[128,2,128]{2,1,0:T(2,128)S(1)}, u32[]{:S(2)}, u32[]{:S(2)}) %all-to-all-start.1) | async-done | bytes 131104 | tf_op jit(solution)/shard_map/all_to_all | solution.py:865
  46.6 0.7 sums.1
  47.3 6.6 %all-to-all-start.2 = ((f32[128,2,128]{2,1,0:T(2,128)}), f32[128,2,128]{2,1,0:T(2,128)S(1)}, u32[]{:S(2)}, u32[]{:S(2)}) async-start(f32[128,2,128]{2,1,0:T(2,128)} %bitcast.74), calls=%async_computation.2 | async-start | bytes 262144 | tf_op jit(solution)/shard_map/all_to_all | solution.py:873
  54.8 1.6 collective-permute-start.6
  56.4 3.8 %collective-permute-start.7 = (f32[16,256]{1,0:T(8,128)}, f32[16,256]{1,0:T(8,128)S(1)}, u32[]{:S(2)}, u32[]{:S(2)}) collective-permute-start(f32[16,256]{1,0:T(8,128)} %get-tuple-element.128), channel_id=1, source_target_pairs={{1,2},{3,4},{5,6},{7,8},{9,10},{11,12},{13,14},{2,1},{4,3},{6,5},{... | collective-permute-start | bytes 49160 | tf_op jit(solution)/shard_map/ppermute | solution.py:773
  60.2 3.1 %all-to-all-done.2 = f32[128,2,128]{2,1,0:T(2,128)S(1)} async-done(((f32[128,2,128]{2,1,0:T(2,128)}), f32[128,2,128]{2,1,0:T(2,128)S(1)}, u32[]{:S(2)}, u32[]{:S(2)}) %all-to-all-start.2) | async-done | bytes 131104 | tf_op jit(solution)/shard_map/all_to_all | solution.py:873
  63.3 1.7 start.1
  65.0 6.1 %all-to-all-start.3 = ((f32[16,40,128]{2,1,0:T(8,128)}), f32[16,40,128]{2,1,0:T(8,128)S(1)}, u32[]{:S(2)}, u32[]{:S(2)}) async-start(f32[16,40,128]{2,1,0:T(8,128)} %bitcast.75), calls=%async_computation.3 | async-start | bytes 655360 | tf_op jit(solution)/shard_map/all_to_all | solution.py:892
  71.0 7.0 %sweep.5 = (f32[16,64,256]{2,1,0:T(8,128)}, f32[128,128]{1,0:T(8,128)}, f32[256,128]{1,0:T(8,128)}, f32[64,256]{1,0:T(8,128)}, f32[64,256]{1,0:T(8,128)}, /*index=5*/f32[16,256]{1,0:T(8,128)}, f32[16,256]{1,0:T(8,128)}) custom-call(s32[2]{0:T(128)S(1)} %pad_add_fusion.at, f32[64,256]{1,0:T(8,128)S(1)} %collective-permute-done.4.xa, ...), custom_call_target="tpu_custom_call" | custom-call | flops 6000000 | bytes 8388608 | tf_op jit(solution)/shard_map/sweep/pallas_call | solution.py:746
  78.0 1.6 all-to-all-done.3
  79.6 4.6 %all-to-all-start.4 = ((f32[8,32,128]{2,1,0:T(8,128)}), f32[8,32,128]{2,1,0:T(8,128)S(1)}, u32[]{:S(2)}, u32[]{:S(2)}) async-start(f32[8,32,128]{2,1,0:T(8,128)} %bitcast.79), calls=%async_computation.4 | async-start | bytes 262144 | tf_op jit(solution)/shard_map/all_to_all | solution.py:908
  84.5 5.9 %all-to-all-done.4 = f32[8,32,128]{2,1,0:T(8,128)S(1)} async-done(((f32[8,32,128]{2,1,0:T(8,128)}), f32[8,32,128]{2,1,0:T(8,128)S(1)}, u32[]{:S(2)}, u32[]{:S(2)}) %all-to-all-start.4) | async-done | bytes 131104 | tf_op jit(solution)/shard_map/all_to_all | solution.py:908
  90.4 2.5 %step.5 = (f32[128,128]{1,0:T(8,128)}, f32[128,128]{1,0:T(8,128)}, f32[128,128]{1,0:T(8,128)}, f32[1024,128]{1,0:T(8,128)}) custom-call(s32[2]{0:T(128)S(1)} %pad_add_fusion.at, s32[4,8]{1,0:T(4,128)S(1)} %bitcast.63, f32[32,128,128]{2,1,0:T(8,128)S(1)} %bitcast.38, f32[640,128]{1,0:T(8,128)S(1)} %bitcast.46, bf16[128,512]{1,0:T(8,128)(2,1)S(1)} %columns.1.chosen, ...), custom_call_target="tpu_custom_call" | custom-call | flops 1000000 | bytes 1000000 | tf_op jit(solution)/shard_map/step/pallas_call | solution.py:56
  92.9 7.2 %all-to-all-start.5 = ((f32[16,64,128]{2,1,0:T(8,128)}), f32[16,64,128]{2,1,0:T(8,128)S(1)}, u32[]{:S(2)}, u32[]{:S(2)}) async-start(f32[16,64,128]{2,1,0:T(8,128)} %bitcast.73), calls=%async_computation.5 | async-start | bytes 1048576 | tf_op jit(solution)/shard_map/all_to_all | solution.py:939
  100.3 0.7 collective-permute-start.9
  101.5 7.5 %all-to-all-done.5 = f32[16,64,128]{2,1,0:T(8,128)S(1)} async-done(((f32[16,64,128]{2,1,0:T(8,128)}), f32[16,64,128]{2,1,0:T(8,128)S(1)}, u32[]{:S(2)}, u32[]{:S(2)}) %all-to-all-start.5) | async-done | bytes 524320 | tf_op jit(solution)/shard_map/all_to_all | solution.py:939
  109.0 2.5 %step.6 = (f32[128,128]{1,0:T(8,128)}, f32[128,128]{1,0:T(8,128)}, f32[128,128]{1,0:T(8,128)}, f32[1152,128]{1,0:T(8,128)}, f32[16,128]{1,0:T(8,128)}, /*index=5*/f32[128,128]{1,0:T(8,128)}) custom-call(s32[2]{0:T(128)S(1)} %pad_add_fusion.at, s32[4,8]{1,0:T(4,128)S(1)} %bitcast.64, f32[32,128,128]{2,1,0:T(8,128)S(1)} %bitcast.39, f32[1024,128]{1,0:T(8,128)S(1)} %bitcast.45, ...), custom_call_target="tpu_custom_call" | custom-call | flops 1000000 | bytes 1000000 | tf_op jit(solution)/shard_map/step/pallas_call | solution.py:56
  111.5 6.0 %all-to-all-start.6 = ((f32[16,72,128]{2,1,0:T(8,128)}), f32[16,72,128]{2,1,0:T(8,128)S(1)}, u32[]{:S(2)}, u32[]{:S(2)}) async-start(f32[16,72,128]{2,1,0:T(8,128)} %bitcast.71), calls=%async_computation.6 | async-start | bytes 1179648 | tf_op jit(solution)/shard_map/all_to_all | solution.py:944
  117.5 0.7 constant_dynamic-update-slice_fusion.1
  118.2 0.7 collective-permute-done.10.rest_0_
  118.9 1.2 collective-permute-start.13
  120.1 1.5 collective-permute-start.12
  121.6 1.5 collective-permute-start.11
  123.0 0.9 collective-permute-done.13.rest_3_
  123.9 1.5 collective-permute-done.12.rest_2_
  125.3 1.2 all-to-all-done.6
  126.5 2.4 %step.7 = (f32[128,128]{1,0:T(8,128)}, f32[128,128]{1,0:T(8,128)}, f32[128,128]{1,0:T(8,128)}, f32[640,128]{1,0:T(8,128)}, f32[16,256]{1,0:T(8,128)}, /*index=5*/f32[16,256]{1,0:T(8,128)}) custom-call(s32[2]{0:T(128)S(1)} %pad_add_fusion.at, s32[4,8]{1,0:T(4,128)S(1)} %bitcast.65, f32[32,128,128]{2,1,0:T(8,128)S(1)} %bitcast.40, f32[1152,128]{1,0:T(8,128)S(1)} %bitcast.43, ...), custom_call_target="tpu_custom_call" | custom-call | flops 1000000 | bytes 1000000 | tf_op jit(solution)/shard_map/step/pallas_call | solution.py:56
  129.0 6.1 %all-to-all-start.7 = ((f32[16,40,128]{2,1,0:T(8,128)}), f32[16,40,128]{2,1,0:T(8,128)S(1)}, u32[]{:S(2)}, u32[]{:S(2)}) async-start(f32[16,40,128]{2,1,0:T(8,128)} %bitcast.76), calls=%async_computation.7 | async-start | bytes 655360 | tf_op jit(solution)/shard_map/all_to_all | solution.py:954
  135.0 6.6 %sweep.6 = (f32[16,64,256]{2,1,0:T(8,128)}, f32[16,64,256]{2,1,0:T(8,128)}, f32[64,256]{1,0:T(8,128)}, f32[64,256]{1,0:T(8,128)}, f32[16,256]{1,0:T(8,128)}, /*index=5*/f32[16,256]{1,0:T(8,128)}) custom-call(s32[2]{0:T(128)S(1)} %pad_add_fusion.at, f32[64,256]{1,0:T(8,128)S(1)} %collective-permute-done.8.xa, f32[64,256]{1,0:T(8,128)S(1)} %collective-permute-done.9.xb, ...), custom_call_target="tpu_custom_call" | custom-call | flops 6000000 | bytes 8388608 | tf_op jit(solution)/shard_map/sweep/pallas_call | solution.py:746
  142.1 2.5 %step.8 = (f32[128,128]{1,0:T(8,128)}, f32[128,128]{1,0:T(8,128)}, f32[128,128]{1,0:T(8,128)}, f32[1152,128]{1,0:T(8,128)}) custom-call(s32[2]{0:T(128)S(1)} %pad_add_fusion.at, s32[4,8]{1,0:T(4,128)S(1)} %bitcast.66, f32[32,128,128]{2,1,0:T(8,128)S(1)} %bitcast.41, f32[640,128]{1,0:T(8,128)S(1)} %bitcast.47, bf16[128,512]{1,0:T(8,128)(2,1)S(1)} %columns.1.chosen, ...), custom_call_target="tpu_custom_call" | custom-call | flops 1000000 | bytes 1000000 | tf_op jit(solution)/shard_map/step/pallas_call | solution.py:56
  144.6 6.9 %all-to-all-start.8 = ((f32[16,72,128]{2,1,0:T(8,128)}), f32[16,72,128]{2,1,0:T(8,128)S(1)}, u32[]{:S(2)}, u32[]{:S(2)}) async-start(f32[16,72,128]{2,1,0:T(8,128)} %bitcast.72), calls=%async_computation.8 | async-start | bytes 1179648 | tf_op jit(solution)/shard_map/all_to_all | solution.py:971
  152.2 1.9 %home.1 = f32[1,512]{1,0:T(1,128)} custom-call(f32[128,128]{1,0:T(8,128)} %get-tuple-element.187.got, s32[1,512]{1,0:T(1,128)} %bitcast.81, s32[1,512]{1,0:T(1,128)} %get-tuple-element.188.slot, s32[1,512]{1,0:T(1,128)} %bitcast.83, f32[1,512]{1,0:T(1,128)} %bitcast.85, f32[128,128]{1,0:T(8,128)} %get-tuple-element.171.rest_3_.rest_0_.x), custom_call_target="tpu_custom_call" | custom-call | flops 1000000 | bytes 1000000 | tf_op jit(solution)/shard_map/home/pallas_call | solution.py:56
  154.1 6.0 %all-to-all-done.8 = f32[16,72,128]{2,1,0:T(8,128)S(1)} async-done(((f32[16,72,128]{2,1,0:T(8,128)}), f32[16,72,128]{2,1,0:T(8,128)S(1)}, u32[]{:S(2)}, u32[]{:S(2)}) %all-to-all-start.8) | async-done | bytes 589856 | tf_op jit(solution)/shard_map/all_to_all | solution.py:971
  160.1 2.2 %step.9 = (f32[128,128]{1,0:T(8,128)}, f32[128,128]{1,0:T(8,128)}, f32[128,128]{1,0:T(8,128)}, f32[16,128]{1,0:T(8,128)}, f32[16,256]{1,0:T(8,128)}, /*index=5*/f32[16,256]{1,0:T(8,128)}) custom-call(s32[2]{0:T(128)S(1)} %pad_add_fusion.at, s32[4,8]{1,0:T(4,128)S(1)} %bitcast.67, f32[32,128,128]{2,1,0:T(8,128)S(1)} %bitcast.42, f32[1152,128]{1,0:T(8,128)S(1)} %bitcast.44, ...), custom_call_target="tpu_custom_call" | custom-call | flops 1000000 | bytes 1000000 | tf_op jit(solution)/shard_map/step/pallas_call | solution.py:56
  162.3 5.4 %all-to-all-start.9 = ((f32[16,1,128]{2,1,0:T(1,128)}), f32[16,1,128]{2,1,0:T(1,128)S(1)}, u32[]{:S(2)}, u32[]{:S(2)}) async-start(f32[16,1,128]{2,1,0:T(1,128)} %bitcast.86), calls=%async_computation.9 | async-start | bytes 16384 | tf_op jit(solution)/shard_map/all_to_all | solution.py:982
  167.6 4.2 %sweep.7 = f32[16,64,256]{2,1,0:T(8,128)} custom-call(s32[2]{0:T(128)S(1)} %pad_add_fusion.at, f32[64,256]{1,0:T(8,128)S(1)} %collective-permute-done.14.xa, f32[64,256]{1,0:T(8,128)S(1)} %collective-permute-done.15.xb, f32[16,256]{1,0:T(8,128)} %get-tuple-element.197.ya, f32[16,256]{1,0:T(8,128)} %get-tuple-element.198.yb, ...), custom_call_target="tpu_custom_call" | custom-call | flops 6000000 | bytes 8388608 | tf_op jit(solution)/shard_map/sweep/pallas_call | solution.py:746
  171.8 2.1 %all-to-all-done.9 = f32[16,1,128]{2,1,0:T(1,128)S(1)} async-done(((f32[16,1,128]{2,1,0:T(1,128)}), f32[16,1,128]{2,1,0:T(1,128)S(1)}, u32[]{:S(2)}, u32[]{:S(2)}) %all-to-all-start.9) | async-done | bytes 8224 | tf_op jit(solution)/shard_map/all_to_all | solution.py:982
  173.9 1.6 final.1
  (40 shorter events, 3.2 us)
Async XLA Ops:
  2.5 19.6 %all-to-all-start = ((f32[128,2,128]{2,1,0:T(2,128)}), f32[128,2,128]{2,1,0:T(2,128)S(1)}, u32[]{:S(2)}, u32[]{:S(2)}) async-start(f32[128,2,128]{2,1,0:T(2,128)} %bitcast.78), calls=%async_computation | async-start | bytes 262144 | tf_op jit(solution)/shard_map/all_to_all | solution.py:842
  12.8 9.4 %copy-start.1 = (f32[1024]{0:T(1024)S(1)}, f32[1024]{0:T(1024)}, u32[]{:S(2)}) copy-start(f32[1024]{0:T(1024)} %param.23) | copy-start | bytes 12292
  12.8 9.4 %copy-start.2 = (s32[8,4]{0,1:T(4,128)S(1)}, s32[8,4]{0,1:T(4,128)}, u32[]{:S(2)}) copy-start(s32[8,4]{0,1:T(4,128)} %param.22) | copy-start | bytes 388
  12.8 9.4 %copy-start.3 = (f32[1024]{0:T(1024)S(1)}, f32[1024]{0:T(1024)}, u32[]{:S(2)}) copy-start(f32[1024]{0:T(1024)} %param.24) | copy-start | bytes 12292
  14.7 12.9 %collective-permute-start.2 = (f32[32,256]{1,0:T(8,128)}, f32[32,256]{1,0:T(8,128)S(1)}, u32[]{:S(2)}, u32[]{:S(2)}) collective-permute-start(f32[32,256]{1,0:T(8,128)} %get-tuple-element.112), channel_id=1, source_target_pairs={{0,1},{2,3},{4,5},{6,7},{8,9},{10,11},{12,13},{14,15},{1,0},{3,2},... | collective-permute-start | bytes 98312 | tf_op jit(solution)/shard_map/ppermute | solution.py:773
  16.2 11.4 %collective-permute-start.3 = (f32[32,256]{1,0:T(8,128)}, f32[32,256]{1,0:T(8,128)S(1)}, u32[]{:S(2)}, u32[]{:S(2)}) collective-permute-start(f32[32,256]{1,0:T(8,128)} %get-tuple-element.113), channel_id=1, source_target_pairs={{1,2},{3,4},{5,6},{7,8},{9,10},{11,12},{13,14},{2,1},{4,3},{6,5},{... | collective-permute-start | bytes 98312 | tf_op jit(solution)/shard_map/ppermute | solution.py:773
  20.0 7.6 %collective-permute-start = (f32[128,256]{1,0:T(8,128)}, f32[128,256]{1,0:T(8,128)S(1)}, u32[]{:S(2)}, u32[]{:S(2)}) collective-permute-start(f32[128,256]{1,0:T(8,128)} %get-tuple-element.110), channel_id=1, source_target_pairs={{0,16},{32,48},{64,80},{96,112},{16,0},{48,32},{80,64},{112,96},{1... | collective-permute-start | bytes 393224 | tf_op jit(solution)/shard_map/ppermute | solution.py:773
  20.1 7.5 %collective-permute-start.1 = (f32[128,256]{1,0:T(8,128)}, f32[128,256]{1,0:T(8,128)S(1)}, u32[]{:S(2)}, u32[]{:S(2)}) collective-permute-start(f32[128,256]{1,0:T(8,128)} %get-tuple-element.111), channel_id=1, source_target_pairs={{16,32},{48,64},{80,96},{32,16},{64,48},{96,80},{17,33},{49,65},{8... | collective-permute-start | bytes 393224 | tf_op jit(solution)/shard_map/ppermute | solution.py:773
  27.6 19.0 %all-to-all-start.1 = ((f32[128,2,128]{2,1,0:T(2,128)}), f32[128,2,128]{2,1,0:T(2,128)S(1)}, u32[]{:S(2)}, u32[]{:S(2)}) async-start(f32[128,2,128]{2,1,0:T(2,128)} %bitcast.77), calls=%async_computation.1 | async-start | bytes 262144 | tf_op jit(solution)/shard_map/all_to_all | solution.py:865
  37.3 26.0 %copy-start = (f32[8,4,128,128]{3,2,1,0:T(8,128)S(1)}, f32[8,4,128,128]{3,2,1,0:T(8,128)}, u32[]{:S(2)}) copy-start(f32[8,4,128,128]{3,2,1,0:T(8,128)} %param.21) | copy-start | bytes 6291460
  47.3 16.0 %all-to-all-start.2 = ((f32[128,2,128]{2,1,0:T(2,128)}), f32[128,2,128]{2,1,0:T(2,128)S(1)}, u32[]{:S(2)}, u32[]{:S(2)}) async-start(f32[128,2,128]{2,1,0:T(2,128)} %bitcast.74), calls=%async_computation.2 | async-start | bytes 262144 | tf_op jit(solution)/shard_map/all_to_all | solution.py:873
  53.9 11.0 %collective-permute-start.4 = (f32[64,256]{1,0:T(8,128)}, f32[64,256]{1,0:T(8,128)S(1)}, u32[]{:S(2)}, u32[]{:S(2)}) collective-permute-start(f32[64,256]{1,0:T(8,128)} %get-tuple-element.125), channel_id=1, source_target_pairs={{0,16},{32,48},{64,80},{96,112},{16,0},{48,32},{80,64},{112,96},{1... | collective-permute-start | bytes 196616 | tf_op jit(solution)/shard_map/ppermute | solution.py:773
  54.2 10.8 %collective-permute-start.5 = (f32[64,256]{1,0:T(8,128)}, f32[64,256]{1,0:T(8,128)S(1)}, u32[]{:S(2)}, u32[]{:S(2)}) collective-permute-start(f32[64,256]{1,0:T(8,128)} %get-tuple-element.126), channel_id=1, source_target_pairs={{16,32},{48,64},{80,96},{32,16},{64,48},{96,80},{17,33},{49,65},{8... | collective-permute-start | bytes 196616 | tf_op jit(solution)/shard_map/ppermute | solution.py:773
  54.8 10.1 %collective-permute-start.6 = (f32[16,256]{1,0:T(8,128)}, f32[16,256]{1,0:T(8,128)S(1)}, u32[]{:S(2)}, u32[]{:S(2)}) collective-permute-start(f32[16,256]{1,0:T(8,128)} %get-tuple-element.127), channel_id=1, source_target_pairs={{0,1},{2,3},{4,5},{6,7},{8,9},{10,11},{12,13},{14,15},{1,0},{3,2},... | collective-permute-start | bytes 49160 | tf_op jit(solution)/shard_map/ppermute | solution.py:773
  56.4 8.5 %collective-permute-start.7 = (f32[16,256]{1,0:T(8,128)}, f32[16,256]{1,0:T(8,128)S(1)}, u32[]{:S(2)}, u32[]{:S(2)}) collective-permute-start(f32[16,256]{1,0:T(8,128)} %get-tuple-element.128), channel_id=1, source_target_pairs={{1,2},{3,4},{5,6},{7,8},{9,10},{11,12},{13,14},{2,1},{4,3},{6,5},{... | collective-permute-start | bytes 49160 | tf_op jit(solution)/shard_map/ppermute | solution.py:773
  65.0 14.6 %all-to-all-start.3 = ((f32[16,40,128]{2,1,0:T(8,128)}), f32[16,40,128]{2,1,0:T(8,128)S(1)}, u32[]{:S(2)}, u32[]{:S(2)}) async-start(f32[16,40,128]{2,1,0:T(8,128)} %bitcast.75), calls=%async_computation.3 | async-start | bytes 655360 | tf_op jit(solution)/shard_map/all_to_all | solution.py:892
  78.0 22.1 %copy-start.5 = (f32[64,256]{1,0:T(8,128)S(1)}, f32[64,256]{1,0:T(8,128)}, u32[]{:S(2)}) copy-start(f32[64,256]{1,0:T(8,128)} %get-tuple-element.150) | copy-start | bytes 196612
  78.0 22.2 %copy-start.4 = (f32[64,256]{1,0:T(8,128)S(1)}, f32[64,256]{1,0:T(8,128)}, u32[]{:S(2)}) copy-start(f32[64,256]{1,0:T(8,128)} %get-tuple-element.151) | copy-start | bytes 196612
  79.6 10.8 %all-to-all-start.4 = ((f32[8,32,128]{2,1,0:T(8,128)}), f32[8,32,128]{2,1,0:T(8,128)S(1)}, u32[]{:S(2)}, u32[]{:S(2)}) async-start(f32[8,32,128]{2,1,0:T(8,128)} %bitcast.79), calls=%async_computation.4 | async-start | bytes 262144 | tf_op jit(solution)/shard_map/all_to_all | solution.py:908
  92.9 16.0 %all-to-all-start.5 = ((f32[16,64,128]{2,1,0:T(8,128)}), f32[16,64,128]{2,1,0:T(8,128)S(1)}, u32[]{:S(2)}, u32[]{:S(2)}) async-start(f32[16,64,128]{2,1,0:T(8,128)} %bitcast.73), calls=%async_computation.5 | async-start | bytes 1048576 | tf_op jit(solution)/shard_map/all_to_all | solution.py:939
  100.2 1.3 collective-permute-start.8
  100.3 1.2 collective-permute-start.9
  111.5 15.0 %all-to-all-start.6 = ((f32[16,72,128]{2,1,0:T(8,128)}), f32[16,72,128]{2,1,0:T(8,128)S(1)}, u32[]{:S(2)}, u32[]{:S(2)}) async-start(f32[16,72,128]{2,1,0:T(8,128)} %bitcast.71), calls=%async_computation.6 | async-start | bytes 1179648 | tf_op jit(solution)/shard_map/all_to_all | solution.py:944
  117.5 1.4 collective-permute-start.10
  118.9 4.9 %collective-permute-start.13 = (f32[32,128]{1,0:T(8,128)S(1)}, f32[32,128]{1,0:T(8,128)S(1)}, u32[]{:S(2)}, u32[]{:S(2)}) collective-permute-start(f32[32,128]{1,0:T(8,128)S(1)} %constant_dynamic-update-slice_fusion), channel_id=1, source_target_pairs={{0,96},{16,112},{32,64},{48,80},{64,32},{80,48},{96,0},{112,16},{1... | collective-permute-start | bytes 49160 | tf_op jit(solution)/shard_map/ppermute | solution.py:948
  120.1 5.2 %collective-permute-start.12 = (f32[32,128]{1,0:T(8,128)S(1)}, f32[32,128]{1,0:T(8,128)S(1)}, u32[]{:S(2)}, u32[]{:S(2)}) collective-permute-start(f32[32,128]{1,0:T(8,128)S(1)} %constant_dynamic-update-slice_fusion), channel_id=1, source_target_pairs={{0,64},{16,80},{32,96},{48,112},{64,0},{80,16},{96,32},{112,48},{1... | collective-permute-start | bytes 49160 | tf_op jit(solution)/shard_map/ppermute | solution.py:948
  121.6 3.8 %collective-permute-start.11 = (f32[32,128]{1,0:T(8,128)S(1)}, f32[32,128]{1,0:T(8,128)S(1)}, u32[]{:S(2)}, u32[]{:S(2)}) collective-permute-start(f32[32,128]{1,0:T(8,128)S(1)} %constant_dynamic-update-slice_fusion), channel_id=1, source_target_pairs={{0,32},{16,48},{32,0},{48,16},{64,96},{80,112},{96,64},{112,80},{1... | collective-permute-start | bytes 49160 | tf_op jit(solution)/shard_map/ppermute | solution.py:948
  129.0 13.1 %all-to-all-start.7 = ((f32[16,40,128]{2,1,0:T(8,128)}), f32[16,40,128]{2,1,0:T(8,128)S(1)}, u32[]{:S(2)}, u32[]{:S(2)}) async-start(f32[16,40,128]{2,1,0:T(8,128)} %bitcast.76), calls=%async_computation.7 | async-start | bytes 655360 | tf_op jit(solution)/shard_map/all_to_all | solution.py:954
  141.6 9.8 %copy-start.7 = (f32[64,256]{1,0:T(8,128)S(1)}, f32[64,256]{1,0:T(8,128)}, u32[]{:S(2)}) copy-start(f32[64,256]{1,0:T(8,128)} %get-tuple-element.189) | copy-start | bytes 196612
  141.6 9.9 %copy-start.6 = (f32[64,256]{1,0:T(8,128)S(1)}, f32[64,256]{1,0:T(8,128)}, u32[]{:S(2)}) copy-start(f32[64,256]{1,0:T(8,128)} %get-tuple-element.190) | copy-start | bytes 196612
  144.6 15.5 %all-to-all-start.8 = ((f32[16,72,128]{2,1,0:T(8,128)}), f32[16,72,128]{2,1,0:T(8,128)S(1)}, u32[]{:S(2)}, u32[]{:S(2)}) async-start(f32[16,72,128]{2,1,0:T(8,128)} %bitcast.72), calls=%async_computation.8 | async-start | bytes 1179648 | tf_op jit(solution)/shard_map/all_to_all | solution.py:971
  151.5 2.6 %collective-permute-start.14 = (f32[64,256]{1,0:T(8,128)S(1)}, f32[64,256]{1,0:T(8,128)S(1)}, u32[]{:S(2)}, u32[]{:S(2)}) collective-permute-start(f32[64,256]{1,0:T(8,128)S(1)} %copy-done.7), channel_id=1, source_target_pairs={{0,16},{32,48},{64,80},{96,112},{16,0},{48,32},{80,64},{112,96},{1... | collective-permute-start | bytes 196616 | tf_op jit(solution)/shard_map/ppermute | solution.py:773
  151.6 2.5 %collective-permute-start.15 = (f32[64,256]{1,0:T(8,128)S(1)}, f32[64,256]{1,0:T(8,128)S(1)}, u32[]{:S(2)}, u32[]{:S(2)}) collective-permute-start(f32[64,256]{1,0:T(8,128)S(1)} %copy-done.6), channel_id=1, source_target_pairs={{16,32},{48,64},{80,96},{32,16},{64,48},{96,80},{17,33},{49,65},{8... | collective-permute-start | bytes 196616 | tf_op jit(solution)/shard_map/ppermute | solution.py:773
  162.3 11.7 %all-to-all-start.9 = ((f32[16,1,128]{2,1,0:T(1,128)}), f32[16,1,128]{2,1,0:T(1,128)S(1)}, u32[]{:S(2)}, u32[]{:S(2)}) async-start(f32[16,1,128]{2,1,0:T(1,128)} %bitcast.86), calls=%async_computation.9 | async-start | bytes 16384 | tf_op jit(solution)/shard_map/all_to_all | solution.py:982

commit v9 on v7

--- a/solution.py
+++ b/solution.py
@@ -516,7 +516,7 @@
 
 
 def final_body(at, got, x, r, d, out):
-    alpha = total(r[...] * r[...]) / total(got[...])
+    alpha = total(r[...] * r[...]) / total(got[pl.ds(0, LANES // CAP, stride=CAP), :])
     here = pl.ds(pl.multiple_of(CAP * at[1], CAP), CAP)
     out[...] = x[here, :] + alpha * d[here, :]
 
@@ -924,7 +924,7 @@
 
     def step(arrived, x, r, d, *more, ride=None, last=False, faces_in=False, faces=(), side=()):
         length = size + (shards + mats if ride == "reduce" else 0) + (2 * nx if faces else 0)
-        outs = [*[sent(LANES, LANES)] * 3, sent(shards * (1 if last else length), LANES)]
+        outs = [*[sent(LANES, LANES)] * 3, sent(shards * (rows if last else length), LANES)]
         if ride == "gather":
             outs += [sent(shards, LANES), sent(LANES, LANES)]
         if faces_in:

time: 179 us -> 179 us (level)
  no operation moved by 1% of the time
where the time goes in v9:
time: 179 us; the launch traced here: 177 us
  starting transfers between devices  86.9 us (49%)
  Pallas kernels  52.2 us (29%)
  waiting for transfers between devices  35.7 us (20%)
    all_to_all x6, starting transfers between devices, body(): arrived = over_frac(send)  37.7 us
    pallas_call x12, Pallas kernels, call(): pl.pallas_call(body, grid=(1,), out_shape=outs, in_specs=[SMEM] * len(sca...  26.3 us
    pallas_call x4, Pallas kernels, sweep(): pl.pallas_call(functools.partial(sweep_body, first=first, last=last, flux...  24 us
    all_to_all x6, waiting for transfers between devices, body(): arrived = over_frac(send)  18.6 us
    ppermute x12, starting transfers between devices, swap(): return lax.ppermute(v, axis, pairs + [(b, a) for a, b in pairs])  13.8 us
    all_to_all x1, starting transfers between devices, body(): got = everyone(send)  10.2 us
    all_to_all x1, starting transfers between devices, body(): reduced = everyone(send)  9.68 us
    all_to_all x1, starting transfers between devices, body(): residuals = everyone(send)  6.6 us
  transfers between devices with their start and end apart: 26, of which 14 were waited for; matrix products, arithmetic and copies ran while one was open for 0% of the time, Pallas kernels for 20%

profile of v9, /device:TPU:32, one launch (start us, length us, event | category | flops | bytes accessed | tf_op | source)
XLA Modules:
  0.0 176.5 jit_solution(8683430393393657667)
XLA Ops:
  0.7 1.8 %pack.1 = (f32[256,128]{1,0:T(8,128)}, s32[1,512]{1,0:T(1,128)}) custom-call(s32[2]{0:T(128)S(1)} %pad_add_fusion.at, s32[4,8]{1,0:T(4,128)} %bitcast.59, s32[1,512]{1,0:T(1,128)} %bitcast.79, s32[1,512]{1,0:T(1,128)} %bitcast.88, s32[1,512]{1,0:T(1,128)} %bitcast.81, f32[1,512]{1,0:T(1,128)} %bitcast.83, f32[8,128]{1,0:T(8,128)} %bitcast.86), custom_call_target="tpu_custom_call" | custom-call | flops 1000000 | bytes 1000000 | tf_op jit(solution)/shard_map/pack/pallas_call | solution.py:56
  2.5 10.2 %all-to-all-start = ((f32[128,2,128]{2,1,0:T(2,128)}), f32[128,2,128]{2,1,0:T(2,128)S(1)}, u32[]{:S(2)}, u32[]{:S(2)}) async-start(f32[128,2,128]{2,1,0:T(2,128)} %bitcast.76), calls=%async_computation | async-start | bytes 262144 | tf_op jit(solution)/shard_map/all_to_all | solution.py:856
  12.8 1.9 %edges.1 = (f32[128,256]{1,0:T(8,128)}, f32[128,256]{1,0:T(8,128)}, f32[32,256]{1,0:T(8,128)}, f32[32,256]{1,0:T(8,128)}) custom-call(s32[2]{0:T(128)S(1)} %pad_add_fusion.at, f32[16,64,256]{2,1,0:T(8,128)} %p_after.1, f32[16,64,256]{2,1,0:T(8,128)} %p_after.1, f32[16,64,256]{2,1,0:T(8,128)} %p_after.1, f32[16,64,256]{2,1,0:T(8,128)} %p_after.1, ...), custom_call_target="tpu_custom_call" | custom-call | tf_op jit(solution)/shard_map/edges/pallas_call | solution.py:547
  14.7 1.5 collective-permute-start.2
  16.2 3.8 %collective-permute-start.3 = (f32[32,256]{1,0:T(8,128)}, f32[32,256]{1,0:T(8,128)S(1)}, u32[]{:S(2)}, u32[]{:S(2)}) collective-permute-start(f32[32,256]{1,0:T(8,128)} %get-tuple-element.113), channel_id=1, source_target_pairs={{1,2},{3,4},{5,6},{7,8},{9,10},{11,12},{13,14},{2,1},{4,3},{6,5},{... | collective-permute-start | bytes 98312 | tf_op jit(solution)/shard_map/ppermute | solution.py:787
  20.1 0.7 collective-permute-start.1
  20.8 1.4 all-to-all-done
  22.2 5.9 %first.1 = (f32[256,128]{1,0:T(8,128)}, f32[128,128]{1,0:T(8,128)}, f32[128,128]{1,0:T(8,128)}, f32[128,128]{1,0:T(8,128)}, f32[128,128]{1,0:T(8,128)}) custom-call(s32[2]{0:T(128)S(1)} %pad_add_fusion.at, s32[4,8]{1,0:T(4,128)S(1)} %bitcast.60, f32[32,128,128]{2,1,0:T(8,128)} %bitcast.34, f32[1024,256]{1,0:T(8,128)} %bitcast.68, f32[256,128]{1,0:T(8,128)S(1)} %bitcast.48, ...), custom_call_target="tpu_custom_call" | custom-call | flops 2000000000 | bytes 1000000 | tf_op jit(solution)/shard_map/first/pallas_call | solution.py:56
  28.1 9.7 %all-to-all-start.1 = ((f32[128,2,128]{2,1,0:T(2,128)}), f32[128,2,128]{2,1,0:T(2,128)S(1)}, u32[]{:S(2)}, u32[]{:S(2)}) async-start(f32[128,2,128]{2,1,0:T(2,128)} %bitcast.75), calls=%async_computation.1 | async-start | bytes 262144 | tf_op jit(solution)/shard_map/all_to_all | solution.py:879
  37.8 6.2 %sweep.4 = (f32[16,64,256]{2,1,0:T(8,128)}, f32[16,64,256]{2,1,0:T(8,128)}, f32[16,64,256]{2,1,0:T(8,128)}, f32[64,256]{1,0:T(8,128)}, f32[64,256]{1,0:T(8,128)}, /*index=5*/f32[16,256]{1,0:T(8,128)}, f32[16,256]{1,0:T(8,128)}) custom-call(s32[2]{0:T(128)S(1)} %pad_add_fusion.at, f32[128,256]{1,0:T(8,128)S(1)} %collective-permute-done.xa.cxa, ...), custom_call_target="tpu_custom_call" | custom-call | flops 6000000 | bytes 8388608 | tf_op jit(solution)/shard_map/sweep/pallas_call | solution.py:760
  44.0 3.2 %all-to-all-done.1 = f32[128,2,128]{2,1,0:T(2,128)S(1)} async-done(((f32[128,2,128]{2,1,0:T(2,128)}), f32[128,2,128]{2,1,0:T(2,128)S(1)}, u32[]{:S(2)}, u32[]{:S(2)}) %all-to-all-start.1) | async-done | bytes 131104 | tf_op jit(solution)/shard_map/all_to_all | solution.py:879
  47.1 0.7 sums.1
  47.8 6.6 %all-to-all-start.2 = ((f32[128,2,128]{2,1,0:T(2,128)}), f32[128,2,128]{2,1,0:T(2,128)S(1)}, u32[]{:S(2)}, u32[]{:S(2)}) async-start(f32[128,2,128]{2,1,0:T(2,128)} %bitcast.72), calls=%async_computation.2 | async-start | bytes 262144 | tf_op jit(solution)/shard_map/all_to_all | solution.py:887
  55.3 1.6 collective-permute-start.6
  56.9 3.8 %collective-permute-start.7 = (f32[16,256]{1,0:T(8,128)}, f32[16,256]{1,0:T(8,128)S(1)}, u32[]{:S(2)}, u32[]{:S(2)}) collective-permute-start(f32[16,256]{1,0:T(8,128)} %get-tuple-element.128), channel_id=1, source_target_pairs={{1,2},{3,4},{5,6},{7,8},{9,10},{11,12},{13,14},{2,1},{4,3},{6,5},{... | collective-permute-start | bytes 49160 | tf_op jit(solution)/shard_map/ppermute | solution.py:787
  60.7 3.1 %all-to-all-done.2 = f32[128,2,128]{2,1,0:T(2,128)S(1)} async-done(((f32[128,2,128]{2,1,0:T(2,128)}), f32[128,2,128]{2,1,0:T(2,128)S(1)}, u32[]{:S(2)}, u32[]{:S(2)}) %all-to-all-start.2) | async-done | bytes 131104 | tf_op jit(solution)/shard_map/all_to_all | solution.py:887
  63.8 1.7 start.1
  65.5 6.1 %all-to-all-start.3 = ((f32[16,40,128]{2,1,0:T(8,128)}), f32[16,40,128]{2,1,0:T(8,128)S(1)}, u32[]{:S(2)}, u32[]{:S(2)}) async-start(f32[16,40,128]{2,1,0:T(8,128)} %bitcast.73), calls=%async_computation.3 | async-start | bytes 655360 | tf_op jit(solution)/shard_map/all_to_all | solution.py:906
  71.5 7.0 %sweep.5 = (f32[16,64,256]{2,1,0:T(8,128)}, f32[128,128]{1,0:T(8,128)}, f32[256,128]{1,0:T(8,128)}, f32[64,256]{1,0:T(8,128)}, f32[64,256]{1,0:T(8,128)}, /*index=5*/f32[16,256]{1,0:T(8,128)}, f32[16,256]{1,0:T(8,128)}) custom-call(s32[2]{0:T(128)S(1)} %pad_add_fusion.at, f32[64,256]{1,0:T(8,128)S(1)} %collective-permute-done.4.xa, ...), custom_call_target="tpu_custom_call" | custom-call | flops 6000000 | bytes 8388608 | tf_op jit(solution)/shard_map/sweep/pallas_call | solution.py:760
  78.6 1.5 all-to-all-done.3
  80.1 4.7 %all-to-all-start.4 = ((f32[8,32,128]{2,1,0:T(8,128)}), f32[8,32,128]{2,1,0:T(8,128)S(1)}, u32[]{:S(2)}, u32[]{:S(2)}) async-start(f32[8,32,128]{2,1,0:T(8,128)} %bitcast.77), calls=%async_computation.4 | async-start | bytes 262144 | tf_op jit(solution)/shard_map/all_to_all | solution.py:922
  85.0 5.9 %all-to-all-done.4 = f32[8,32,128]{2,1,0:T(8,128)S(1)} async-done(((f32[8,32,128]{2,1,0:T(8,128)}), f32[8,32,128]{2,1,0:T(8,128)S(1)}, u32[]{:S(2)}, u32[]{:S(2)}) %all-to-all-start.4) | async-done | bytes 131104 | tf_op jit(solution)/shard_map/all_to_all | solution.py:922
  91.0 2.6 %step.5 = (f32[128,128]{1,0:T(8,128)}, f32[128,128]{1,0:T(8,128)}, f32[128,128]{1,0:T(8,128)}, f32[1024,128]{1,0:T(8,128)}) custom-call(s32[2]{0:T(128)S(1)} %pad_add_fusion.at, s32[4,8]{1,0:T(4,128)S(1)} %bitcast.62, f32[32,128,128]{2,1,0:T(8,128)S(1)} %bitcast.36, f32[640,128]{1,0:T(8,128)S(1)} %bitcast.44, bf16[128,512]{1,0:T(8,128)(2,1)S(1)} %columns.1.chosen, ...), custom_call_target="tpu_custom_call" | custom-call | flops 1000000 | bytes 1000000 | tf_op jit(solution)/shard_map/step/pallas_call | solution.py:56
  93.5 7.2 %all-to-all-start.5 = ((f32[16,64,128]{2,1,0:T(8,128)}), f32[16,64,128]{2,1,0:T(8,128)S(1)}, u32[]{:S(2)}, u32[]{:S(2)}) async-start(f32[16,64,128]{2,1,0:T(8,128)} %bitcast.71), calls=%async_computation.5 | async-start | bytes 1048576 | tf_op jit(solution)/shard_map/all_to_all | solution.py:953
  100.9 0.7 collective-permute-start.9
  102.1 7.5 %all-to-all-done.5 = f32[16,64,128]{2,1,0:T(8,128)S(1)} async-done(((f32[16,64,128]{2,1,0:T(8,128)}), f32[16,64,128]{2,1,0:T(8,128)S(1)}, u32[]{:S(2)}, u32[]{:S(2)}) %all-to-all-start.5) | async-done | bytes 524320 | tf_op jit(solution)/shard_map/all_to_all | solution.py:953
  109.6 2.6 %step.6 = (f32[128,128]{1,0:T(8,128)}, f32[128,128]{1,0:T(8,128)}, f32[128,128]{1,0:T(8,128)}, f32[1152,128]{1,0:T(8,128)}, f32[16,128]{1,0:T(8,128)}, /*index=5*/f32[128,128]{1,0:T(8,128)}) custom-call(s32[2]{0:T(128)S(1)} %pad_add_fusion.at, s32[4,8]{1,0:T(4,128)S(1)} %bitcast.63, f32[32,128,128]{2,1,0:T(8,128)S(1)} %bitcast.37, f32[1024,128]{1,0:T(8,128)S(1)} %bitcast.43, ...), custom_call_target="tpu_custom_call" | custom-call | flops 1000000 | bytes 1000000 | tf_op jit(solution)/shard_map/step/pallas_call | solution.py:56
  112.2 6.0 %all-to-all-start.6 = ((f32[16,72,128]{2,1,0:T(8,128)}), f32[16,72,128]{2,1,0:T(8,128)S(1)}, u32[]{:S(2)}, u32[]{:S(2)}) async-start(f32[16,72,128]{2,1,0:T(8,128)} %bitcast.69), calls=%async_computation.6 | async-start | bytes 1179648 | tf_op jit(solution)/shard_map/all_to_all | solution.py:958
  118.2 0.7 constant_dynamic-update-slice_fusion.1
  118.9 0.7 collective-permute-done.10.rest_0_
  119.6 1.2 collective-permute-start.13
  120.8 1.5 collective-permute-start.12
  122.2 1.5 collective-permute-start.11
  123.7 0.9 collective-permute-done.13.rest_3_
  124.5 1.5 collective-permute-done.12.rest_2_
  126.0 1.2 all-to-all-done.6
  127.2 2.5 %step.7 = (f32[128,128]{1,0:T(8,128)}, f32[128,128]{1,0:T(8,128)}, f32[128,128]{1,0:T(8,128)}, f32[640,128]{1,0:T(8,128)}, f32[16,256]{1,0:T(8,128)}, /*index=5*/f32[16,256]{1,0:T(8,128)}) custom-call(s32[2]{0:T(128)S(1)} %pad_add_fusion.at, s32[4,8]{1,0:T(4,128)S(1)} %bitcast.64, f32[32,128,128]{2,1,0:T(8,128)S(1)} %bitcast.38, f32[1152,128]{1,0:T(8,128)S(1)} %bitcast.41, ...), custom_call_target="tpu_custom_call" | custom-call | flops 1000000 | bytes 1000000 | tf_op jit(solution)/shard_map/step/pallas_call | solution.py:56
  129.7 6.1 %all-to-all-start.7 = ((f32[16,40,128]{2,1,0:T(8,128)}), f32[16,40,128]{2,1,0:T(8,128)S(1)}, u32[]{:S(2)}, u32[]{:S(2)}) async-start(f32[16,40,128]{2,1,0:T(8,128)} %bitcast.74), calls=%async_computation.7 | async-start | bytes 655360 | tf_op jit(solution)/shard_map/all_to_all | solution.py:968
  135.7 6.6 %sweep.6 = (f32[16,64,256]{2,1,0:T(8,128)}, f32[16,64,256]{2,1,0:T(8,128)}, f32[64,256]{1,0:T(8,128)}, f32[64,256]{1,0:T(8,128)}, f32[16,256]{1,0:T(8,128)}, /*index=5*/f32[16,256]{1,0:T(8,128)}) custom-call(s32[2]{0:T(128)S(1)} %pad_add_fusion.at, f32[64,256]{1,0:T(8,128)S(1)} %collective-permute-done.8.xa, f32[64,256]{1,0:T(8,128)S(1)} %collective-permute-done.9.xb, ...), custom_call_target="tpu_custom_call" | custom-call | flops 6000000 | bytes 8388608 | tf_op jit(solution)/shard_map/sweep/pallas_call | solution.py:760
  142.8 2.6 %step.8 = (f32[128,128]{1,0:T(8,128)}, f32[128,128]{1,0:T(8,128)}, f32[128,128]{1,0:T(8,128)}, f32[1152,128]{1,0:T(8,128)}) custom-call(s32[2]{0:T(128)S(1)} %pad_add_fusion.at, s32[4,8]{1,0:T(4,128)S(1)} %bitcast.65, f32[32,128,128]{2,1,0:T(8,128)S(1)} %bitcast.39, f32[640,128]{1,0:T(8,128)S(1)} %bitcast.45, bf16[128,512]{1,0:T(8,128)(2,1)S(1)} %columns.1.chosen, ...), custom_call_target="tpu_custom_call" | custom-call | flops 1000000 | bytes 1000000 | tf_op jit(solution)/shard_map/step/pallas_call | solution.py:56
  145.4 6.9 %all-to-all-start.8 = ((f32[16,72,128]{2,1,0:T(8,128)}), f32[16,72,128]{2,1,0:T(8,128)S(1)}, u32[]{:S(2)}, u32[]{:S(2)}) async-start(f32[16,72,128]{2,1,0:T(8,128)} %bitcast.70), calls=%async_computation.8 | async-start | bytes 1179648 | tf_op jit(solution)/shard_map/all_to_all | solution.py:985
  153.0 1.9 %home.1 = f32[1,512]{1,0:T(1,128)} custom-call(f32[128,128]{1,0:T(8,128)} %get-tuple-element.187.got, s32[1,512]{1,0:T(1,128)} %bitcast.80, s32[1,512]{1,0:T(1,128)} %get-tuple-element.188.slot, s32[1,512]{1,0:T(1,128)} %bitcast.82, f32[1,512]{1,0:T(1,128)} %bitcast.84, f32[128,128]{1,0:T(8,128)} %get-tuple-element.171.rest_3_.rest_0_.x), custom_call_target="tpu_custom_call" | custom-call | flops 1000000 | bytes 1000000 | tf_op jit(solution)/shard_map/home/pallas_call | solution.py:56
  154.9 6.0 %all-to-all-done.8 = f32[16,72,128]{2,1,0:T(8,128)S(1)} async-done(((f32[16,72,128]{2,1,0:T(8,128)}), f32[16,72,128]{2,1,0:T(8,128)S(1)}, u32[]{:S(2)}, u32[]{:S(2)}) %all-to-all-start.8) | async-done | bytes 589856 | tf_op jit(solution)/shard_map/all_to_all | solution.py:985
  160.9 2.3 %step.9 = (f32[128,128]{1,0:T(8,128)}, f32[128,128]{1,0:T(8,128)}, f32[128,128]{1,0:T(8,128)}, f32[128,128]{1,0:T(8,128)}, f32[16,256]{1,0:T(8,128)}, /*index=5*/f32[16,256]{1,0:T(8,128)}) custom-call(s32[2]{0:T(128)S(1)} %pad_add_fusion.at, s32[4,8]{1,0:T(4,128)S(1)} %bitcast.66, f32[32,128,128]{2,1,0:T(8,128)S(1)} %bitcast.40, f32[1152,128]{1,0:T(8,128)S(1)} %bitcast.42, ...), custom_call_target="tpu_custom_call" | custom-call | flops 1000000 | bytes 1000000 | tf_op jit(solution)/shard_map/step/pallas_call | solution.py:56
  163.2 5.4 %all-to-all-start.9 = ((f32[16,8,128]{2,1,0:T(8,128)}), f32[16,8,128]{2,1,0:T(8,128)S(1)}, u32[]{:S(2)}, u32[]{:S(2)}) async-start(f32[16,8,128]{2,1,0:T(8,128)} %bitcast.78), calls=%async_computation.9 | async-start | bytes 131072 | tf_op jit(solution)/shard_map/all_to_all | solution.py:996
  168.6 4.2 %sweep.7 = f32[16,64,256]{2,1,0:T(8,128)} custom-call(s32[2]{0:T(128)S(1)} %pad_add_fusion.at, f32[64,256]{1,0:T(8,128)S(1)} %collective-permute-done.14.xa, f32[64,256]{1,0:T(8,128)S(1)} %collective-permute-done.15.xb, f32[16,256]{1,0:T(8,128)} %get-tuple-element.197.ya, f32[16,256]{1,0:T(8,128)} %get-tuple-element.198.yb, ...), custom_call_target="tpu_custom_call" | custom-call | flops 6000000 | bytes 8388608 | tf_op jit(solution)/shard_map/sweep/pallas_call | solution.py:760
  172.7 2.2 %all-to-all-done.9 = f32[16,8,128]{2,1,0:T(8,128)S(1)} async-done(((f32[16,8,128]{2,1,0:T(8,128)}), f32[16,8,128]{2,1,0:T(8,128)S(1)}, u32[]{:S(2)}, u32[]{:S(2)}) %all-to-all-start.9) | async-done | bytes 65568 | tf_op jit(solution)/shard_map/all_to_all | solution.py:996
  174.9 1.6 final.1
  (40 shorter events, 3.1 us)
Async XLA Ops:
  2.5 19.6 %all-to-all-start = ((f32[128,2,128]{2,1,0:T(2,128)}), f32[128,2,128]{2,1,0:T(2,128)S(1)}, u32[]{:S(2)}, u32[]{:S(2)}) async-start(f32[128,2,128]{2,1,0:T(2,128)} %bitcast.76), calls=%async_computation | async-start | bytes 262144 | tf_op jit(solution)/shard_map/all_to_all | solution.py:856
  12.8 9.4 %copy-start.1 = (f32[1024]{0:T(1024)S(1)}, f32[1024]{0:T(1024)}, u32[]{:S(2)}) copy-start(f32[1024]{0:T(1024)} %param.23) | copy-start | bytes 12292
  12.8 9.4 %copy-start.2 = (s32[8,4]{0,1:T(4,128)S(1)}, s32[8,4]{0,1:T(4,128)}, u32[]{:S(2)}) copy-start(s32[8,4]{0,1:T(4,128)} %param.22) | copy-start | bytes 388
  12.8 9.4 %copy-start.3 = (f32[1024]{0:T(1024)S(1)}, f32[1024]{0:T(1024)}, u32[]{:S(2)}) copy-start(f32[1024]{0:T(1024)} %param.24) | copy-start | bytes 12292
  14.7 13.4 %collective-permute-start.2 = (f32[32,256]{1,0:T(8,128)}, f32[32,256]{1,0:T(8,128)S(1)}, u32[]{:S(2)}, u32[]{:S(2)}) collective-permute-start(f32[32,256]{1,0:T(8,128)} %get-tuple-element.112), channel_id=1, source_target_pairs={{0,1},{2,3},{4,5},{6,7},{8,9},{10,11},{12,13},{14,15},{1,0},{3,2},... | collective-permute-start | bytes 98312 | tf_op jit(solution)/shard_map/ppermute | solution.py:787
  16.2 11.9 %collective-permute-start.3 = (f32[32,256]{1,0:T(8,128)}, f32[32,256]{1,0:T(8,128)S(1)}, u32[]{:S(2)}, u32[]{:S(2)}) collective-permute-start(f32[32,256]{1,0:T(8,128)} %get-tuple-element.113), channel_id=1, source_target_pairs={{1,2},{3,4},{5,6},{7,8},{9,10},{11,12},{13,14},{2,1},{4,3},{6,5},{... | collective-permute-start | bytes 98312 | tf_op jit(solution)/shard_map/ppermute | solution.py:787
  20.0 8.1 %collective-permute-start = (f32[128,256]{1,0:T(8,128)}, f32[128,256]{1,0:T(8,128)S(1)}, u32[]{:S(2)}, u32[]{:S(2)}) collective-permute-start(f32[128,256]{1,0:T(8,128)} %get-tuple-element.110), channel_id=1, source_target_pairs={{0,16},{32,48},{64,80},{96,112},{16,0},{48,32},{80,64},{112,96},{1... | collective-permute-start | bytes 393224 | tf_op jit(solution)/shard_map/ppermute | solution.py:787
  20.1 8.0 %collective-permute-start.1 = (f32[128,256]{1,0:T(8,128)}, f32[128,256]{1,0:T(8,128)S(1)}, u32[]{:S(2)}, u32[]{:S(2)}) collective-permute-start(f32[128,256]{1,0:T(8,128)} %get-tuple-element.111), channel_id=1, source_target_pairs={{16,32},{48,64},{80,96},{32,16},{64,48},{96,80},{17,33},{49,65},{8... | collective-permute-start | bytes 393224 | tf_op jit(solution)/shard_map/ppermute | solution.py:787
  28.1 19.0 %all-to-all-start.1 = ((f32[128,2,128]{2,1,0:T(2,128)}), f32[128,2,128]{2,1,0:T(2,128)S(1)}, u32[]{:S(2)}, u32[]{:S(2)}) async-start(f32[128,2,128]{2,1,0:T(2,128)} %bitcast.75), calls=%async_computation.1 | async-start | bytes 262144 | tf_op jit(solution)/shard_map/all_to_all | solution.py:879
  37.8 26.0 %copy-start = (f32[8,4,128,128]{3,2,1,0:T(8,128)S(1)}, f32[8,4,128,128]{3,2,1,0:T(8,128)}, u32[]{:S(2)}) copy-start(f32[8,4,128,128]{3,2,1,0:T(8,128)} %param.21) | copy-start | bytes 6291460
  47.8 16.0 %all-to-all-start.2 = ((f32[128,2,128]{2,1,0:T(2,128)}), f32[128,2,128]{2,1,0:T(2,128)S(1)}, u32[]{:S(2)}, u32[]{:S(2)}) async-start(f32[128,2,128]{2,1,0:T(2,128)} %bitcast.72), calls=%async_computation.2 | async-start | bytes 262144 | tf_op jit(solution)/shard_map/all_to_all | solution.py:887
  54.4 11.0 %collective-permute-start.4 = (f32[64,256]{1,0:T(8,128)}, f32[64,256]{1,0:T(8,128)S(1)}, u32[]{:S(2)}, u32[]{:S(2)}) collective-permute-start(f32[64,256]{1,0:T(8,128)} %get-tuple-element.125), channel_id=1, source_target_pairs={{0,16},{32,48},{64,80},{96,112},{16,0},{48,32},{80,64},{112,96},{1... | collective-permute-start | bytes 196616 | tf_op jit(solution)/shard_map/ppermute | solution.py:787
  54.7 10.8 %collective-permute-start.5 = (f32[64,256]{1,0:T(8,128)}, f32[64,256]{1,0:T(8,128)S(1)}, u32[]{:S(2)}, u32[]{:S(2)}) collective-permute-start(f32[64,256]{1,0:T(8,128)} %get-tuple-element.126), channel_id=1, source_target_pairs={{16,32},{48,64},{80,96},{32,16},{64,48},{96,80},{17,33},{49,65},{8... | collective-permute-start | bytes 196616 | tf_op jit(solution)/shard_map/ppermute | solution.py:787
  55.3 10.2 %collective-permute-start.6 = (f32[16,256]{1,0:T(8,128)}, f32[16,256]{1,0:T(8,128)S(1)}, u32[]{:S(2)}, u32[]{:S(2)}) collective-permute-start(f32[16,256]{1,0:T(8,128)} %get-tuple-element.127), channel_id=1, source_target_pairs={{0,1},{2,3},{4,5},{6,7},{8,9},{10,11},{12,13},{14,15},{1,0},{3,2},... | collective-permute-start | bytes 49160 | tf_op jit(solution)/shard_map/ppermute | solution.py:787
  56.9 8.5 %collective-permute-start.7 = (f32[16,256]{1,0:T(8,128)}, f32[16,256]{1,0:T(8,128)S(1)}, u32[]{:S(2)}, u32[]{:S(2)}) collective-permute-start(f32[16,256]{1,0:T(8,128)} %get-tuple-element.128), channel_id=1, source_target_pairs={{1,2},{3,4},{5,6},{7,8},{9,10},{11,12},{13,14},{2,1},{4,3},{6,5},{... | collective-permute-start | bytes 49160 | tf_op jit(solution)/shard_map/ppermute | solution.py:787
  65.5 14.6 %all-to-all-start.3 = ((f32[16,40,128]{2,1,0:T(8,128)}), f32[16,40,128]{2,1,0:T(8,128)S(1)}, u32[]{:S(2)}, u32[]{:S(2)}) async-start(f32[16,40,128]{2,1,0:T(8,128)} %bitcast.73), calls=%async_computation.3 | async-start | bytes 655360 | tf_op jit(solution)/shard_map/all_to_all | solution.py:906
  78.6 22.2 %copy-start.5 = (f32[64,256]{1,0:T(8,128)S(1)}, f32[64,256]{1,0:T(8,128)}, u32[]{:S(2)}) copy-start(f32[64,256]{1,0:T(8,128)} %get-tuple-element.150) | copy-start | bytes 196612
  78.6 22.3 %copy-start.4 = (f32[64,256]{1,0:T(8,128)S(1)}, f32[64,256]{1,0:T(8,128)}, u32[]{:S(2)}) copy-start(f32[64,256]{1,0:T(8,128)} %get-tuple-element.151) | copy-start | bytes 196612
  80.1 10.8 %all-to-all-start.4 = ((f32[8,32,128]{2,1,0:T(8,128)}), f32[8,32,128]{2,1,0:T(8,128)S(1)}, u32[]{:S(2)}, u32[]{:S(2)}) async-start(f32[8,32,128]{2,1,0:T(8,128)} %bitcast.77), calls=%async_computation.4 | async-start | bytes 262144 | tf_op jit(solution)/shard_map/all_to_all | solution.py:922
  93.5 16.0 %all-to-all-start.5 = ((f32[16,64,128]{2,1,0:T(8,128)}), f32[16,64,128]{2,1,0:T(8,128)S(1)}, u32[]{:S(2)}, u32[]{:S(2)}) async-start(f32[16,64,128]{2,1,0:T(8,128)} %bitcast.71), calls=%async_computation.5 | async-start | bytes 1048576 | tf_op jit(solution)/shard_map/all_to_all | solution.py:953
  100.8 1.3 collective-permute-start.8
  100.9 1.2 collective-permute-start.9
  112.2 15.0 %all-to-all-start.6 = ((f32[16,72,128]{2,1,0:T(8,128)}), f32[16,72,128]{2,1,0:T(8,128)S(1)}, u32[]{:S(2)}, u32[]{:S(2)}) async-start(f32[16,72,128]{2,1,0:T(8,128)} %bitcast.69), calls=%async_computation.6 | async-start | bytes 1179648 | tf_op jit(solution)/shard_map/all_to_all | solution.py:958
  118.2 1.4 collective-permute-start.10
  119.6 4.9 %collective-permute-start.13 = (f32[32,128]{1,0:T(8,128)S(1)}, f32[32,128]{1,0:T(8,128)S(1)}, u32[]{:S(2)}, u32[]{:S(2)}) collective-permute-start(f32[32,128]{1,0:T(8,128)S(1)} %constant_dynamic-update-slice_fusion), channel_id=1, source_target_pairs={{0,96},{16,112},{32,64},{48,80},{64,32},{80,48},{96,0},{112,16},{1... | collective-permute-start | bytes 49160 | tf_op jit(solution)/shard_map/ppermute | solution.py:962
  120.8 5.2 %collective-permute-start.12 = (f32[32,128]{1,0:T(8,128)S(1)}, f32[32,128]{1,0:T(8,128)S(1)}, u32[]{:S(2)}, u32[]{:S(2)}) collective-permute-start(f32[32,128]{1,0:T(8,128)S(1)} %constant_dynamic-update-slice_fusion), channel_id=1, source_target_pairs={{0,64},{16,80},{32,96},{48,112},{64,0},{80,16},{96,32},{112,48},{1... | collective-permute-start | bytes 49160 | tf_op jit(solution)/shard_map/ppermute | solution.py:962
  122.2 3.8 %collective-permute-start.11 = (f32[32,128]{1,0:T(8,128)S(1)}, f32[32,128]{1,0:T(8,128)S(1)}, u32[]{:S(2)}, u32[]{:S(2)}) collective-permute-start(f32[32,128]{1,0:T(8,128)S(1)} %constant_dynamic-update-slice_fusion), channel_id=1, source_target_pairs={{0,32},{16,48},{32,0},{48,16},{64,96},{80,112},{96,64},{112,80},{1... | collective-permute-start | bytes 49160 | tf_op jit(solution)/shard_map/ppermute | solution.py:962
  129.7 13.1 %all-to-all-start.7 = ((f32[16,40,128]{2,1,0:T(8,128)}), f32[16,40,128]{2,1,0:T(8,128)S(1)}, u32[]{:S(2)}, u32[]{:S(2)}) async-start(f32[16,40,128]{2,1,0:T(8,128)} %bitcast.74), calls=%async_computation.7 | async-start | bytes 655360 | tf_op jit(solution)/shard_map/all_to_all | solution.py:968
  142.4 9.9 %copy-start.7 = (f32[64,256]{1,0:T(8,128)S(1)}, f32[64,256]{1,0:T(8,128)}, u32[]{:S(2)}) copy-start(f32[64,256]{1,0:T(8,128)} %get-tuple-element.189) | copy-start | bytes 196612
  142.4 10.0 %copy-start.6 = (f32[64,256]{1,0:T(8,128)S(1)}, f32[64,256]{1,0:T(8,128)}, u32[]{:S(2)}) copy-start(f32[64,256]{1,0:T(8,128)} %get-tuple-element.190) | copy-start | bytes 196612
  145.4 15.5 %all-to-all-start.8 = ((f32[16,72,128]{2,1,0:T(8,128)}), f32[16,72,128]{2,1,0:T(8,128)S(1)}, u32[]{:S(2)}, u32[]{:S(2)}) async-start(f32[16,72,128]{2,1,0:T(8,128)} %bitcast.70), calls=%async_computation.8 | async-start | bytes 1179648 | tf_op jit(solution)/shard_map/all_to_all | solution.py:985
  152.3 2.6 %collective-permute-start.14 = (f32[64,256]{1,0:T(8,128)S(1)}, f32[64,256]{1,0:T(8,128)S(1)}, u32[]{:S(2)}, u32[]{:S(2)}) collective-permute-start(f32[64,256]{1,0:T(8,128)S(1)} %copy-done.7), channel_id=1, source_target_pairs={{0,16},{32,48},{64,80},{96,112},{16,0},{48,32},{80,64},{112,96},{1... | collective-permute-start | bytes 196616 | tf_op jit(solution)/shard_map/ppermute | solution.py:787
  152.4 2.5 %collective-permute-start.15 = (f32[64,256]{1,0:T(8,128)S(1)}, f32[64,256]{1,0:T(8,128)S(1)}, u32[]{:S(2)}, u32[]{:S(2)}) collective-permute-start(f32[64,256]{1,0:T(8,128)S(1)} %copy-done.6), channel_id=1, source_target_pairs={{16,32},{48,64},{80,96},{32,16},{64,48},{96,80},{17,33},{49,65},{8... | collective-permute-start | bytes 196616 | tf_op jit(solution)/shard_map/ppermute | solution.py:787
  163.2 11.7 %all-to-all-start.9 = ((f32[16,8,128]{2,1,0:T(8,128)}), f32[16,8,128]{2,1,0:T(8,128)S(1)}, u32[]{:S(2)}, u32[]{:S(2)}) async-start(f32[16,8,128]{2,1,0:T(8,128)} %bitcast.78), calls=%async_computation.9 | async-start | bytes 131072 | tf_op jit(solution)/shard_map/all_to_all | solution.py:996
